TPU v7x, 32 devices: a whole 2x2x4 slice. The times are simulated.
32 devices in a mesh: seq: 4 (over z), fsdp: 8 (over y, x, core).
Axes of the slice: x: 2, y: 2, z: 4, core: 2. Of those that a mesh axis runs over, the one named last changes fastest.
Arguments:
- video: bfloat16 [8, 4096, 1152], P('fsdp', 'seq'), may hold values from -4 to 4
- context: bfloat16 [8, 120, 1152], P('fsdp'), may hold values from -4 to 4
- modulation: float32 [8, 1, 6, 1152], P('fsdp'), may hold values from -0.6 to 0.6
- adapter_index: int32 [8], P('fsdp'), may hold values from 0 to 7
- cotangent: bfloat16 [8, 4096, 1152], P('fsdp', 'seq'), may hold values from -6 to 6
- qkv_weights: bfloat16 [1, 9, 1152, 1152], P(None, None, 'fsdp'), may hold values from -0.1875 to 0.1875
- out_weights: bfloat16 [1, 3, 1152, 1152], P(None, None, 'fsdp'), may hold values from -0.375 to 0.375
- ffn_up: bfloat16 [1, 1152, 4608], P(None, 'fsdp'), may hold values from -0.1875 to 0.1875
- ffn_down: bfloat16 [1, 4608, 1152], P(None, 'fsdp'), may hold values from -0.09375 to 0.09375
- adapt_wide: bfloat16 [1, 26, 8, 16, 1152], P(None, None, None, None, 'fsdp'), may hold values from -0.375 to 0.375
- adapt_ff: bfloat16 [1, 2, 8, 16, 4608], P(None, None, None, None, 'fsdp'), may hold values from -0.1875 to 0.1875
Outputs:
- output: bfloat16 [8, 4096, 1152], P('fsdp', 'seq')
- input_grad: bfloat16 [8, 4096, 1152], P('fsdp', 'seq')
- adapt_wide_grad: float32 [1, 26, 8, 16, 1152], P(None, None, None, None, 'fsdp')
- adapt_ff_grad: float32 [1, 2, 8, 16, 4608], P(None, None, None, None, 'fsdp')
Inputs may be any that keep to these rules, and one draw needn't show every extreme that they name: `adapter_index`: each clip's adapter.
All inputs are finite; a program needn't handle non-finite values.
Results may differ from a plain program's by a relative error of at most 0.022.
Values may be sent and summed in bfloat16 or wider, within the bound.
No kernel may reach another device: no remote copies, remote signals or barrier semaphores. Data moves between devices by JAX's collectives and lax.ppermute only.
A program may use at most 448 MiB of HBM per device.

v0:
```python
import jax
import jax.numpy as jnp
from jax import lax
from jax.sharding import PartitionSpec as P

HEAD_DIM = 72
FRAMES = 16
SPATIAL = 256


HIGHEST = lax.Precision.HIGHEST


def for_sending(shard):

    def short(part):
        return part.astype(jnp.bfloat16) if part.dtype == jnp.float32 else part

    return jax.tree.map(short, shard)


def fetch_layer(qkv_part, out_part, up_part, down_part, wide_part, narrow_part):
    return (
        lax.all_gather(for_sending(qkv_part), "fsdp", axis=1, tiled=True).astype(qkv_part.dtype),
        lax.all_gather(for_sending(out_part), "fsdp", axis=1, tiled=True).astype(out_part.dtype),
        lax.all_gather(for_sending(up_part), "fsdp", axis=0, tiled=True).astype(up_part.dtype),
        lax.all_gather(for_sending(down_part), "fsdp", axis=0, tiled=True).astype(down_part.dtype),
        lax.all_gather(for_sending(wide_part), "fsdp", axis=3, tiled=True).astype(wide_part.dtype),
        lax.all_gather(for_sending(narrow_part), "fsdp", axis=3, tiled=True).astype(
            narrow_part.dtype
        ),
    )


def fetch_again(qkv_part, out_part, up_part, down_part, wide_part, narrow_part):
    return (
        lax.all_gather(for_sending(qkv_part), "fsdp", axis=1, tiled=True).astype(qkv_part.dtype),
        lax.all_gather(for_sending(out_part), "fsdp", axis=1, tiled=True).astype(out_part.dtype),
        lax.all_gather(for_sending(up_part), "fsdp", axis=0, tiled=True).astype(up_part.dtype),
        lax.all_gather(for_sending(down_part), "fsdp", axis=0, tiled=True).astype(down_part.dtype),
        lax.all_gather(for_sending(wide_part), "fsdp", axis=3, tiled=True).astype(wide_part.dtype),
        lax.all_gather(for_sending(narrow_part), "fsdp", axis=3, tiled=True).astype(
            narrow_part.dtype
        ),
    )


def regroup(queries, keys_in, values):
    return (
        lax.all_to_all(for_sending(queries), "seq", split_axis=2, concat_axis=1, tiled=True).astype(
            queries.dtype
        ),
        lax.all_to_all(for_sending(keys_in), "seq", split_axis=2, concat_axis=1, tiled=True).astype(
            keys_in.dtype
        ),
        lax.all_to_all(for_sending(values), "seq", split_axis=2, concat_axis=1, tiled=True).astype(
            values.dtype
        ),
    )


def restore(attended):
    return jax.tree.map(
        lambda part, own: part.astype(own.dtype),
        lax.all_to_all(for_sending(attended), "seq", split_axis=1, concat_axis=2, tiled=True),
        attended,
    )


def spread_grad(grad_out):
    return jax.tree.map(
        lambda part, own: part.astype(own.dtype),
        lax.all_to_all(for_sending(grad_out), "seq", split_axis=2, concat_axis=1, tiled=True),
        grad_out,
    )


def collect_grads(grad_q, grad_k, grad_v):
    return (
        lax.all_to_all(for_sending(grad_q), "seq", split_axis=1, concat_axis=2, tiled=True).astype(
            grad_q.dtype
        ),
        lax.all_to_all(for_sending(grad_k), "seq", split_axis=1, concat_axis=2, tiled=True).astype(
            grad_k.dtype
        ),
        lax.all_to_all(for_sending(grad_v), "seq", split_axis=1, concat_axis=2, tiled=True).astype(
            grad_v.dtype
        ),
    )


def head_columns(width):
    col_width = width // lax.axis_size("seq")
    return (lax.axis_index("seq") * col_width, col_width)


def modulate(stream, shift_rows, scaling):
    average = jnp.mean(stream, -1, keepdims=True)
    centred = stream - average
    normal = centred * lax.rsqrt(jnp.mean(centred * centred, -1, keepdims=True) + 1e-06)
    return normal * (1.0 + scaling) + shift_rows


def modulate_back(stream, shift_rows, scaling, grad_out):
    primal, pullback = jax.vjp(lambda rows_in: modulate(rows_in, shift_rows, scaling), stream)
    return pullback(grad_out)[0]


def project(inputs, weight, down_map, up_map):
    main_term = jnp.einsum("cni,io->cno", inputs, weight, preferred_element_type=jnp.float32)
    rank_term = jnp.einsum(
        "cni,cri->cnr", inputs, down_map, preferred_element_type=jnp.float32
    ).astype(jnp.bfloat16)
    return (
        main_term
        + jnp.einsum("cnr,cro->cno", rank_term, up_map, preferred_element_type=jnp.float32),
        rank_term,
    )


def project_back(inputs, rank_term, weight, down_map, up_map, grad_out):
    grad_rank = jnp.einsum(
        "cno,cro->cnr", grad_out, up_map, preferred_element_type=jnp.float32
    ).astype(jnp.bfloat16)
    grad_in = jnp.einsum("cno,io->cni", grad_out, weight, preferred_element_type=jnp.float32)
    grad_in = grad_in + jnp.einsum(
        "cnr,cri->cni", grad_rank, down_map, preferred_element_type=jnp.float32
    )
    grad_down = jnp.einsum("cnr,cni->cri", grad_rank, inputs, preferred_element_type=jnp.float32)
    grad_up = jnp.einsum("cnr,cno->cro", rank_term, grad_out, preferred_element_type=jnp.float32)
    return (grad_in, grad_down, grad_up)


def context_project(context, weight, down_map, up_map, col_start, col_width):
    rank_term = jnp.einsum(
        "cni,cri->cnr", context, down_map, preferred_element_type=jnp.float32
    ).astype(jnp.bfloat16)
    columns = lax.dynamic_slice_in_dim(weight, col_start, col_width, 1)
    up_cols = lax.dynamic_slice_in_dim(up_map, col_start, col_width, 2)
    main_term = jnp.einsum("cni,io->cno", context, columns, preferred_element_type=jnp.float32)
    total = main_term + jnp.einsum(
        "cnr,cro->cno", rank_term, up_cols, preferred_element_type=jnp.float32
    )
    return (total.astype(jnp.bfloat16), rank_term)


def context_back(context, rank_term, up_map, col_start, col_width, grad_out):
    up_cols = lax.dynamic_slice_in_dim(up_map, col_start, col_width, 2).astype(jnp.float32)
    grad_up = jnp.einsum("cnr,cno->cro", rank_term.astype(jnp.float32), grad_out, precision=HIGHEST)
    grad_rank = jnp.einsum("cno,cro->cnr", grad_out, up_cols, precision=HIGHEST)
    grad_down = jnp.einsum(
        "cnr,cni->cri", grad_rank, context.astype(jnp.float32), precision=HIGHEST
    )
    full_up = lax.dynamic_update_slice_in_dim(
        jnp.zeros(up_map.shape, jnp.float32), grad_up, col_start, 2
    )
    return (grad_down, full_up)


def attend(queries, keys_in, values):
    scaling = HEAD_DIM ** (-0.5)
    scores = (
        jnp.einsum("gqhe,gkhe->ghqk", queries, keys_in, preferred_element_type=jnp.float32)
        * scaling
    )
    highest = jnp.max(scores, -1, keepdims=True)
    logsum = highest + jnp.log(jnp.sum(jnp.exp(scores - highest), -1, keepdims=True))
    weights = jnp.exp(scores - logsum).astype(jnp.bfloat16)
    result = jnp.einsum("ghqk,gkhe->gqhe", weights, values, preferred_element_type=jnp.float32)
    return (result.astype(jnp.bfloat16), logsum)


def attend_back(queries, keys_in, values, logsum, grad_out):
    scaling = HEAD_DIM ** (-0.5)
    scores = (
        jnp.einsum("gqhe,gkhe->ghqk", queries, keys_in, preferred_element_type=jnp.float32)
        * scaling
    )
    probabilities = jnp.exp(scores - logsum)
    grad_probs = jnp.einsum("gqhe,gkhe->ghqk", grad_out, values, preferred_element_type=jnp.float32)
    inner_sum = jnp.sum(probabilities * grad_probs, -1, keepdims=True)
    grad_scores = (probabilities * (grad_probs - inner_sum)).astype(jnp.bfloat16)
    grad_q = (
        jnp.einsum("ghqk,gkhe->gqhe", grad_scores, keys_in, preferred_element_type=jnp.float32)
        * scaling
    )
    grad_k = (
        jnp.einsum("ghqk,gqhe->gkhe", grad_scores, queries, preferred_element_type=jnp.float32)
        * scaling
    )
    grad_v = jnp.einsum(
        "ghqk,gqhe->gkhe",
        probabilities.astype(jnp.bfloat16),
        grad_out,
        preferred_element_type=jnp.float32,
    )
    return (grad_q, grad_k, grad_v)


def frame_view(array_in):
    head_count = array_in.shape[2] // HEAD_DIM
    return array_in.reshape(-1, SPATIAL, head_count, HEAD_DIM)


def frame_back(array_in, clip_count):
    return array_in.reshape(clip_count, -1, array_in.shape[2] * array_in.shape[3])


def time_view(array_in):
    clip_count = array_in.shape[0]
    head_count = array_in.shape[2] // HEAD_DIM
    shaped = array_in.reshape(clip_count, FRAMES, SPATIAL, head_count, HEAD_DIM).transpose(
        0, 2, 1, 3, 4
    )
    return shaped.reshape(clip_count * SPATIAL, FRAMES, head_count, HEAD_DIM)


def time_back(array_in, clip_count):
    head_count = array_in.shape[2]
    shaped = array_in.reshape(clip_count, SPATIAL, FRAMES, head_count, HEAD_DIM).transpose(
        0, 2, 1, 3, 4
    )
    return shaped.reshape(clip_count, FRAMES * SPATIAL, head_count * HEAD_DIM)


def cross_view(array_in):
    return array_in.reshape(
        array_in.shape[0], array_in.shape[1], array_in.shape[2] // HEAD_DIM, HEAD_DIM
    )


def cross_back(array_in):
    return array_in.reshape(
        array_in.shape[0], array_in.shape[1], array_in.shape[2] * array_in.shape[3]
    )


def layer_forward(stream, context, modulators, weights, choose):
    qkv_w, out_w, up_w, down_w, wide_full, narrow_full = weights
    wide_sel = jnp.einsum(
        "ca,kard->ckrd", choose, wide_full, preferred_element_type=jnp.float32
    ).astype(jnp.bfloat16)
    narrow_sel = jnp.einsum(
        "ca,kard->ckrd", choose, narrow_full, preferred_element_type=jnp.float32
    ).astype(jnp.bfloat16)
    clip_count = stream.shape[0]
    records = {"wide": wide_sel, "narrow": narrow_sel, "spatial_in": stream}
    normed = modulate(stream, modulators[:, 0:1], modulators[:, 1:2]).astype(jnp.bfloat16)
    projected = [
        project(normed, qkv_w[number], wide_sel[:, 2 * number], wide_sel[:, 2 * number + 1])
        for number in range(3)
    ]
    q_tok = projected[0][0].astype(jnp.bfloat16)
    k_tok = projected[1][0].astype(jnp.bfloat16)
    v_tok = projected[2][0].astype(jnp.bfloat16)
    spatial = regroup(q_tok, k_tok, v_tok)
    attended, logsum = attend(
        frame_view(spatial[0]), frame_view(spatial[1]), frame_view(spatial[2])
    )
    attended = frame_back(attended, clip_count)
    attended = restore(attended)
    branch, rank_out = project(attended, out_w[0], wide_sel[:, 6], wide_sel[:, 7])
    records["spatial"] = (
        normed,
        [entry[1] for entry in projected],
        spatial,
        logsum,
        attended,
        rank_out,
    )
    stream = stream + modulators[:, 2:3] * branch
    inputs = stream.astype(jnp.bfloat16)
    projected = [
        project(inputs, qkv_w[3 + number], wide_sel[:, 8 + 2 * number], wide_sel[:, 9 + 2 * number])
        for number in range(3)
    ]
    temporal = regroup(
        projected[0][0].astype(jnp.bfloat16),
        projected[1][0].astype(jnp.bfloat16),
        projected[2][0].astype(jnp.bfloat16),
    )
    attended, logsum = attend(
        time_view(temporal[0]), time_view(temporal[1]), time_view(temporal[2])
    )
    attended = restore(time_back(attended, clip_count))
    branch, rank_out = project(attended, out_w[1], wide_sel[:, 14], wide_sel[:, 15])
    records["temporal"] = (
        inputs,
        [entry[1] for entry in projected],
        temporal,
        logsum,
        attended,
        rank_out,
    )
    stream = stream + modulators[:, 2:3] * branch
    inputs = stream.astype(jnp.bfloat16)
    q_full, rank_query = project(inputs, qkv_w[6], wide_sel[:, 16], wide_sel[:, 17])
    q_tok = q_full.astype(jnp.bfloat16)
    col_start, col_width = head_columns(q_tok.shape[2])
    q_heads = lax.all_to_all(q_tok, "seq", split_axis=2, concat_axis=1, tiled=True)
    k_ctx, rank_key = context_project(
        context, qkv_w[7], wide_sel[:, 18], wide_sel[:, 19], col_start, col_width
    )
    v_ctx, rank_value = context_project(
        context, qkv_w[8], wide_sel[:, 20], wide_sel[:, 21], col_start, col_width
    )
    attended, logsum = attend(cross_view(q_heads), cross_view(k_ctx), cross_view(v_ctx))
    attended = cross_back(attended)
    attended = restore(attended)
    branch, rank_out = project(attended, out_w[2], wide_sel[:, 22], wide_sel[:, 23])
    records["cross"] = (
        inputs,
        rank_query,
        q_heads,
        k_ctx,
        v_ctx,
        rank_key,
        rank_value,
        logsum,
        attended,
        rank_out,
    )
    stream = stream + branch
    normed = modulate(stream, modulators[:, 3:4], modulators[:, 4:5]).astype(jnp.bfloat16)
    hidden, rank_up = project(normed, up_w, wide_sel[:, 24], narrow_sel[:, 0])
    activated = jax.nn.gelu(hidden, approximate=True).astype(jnp.bfloat16)
    branch, rank_down = project(activated, down_w, narrow_sel[:, 1], wide_sel[:, 25])
    records["mlp"] = (stream, normed, hidden, rank_up, activated, rank_down)
    stream = stream + modulators[:, 5:6] * branch
    return (stream, records)


def layer_backward(grad_stream, records, context, modulators, weights):
    qkv_w, out_w, up_w, down_w = (weights[0], weights[1], weights[2], weights[3])
    wide_sel, narrow_sel = (records["wide"], records["narrow"])
    clip_count = grad_stream.shape[0]
    wide_grads = [None] * 26
    narrow_grads = [None] * 2
    before_mlp, normed, hidden, rank_up, activated, rank_down = records["mlp"]
    grad_branch = (modulators[:, 5:6] * grad_stream).astype(jnp.bfloat16)
    grad_acted, narrow_grads[1], wide_grads[25] = project_back(
        activated, rank_down, down_w, narrow_sel[:, 1], wide_sel[:, 25], grad_branch
    )
    gelu_out, gelu_pull = jax.vjp(
        lambda values_in: jax.nn.gelu(values_in, approximate=True), hidden
    )
    grad_hidden = gelu_pull(grad_acted)[0].astype(jnp.bfloat16)
    grad_normed, wide_grads[24], narrow_grads[0] = project_back(
        normed, rank_up, up_w, wide_sel[:, 24], narrow_sel[:, 0], grad_hidden
    )
    grad_stream = grad_stream + modulate_back(
        before_mlp, modulators[:, 3:4], modulators[:, 4:5], grad_normed
    )
    inputs, rank_query, q_heads, k_ctx, v_ctx, rank_key, rank_value, logsum, attended, rank_out = (
        records["cross"]
    )
    col_start, col_width = head_columns(qkv_w.shape[2])
    grad_branch = grad_stream.astype(jnp.bfloat16)
    grad_att, wide_grads[22], wide_grads[23] = project_back(
        attended, rank_out, out_w[2], wide_sel[:, 22], wide_sel[:, 23], grad_branch
    )
    grad_att = grad_att.astype(jnp.bfloat16)
    grad_att = spread_grad(grad_att)
    grad_q, grad_k, grad_v = attend_back(
        cross_view(q_heads), cross_view(k_ctx), cross_view(v_ctx), logsum, cross_view(grad_att)
    )
    grad_query = cross_back(grad_q).astype(jnp.bfloat16)
    grad_query = lax.all_to_all(grad_query, "seq", split_axis=1, concat_axis=2, tiled=True)
    wide_grads[18], wide_grads[19] = context_back(
        context, rank_key, wide_sel[:, 19], col_start, col_width, cross_back(grad_k)
    )
    wide_grads[20], wide_grads[21] = context_back(
        context, rank_value, wide_sel[:, 21], col_start, col_width, cross_back(grad_v)
    )
    grad_in, wide_grads[16], wide_grads[17] = project_back(
        inputs, rank_query, qkv_w[6], wide_sel[:, 16], wide_sel[:, 17], grad_query
    )
    grad_stream = grad_stream + grad_in
    inputs, rank_terms, temporal, logsum, attended, rank_out = records["temporal"]
    grad_branch = (modulators[:, 2:3] * grad_stream).astype(jnp.bfloat16)
    grad_att, wide_grads[14], wide_grads[15] = project_back(
        attended, rank_out, out_w[1], wide_sel[:, 14], wide_sel[:, 15], grad_branch
    )
    grad_att = spread_grad(grad_att.astype(jnp.bfloat16))
    grad_q, grad_k, grad_v = attend_back(
        time_view(temporal[0]),
        time_view(temporal[1]),
        time_view(temporal[2]),
        logsum,
        time_view(grad_att),
    )
    grad_parts = collect_grads(
        time_back(grad_q, clip_count).astype(jnp.bfloat16),
        time_back(grad_k, clip_count).astype(jnp.bfloat16),
        time_back(grad_v, clip_count).astype(jnp.bfloat16),
    )
    for number in range(3):
        grad_in, wide_grads[8 + 2 * number], wide_grads[9 + 2 * number] = project_back(
            inputs,
            rank_terms[number],
            qkv_w[3 + number],
            wide_sel[:, 8 + 2 * number],
            wide_sel[:, 9 + 2 * number],
            grad_parts[number],
        )
        grad_stream = grad_stream + grad_in
    normed, rank_terms, spatial, logsum, attended, rank_out = records["spatial"]
    grad_branch = (modulators[:, 2:3] * grad_stream).astype(jnp.bfloat16)
    grad_att, wide_grads[6], wide_grads[7] = project_back(
        attended, rank_out, out_w[0], wide_sel[:, 6], wide_sel[:, 7], grad_branch
    )
    grad_att = grad_att.astype(jnp.bfloat16)
    grad_att = spread_grad(grad_att)
    grad_q, grad_k, grad_v = attend_back(
        frame_view(spatial[0]),
        frame_view(spatial[1]),
        frame_view(spatial[2]),
        logsum,
        frame_view(grad_att),
    )
    grad_parts = (
        frame_back(grad_q, clip_count).astype(jnp.bfloat16),
        frame_back(grad_k, clip_count).astype(jnp.bfloat16),
        frame_back(grad_v, clip_count).astype(jnp.bfloat16),
    )
    grad_parts = collect_grads(grad_parts[0], grad_parts[1], grad_parts[2])
    grad_normed = jnp.zeros(grad_stream.shape, jnp.float32)
    for number in range(3):
        grad_in, wide_grads[2 * number], wide_grads[2 * number + 1] = project_back(
            normed,
            rank_terms[number],
            qkv_w[number],
            wide_sel[:, 2 * number],
            wide_sel[:, 2 * number + 1],
            grad_parts[number],
        )
        grad_normed = grad_normed + grad_in
    grad_stream = grad_stream + modulate_back(
        records["spatial_in"], modulators[:, 0:1], modulators[:, 1:2], grad_normed
    )
    return (grad_stream, wide_grads, narrow_grads)


def on_device(
    video,
    context,
    modulation,
    adapter_index,
    cotangent,
    qkv_weights,
    out_weights,
    ffn_up,
    ffn_down,
    adapt_wide,
    adapt_ff,
):
    adapter_count = adapt_wide.shape[2]
    picked = adapter_index[:, None] == jnp.arange(adapter_count)[None, :]
    choose_low = picked.astype(jnp.bfloat16)
    choose_full = picked.astype(jnp.float32)
    layer_mods = jnp.moveaxis(modulation, 1, 0)
    layer_items = (qkv_weights, out_weights, ffn_up, ffn_down, adapt_wide, adapt_ff, layer_mods)

    def forward_step(stream, items):
        qkv_l, out_l, up_l, down_l, wide_l, narrow_l, mods = items
        weights = fetch_layer(qkv_l, out_l, up_l, down_l, wide_l, narrow_l)
        stream, records = layer_forward(stream, context, mods, weights, choose_low)
        return (stream, (records, ()))

    stream, (all_records, kept) = lax.scan(forward_step, video.astype(jnp.float32), layer_items)
    output = stream.astype(jnp.bfloat16)

    def backward_step(grad_stream, items):
        records, kept_weights, qkv_l, out_l, up_l, down_l, wide_l, narrow_l, mods = items
        weights = fetch_again(qkv_l, out_l, up_l, down_l, wide_l, narrow_l)
        grad_stream, wide_grads, narrow_grads = layer_backward(
            grad_stream, records, context, mods, weights
        )
        return (grad_stream, (jnp.stack(wide_grads, 1), jnp.stack(narrow_grads, 1)))

    grad_stream, (wide_stack, narrow_stack) = lax.scan(
        backward_step,
        cotangent.astype(jnp.float32),
        (all_records, kept) + layer_items,
        reverse=True,
    )
    wide_each = jnp.moveaxis(wide_stack, 0, 1)
    narrow_each = jnp.moveaxis(narrow_stack, 0, 1)
    wide_table = jnp.einsum("ca,clkrd->lkard", choose_full, wide_each, precision=HIGHEST)
    narrow_table = jnp.einsum("ca,clkrd->lkard", choose_full, narrow_each, precision=HIGHEST)
    shares = (
        lax.psum_scatter(
            wide_table.astype(jnp.bfloat16), "fsdp", scatter_dimension=4, tiled=True
        ).astype(jnp.float32),
        lax.psum_scatter(
            narrow_table.astype(jnp.bfloat16), "fsdp", scatter_dimension=4, tiled=True
        ).astype(jnp.float32),
    )
    totals = (
        lax.psum(shares[0].astype(jnp.bfloat16), "seq").astype(jnp.float32),
        lax.psum(shares[1].astype(jnp.bfloat16), "seq").astype(jnp.float32),
    )
    return (output, grad_stream.astype(jnp.bfloat16), totals[0], totals[1])


def solution(mesh):
    return jax.shard_map(
        on_device,
        mesh=mesh,
        in_specs=(
            P("fsdp", "seq", None),
            P("fsdp", None, None),
            P("fsdp", None, None, None),
            P("fsdp"),
            P("fsdp", "seq", None),
            P(None, None, "fsdp", None),
            P(None, None, "fsdp", None),
            P(None, "fsdp", None),
            P(None, "fsdp", None),
            P(None, None, None, None, "fsdp"),
            P(None, None, None, None, "fsdp"),
        ),
        out_specs=(
            P("fsdp", "seq", None),
            P("fsdp", "seq", None),
            P(None, None, None, None, "fsdp"),
            P(None, None, None, None, "fsdp"),
        ),
        check_vma=False,
    )
```

profile of v0, /device:TPU:0, one launch (start us, length us, event | category | flops | bytes accessed | tf_op | source)
XLA Modules:
  0.0 3477.2 jit_solution(753683892979543447)
XLA Ops:
  20.6 176.0 %all-gather.15.cloned.1.call-done = bf16[1,26,8,16,1152]{1,3,2,0,4:T(8,128)(2,1)} async-done(((bf16[1,26,8,16,144]{1,3,2,0,4:T(8,128)(2,1)}), bf16[1,26,8,16,1152]{1,3,2,0,4:T(8,128)(2,1)}) %all-gather.15.cloned.1.call-update) | async-done | bytes 7667728 | tf_op jit(solution)/shard_map/while/body/eval_jaxpr/all_gather | solution.py:28
  196.6 52.6 %copy.274 = bf16[26,8,16,1152]{3,1,2,0:T(8,128)(2,1)} copy(bf16[26,8,16,1152]{0,2,1,3:T(8,128)(2,1)} %bitcast.863) | data formatting | bytes 15335424 | tf_op jit(solution)/shard_map/while/body/eval_jaxpr/all_gather | solution.py:28
  258.7 59.7 %all-gather.13.cloned.1.call-done = bf16[1,9,1152,1152]{3,2,1,0:T(8,128)(2,1)} async-done(((bf16[1,9,144,1152]{3,2,1,0:T(8,128)(2,1)}), bf16[1,9,1152,1152]{3,2,1,0:T(8,128)(2,1)}) %all-gather.13.cloned.1.call-update) | async-done | bytes 23887888 | tf_op jit(solution)/shard_map/while/body/eval_jaxpr/all_gather | solution.py:24
  594.6 21.8 reshape.1451
  616.4 68.6 %reduce.33 = bf16[4096,288]{1,0:T(8,128)(2,1)} reduce(bf16[4096,1,288]{2,1,0:T(2,128)(2,1)} %bitcast.866, bf16[]{:T(256)} %broadcast.367), dimensions={1}, to_apply=%bitcast.652.reduce_sub_computation | reduce | bytes 4718594
  696.8 52.7 %all-to-all-done.3 = bf16[4,2,147456]{2,1,0:T(2,128)(2,1)} async-done(((bf16[4,2,147456]{2,1,0:T(2,128)(2,1)}), bf16[4,2,147456]{2,1,0:T(2,128)(2,1)}, u32[]{:S(2)}, u32[]{:S(2)}) %all-to-all-start.3) | async-done | bytes 2359328 | tf_op jit(solution)/shard_map/while/body/eval_jaxpr/all_to_all | solution.py:65
  1041.5 22.0 reshape.1452
  1063.5 67.0 %reduce.37 = bf16[4096,288]{1,0:T(8,128)(2,1)S(1)} reduce(bf16[4096,1,288]{2,1,0:T(2,128)(2,1)} %bitcast.867, bf16[]{:T(256)} %broadcast.367), dimensions={1}, to_apply=%bitcast.660.reduce_sub_computation | reduce | bytes 4718594
  1139.9 52.7 %all-to-all-done.7 = bf16[4,2,147456]{2,1,0:T(2,128)(2,1)S(1)} async-done(((bf16[4,2,147456]{2,1,0:T(2,128)(2,1)}), bf16[4,2,147456]{2,1,0:T(2,128)(2,1)S(1)}, u32[]{:S(2)}, u32[]{:S(2)}) %all-to-all-start.7) | async-done | bytes 2359328 | tf_op jit(solution)/shard_map/while/body/eval_jaxpr/all_to_all | solution.py:65
  1274.5 45.2 %all-to-all-done.8 = bf16[4,2,147456]{2,1,0:T(2,128)(2,1)S(1)} async-done(((bf16[4,2,147456]{2,1,0:T(2,128)(2,1)}), bf16[4,2,147456]{2,1,0:T(2,128)(2,1)S(1)}, u32[]{:S(2)}, u32[]{:S(2)}) %all-to-all-start.8) | async-done | bytes 2359328 | tf_op jit(solution)/shard_map/while/body/eval_jaxpr/all_to_all | solution.py:300
  1351.6 67.4 %reduce.39 = bf16[4096,288]{1,0:T(8,128)(2,1)S(1)} reduce(bf16[4096,1,288]{2,1,0:T(2,128)(2,1)} %bitcast.868, bf16[]{:T(256)} %broadcast.367), dimensions={1}, to_apply=%bitcast.664.reduce_sub_computation | reduce | bytes 4718594
  1534.0 26.5 multiply_convert_fusion
  1560.4 29.0 fusion.6
  1659.8 57.9 %all_to_all.380 = bf16[4,2,147456]{2,1,0:T(2,128)(2,1)} all-to-all(bf16[4,2,147456]{2,1,0:T(2,128)(2,1)} %reshape.1489), channel_id=1, replica_groups=mesh['seq'=4,'fsdp'=8] {'seq'}, dimensions={0} | all-to-all | bytes 4718592 | tf_op jit(solution)/shard_map/while/body/eval_jaxpr/all_to_all | solution.py:73
  1763.0 68.8 %reduce.41 = bf16[4096,288]{1,0:T(8,128)(2,1)} reduce(bf16[4096,1,288]{2,1,0:T(2,128)(2,1)} %bitcast.869, bf16[]{:T(256)} %broadcast.367), dimensions={1}, to_apply=%bitcast.668.reduce_sub_computation | reduce | bytes 4718594
  1838.5 57.3 %all_to_all.381 = bf16[4,2,147456]{2,1,0:T(2,128)(2,1)} all-to-all(bf16[4,2,147456]{2,1,0:T(2,128)(2,1)} %reshape.1491), channel_id=1, replica_groups=mesh['seq'=4,'fsdp'=8] {'seq'}, dimensions={0} | all-to-all | bytes 4718592 | tf_op jit(solution)/shard_map/while/body/eval_jaxpr/all_to_all | solution.py:368
  1970.3 56.7 %all_to_all.382 = bf16[4,2,147456]{2,1,0:T(2,128)(2,1)S(1)} all-to-all(bf16[4,2,147456]{2,1,0:T(2,128)(2,1)} %reshape.1493), channel_id=1, replica_groups=mesh['seq'=4,'fsdp'=8] {'seq'}, dimensions={0} | all-to-all | bytes 4718592 | tf_op jit(solution)/shard_map/while/body/eval_jaxpr/all_to_all | solution.py:73
  2075.0 22.0 reshape.1453
  2097.0 68.6 %reduce.45 = bf16[4096,288]{1,0:T(8,128)(2,1)} reduce(bf16[4096,1,288]{2,1,0:T(2,128)(2,1)} %bitcast.870, bf16[]{:T(256)} %broadcast.367), dimensions={1}, to_apply=%bitcast.676.reduce_sub_computation | reduce | bytes 4718594
  2187.5 21.8 reshape.1455
  2209.3 67.0 %reduce.43 = bf16[4096,288]{1,0:T(8,128)(2,1)S(1)} reduce(bf16[4096,1,288]{2,1,0:T(2,128)(2,1)} %bitcast.871, bf16[]{:T(256)} %broadcast.367), dimensions={1}, to_apply=%bitcast.672.reduce_sub_computation | reduce | bytes 4718594
  2317.0 67.0 %reduce.44 = bf16[4096,288]{1,0:T(8,128)(2,1)S(1)} reduce(bf16[4096,1,288]{2,1,0:T(2,128)(2,1)} %bitcast.872, bf16[]{:T(256)} %broadcast.367), dimensions={1}, to_apply=%bitcast.674.reduce_sub_computation | reduce | bytes 4718594
  2543.8 56.7 %all_to_all.383 = bf16[4,2,147456]{2,1,0:T(2,128)(2,1)S(1)} all-to-all(bf16[4,2,147456]{2,1,0:T(2,128)(2,1)} %reshape.1501), channel_id=1, replica_groups=mesh['seq'=4,'fsdp'=8] {'seq'}, dimensions={0} | all-to-all | bytes 4718592 | tf_op jit(solution)/shard_map/while/body/eval_jaxpr/all_to_all | solution.py:73
  2655.6 68.9 %reduce.49 = bf16[4096,288]{1,0:T(8,128)(2,1)} reduce(bf16[4096,1,288]{2,1,0:T(2,128)(2,1)} %bitcast.873, bf16[]{:T(256)} %broadcast.367), dimensions={1}, to_apply=%bitcast.684.reduce_sub_computation | reduce | bytes 4718594
  2773.6 21.8 reshape.1456
  2795.4 67.1 %reduce.47 = bf16[4096,288]{1,0:T(8,128)(2,1)S(1)} reduce(bf16[4096,1,288]{2,1,0:T(2,128)(2,1)} %bitcast.874, bf16[]{:T(256)} %broadcast.367), dimensions={1}, to_apply=%bitcast.680.reduce_sub_computation | reduce | bytes 4718594
  2892.0 21.8 reshape.1457
  2913.8 67.0 %reduce.48 = bf16[4096,288]{1,0:T(8,128)(2,1)S(1)} reduce(bf16[4096,1,288]{2,1,0:T(2,128)(2,1)} %bitcast.865, bf16[]{:T(256)} %broadcast.367), dimensions={1}, to_apply=%bitcast.682.reduce_sub_computation | reduce | bytes 4718594
  3007.7 23.0 reshape.1461
  3177.1 52.8 %copy.293 = bf16[1,26,8,16,1152]{3,2,1,0,4:T(8,128)(2,1)} copy(bf16[1,26,8,16,1152]{4,3,2,1,0:T(8,128)(2,1)} %fusion.14) | data formatting | bytes 15335424
  3229.9 61.5 %reshape.1459 = bf16[1152,3328]{1,0:T(8,128)(2,1)} reshape(bf16[1152,1,26,8,16]{4,3,2,1,0:T(8,128)(2,1)} %bitcast.849) | data formatting | bytes 15335424
  3385.9 79.0 %all-reduce.3.cloned.1.call-done = (bf16[1,26,8,16,144]{4,3,2,1,0:T(8,128)(2,1)}, bf16[1,2,8,16,576]{4,3,2,1,0:T(8,128)(2,1)}) async-done(((bf16[1,26,8,16,144]{4,3,2,1,0:T(8,128)(2,1)}, bf16[1,2,8,16,576]{4,3,2,1,0:T(8,128)(2,1)}), (bf16[1,26,8,16,144]{4,3,2,1,0:T(8,128)(2,1)}, bf16[1,2,8,16,576]{4,3,2,1,0:T(8,128)(2,1)})) %all-reduce.3.cloned.1.call-update) | async-done | bytes 1253392 | tf_op jit(solution)/shard_map/psum | solution.py:500
  (674 shorter events, 1712.4 us)
Async XLA Ops:
  7.2 1259.3 %copy-start = (bf16[1,120,1152]{2,1,0:T(8,128)(2,1)S(1)}, bf16[1,120,1152]{2,1,0:T(8,128)(2,1)}, u32[]{:S(2)}) copy-start(bf16[1,120,1152]{2,1,0:T(8,128)(2,1)} %param.12) | copy-start | bytes 829444
  7.2 189.4 %all-gather.15.cloned.1.call-start = ((), (), s32[]{:S(2)}) async-start(), calls=%async_computation.23 | async-start | bytes 42467328 | tf_op jit(solution)/shard_map/while/body/eval_jaxpr/all_gather | solution.py:28
  14.2 304.3 %all-gather.13.cloned.1.call-start = ((), (), s32[]{:S(2)}) async-start(), calls=%async_computation.22 | async-start | bytes 26873856 | tf_op jit(solution)/shard_map/while/body/eval_jaxpr/all_gather | solution.py:24
  14.9 766.5 %all-gather.17.cloned.1.call-start = ((), (), s32[]{:S(2)}) async-start(), calls=%async_computation.24 | async-start | bytes 8957952 | tf_op jit(solution)/shard_map/while/body/eval_jaxpr/all_gather | solution.py:25
  17.5 231.8 %copy-start.120 = (f32[1152]{0:T(1024)}, f32[1152]{0:T(1024)S(1)}, u32[]{:S(2)}) copy-start(f32[1152]{0:T(1024)S(1)} %get-tuple-element.207) | copy-start | bytes 13828
  17.5 1209.7 %copy-start.114 = (f32[1152]{0:T(1024)}, f32[1152]{0:T(1024)S(1)}, u32[]{:S(2)}) copy-start(f32[1152]{0:T(1024)S(1)} %get-tuple-element.208) | copy-start | bytes 13828
  17.5 231.8 %copy-start.116 = (f32[1024]{0:T(1024)}, f32[1024]{0:T(1024)S(1)}, u32[]{:S(2)}) copy-start(f32[1024]{0:T(1024)S(1)} %broadcast_multiply_fusion.1) | copy-start | bytes 12292
  18.2 231.0 %copy-start.131 = (f32[1024]{0:T(1024)}, f32[1024]{0:T(1024)S(1)}, u32[]{:S(2)}) copy-start(f32[1024]{0:T(1024)S(1)} %fusion.30) | copy-start | bytes 12292
  18.3 231.0 %copy-start.125 = (f32[1024]{0:T(1024)}, f32[1024]{0:T(1024)S(1)}, u32[]{:S(2)}) copy-start(f32[1024]{0:T(1024)S(1)} %fusion.249) | copy-start | bytes 12292
  359.5 59.3 %all-to-all-start = ((bf16[4,2,147456]{2,1,0:T(2,128)(2,1)}), bf16[4,2,147456]{2,1,0:T(2,128)(2,1)}, u32[]{:S(2)}, u32[]{:S(2)}) async-start(bf16[4,2,147456]{2,1,0:T(2,128)(2,1)} %reshape.1469), calls=%async_computation | async-start | bytes 4718592 | tf_op jit(solution)/shard_map/while/body/eval_jaxpr/all_to_all | solution.py:56
  418.9 58.2 %all-to-all-start.1 = ((bf16[4,2,147456]{2,1,0:T(2,128)(2,1)}), bf16[4,2,147456]{2,1,0:T(2,128)(2,1)}, u32[]{:S(2)}, u32[]{:S(2)}) async-start(bf16[4,2,147456]{2,1,0:T(2,128)(2,1)} %reshape.1473), calls=%async_computation.1 | async-start | bytes 4718592 | tf_op jit(solution)/shard_map/while/body/eval_jaxpr/all_to_all | solution.py:50
  477.0 57.9 %all-to-all-start.2 = ((bf16[4,2,147456]{2,1,0:T(2,128)(2,1)}), bf16[4,2,147456]{2,1,0:T(2,128)(2,1)}, u32[]{:S(2)}, u32[]{:S(2)}) async-start(bf16[4,2,147456]{2,1,0:T(2,128)(2,1)} %reshape.1471), calls=%async_computation.2 | async-start | bytes 4718592 | tf_op jit(solution)/shard_map/while/body/eval_jaxpr/all_to_all | solution.py:53
  481.5 947.2 %all-gather.21.cloned.1.call-start = ((), (), s32[]{:S(2)}) async-start(), calls=%async_computation.26 | async-start | bytes 21233664 | tf_op jit(solution)/shard_map/while/body/eval_jaxpr/all_gather | solution.py:29
  691.7 57.8 %all-to-all-start.3 = ((bf16[4,2,147456]{2,1,0:T(2,128)(2,1)}), bf16[4,2,147456]{2,1,0:T(2,128)(2,1)}, u32[]{:S(2)}, u32[]{:S(2)}) async-start(bf16[4,2,147456]{2,1,0:T(2,128)(2,1)} %reshape.1475), calls=%async_computation.3 | async-start | bytes 4718592 | tf_op jit(solution)/shard_map/while/body/eval_jaxpr/all_to_all | solution.py:65
  696.2 837.8 %all-gather.19.cloned.1.call-start = ((), (), s32[]{:S(2)}) async-start(), calls=%async_computation.25 | async-start | bytes 11943936 | tf_op jit(solution)/shard_map/while/body/eval_jaxpr/all_gather | solution.py:26
  830.0 57.9 %all-to-all-start.5 = ((bf16[4,2,147456]{2,1,0:T(2,128)(2,1)}), bf16[4,2,147456]{2,1,0:T(2,128)(2,1)}, u32[]{:S(2)}, u32[]{:S(2)}) async-start(bf16[4,2,147456]{2,1,0:T(2,128)(2,1)} %reshape.1479), calls=%async_computation.5 | async-start | bytes 4718592 | tf_op jit(solution)/shard_map/while/body/eval_jaxpr/all_to_all | solution.py:50
  887.9 57.9 %all-to-all-start.6 = ((bf16[4,2,147456]{2,1,0:T(2,128)(2,1)}), bf16[4,2,147456]{2,1,0:T(2,128)(2,1)}, u32[]{:S(2)}, u32[]{:S(2)}) async-start(bf16[4,2,147456]{2,1,0:T(2,128)(2,1)} %reshape.1481), calls=%async_computation.6 | async-start | bytes 4718592 | tf_op jit(solution)/shard_map/while/body/eval_jaxpr/all_to_all | solution.py:53
  945.8 57.3 %all-to-all-start.4 = ((bf16[4,2,147456]{2,1,0:T(2,128)(2,1)}), bf16[4,2,147456]{2,1,0:T(2,128)(2,1)S(1)}, u32[]{:S(2)}, u32[]{:S(2)}) async-start(bf16[4,2,147456]{2,1,0:T(2,128)(2,1)} %reshape.1477), calls=%async_computation.4 | async-start | bytes 4718592 | tf_op jit(solution)/shard_map/while/body/eval_jaxpr/all_to_all | solution.py:56
  1135.7 56.9 %all-to-all-start.7 = ((bf16[4,2,147456]{2,1,0:T(2,128)(2,1)}), bf16[4,2,147456]{2,1,0:T(2,128)(2,1)S(1)}, u32[]{:S(2)}, u32[]{:S(2)}) async-start(bf16[4,2,147456]{2,1,0:T(2,128)(2,1)} %reshape.1483), calls=%async_computation.7 | async-start | bytes 4718592 | tf_op jit(solution)/shard_map/while/body/eval_jaxpr/all_to_all | solution.py:65
  1139.4 421.1 %all-gather.23.cloned.1.call-start = ((), (), s32[]{:S(2)}) async-start(), calls=%async_computation.27 | async-start | bytes 11943936 | tf_op jit(solution)/shard_map/while/body/eval_jaxpr/all_gather | solution.py:27
  1262.8 56.8 %all-to-all-start.8 = ((bf16[4,2,147456]{2,1,0:T(2,128)(2,1)}), bf16[4,2,147456]{2,1,0:T(2,128)(2,1)S(1)}, u32[]{:S(2)}, u32[]{:S(2)}) async-start(bf16[4,2,147456]{2,1,0:T(2,128)(2,1)} %reshape.1485), calls=%async_computation.8 | async-start | bytes 4718592 | tf_op jit(solution)/shard_map/while/body/eval_jaxpr/all_to_all | solution.py:300
  1424.2 57.9 %all-to-all-start.9 = ((bf16[4,2,147456]{2,1,0:T(2,128)(2,1)}), bf16[4,2,147456]{2,1,0:T(2,128)(2,1)}, u32[]{:S(2)}, u32[]{:S(2)}) async-start(bf16[4,2,147456]{2,1,0:T(2,128)(2,1)} %reshape.1487), calls=%async_computation.9 | async-start | bytes 4718592 | tf_op jit(solution)/shard_map/while/body/eval_jaxpr/all_to_all | solution.py:65
  1451.1 138.3 %copy-start.63 = (bf16[1,2,16,4608]{3,2,1,0:T(8,128)(2,1)}, bf16[1,2,16,4608]{3,2,1,0:T(8,128)(2,1)S(1)}, u32[]{:S(2)}) copy-start(bf16[1,2,16,4608]{3,2,1,0:T(8,128)(2,1)S(1)} %copy.350) | copy-start | bytes 884740
  2172.3 109.3 %all-to-all-start.13 = ((bf16[4,2,147456]{2,1,0:T(2,128)(2,1)}), bf16[4,2,147456]{2,1,0:T(2,128)(2,1)}, u32[]{:S(2)}, u32[]{:S(2)}) async-start(bf16[4,2,147456]{2,1,0:T(2,128)(2,1)} %reshape.1499), calls=%async_computation.13 | async-start | bytes 4718592 | tf_op jit(solution)/shard_map/while/body/eval_jaxpr/all_to_all | solution.py:80
  2281.6 107.7 %all-to-all-start.15 = ((bf16[4,2,147456]{2,1,0:T(2,128)(2,1)}), bf16[4,2,147456]{2,1,0:T(2,128)(2,1)}, u32[]{:S(2)}, u32[]{:S(2)}) async-start(bf16[4,2,147456]{2,1,0:T(2,128)(2,1)} %reshape.1495), calls=%async_computation.15 | async-start | bytes 4718592 | tf_op jit(solution)/shard_map/while/body/eval_jaxpr/all_to_all | solution.py:86
  2389.3 66.3 %all-to-all-start.14 = ((bf16[4,2,147456]{2,1,0:T(2,128)(2,1)}), bf16[4,2,147456]{2,1,0:T(2,128)(2,1)}, u32[]{:S(2)}, u32[]{:S(2)}) async-start(bf16[4,2,147456]{2,1,0:T(2,128)(2,1)} %reshape.1497), calls=%async_computation.14 | async-start | bytes 4718592 | tf_op jit(solution)/shard_map/while/body/eval_jaxpr/all_to_all | solution.py:83
  2731.3 136.5 %all-to-all-start.19 = ((bf16[4,2,147456]{2,1,0:T(2,128)(2,1)}), bf16[4,2,147456]{2,1,0:T(2,128)(2,1)}, u32[]{:S(2)}, u32[]{:S(2)}) async-start(bf16[4,2,147456]{2,1,0:T(2,128)(2,1)} %reshape.1507), calls=%async_computation.19 | async-start | bytes 4718592 | tf_op jit(solution)/shard_map/while/body/eval_jaxpr/all_to_all | solution.py:86
  2867.9 118.4 %all-to-all-start.17 = ((bf16[4,2,147456]{2,1,0:T(2,128)(2,1)}), bf16[4,2,147456]{2,1,0:T(2,128)(2,1)}, u32[]{:S(2)}, u32[]{:S(2)}) async-start(bf16[4,2,147456]{2,1,0:T(2,128)(2,1)} %reshape.1503), calls=%async_computation.17 | async-start | bytes 4718592 | tf_op jit(solution)/shard_map/while/body/eval_jaxpr/all_to_all | solution.py:80
  2986.3 125.0 %all-to-all-start.18 = ((bf16[4,2,147456]{2,1,0:T(2,128)(2,1)}), bf16[4,2,147456]{2,1,0:T(2,128)(2,1)}, u32[]{:S(2)}, u32[]{:S(2)}) async-start(bf16[4,2,147456]{2,1,0:T(2,128)(2,1)} %reshape.1505), calls=%async_computation.18 | async-start | bytes 4718592 | tf_op jit(solution)/shard_map/while/body/eval_jaxpr/all_to_all | solution.py:83
  2991.5 320.7 %reduce-scatter.9.cloned.1.call-start = ((), (), s32[]{:S(2)}) async-start(), calls=%async_computation.29 | async-start | bytes 2654208
  3030.7 330.1 %reduce-scatter.7.cloned.1.call-start = ((), (), s32[]{:S(2)}) async-start(), calls=%async_computation.28 | async-start | bytes 8626176
  3291.4 173.5 %all-reduce.3.cloned.1.call-start = ((), (), s32[]{:S(2)}) async-start(), calls=%async_computation.30 | async-start | bytes 4063232 | tf_op jit(solution)/shard_map/psum | solution.py:500
  (142 other events, 1130.1 us)
Sparse Core Ops, SparseCore 0:
  14.3 182.2 all-gather.14
  198.5 119.8 all-gather.12
  320.3 52.5 all-gather.16
  484.8 99.1 all-gather.20
  698.6 64.2 all-gather.18
  1141.8 64.4 all-gather.22
  3030.8 43.2 reduce-scatter.8
  3291.6 69.2 reduce-scatter.6
  3380.5 84.4 all-reduce.2
where the time goes:
time: 3500 us; the launch traced here: 3480 us
  local copies, waits for them, and re-layouts  1210 us (35%)
  other arithmetic  895 us (26%)
  waiting for transfers between devices  575 us (16%)
  matrix products  478 us (14%)
  blocking collectives  229 us (7%)
  starting transfers between devices  74.4 us (2%)
    unnamed x27, other arithmetic  826 us
    unnamed x361, local copies, waits for them, and re-layouts  464 us
    all_gather x1, waiting for transfers between devices, fetch_layer(): lax.all_gather(for_sending(wide_part), 'fsdp', axis=3, tiled=True)  176 us
    all_to_all x3, blocking collectives, spread_grad(): lax.all_to_all(for_sending(grad_out), 'seq', split_axis=2, concat_axis=1,...  171 us
    all_to_all x3, waiting for transfers between devices, restore(): lax.all_to_all(for_sending(attended), 'seq', split_axis=1, concat_axis=2,...  126 us
    dot_general x12, matrix products, project_back(): jnp.einsum('cno,io->cni', grad_out, weight, preferred_element_type=jnp.fl...  99.9 us
    dot_general x12, matrix products, project(): jnp.einsum('cni,io->cno', inputs, weight, preferred_element_type=jnp.floa...  99.2 us
    psum x1, waiting for transfers between devices, on_device(): lax.psum(shares[0].astype(jnp.bfloat16), 'seq').astype(jnp.float32)  79 us
  transfers between devices with their start and end apart: 25, of which 14 were waited for; matrix products, arithmetic and copies ran while one was open for 53% of the time, Pallas kernels for 0%

commit v1 on v0

v1 whole, which is shorter than its diff:
```python
import math

import jax
import jax.numpy as jnp
from jax import lax
from jax.experimental import pallas as pl
from jax.experimental.pallas import tpu as pltpu
from jax.sharding import PartitionSpec as P

HEAD_DIM = 72
HEADS = 16
FRAMES = 16
SPATIAL = 256
RANK = 16
ROWS = 256
PAIRS = HEADS // 2
PAD = 128
SCALE = HEAD_DIM ** (-0.5)
EXP_SCALE = SCALE * math.log2(math.e)
HIGHEST = lax.Precision.HIGHEST
F32 = jnp.float32
BF16 = jnp.bfloat16
VMEM_LIMIT = 60 * 1024 * 1024


def nn(left, right):
    return lax.dot_general(left, right, (((1,), (0,)), ((), ())), preferred_element_type=F32)


def nt(left, right):
    return lax.dot_general(left, right, (((1,), (1,)), ((), ())), preferred_element_type=F32)


def tn(left, right):
    return lax.dot_general(left, right, (((0,), (0,)), ((), ())), preferred_element_type=F32)


def window(pair):
    return slice(128 * pair, 128 * pair + 256)


def normalize(stream):
    average = jnp.mean(stream, -1, keepdims=True)
    centred = stream - average
    inverse = lax.rsqrt(jnp.mean(centred * centred, -1, keepdims=True) + 1e-06)
    return centred * inverse, inverse


def normalize_back(normal, inverse, grad):
    mean_grad = jnp.mean(grad, -1, keepdims=True)
    mean_both = jnp.mean(grad * normal, -1, keepdims=True)
    return inverse * (grad - mean_grad - normal * mean_both)


def spread_rank(ad_ref, base, number):
    rows = ad_ref[base + 2 * number + 1]
    nothing = jnp.zeros_like(rows)
    return jnp.concatenate([rows if i == number else nothing for i in range(3)], 0)


def three_downs(ad_ref, base):
    return jnp.concatenate([ad_ref[base], ad_ref[base + 2], ad_ref[base + 4]], 0)


class Loads:
    def __init__(self, entries, sems):
        self.first = pl.program_id(0) == 0
        self.entries = entries
        self.sems = sems

    def copy(self, index):
        source, target = self.entries[index]
        return pltpu.make_async_copy(source, target, self.sems.at[index])

    def start(self):
        @pl.when(self.first)
        def _():
            for index in range(len(self.entries)):
                self.copy(index).start()

    def ready(self, index):
        @pl.when(self.first)
        def _():
            self.copy(index).wait()


def head_masks():
    lane = jnp.arange(256)[None, :]
    begin = jnp.array([16 * (h // 2) + HEAD_DIM * (h % 2) for h in range(HEADS)])[:, None]
    return ((lane >= begin) & (lane < begin + HEAD_DIM)).astype(BF16)


def same_place(shape):
    rows = lax.broadcasted_iota(jnp.int32, shape, 0)
    cols = lax.broadcasted_iota(jnp.int32, shape, 1)
    return jnp.where(rows % 16 == cols % 16, 0.0, -1e30).astype(F32)


def attend(q_ref, k_ref, v_ref, mask_ref, bias, put_out, stat_ref):
    carried = None
    for pair in range(PAIRS):
        win = window(pair)
        q_win, k_win, v_win = q_ref[:, win], k_ref[:, win], v_ref[:, win]
        out = None
        for head in (2 * pair, 2 * pair + 1):
            mask = mask_ref[head : head + 1, :]
            scores = nt(k_win * mask, q_win) * EXP_SCALE
            if bias is not None:
                scores = scores + bias[...]
            top = jnp.max(scores, 0, keepdims=True)
            grown = jnp.exp2(scores - top)
            total = jnp.sum(grown, 0, keepdims=True)
            stat_ref[head : head + 1, :] = top + jnp.log2(total)
            weights = (grown * (1.0 / total)).astype(BF16)
            part = tn(weights, v_win * mask)
            out = part if out is None else out + part
        low = out[:, :128]
        put_out(pair, low if carried is None else low + carried)
        carried = out[:, 128:]
    put_out(PAIRS, carried)


def attend_back(q_ref, k_ref, v_ref, do_ref, mask_ref, bias, stat_ref, put):
    carried = None
    for pair in range(PAIRS):
        win = window(pair)
        q_win, k_win, v_win, do_win = q_ref[:, win], k_ref[:, win], v_ref[:, win], do_ref[:, win]
        grads = None
        for head in (2 * pair, 2 * pair + 1):
            mask = mask_ref[head : head + 1, :]
            k_own = k_win * mask
            scores = nt(k_own, q_win) * EXP_SCALE
            if bias is not None:
                scores = scores + bias[...]
            probs = jnp.exp2(scores - stat_ref[head : head + 1, :])
            grad_probs = nt(v_win * mask, do_win)
            inner = jnp.sum(probs * grad_probs, 0, keepdims=True)
            grad_scores = (probs * (grad_probs - inner)).astype(BF16)
            parts = (
                tn(grad_scores, k_own),
                nn(grad_scores, q_win * mask),
                nn(probs.astype(BF16), do_win * mask),
            )
            grads = parts if grads is None else tuple(a + b for a, b in zip(grads, parts))
        lows = tuple(g[:, :128] for g in grads)
        if carried is not None:
            lows = tuple(a + b for a, b in zip(lows, carried))
        put(pair, lows)
        carried = tuple(g[:, 128:] for g in grads)
    put(PAIRS, carried)


def tile(index):
    return slice(128 * index, 128 * index + 128)


def three_projections(inputs, ad_ref, base, weights, loads, first_load, outs, rank_ref):
    ranks = nt(inputs, three_downs(ad_ref, base)).astype(BF16)
    rank_ref[...] = ranks
    for number in range(3):
        loads.ready(first_load + number)
        total = nn(inputs, weights[first_load + number]) + nn(
            ranks, spread_rank(ad_ref, base, number)
        )
        outs[number][...] = total.astype(BF16)


def one_projection(inputs, ad_ref, base, weight_ref, rank_ref):
    ranks = nt(inputs, ad_ref[base]).astype(BF16)
    rank_ref[...] = ranks
    return nn(inputs, weight_ref[...]) + nn(ranks, ad_ref[base + 1])


def one_back(grad, kept, ranks, ad_ref, base, weight_ref, grad_ref, at):
    grad_rank = nt(grad, ad_ref[base + 1]).astype(BF16)
    grad_ref[at] += tn(grad_rank, kept)
    grad_ref[at + 1] += tn(ranks, grad)
    return nt(grad, weight_ref[...]) + nn(grad_rank, ad_ref[base])


def three_back(grads, inputs, ranks, ad_ref, base, weights, loads, first_load, grad_ref, at):
    grad_ranks = None
    total = None
    for number in range(3):
        grad = grads[number][...]
        part = nt(grad, spread_rank(ad_ref, base, number))
        grad_ranks = part if grad_ranks is None else grad_ranks + part
        ups = tn(ranks, grad)
        grad_ref[at + 2 * number + 1] += ups[RANK * number : RANK * (number + 1)]
        loads.ready(first_load + number)
        part = nt(grad, weights[first_load + number])
        total = part if total is None else total + part
    grad_ranks = grad_ranks.astype(BF16)
    downs = tn(grad_ranks, inputs)
    for number in range(3):
        grad_ref[at + 2 * number] += downs[RANK * number : RANK * (number + 1)]
    return total + nn(grad_ranks, three_downs(ad_ref, base))


def spatial_forward(
    x_ref, mod_ref, mask_ref, ad_ref, w_hbm, x1_ref, q_ref, k_ref, v_ref, o_ref, stat_ref, rq_ref, ro_ref, w_ref, sems
):
    loads = Loads([(w_hbm.at[i], w_ref.at[i]) for i in range(4)], sems)
    loads.start()
    stream = x_ref[0].astype(F32)
    normal, _ = normalize(stream)
    inputs = (normal * (1.0 + mod_ref[1:2, :]) + mod_ref[0:1, :]).astype(BF16)
    q, k, v, o = q_ref.at[0], k_ref.at[0], v_ref.at[0], o_ref.at[0]
    three_projections(inputs, ad_ref, 0, w_ref, loads, 0, (q, k, v), rq_ref.at[0])

    def put_out(index, value):
        o[:, tile(index)] = value.astype(BF16)

    attend(q, k, v, mask_ref, None, put_out, stat_ref.at[0])
    loads.ready(3)
    branch = one_projection(o[...], ad_ref, 6, w_ref.at[3], ro_ref.at[0])
    result = (stream + mod_ref[2:3, :] * branch).astype(BF16)
    x1_ref[...] = result.reshape(x1_ref.shape)


def temporal_cross_forward(
    x_ref, ctx_ref, mod_ref, mask_ref, ad_ref, wt_hbm, wc_hbm,
    q_ref, k_ref, v_ref, o_ref, stat_ref, rq_ref, ro_ref,
    u2_ref, qc_ref, oc_ref, statc_ref, rqc_ref, roc_ref, kp_ref, vp_ref, rk_ref, rv_ref, x3_ref,
    w_ref, bias_ref, q_s, k_s, v_s, o_s, sems,
):
    first = pl.program_id(0) == 0
    loads = Loads(
        [(wt_hbm.at[i], w_ref.at[i]) for i in range(4)]
        + [(wc_hbm.at[i], w_ref.at[4 + i]) for i in range(4)],
        sems,
    )
    loads.start()

    @pl.when(first)
    def _():
        bias_ref[...] = same_place(bias_ref.shape)

    loaded = x_ref[...].reshape(ROWS, x_ref.shape[2])
    stream = loaded.astype(F32)
    three_projections(loaded, ad_ref, 8, w_ref, loads, 0, (q_s, k_s, v_s), rq_ref.at[0])
    q_ref[...] = q_s[...].reshape(q_ref.shape)
    k_ref[...] = k_s[...].reshape(k_ref.shape)
    v_ref[...] = v_s[...].reshape(v_ref.shape)

    def put_out(index, value):
        o_s[:, tile(index)] = value.astype(BF16)

    attend(q_s, k_s, v_s, mask_ref, bias_ref, put_out, stat_ref.at[0])
    o_ref[...] = o_s[...].reshape(o_ref.shape)
    loads.ready(3)
    branch = one_projection(o_s[...], ad_ref, 14, w_ref.at[3], ro_ref.at[0])
    stream = stream + mod_ref[2:3, :] * branch
    inputs = stream.astype(BF16)
    u2_ref[...] = inputs.reshape(u2_ref.shape)
    loads.ready(4)
    queries = one_projection(inputs, ad_ref, 16, w_ref.at[4], rqc_ref.at[0])
    q_s[...] = queries.astype(BF16)
    qc_ref[...] = q_s[...].reshape(qc_ref.shape)
    loads.ready(5)
    loads.ready(6)

    @pl.when(first)
    def _():
        for base, at, rank_ref, pair_ref in ((18, 5, rk_ref, kp_ref), (20, 6, rv_ref, vp_ref)):
            made = one_projection(ctx_ref[...], ad_ref, base, w_ref.at[at], rank_ref).astype(BF16)
            k_s[:PAD, :] = made
            for pair in range(PAIRS):
                piece = k_s[:PAD, window(pair)]
                pair_ref[pair, :PAD, :] = piece * mask_ref[2 * pair : 2 * pair + 1, :]
                pair_ref[pair, PAD:, :] = piece * mask_ref[2 * pair + 1 : 2 * pair + 2, :]

    carried = None
    count = rk_ref.shape[0] - (PAD - 120)
    for pair in range(PAIRS):
        scores = nt(kp_ref[pair], q_s[:, window(pair)]) * EXP_SCALE
        pieces = []
        for sub in range(2):
            own = scores[PAD * sub : PAD * sub + count]
            top = jnp.max(own, 0, keepdims=True)
            grown = jnp.exp2(own - top)
            total = jnp.sum(grown, 0, keepdims=True)
            statc_ref[0, 2 * pair + sub : 2 * pair + sub + 1, :] = top + jnp.log2(total)
            pieces += [grown * (1.0 / total), jnp.zeros((PAD - count, ROWS), F32)]
        weights = jnp.concatenate(pieces, 0).astype(BF16)
        out = tn(weights, vp_ref[pair])
        low = out[:, :128]
        put_out(pair, low if carried is None else low + carried)
        carried = out[:, 128:]
    put_out(PAIRS, carried)
    oc_ref[...] = o_s[...].reshape(oc_ref.shape)
    loads.ready(7)
    stream = stream + one_projection(o_s[...], ad_ref, 22, w_ref.at[7], roc_ref.at[0])
    x3_ref[...] = stream.reshape(x3_ref.shape)


def gelu_both(hidden):
    root = math.sqrt(2.0 / math.pi)
    square = hidden * hidden
    inner = root * (hidden + 0.044715 * (square * hidden))
    bent = jnp.tanh(inner)
    half = 0.5 * (1.0 + bent)
    slope = half + 0.5 * hidden * (1.0 - bent * bent) * (root * (1.0 + 3.0 * 0.044715 * square))
    return hidden * half, slope


def feed_forward(
    x3_ref, cot_ref, mod_ref, ad_ref, ff_ref, up_hbm, down_hbm,
    x4_ref, g3_ref, gw_ref, gf_ref, up_ref, down_ref, sems,
):
    width = x3_ref.shape[1]
    chunks = down_ref.shape[0]
    loads = Loads(
        [(up_hbm.at[:, pl.ds(c * width, width)], up_ref.at[c]) for c in range(chunks)]
        + [(down_hbm.at[pl.ds(c * width, width), :], down_ref.at[c]) for c in range(chunks)],
        sems,
    )
    loads.start()

    @pl.when(pl.program_id(0) == 0)
    def _():
        gw_ref[...] = jnp.zeros_like(gw_ref)
        gf_ref[...] = jnp.zeros_like(gf_ref)

    stream = x3_ref[...]
    normal, inverse = normalize(stream)
    inputs = (normal * (1.0 + mod_ref[4:5, :]) + mod_ref[3:4, :]).astype(BF16)
    cot = cot_ref[...].astype(F32)
    grad_branch = (mod_ref[5:6, :] * cot).astype(BF16)
    rank_up = nt(inputs, ad_ref[0]).astype(BF16)
    grad_rank_down = nt(grad_branch, ad_ref[1]).astype(BF16)
    branch = None
    rank_down = None
    grad_in = None
    grad_rank_up = None

    def add(old, new):
        return new if old is None else old + new

    for c in range(chunks):
        cols = slice(c * width, c * width + width)
        loads.ready(c)
        hidden = nn(inputs, up_ref[c]) + nn(rank_up, ff_ref[0, :, cols])
        active, slope = gelu_both(hidden)
        active = active.astype(BF16)
        loads.ready(chunks + c)
        grad_active = nt(grad_branch, down_ref[c]) + nn(grad_rank_down, ff_ref[1, :, cols])
        grad_hidden = (slope * grad_active).astype(BF16)
        branch = add(branch, nn(active, down_ref[c]))
        rank_down = add(rank_down, nt(active, ff_ref[1, :, cols]))
        grad_in = add(grad_in, nt(grad_hidden, up_ref[c]))
        grad_rank_up = add(grad_rank_up, nt(grad_hidden, ff_ref[0, :, cols]))
        gf_ref[0, :, cols] += tn(rank_up, grad_hidden)
        gf_ref[1, :, cols] += tn(grad_rank_down, active)
    rank_down = rank_down.astype(BF16)
    grad_rank_up = grad_rank_up.astype(BF16)
    branch = branch + nn(rank_down, ad_ref[1])
    x4_ref[...] = (stream + mod_ref[5:6, :] * branch).astype(BF16)
    grad_in = grad_in + nn(grad_rank_up, ad_ref[0])
    gw_ref[0] += tn(grad_rank_up, inputs)
    gw_ref[1] += tn(rank_down, grad_branch)
    g3_ref[...] = cot + normalize_back(normal, inverse, grad_in * (1.0 + mod_ref[4:5, :]))


def cross_temporal_backward(
    g3_ref, u1_ref, q_ref, k_ref, v_ref, o_ref, stat_ref, rq_ref, ro_ref,
    u2_ref, qc_ref, oc_ref, statc_ref, rqc_ref, roc_ref, kp_ref, vp_ref, rk_ref, rv_ref,
    ctx_ref, mod_ref, mask_ref, ad_ref, wt_hbm, wc_hbm,
    g1_ref, gw_ref,
    w_ref, bias_ref, dk_acc, dv_acc, q_s, k_s, v_s, do_s, dq_s, dk_s, dv_s, ctx_s, sems,
):
    step = pl.program_id(0)
    first = step == 0
    loads = Loads(
        [(wc_hbm.at[3], w_ref.at[0]), (wc_hbm.at[0], w_ref.at[1]), (wt_hbm.at[3], w_ref.at[2])]
        + [(wt_hbm.at[i], w_ref.at[3 + i]) for i in range(3)],
        sems,
    )
    loads.start()

    @pl.when(first)
    def _():
        bias_ref[...] = same_place(bias_ref.shape)
        gw_ref[...] = jnp.zeros_like(gw_ref)
        dk_acc[...] = jnp.zeros_like(dk_acc)
        dv_acc[...] = jnp.zeros_like(dv_acc)

    def rows(ref):
        return ref[...].reshape(ROWS, ref.shape[2])

    grad = rows(g3_ref)
    loads.ready(0)
    do_s[...] = one_back(
        grad.astype(BF16), rows(oc_ref), roc_ref[0], ad_ref, 22, w_ref.at[0], gw_ref, 14
    ).astype(BF16)
    q_s[...] = rows(qc_ref)
    count = 120
    carried = None
    for pair in range(PAIRS):
        win = window(pair)
        q_win, do_win = q_s[:, win], do_s[:, win]
        scores = nt(kp_ref[pair], q_win) * EXP_SCALE
        grad_probs = nt(vp_ref[pair], do_win)
        all_probs, all_grads = [], []
        nothing = jnp.zeros((PAD - count, ROWS), F32)
        for sub in range(2):
            span = slice(PAD * sub, PAD * sub + count)
            row = 2 * pair + sub
            probs = jnp.exp2(scores[span] - statc_ref[0, row : row + 1, :])
            own = grad_probs[span]
            inner = jnp.sum(probs * own, 0, keepdims=True)
            all_probs += [probs, nothing]
            all_grads += [probs * (own - inner), nothing]
        probs = jnp.concatenate(all_probs, 0).astype(BF16)
        grad_scores = jnp.concatenate(all_grads, 0).astype(BF16)
        dk_acc[pair] += nn(grad_scores, q_win)
        dv_acc[pair] += nn(probs, do_win)
        out = tn(grad_scores, kp_ref[pair])
        low = out[:, :128]
        dq_s[:, tile(pair)] = ((low if carried is None else low + carried) * SCALE).astype(BF16)
        carried = out[:, 128:]
    dq_s[:, tile(PAIRS)] = (carried * SCALE).astype(BF16)
    loads.ready(1)
    grad = grad + one_back(
        dq_s[...], rows(u2_ref), rqc_ref[0], ad_ref, 16, w_ref.at[1], gw_ref, 8
    )
    loads.ready(2)
    do_s[...] = one_back(
        (mod_ref[2:3, :] * grad).astype(BF16), rows(o_ref), ro_ref[0], ad_ref, 14, w_ref.at[2], gw_ref, 6
    ).astype(BF16)
    q_s[...] = rows(q_ref)
    k_s[...] = rows(k_ref)
    v_s[...] = rows(v_ref)

    def put(index, values):
        dq_s[:, tile(index)] = (values[0] * SCALE).astype(BF16)
        dk_s[:, tile(index)] = (values[1] * SCALE).astype(BF16)
        dv_s[:, tile(index)] = values[2].astype(BF16)

    attend_back(q_s, k_s, v_s, do_s, mask_ref, bias_ref, stat_ref.at[0], put)
    grad = grad + three_back(
        (dq_s, dk_s, dv_s), rows(u1_ref), rq_ref[0], ad_ref, 8, w_ref, loads, 3, gw_ref, 0
    )
    g1_ref[...] = grad.astype(BF16).reshape(g1_ref.shape)

    @pl.when(step == pl.num_programs(0) - 1)
    def _():
        context = ctx_ref[...].astype(F32)
        for acc, factor, rank_ref, base, at in (
            (dk_acc, SCALE, rk_ref, 18, 10),
            (dv_acc, 1.0, rv_ref, 20, 12),
        ):
            held = None
            for pair in range(PAIRS):
                whole = acc[pair]
                out = whole[:PAD] * mask_ref[2 * pair : 2 * pair + 1, :].astype(F32)
                out = out + whole[PAD:] * mask_ref[2 * pair + 1 : 2 * pair + 2, :].astype(F32)
                out = out * factor
                low = out[:, :128]
                ctx_s[:, tile(pair)] = low if held is None else low + held
                held = out[:, 128:]
            ctx_s[:, tile(PAIRS)] = held
            grad_kv = ctx_s[...]
            grad_rank = lax.dot_general(
                grad_kv, ad_ref[base + 1].astype(F32), (((1,), (1,)), ((), ())),
                precision=HIGHEST, preferred_element_type=F32,
            )
            gw_ref[at] = lax.dot_general(
                grad_rank, context, (((0,), (0,)), ((), ())),
                precision=HIGHEST, preferred_element_type=F32,
            )
            gw_ref[at + 1] = lax.dot_general(
                rank_ref[...].astype(F32), grad_kv, (((0,), (0,)), ((), ())),
                precision=HIGHEST, preferred_element_type=F32,
            )


def spatial_backward(
    g1_ref, x_ref, q_ref, k_ref, v_ref, o_ref, stat_ref, rq_ref, ro_ref, mod_ref, mask_ref, ad_ref, w_hbm,
    g0_ref, gw_ref, w_ref, do_s, dq_s, dk_s, dv_s, sems,
):
    loads = Loads(
        [(w_hbm.at[3], w_ref.at[0])] + [(w_hbm.at[i], w_ref.at[1 + i]) for i in range(3)], sems
    )
    loads.start()

    @pl.when(pl.program_id(0) == 0)
    def _():
        gw_ref[...] = jnp.zeros_like(gw_ref)

    grad = g1_ref[...].reshape(ROWS, g1_ref.shape[3]).astype(F32)
    loads.ready(0)
    do_s[...] = one_back(
        (mod_ref[2:3, :] * grad).astype(BF16), o_ref[0], ro_ref[0], ad_ref, 6, w_ref.at[0], gw_ref, 6
    ).astype(BF16)

    def put(index, values):
        dq_s[:, tile(index)] = (values[0] * SCALE).astype(BF16)
        dk_s[:, tile(index)] = (values[1] * SCALE).astype(BF16)
        dv_s[:, tile(index)] = values[2].astype(BF16)

    attend_back(
        q_ref.at[0], k_ref.at[0], v_ref.at[0], do_s, mask_ref, None, stat_ref.at[0], put
    )
    normal, inverse = normalize(x_ref[0].astype(F32))
    inputs = (normal * (1.0 + mod_ref[1:2, :]) + mod_ref[0:1, :]).astype(BF16)
    grad_in = three_back(
        (dq_s, dk_s, dv_s), inputs, rq_ref[0], ad_ref, 0, w_ref, loads, 1, gw_ref, 0
    )
    grad = grad + normalize_back(normal, inverse, grad_in * (1.0 + mod_ref[1:2, :]))
    g0_ref[0] = grad.astype(BF16)


def whole_block(array):
    zeros = (0,) * array.ndim
    return pl.BlockSpec(array.shape, lambda i: zeros)


def anywhere():
    return pl.BlockSpec(memory_space=pl.ANY)


def like(shape, dtype):
    return jax.ShapeDtypeStruct(shape, dtype)


PARAMS = pltpu.CompilerParams(
    dimension_semantics=("arbitrary",), vmem_limit_bytes=VMEM_LIMIT
)


def cost(flops, read):
    return pl.CostEstimate(flops=flops, bytes_accessed=read, transcendentals=flops // 4096)


def run_spatial_forward(video, mods, masks, wide, w_s, parts):
    frames, rows, d = video.shape
    places = rows // parts
    by_frame = lambda i: (i, 0, 0)
    row_block = pl.BlockSpec((1, rows, d), by_frame)
    return pl.pallas_call(
        spatial_forward,
        grid=(frames,),
        in_specs=[row_block, whole_block(mods), whole_block(masks), whole_block(wide), anywhere()],
        out_specs=[
            pl.BlockSpec((parts, 1, places, d), lambda i: (0, i, 0, 0)),
            row_block,
            row_block,
            row_block,
            row_block,
            pl.BlockSpec((1, HEADS, rows), by_frame),
            pl.BlockSpec((1, rows, 3 * RANK), by_frame),
            pl.BlockSpec((1, rows, RANK), by_frame),
        ],
        out_shape=[like((parts, frames, places, d), BF16)]
        + [like(video.shape, BF16)] * 4
        + [
            like((frames, HEADS, rows), F32),
            like((frames, rows, 3 * RANK), BF16),
            like((frames, rows, RANK), BF16),
        ],
        scratch_shapes=[pltpu.VMEM((4, d, d), BF16), pltpu.SemaphoreType.DMA((4,))],
        compiler_params=PARAMS,
        cost_estimate=cost(10 * frames * rows * d * d, 30_000_000),
        name="spatial_forward",
    )(video, mods, masks, wide, w_s)


def run_temporal_cross_forward(x1, context, mods, masks, wide, w_t, w_c):
    frames, places, d = x1.shape
    groups = places * frames // ROWS
    across = pl.BlockSpec((frames, ROWS // frames, d), lambda i: (0, i, 0))
    by_group = lambda i: (i, 0, 0)
    stat = pl.BlockSpec((1, HEADS, ROWS), by_group)
    three = pl.BlockSpec((1, ROWS, 3 * RANK), by_group)
    one = pl.BlockSpec((1, ROWS, RANK), by_group)
    full = lambda *shape: pl.BlockSpec(shape, lambda i: (0,) * len(shape))
    act = like(x1.shape, BF16)
    stat_shape = like((groups, HEADS, ROWS), F32)
    one_shape = like((groups, ROWS, RANK), BF16)
    return pl.pallas_call(
        temporal_cross_forward,
        grid=(groups,),
        in_specs=[across, whole_block(context), whole_block(mods), whole_block(masks), whole_block(wide), anywhere(), anywhere()],
        out_specs=[across] * 4 + [stat, three, one] + [across] * 3 + [stat, one, one]
        + [full(PAIRS, 2 * PAD, 256)] * 2 + [full(PAD, RANK)] * 2 + [across],
        out_shape=[act] * 4 + [stat_shape, like((groups, ROWS, 3 * RANK), BF16), one_shape]
        + [act] * 3 + [stat_shape, one_shape, one_shape]
        + [like((PAIRS, 2 * PAD, 256), BF16)] * 2 + [like((PAD, RANK), BF16)] * 2
        + [like(x1.shape, F32)],
        scratch_shapes=[pltpu.VMEM((8, d, d), BF16), pltpu.VMEM((ROWS, ROWS), F32)]
        + [pltpu.VMEM((ROWS, d), BF16)] * 4
        + [pltpu.SemaphoreType.DMA((8,))],
        compiler_params=PARAMS,
        cost_estimate=cost(14 * places * frames * d * d, 50_000_000),
        name="temporal_cross_forward",
    )(x1, context, mods, masks, wide, w_t, w_c)


def run_feed_forward(x3, cot, mods, wide_ff, narrow, up, down):
    tokens, d = x3.shape
    hidden = up.shape[1]
    chunks = hidden // d
    rows = pl.BlockSpec((ROWS, d), lambda i: (i, 0))
    return pl.pallas_call(
        feed_forward,
        grid=(tokens // ROWS,),
        in_specs=[rows, rows, whole_block(mods), whole_block(wide_ff), whole_block(narrow), anywhere(), anywhere()],
        out_specs=[
            rows,
            rows,
            pl.BlockSpec((2, RANK, d), lambda i: (0, 0, 0)),
            pl.BlockSpec((2, RANK, hidden), lambda i: (0, 0, 0)),
        ],
        out_shape=[
            like((tokens, d), BF16),
            like((tokens, d), F32),
            like((2, RANK, d), F32),
            like((2, RANK, hidden), F32),
        ],
        scratch_shapes=[
            pltpu.VMEM((chunks, d, d), BF16),
            pltpu.VMEM((chunks, d, d), BF16),
            pltpu.SemaphoreType.DMA((2 * chunks,)),
        ],
        compiler_params=PARAMS,
        cost_estimate=cost(8 * tokens * d * hidden, 50_000_000),
        name="feed_forward",
    )(x3, cot, mods, wide_ff, narrow, up, down)


def run_cross_temporal_backward(g3, u1, saved, context, mods, masks, wide, w_t, w_c):
    frames, places, d = u1.shape
    groups = places * frames // ROWS
    across = pl.BlockSpec((frames, ROWS // frames, d), lambda i: (0, i, 0))
    by_group = lambda i: (i, 0, 0)
    stat = pl.BlockSpec((1, HEADS, ROWS), by_group)
    three = pl.BlockSpec((1, ROWS, 3 * RANK), by_group)
    one = pl.BlockSpec((1, ROWS, RANK), by_group)
    kp, vp, rk, rv = saved[13:17]
    return pl.pallas_call(
        cross_temporal_backward,
        grid=(groups,),
        in_specs=[across, across] + [across] * 4 + [stat, three, one] + [across] * 3 + [stat, one, one]
        + [whole_block(kp), whole_block(vp), whole_block(rk), whole_block(rv)]
        + [whole_block(context), whole_block(mods), whole_block(masks), whole_block(wide), anywhere(), anywhere()],
        out_specs=[across, pl.BlockSpec((16, RANK, d), lambda i: (0, 0, 0))],
        out_shape=[like(u1.shape, BF16), like((16, RANK, d), F32)],
        scratch_shapes=[
            pltpu.VMEM((6, d, d), BF16),
            pltpu.VMEM((ROWS, ROWS), F32),
            pltpu.VMEM((PAIRS, 2 * PAD, 256), F32),
            pltpu.VMEM((PAIRS, 2 * PAD, 256), F32),
        ]
        + [pltpu.VMEM((ROWS, d), BF16)] * 7
        + [pltpu.VMEM((PAD, d), F32), pltpu.SemaphoreType.DMA((6,))],
        compiler_params=PARAMS,
        cost_estimate=cost(14 * places * frames * d * d, 50_000_000),
        name="cross_temporal_backward",
    )(g3, u1, *saved[:17], context, mods, masks, wide, w_t, w_c)


def run_spatial_backward(g1, video, saved, mods, masks, wide, w_s):
    frames, rows, d = video.shape
    parts, _, places, _ = g1.shape
    by_frame = lambda i: (i, 0, 0)
    row_block = pl.BlockSpec((1, rows, d), by_frame)
    return pl.pallas_call(
        spatial_backward,
        grid=(frames,),
        in_specs=[pl.BlockSpec((parts, 1, places, d), lambda i: (0, i, 0, 0))]
        + [row_block] * 5
        + [
            pl.BlockSpec((1, HEADS, rows), by_frame),
            pl.BlockSpec((1, rows, 3 * RANK), by_frame),
            pl.BlockSpec((1, rows, RANK), by_frame),
            whole_block(mods),
            whole_block(masks),
            whole_block(wide),
            anywhere(),
        ],
        out_specs=[row_block, pl.BlockSpec((8, RANK, d), lambda i: (0, 0, 0))],
        out_shape=[like(video.shape, BF16), like((8, RANK, d), F32)],
        scratch_shapes=[pltpu.VMEM((4, d, d), BF16)]
        + [pltpu.VMEM((ROWS, d), BF16)] * 4
        + [pltpu.SemaphoreType.DMA((4,))],
        compiler_params=PARAMS,
        cost_estimate=cost(10 * frames * rows * d * d, 30_000_000),
        name="spatial_backward",
    )(g1, video, *saved, mods, masks, wide, w_s)


def exchange(array):
    return lax.all_to_all(array, "seq", split_axis=0, concat_axis=0, tiled=True)


def exchange_clips(array):
    return lax.all_to_all(array, "fsdp", split_axis=0, concat_axis=0, tiled=True)


def fetch_adapters(choice, adapt_wide, adapt_ff):
    clips = choice.shape[0]
    narrow_cols, cols = adapt_ff.shape[-1], adapt_wide.shape[-1]
    times = narrow_cols // cols
    narrow = adapt_ff.reshape(adapt_ff.shape[:-1] + (times, cols))
    narrow = jnp.moveaxis(narrow, 3, 1).reshape(2 * times, *adapt_wide.shape[1:])
    table = jnp.concatenate([adapt_wide, narrow], 0)
    picked = jnp.sum(
        choice[:, None, :, None, None] * table[None].astype(F32), axis=2
    ).astype(BF16)
    got = exchange_clips(picked)
    count = adapt_wide.shape[0]
    wide = jnp.moveaxis(got[:, :count], 0, 2).reshape(count, RANK, clips * cols)
    narrow = got[:, count:].reshape(clips, 2, times, RANK, cols)
    narrow = narrow.transpose(1, 3, 0, 2, 4).reshape(2, RANK, clips * narrow_cols)
    return wide, narrow


def collect_grads(choice, wide, narrow):
    clips = choice.shape[0]
    count, _, d = wide.shape
    cols = d // clips
    times = narrow.shape[-1] // d
    wide = jnp.moveaxis(wide.astype(BF16).reshape(count, RANK, clips, cols), 2, 0)
    narrow = narrow.astype(BF16).reshape(2, RANK, clips, times, cols)
    narrow = narrow.transpose(2, 0, 3, 1, 4).reshape(clips, 2 * times, RANK, cols)
    got = exchange_clips(jnp.concatenate([wide, narrow], 1))
    table = jnp.sum(
        choice[:, None, :, None, None] * got[:, :, None].astype(F32), axis=0
    )
    total = lax.psum(table.astype(BF16), "seq").astype(F32)
    wide_out = total[:count]
    narrow_out = total[count:].reshape(2, times, -1, RANK, cols)
    narrow_out = jnp.moveaxis(narrow_out, 1, 3).reshape(2, -1, RANK, times * cols)
    return wide_out, narrow_out


def on_device(
    video,
    context,
    modulation,
    adapter_index,
    cotangent,
    qkv_weights,
    out_weights,
    ffn_up,
    ffn_down,
    adapt_wide,
    adapt_ff,
):
    parts = lax.axis_size("seq")
    clips = lax.axis_size("fsdp")
    d = video.shape[-1]
    places = SPATIAL // parts
    frames = FRAMES // parts
    mods = modulation[0, 0]
    masks = head_masks()
    ctx = jnp.pad(context[0], ((0, PAD - context.shape[1]), (0, 0)))

    def gather(array, axis):
        return lax.all_gather(array, "fsdp", axis=axis, tiled=True)

    all_index = exchange_clips(jnp.broadcast_to(adapter_index, (clips,)))
    choice = (all_index[:, None] == jnp.arange(adapt_wide.shape[2])[None, :]).astype(F32)
    wide, narrow = fetch_adapters(choice, adapt_wide[0], adapt_ff[0])
    quads = [
        gather(jnp.concatenate([qkv_weights[0, 3 * j : 3 * j + 3], out_weights[0, j : j + 1]], 0), 1)
        for j in range(3)
    ]
    down = gather(ffn_down[0], 0)
    up = gather(ffn_up[0], 0)

    cot = cotangent.reshape(frames, parts, places, d).transpose(1, 0, 2, 3)
    cot = exchange(cot).reshape(FRAMES * places, d)
    frames_in = video.reshape(frames, SPATIAL, d)
    x1, *kept_s = run_spatial_forward(frames_in, mods, masks, wide, quads[0], parts)
    u1 = exchange(x1).reshape(FRAMES, places, d)
    *kept_t, x3 = run_temporal_cross_forward(u1, ctx, mods, masks, wide, quads[1], quads[2])
    x4, g3, grads_f, narrow_grads = run_feed_forward(
        x3.reshape(FRAMES * places, d), cot, mods, wide[24:26], narrow, up, down
    )
    output = exchange(x4.reshape(parts, frames, places, d))
    output = output.transpose(1, 0, 2, 3).reshape(video.shape)
    g1, grads_t = run_cross_temporal_backward(
        g3.reshape(FRAMES, places, d), u1, kept_t, ctx, mods, masks, wide, quads[1], quads[2]
    )
    g1 = exchange(g1.reshape(parts, frames, places, d))
    g0, grads_s = run_spatial_backward(g1, frames_in, kept_s, mods, masks, wide, quads[0])
    wide_grads = jnp.concatenate([grads_s, grads_t, grads_f], 0)
    wide_out, narrow_out = collect_grads(choice, wide_grads, narrow_grads)
    return (output, g0.reshape(video.shape), wide_out[None], narrow_out[None])


def solution(mesh):
    return jax.shard_map(
        on_device,
        mesh=mesh,
        in_specs=(
            P("fsdp", "seq", None),
            P("fsdp", None, None),
            P("fsdp", None, None, None),
            P("fsdp"),
            P("fsdp", "seq", None),
            P(None, None, "fsdp", None),
            P(None, None, "fsdp", None),
            P(None, "fsdp", None),
            P(None, "fsdp", None),
            P(None, None, None, None, "fsdp"),
            P(None, None, None, None, "fsdp"),
        ),
        out_specs=(
            P("fsdp", "seq", None),
            P("fsdp", "seq", None),
            P(None, None, None, None, "fsdp"),
            P(None, None, None, None, "fsdp"),
        ),
        check_vma=False,
    )
```

time: 3500 us -> 832 us (0.24)
  local copies, waits for them, and re-layouts: 1210 us -> 30 us
  other arithmetic: 895 us -> 32.9 us
  matrix products: 478 us -> 0 us
  Pallas kernels: 0 us -> 334 us
  waiting for transfers between devices: 575 us -> 354 us
  blocking collectives: 229 us -> 31.2 us
  starting transfers between devices: 74.4 us -> 27.2 us
    unnamed x27 -> x0, other arithmetic: 826 us -> none
    dot_general x128 -> x0, matrix products: 478 us -> none  [the longest x12 99.9 us: project_back(): jnp.einsum('cno,io->cni', grad_out, weight, preferred_element_type=jnp.fl...]
    unnamed x361 -> x23, local copies, waits for them, and re-layouts: 464 us -> 1.92 us
    pallas_call x0 -> x5, Pallas kernels: none -> 334 us  [the longest x1 89.4 us: run_feed_forward(): pl.pallas_call(feed_forward, grid=(tokens // ROWS,), in_specs=[rows, rows...]
    convert_element_type x23 -> x0, local copies, waits for them, and re-layouts: 272 us -> none  [the longest x2 28.7 us: layer_backward(): frame_back(grad_v, clip_count).astype(jnp.bfloat16)]
    all_to_all x40 -> x0, local copies, waits for them, and re-layouts: 250 us -> none  [the longest x9 66 us: restore(): lax.all_to_all(for_sending(attended), 'seq', split_axis=1, concat_axis=2,...]
    all_to_all x4 -> x1, blocking collectives: 229 us -> 31.2 us  [exchange_clips(): lax.all_to_all(array, 'fsdp', split_axis=0, concat_axis=0, tiled=True)]
    all_gather x6 -> x5, waiting for transfers between devices: 236 us -> 82.3 us  [gather(): return lax.all_gather(array, 'fsdp', axis=axis, tiled=True)]
  transfers between devices with their start and end apart: 25 -> 12, of which waited for: 14 -> 9; matrix products, arithmetic and copies ran while one was open for 53% -> 6% of each run, Pallas kernels for 0% -> 14%
where the time goes in v1:
time: 832 us; the launch traced here: 825 us
  waiting for transfers between devices  354 us (43%)
  Pallas kernels  334 us (40%)
  other arithmetic  32.9 us (4%)
  blocking collectives  31.2 us (4%)
  local copies, waits for them, and re-layouts  30 us (4%)
  starting transfers between devices  27.2 us (3%)
  between operations  15.3 us (2%)
    all_to_all x4, waiting for transfers between devices, exchange(): return lax.all_to_all(array, 'seq', split_axis=0, concat_axis=0, tiled=True)  179 us
    pallas_call x1, Pallas kernels, run_feed_forward(): pl.pallas_call(feed_forward, grid=(tokens // ROWS,), in_specs=[rows, rows...  89.4 us
    all_gather x5, waiting for transfers between devices, gather(): return lax.all_gather(array, 'fsdp', axis=axis, tiled=True)  82.3 us
    pallas_call x1, Pallas kernels, run_cross_temporal_backward(): pl.pallas_call(cross_temporal_backward, grid=(groups,), in_specs=[across,...  79.7 us
    pallas_call x1, Pallas kernels, run_temporal_cross_forward(): pl.pallas_call(temporal_cross_forward, grid=(groups,), in_specs=[across,...  73.4 us
    pallas_call x1, Pallas kernels, run_spatial_backward(): pl.pallas_call(spatial_backward, grid=(frames,), in_specs=[pl.BlockSpec((...  49.7 us
    all_to_all x2, waiting for transfers between devices, exchange_clips(): lax.all_to_all(array, 'fsdp', split_axis=0, concat_axis=0, tiled=True)  48.6 us
    psum x1, waiting for transfers between devices, collect_grads(): total = lax.psum(table.astype(BF16), 'seq').astype(F32)  43.3 us
  transfers between devices with their start and end apart: 12, of which 9 were waited for; matrix products, arithmetic and copies ran while one was open for 6% of the time, Pallas kernels for 14%

profile of v1, /device:TPU:0, one launch (start us, length us, event | category | flops | bytes accessed | tf_op | source)
XLA Modules:
  0.0 824.9 jit_solution(10507555159538796077)
XLA Ops:
  8.5 2.0 slice_bitcast_fusion.2
  16.8 5.2 all-to-all-start
  22.4 2.5 maximum_convert_fusion
  25.0 1.6 all-to-all-done
  26.9 10.1 %multiply_reduce_fusion.1 = bf16[8,34,16,144]{3,2,1,0:T(8,128)(2,1)} fusion(f32[34,8,16,144]{3,2,1,0:T(8,128)} %maximum_convert_fusion, f32[8,8]{1,0:T(8,128)S(1)} %fusion.2), kind=kLoop, calls=%fused_computation.1 | loop fusion | flops 9400320 | bytes 3760384 | tf_op jit(solution)/shard_map/reduce_sum | solution.py:708
  37.0 3.9 all-to-all-start.1
  42.2 47.1 %all-to-all-done.1 = bf16[8,34,16,144]{3,2,1,0:T(8,128)(2,1)S(1)} async-done(((bf16[8,34,16,144]{3,2,1,0:T(8,128)(2,1)}), bf16[8,34,16,144]{3,2,1,0:T(8,128)(2,1)S(1)}, u32[]{:S(2)}, u32[]{:S(2)}) %all-to-all-start.1) | async-done | bytes 1253408 | tf_op jit(solution)/shard_map/all_to_all | solution.py:698
  90.7 2.1 copy.46
  92.8 3.9 reshape.115.ad_ref
  96.7 1.8 all-gather.8.cloned.1.call-done.w_hbm
  98.5 41.9 %spatial_forward.1 = (bf16[4,4,64,1152]{3,2,1,0:T(8,128)(2,1)}, bf16[4,256,1152]{2,1,0:T(8,128)(2,1)}, bf16[4,256,1152]{2,1,0:T(8,128)(2,1)}, bf16[4,256,1152]{2...) custom-call(bf16[4,256,1152]{2,1,0:T(8,128)(2,1)} %bitcast.79, ...), custom_call_target="tpu_custom_call" | custom-call | flops 13589544960 | bytes 30000000 | tf_op jit(solution)/shard_map/spatial_forward/pallas_call | solution.py:541
  140.4 4.9 all-to-all-start.2
  145.3 3.4 copy.60
  148.7 51.0 %all-to-all-done.2 = bf16[4,4,64,1152]{3,2,1,0:T(8,128)(2,1)} async-done(((bf16[4,4,64,1152]{3,2,1,0:T(8,128)(2,1)}), bf16[4,4,64,1152]{3,2,1,0:T(8,128)(2,1)}, u32[]{:S(2)}, u32[]{:S(2)}) %all-to-all-start.2) | async-done | bytes 2359328 | tf_op jit(solution)/shard_map/all_to_all | solution.py:694
  199.7 4.6 all-to-all-start.3
  207.7 22.7 %all-gather.10.cloned.1.call-done.wt_hbm = bf16[4,1152,1152]{2,1,0:T(8,128)(2,1)} async-done(((bf16[4,144,1152]{2,1,0:T(8,128)(2,1)}), bf16[4,1152,1152]{2,1,0:T(8,128)(2,1)}) %all-gather.10.cloned.1.call-update) | async-done | bytes 10616848 | tf_op jit(solution)/shard_map/all_gather | solution.py:761
  230.4 73.4 %temporal_cross_forward.1 = (bf16[16,64,1152]{2,1,0:T(8,128)(2,1)}, bf16[16,64,1152]{2,1,0:T(8,128)(2,1)}, bf16[16,64,1152]{2,1,0:T(8,128)(2,1)}, bf16[16,64,115...) custom-call(bf16[16,64,1152]{2,1,0:T(8,128)(2,1)} %bitcast.8.x_ref.u, ...), custom_call_target="tpu_custom_call" | custom-call | flops 19025362944 | bytes 50000000 | tf_op jit(solution)/shard_map/temporal_cross_forward/pallas_call | solution.py:581
  303.8 57.8 %all-gather.16.cloned.1.call-done = bf16[1,4608,1152]{2,1,0:T(8,128)(2,1)} async-done(((bf16[1,576,1152]{2,1,0:T(8,128)(2,1)}), bf16[1,4608,1152]{2,1,0:T(8,128)(2,1)}) %all-gather.16.cloned.1.call-update) | async-done | bytes 10616848 | tf_op jit(solution)/shard_map/all_gather | solution.py:761
  361.5 89.4 %feed_forward.1 = (bf16[1024,1152]{1,0:T(8,128)(2,1)}, f32[1024,1152]{1,0:T(8,128)}, f32[2,16,1152]{2,1,0:T(8,128)}, f32[2,16,4608]{2,1,0:T(8,128)}) custom-call(f32[1024,1152]{1,0:T(8,128)} %bitcast.81, bf16[1024,1152]{1,0:T(8,128)(2,1)} %bitcast.17.cot_ref, f32[6,1152]{1,0:T(8,128)} %bitcast.74, bf16[2,16,1152]{2,1,0:T(8,128)(2,1)} %slice.44.ad_ref, ...), custom_call_target="tpu_custom_call" | custom-call | flops 43486543872 | bytes 50000000 | tf_op jit(solution)/shard_map/feed_forward/pallas_call | solution.py:605
  450.9 79.7 %cross_temporal_backward.1 = (bf16[16,64,1152]{2,1,0:T(8,128)(2,1)}, f32[16,16,1152]{2,1,0:T(8,128)}) custom-call(f32[16,64,1152]{2,1,0:T(8,128)} %bitcast.82, bf16[16,64,1152]{2,1,0:T(8,128)(2,1)} %bitcast.8.x_ref.u1_ref, bf16[16,64,1152]{2,1,0:T(8,128)(2,1)} %get-tuple-element.42.q_ref, bf16[16,64,1152]{2,1,0:T(8,128)(2,1)} %get-tuple-element.43.k_ref, ...), custom_call_target="tpu_custom_call" | custom-call | flops 19025362944 | bytes 50000000 | tf_op jit(solution)/shard_map/cross_temporal_backward/pallas_call | solution.py:641
  530.7 4.7 all-to-all-start.5
  538.6 51.3 %all-to-all-done.5.g1_ref = bf16[4,4,64,1152]{3,2,1,0:T(8,128)(2,1)} async-done(((bf16[4,4,64,1152]{3,2,1,0:T(8,128)(2,1)}), bf16[4,4,64,1152]{3,2,1,0:T(8,128)(2,1)}, u32[]{:S(2)}, u32[]{:S(2)}) %all-to-all-start.5) | async-done | bytes 2359328 | tf_op jit(solution)/shard_map/all_to_all | solution.py:694
  589.9 49.7 %spatial_backward.1 = (bf16[4,256,1152]{2,1,0:T(8,128)(2,1)}, f32[8,16,1152]{2,1,0:T(8,128)}) custom-call(bf16[4,4,64,1152]{3,2,1,0:T(8,128)(2,1)} %all-to-all-done.5.g1_ref, bf16[4,256,1152]{2,1,0:T(8,128)(2,1)} %bitcast.80, bf16[4,256,1152]{2,1,0:T(8,128)(2,1)} %get-tuple-element.60.q_ref, bf16[4,256,1152]{2,1,0:T(8,128)(2,1)} %get-tuple-element.61.k_ref, ...), custom_call_target="tpu_custom_call" | custom-call | flops 13589544960 | bytes 30000000 | tf_op jit(solution)/shard_map/spatial_backward/pallas_call | solution.py:668
  642.2 31.2 %all_to_all.36 = bf16[8,34,16,144]{3,2,1,0:T(8,128)(2,1)} all-to-all(bf16[8,34,16,144]{3,2,1,0:T(8,128)(2,1)S(1)} %pad_maximum_fusion), channel_id=1, replica_groups=mesh['seq'=4,'fsdp'=8] {'fsdp'}, dimensions={0} | all-to-all | bytes 2506752 | tf_op jit(solution)/shard_map/all_to_all | solution.py:698
  673.3 3.6 all-to-all-start.4
  677.0 4.3 convert_element_type.43
  681.4 8.7 %multiply_reduce_fusion = bf16[34,8,16,144]{3,2,1,0:T(8,128)(2,1)} fusion(f32[8,34,16,144]{3,2,1,0:T(8,128)} %convert_element_type.43, f32[8,8]{1,0:T(8,128)S(1)} %fusion.2), kind=kLoop, calls=%fused_computation | loop fusion | flops 9400320 | bytes 3760384 | tf_op jit(solution)/shard_map/reduce_sum | solution.py:728
  690.1 76.6 %all-to-all-done.4 = bf16[4,4,64,1152]{3,2,1,0:T(8,128)(2,1)S(1)} async-done(((bf16[4,4,64,1152]{3,2,1,0:T(8,128)(2,1)}), bf16[4,4,64,1152]{3,2,1,0:T(8,128)(2,1)S(1)}, u32[]{:S(2)}, u32[]{:S(2)}) %all-to-all-start.4) | async-done | bytes 2359328 | tf_op jit(solution)/shard_map/all_to_all | solution.py:694
  766.8 1.6 copy.50
  768.4 43.3 %all-reduce.3.cloned.1.call-done = bf16[34,8,16,144]{3,2,1,0:T(8,128)(2,1)} async-done(((bf16[34,8,16,144]{3,2,1,0:T(8,128)(2,1)}), bf16[34,8,16,144]{3,2,1,0:T(8,128)(2,1)}) %all-reduce.3.cloned.1.call-update) | async-done | bytes 1253392 | tf_op jit(solution)/shard_map/psum | solution.py:731
  813.6 1.5 broadcast_in_dim_reshape.3
  815.7 2.1 slice_bitcast_fusion
  (74 shorter events, 21.9 us)
Async XLA Ops:
  7.2 91.4 %all-gather.8.cloned.1.call-start = ((), (), s32[]{:S(2)}) async-start(), calls=%async_computation.7 | async-start | bytes 11943936 | tf_op jit(solution)/shard_map/all_gather | solution.py:761
  11.7 196.0 %all-gather.12.cloned.1.call-start = ((), (), s32[]{:S(2)}) async-start(), calls=%async_computation.9 | async-start | bytes 11943936 | tf_op jit(solution)/shard_map/all_gather | solution.py:761
  13.1 217.3 %all-gather.10.cloned.1.call-start = ((), (), s32[]{:S(2)}) async-start(), calls=%async_computation.8 | async-start | bytes 11943936 | tf_op jit(solution)/shard_map/all_gather | solution.py:761
  14.4 7.6 copy-start.5
  14.4 8.1 copy-start.2
  14.4 289.4 %all-gather.14.cloned.1.call-start = ((), (), s32[]{:S(2)}) async-start(), calls=%async_computation.11 | async-start | bytes 11943936 | tf_op jit(solution)/shard_map/all_gather | solution.py:761
  15.0 346.5 %all-gather.16.cloned.1.call-start = ((), (), s32[]{:S(2)}) async-start(), calls=%async_computation.12 | async-start | bytes 11943936 | tf_op jit(solution)/shard_map/all_gather | solution.py:761
  16.8 9.8 %all-to-all-start = ((s32[8,1,1]{2,1,0:T(1,128)}), s32[8,1,1]{2,1,0:T(1,128)S(1)}, u32[]{:S(2)}, u32[]{:S(2)}) async-start(s32[8,1,1]{2,1,0:T(1,128)} %broadcast_in_dim.7), calls=%async_computation | async-start | bytes 8192 | tf_op jit(solution)/shard_map/all_to_all | solution.py:698
  37.0 3.9 copy-start.8
  37.0 4.6 copy-start.9
  37.0 4.6 copy-start.10
  37.0 52.3 %all-to-all-start.1 = ((bf16[8,34,16,144]{3,2,1,0:T(8,128)(2,1)}), bf16[8,34,16,144]{3,2,1,0:T(8,128)(2,1)S(1)}, u32[]{:S(2)}, u32[]{:S(2)}) async-start(bf16[8,34,16,144]{3,2,1,0:T(8,128)(2,1)} %multiply_reduce_fusion.1), calls=%async_computation.1 | async-start | bytes 4456448 | tf_op jit(solution)/shard_map/all_to_all | solution.py:698
  89.4 1.3 copy-start
  140.4 59.2 %all-to-all-start.2 = ((bf16[4,4,64,1152]{3,2,1,0:T(8,128)(2,1)}), bf16[4,4,64,1152]{3,2,1,0:T(8,128)(2,1)}, u32[]{:S(2)}, u32[]{:S(2)}) async-start(bf16[4,4,64,1152]{3,2,1,0:T(8,128)(2,1)} %get-tuple-element.38), calls=%async_computation.2 | async-start | bytes 4718592 | tf_op jit(solution)/shard_map/all_to_all | solution.py:694
  199.7 4.6 copy-start.6
  199.7 104.1 %all-to-all-start.3 = ((bf16[4,4,64,1152]{3,2,1,0:T(8,128)(2,1)}), bf16[4,4,64,1152]{3,2,1,0:T(8,128)(2,1)}, u32[]{:S(2)}, u32[]{:S(2)}) async-start(bf16[4,4,64,1152]{3,2,1,0:T(8,128)(2,1)} %bitcast.54), calls=%async_computation.3 | async-start | bytes 4718592 | tf_op jit(solution)/shard_map/all_to_all | solution.py:694
  204.3 2.5 slice-start
  530.6 4.8 copy-start.7
  530.6 5.0 copy-start.4
  530.7 59.2 %all-to-all-start.5 = ((bf16[4,4,64,1152]{3,2,1,0:T(8,128)(2,1)}), bf16[4,4,64,1152]{3,2,1,0:T(8,128)(2,1)}, u32[]{:S(2)}, u32[]{:S(2)}) async-start(bf16[4,4,64,1152]{3,2,1,0:T(8,128)(2,1)} %bitcast.62), calls=%async_computation.5 | async-start | bytes 4718592 | tf_op jit(solution)/shard_map/all_to_all | solution.py:694
  535.4 1.5 copy-start.3
  673.3 93.4 %all-to-all-start.4 = ((bf16[4,4,64,1152]{3,2,1,0:T(8,128)(2,1)}), bf16[4,4,64,1152]{3,2,1,0:T(8,128)(2,1)S(1)}, u32[]{:S(2)}, u32[]{:S(2)}) async-start(bf16[4,4,64,1152]{3,2,1,0:T(8,128)(2,1)} %bitcast.61), calls=%async_computation.4 | async-start | bytes 4718592 | tf_op jit(solution)/shard_map/all_to_all | solution.py:694
  677.0 134.7 %all-reduce.3.cloned.1.call-start = ((), (), s32[]{:S(2)}) async-start(), calls=%async_computation.10 | async-start | bytes 4456448 | tf_op jit(solution)/shard_map/psum | solution.py:731
  812.8 2.2 copy-start.1
Sparse Core Ops, SparseCore 0:
  11.8 86.6 all-gather.7
  100.4 64.1 all-gather.11
  166.5 63.8 all-gather.9
  232.1 63.8 all-gather.13
  297.7 63.7 all-gather.15
  690.2 121.3 all-reduce.2

commit v2 on v1

v2 whole, which is shorter than its diff:
```python
import math

import jax
import jax.numpy as jnp
from jax import lax
from jax.experimental import pallas as pl
from jax.experimental.pallas import tpu as pltpu
from jax.sharding import PartitionSpec as P

HEAD_DIM = 72
HEADS = 16
FRAMES = 16
SPATIAL = 256
RANK = 16
ROWS = 256
PAIRS = HEADS // 2
PAD = 128
SCALE = HEAD_DIM ** (-0.5)
EXP_SCALE = SCALE * math.log2(math.e)
HIGHEST = lax.Precision.HIGHEST
F32 = jnp.float32
BF16 = jnp.bfloat16
VMEM_LIMIT = 60 * 1024 * 1024


def nn(left, right):
    return lax.dot_general(left, right, (((1,), (0,)), ((), ())), preferred_element_type=F32)


def nt(left, right):
    return lax.dot_general(left, right, (((1,), (1,)), ((), ())), preferred_element_type=F32)


def tn(left, right):
    return lax.dot_general(left, right, (((0,), (0,)), ((), ())), preferred_element_type=F32)


def window(pair):
    return slice(128 * pair, 128 * pair + 256)


def normalize(stream):
    average = jnp.mean(stream, -1, keepdims=True)
    centred = stream - average
    inverse = lax.rsqrt(jnp.mean(centred * centred, -1, keepdims=True) + 1e-06)
    return centred * inverse, inverse


def normalize_back(normal, inverse, grad):
    mean_grad = jnp.mean(grad, -1, keepdims=True)
    mean_both = jnp.mean(grad * normal, -1, keepdims=True)
    return inverse * (grad - mean_grad - normal * mean_both)


def up_rows(ad_ref, number, slot, width):
    rows = ad_ref[2 * number + 1]
    before = jnp.zeros((RANK * slot, width), BF16)
    after = jnp.zeros((PAD - RANK * (slot + 1), width), BF16)
    return jnp.concatenate(([before] if slot else []) + [rows, after], 0)


def three_downs(ad_ref, number):
    return jnp.concatenate([ad_ref[2 * (number + i)] for i in range(3)], 0)


class Loads:
    def __init__(self, entries, sems):
        self.first = pl.program_id(0) == 0
        self.entries = entries
        self.sems = sems

    def copy(self, index):
        source, target = self.entries[index]
        return pltpu.make_async_copy(source, target, self.sems.at[index])

    def start(self):
        @pl.when(self.first)
        def _():
            for index in range(len(self.entries)):
                self.copy(index).start()

    def ready(self, index):
        @pl.when(self.first)
        def _():
            self.copy(index).wait()


def head_masks():
    lane = jnp.arange(256)[None, :]
    begin = jnp.array([16 * (h // 2) + HEAD_DIM * (h % 2) for h in range(HEADS)])[:, None]
    return ((lane >= begin) & (lane < begin + HEAD_DIM)).astype(BF16)


def same_place(shape):
    rows = lax.broadcasted_iota(jnp.int32, shape, 0)
    cols = lax.broadcasted_iota(jnp.int32, shape, 1)
    return jnp.where(rows % 16 == cols % 16, 0.0, -1e30).astype(F32)


def attend(q_ref, k_ref, v_ref, mask_ref, bias, put_out, stat_ref):
    carried = None
    for pair in range(PAIRS):
        win = window(pair)
        q_win, k_win, v_win = q_ref[:, win], k_ref[:, win], v_ref[:, win]
        out = None
        for head in (2 * pair, 2 * pair + 1):
            mask = mask_ref[head : head + 1, :]
            scores = nt(k_win * mask, q_win) * EXP_SCALE
            if bias is not None:
                scores = scores + bias[...]
            top = jnp.max(scores, 0, keepdims=True)
            grown = jnp.exp2(scores - top)
            total = jnp.sum(grown, 0, keepdims=True)
            stat_ref[head : head + 1, :] = top + jnp.log2(total)
            weights = (grown * (1.0 / total)).astype(BF16)
            part = tn(weights, v_win * mask)
            out = part if out is None else out + part
        low = out[:, :128]
        put_out(pair, low if carried is None else low + carried)
        carried = out[:, 128:]
    put_out(PAIRS, carried)


def attend_back(q_ref, k_ref, v_ref, do_ref, mask_ref, bias, stat_ref, put):
    carried = None
    for pair in range(PAIRS):
        win = window(pair)
        q_win, k_win, v_win, do_win = q_ref[:, win], k_ref[:, win], v_ref[:, win], do_ref[:, win]
        grads = None
        for head in (2 * pair, 2 * pair + 1):
            mask = mask_ref[head : head + 1, :]
            k_own = k_win * mask
            scores = nt(k_own, q_win) * EXP_SCALE
            if bias is not None:
                scores = scores + bias[...]
            probs = jnp.exp2(scores - stat_ref[head : head + 1, :])
            grad_probs = nt(v_win * mask, do_win)
            inner = jnp.sum(probs * grad_probs, 0, keepdims=True)
            grad_scores = (probs * (grad_probs - inner)).astype(BF16)
            parts = (
                tn(grad_scores, k_own),
                nn(grad_scores, q_win * mask),
                nn(probs.astype(BF16), do_win * mask),
            )
            grads = parts if grads is None else tuple(a + b for a, b in zip(grads, parts))
        lows = tuple(g[:, :128] for g in grads)
        if carried is not None:
            lows = tuple(a + b for a, b in zip(lows, carried))
        put(pair, lows)
        carried = tuple(g[:, 128:] for g in grads)
    put(PAIRS, carried)


def tile(index):
    return slice(128 * index, 128 * index + 128)


def three_projections(lhs_ref, ad_ref, number, weights, loads, first_load, outs, rank_ref):
    width = weights.shape[2]
    ranks = nt(lhs_ref[:, :width], three_downs(ad_ref, number)).astype(BF16)
    rank_ref[...] = ranks
    lhs_ref[:, width : width + 3 * RANK] = ranks
    for i in range(3):
        loads.ready(first_load + i)
        outs[i][...] = nn(lhs_ref[...], weights[first_load + i]).astype(BF16)


def one_projection(lhs_ref, ad_ref, number, weight_ref, rank_ref):
    width = weight_ref.shape[1]
    ranks = nt(lhs_ref[:, :width], ad_ref[2 * number]).astype(BF16)
    rank_ref[...] = ranks
    lhs_ref[:, width : width + RANK] = ranks
    return nn(lhs_ref[...], weight_ref[...])


def block_rows(index):
    return slice(RANK * index, RANK * (index + 1))


def one_back(grad, kept, ranks, ad_ref, number, weight_ref, grad_ref, at):
    width = weight_ref.shape[1]
    both = nt(grad, weight_ref[...])
    grad_rank = both[:, width : width + RANK].astype(BF16)
    grad_ref[block_rows(at), :] += tn(grad_rank, kept)
    grad_ref[block_rows(at + 1), :] += tn(ranks, grad)
    return both[:, :width] + nn(grad_rank, ad_ref[2 * number])


def three_back(grads, inputs, ranks, ad_ref, number, weights, loads, first_load, grad_ref, at):
    width = weights.shape[2]
    both = None
    for i in range(3):
        grad = grads[i][...]
        ups = tn(ranks, grad)
        grad_ref[block_rows(at + 2 * i + 1), :] += ups[block_rows(i)]
        loads.ready(first_load + i)
        part = nt(grad, weights[first_load + i])
        both = part if both is None else both + part
    grad_ranks = both[:, width : width + 3 * RANK].astype(BF16)
    downs = tn(grad_ranks, inputs)
    for i in range(3):
        grad_ref[block_rows(at + 2 * i), :] += downs[block_rows(i)]
    return both[:, :width] + nn(grad_ranks, three_downs(ad_ref, number))


def spatial_forward(
    x_ref, mod_ref, mask_ref, ad_ref, w_hbm, x1_ref, q_ref, k_ref, v_ref, o_ref, stat_ref, rq_ref, ro_ref,
    w_ref, lhs_ref, sems,
):
    width = x_ref.shape[2]
    loads = Loads([(w_hbm.at[i], w_ref.at[i, pl.ds(0, width), :]) for i in range(4)], sems)
    loads.start()

    @pl.when(loads.first)
    def _():
        lhs_ref[:, width:] = jnp.zeros((ROWS, PAD), BF16)
        for i in range(4):
            w_ref[i, width:, :] = up_rows(ad_ref, i, i % 3, width)

    stream = x_ref[0].astype(F32)
    normal, _ = normalize(stream)
    lhs_ref[:, :width] = (normal * (1.0 + mod_ref[1:2, :]) + mod_ref[0:1, :]).astype(BF16)
    q, k, v = q_ref.at[0], k_ref.at[0], v_ref.at[0]
    three_projections(lhs_ref, ad_ref, 0, w_ref, loads, 0, (q, k, v), rq_ref.at[0])

    def put_out(index, value):
        value = value.astype(BF16)
        o_ref[0, :, tile(index)] = value
        lhs_ref[:, tile(index)] = value

    attend(q, k, v, mask_ref, None, put_out, stat_ref.at[0])
    loads.ready(3)
    branch = one_projection(lhs_ref, ad_ref, 3, w_ref.at[3], ro_ref.at[0])
    result = (stream + mod_ref[2:3, :] * branch).astype(BF16)
    x1_ref[...] = result.reshape(x1_ref.shape)


def temporal_cross_forward(
    x_ref, ctx_ref, mod_ref, mask_ref, ad_ref, w_hbm,
    q_ref, k_ref, v_ref, o_ref, stat_ref, rq_ref, ro_ref,
    u2_ref, qc_ref, oc_ref, statc_ref, rqc_ref, roc_ref, kp_ref, vp_ref, rk_ref, rv_ref, x3_ref,
    w_ref, bias_ref, lhs_ref, q_s, k_s, v_s, o_s, sems,
):
    width = x_ref.shape[2]
    first = pl.program_id(0) == 0
    loads = Loads([(w_hbm.at[i], w_ref.at[i, pl.ds(0, width), :]) for i in range(8)], sems)
    loads.start()

    @pl.when(first)
    def _():
        bias_ref[...] = same_place(bias_ref.shape)
        lhs_ref[:, width:] = jnp.zeros((ROWS, PAD), BF16)
        for i in range(8):
            w_ref[i, width:, :] = up_rows(ad_ref, 4 + i, i if i < 3 else 0, width)

    loaded = x_ref[...].reshape(ROWS, width)
    stream = loaded.astype(F32)
    lhs_ref[:, :width] = loaded
    three_projections(lhs_ref, ad_ref, 4, w_ref, loads, 0, (q_s, k_s, v_s), rq_ref.at[0])
    q_ref[...] = q_s[...].reshape(q_ref.shape)
    k_ref[...] = k_s[...].reshape(k_ref.shape)
    v_ref[...] = v_s[...].reshape(v_ref.shape)

    def put_out(index, value):
        o_s[:, tile(index)] = value.astype(BF16)

    attend(q_s, k_s, v_s, mask_ref, bias_ref, put_out, stat_ref.at[0])
    lhs_ref[:, :width] = o_s[...]
    o_ref[...] = o_s[...].reshape(o_ref.shape)
    loads.ready(3)
    branch = one_projection(lhs_ref, ad_ref, 7, w_ref.at[3], ro_ref.at[0])
    stream = stream + mod_ref[2:3, :] * branch
    inputs = stream.astype(BF16)
    u2_ref[...] = inputs.reshape(u2_ref.shape)
    lhs_ref[:, :width] = inputs
    loads.ready(4)
    q_s[...] = one_projection(lhs_ref, ad_ref, 8, w_ref.at[4], rqc_ref.at[0]).astype(BF16)
    qc_ref[...] = q_s[...].reshape(qc_ref.shape)
    loads.ready(5)
    loads.ready(6)

    @pl.when(first)
    def _():
        for number, at, rank_ref, pair_ref in ((9, 5, rk_ref, kp_ref), (10, 6, rv_ref, vp_ref)):
            ranks = nt(ctx_ref[...], ad_ref[2 * number]).astype(BF16)
            rank_ref[...] = ranks
            made = nn(ctx_ref[...], w_ref[at, :width, :]) + nn(ranks, ad_ref[2 * number + 1])
            k_s[:PAD, :] = made.astype(BF16)
            for pair in range(PAIRS):
                piece = k_s[:PAD, window(pair)]
                pair_ref[pair, :PAD, :] = piece * mask_ref[2 * pair : 2 * pair + 1, :]
                pair_ref[pair, PAD:, :] = piece * mask_ref[2 * pair + 1 : 2 * pair + 2, :]

    carried = None
    count = 120
    for pair in range(PAIRS):
        scores = nt(kp_ref[pair], q_s[:, window(pair)]) * EXP_SCALE
        pieces = []
        for sub in range(2):
            own = scores[PAD * sub : PAD * sub + count]
            top = jnp.max(own, 0, keepdims=True)
            grown = jnp.exp2(own - top)
            total = jnp.sum(grown, 0, keepdims=True)
            statc_ref[0, 2 * pair + sub : 2 * pair + sub + 1, :] = top + jnp.log2(total)
            pieces += [grown * (1.0 / total), jnp.zeros((PAD - count, ROWS), F32)]
        weights = jnp.concatenate(pieces, 0).astype(BF16)
        out = tn(weights, vp_ref[pair])
        low = out[:, :128]
        put_out(pair, low if carried is None else low + carried)
        carried = out[:, 128:]
    put_out(PAIRS, carried)
    lhs_ref[:, :width] = o_s[...]
    oc_ref[...] = o_s[...].reshape(oc_ref.shape)
    loads.ready(7)
    stream = stream + one_projection(lhs_ref, ad_ref, 11, w_ref.at[7], roc_ref.at[0])
    x3_ref[...] = stream.reshape(x3_ref.shape)


def gelu_both(hidden):
    root = math.sqrt(2.0 / math.pi)
    square = hidden * hidden
    inner = root * (hidden + 0.044715 * (square * hidden))
    bent = jnp.tanh(inner)
    half = 0.5 * (1.0 + bent)
    slope = half + 0.5 * hidden * (1.0 - bent * bent) * (root * (1.0 + 3.0 * 0.044715 * square))
    return hidden * half, slope


def transposed_map(rows):
    wide = jnp.concatenate([rows.astype(F32), jnp.zeros((PAD - RANK, rows.shape[1]), F32)], 0)
    return wide.T.astype(BF16)


def down_loads(down_hbm, down_ref, first):
    chunks, width, _ = down_ref.shape
    return [(down_hbm.at[first + c], down_ref.at[c, :, pl.ds(0, width)]) for c in range(chunks)]


def feed_forward(
    x3_ref, cot_ref, mod_ref, ad_ref, w_hbm,
    act_ref, g3_ref, gd_ref, gu_ref, up_ref, down_ref, lhs_ref, dlhs_ref, sems,
):
    width = x3_ref.shape[1]
    chunks = down_ref.shape[0]
    loads = Loads(
        [(w_hbm.at[c], up_ref.at[c, pl.ds(0, width), :]) for c in range(chunks)]
        + down_loads(w_hbm, down_ref, chunks),
        sems,
    )
    loads.start()

    @pl.when(loads.first)
    def _():
        gd_ref[...] = jnp.zeros_like(gd_ref)
        gu_ref[...] = jnp.zeros_like(gu_ref)
        lhs_ref[:, width:] = jnp.zeros((ROWS, PAD), BF16)
        dlhs_ref[:, width:] = jnp.zeros((ROWS, PAD), BF16)
        for c in range(chunks):
            rows = ad_ref[2 + c]
            up_ref[c, width:, :] = jnp.concatenate([rows, jnp.zeros((PAD - RANK, width), BF16)], 0)
            down_ref[c, :, width:] = transposed_map(ad_ref[2 + chunks + c])

    normal, inverse = normalize(x3_ref[...])
    inputs = (normal * (1.0 + mod_ref[4:5, :]) + mod_ref[3:4, :]).astype(BF16)
    cot = cot_ref[...].astype(F32)
    grad_branch = (mod_ref[5:6, :] * cot).astype(BF16)
    rank_up = nt(inputs, ad_ref[0]).astype(BF16)
    lhs_ref[:, :width] = inputs
    lhs_ref[:, width : width + RANK] = rank_up
    dlhs_ref[:, :width] = grad_branch
    dlhs_ref[:, width : width + RANK] = nt(grad_branch, ad_ref[1]).astype(BF16)
    both = None
    for c in range(chunks):
        loads.ready(c)
        hidden = nn(lhs_ref[...], up_ref[c])
        active, slope = gelu_both(hidden)
        act_ref[:, c * width : (c + 1) * width] = active.astype(BF16)
        loads.ready(chunks + c)
        grad_active = nt(dlhs_ref[...], down_ref[c])
        grad_hidden = (slope * grad_active).astype(BF16)
        part = nt(grad_hidden, up_ref[c])
        both = part if both is None else both + part
        gu_ref[block_rows(c), :] += tn(rank_up, grad_hidden)
    grad_rank = both[:, width : width + RANK].astype(BF16)
    grad_in = both[:, :width] + nn(grad_rank, ad_ref[0])
    gd_ref[...] += tn(grad_rank, lhs_ref[:, :width])
    g3_ref[...] = cot + normalize_back(normal, inverse, grad_in * (1.0 + mod_ref[4:5, :]))


def feed_forward_out(
    act_ref, x3_ref, cot_ref, mod_ref, ad_ref, w_hbm, x4_ref, gu_ref, gd_ref, down_ref, sems
):
    width = x3_ref.shape[1]
    chunks = down_ref.shape[0]
    loads = Loads(down_loads(w_hbm, down_ref, chunks), sems)
    loads.start()

    @pl.when(loads.first)
    def _():
        gu_ref[...] = jnp.zeros_like(gu_ref)
        gd_ref[...] = jnp.zeros_like(gd_ref)
        for c in range(chunks):
            down_ref[c, :, width:] = transposed_map(ad_ref[2 + chunks + c])

    grad_branch = (mod_ref[5:6, :] * cot_ref[...].astype(F32)).astype(BF16)
    grad_rank = nt(grad_branch, ad_ref[1]).astype(BF16)
    both = None
    for c in range(chunks):
        active = act_ref[:, c * width : (c + 1) * width]
        loads.ready(c)
        part = nn(active, down_ref[c])
        both = part if both is None else both + part
        gd_ref[block_rows(c), :] += tn(grad_rank, active)
    ranks = both[:, width : width + RANK].astype(BF16)
    branch = both[:, :width] + nn(ranks, ad_ref[1])
    gu_ref[...] += tn(ranks, grad_branch)
    x4_ref[...] = (x3_ref[...] + mod_ref[5:6, :] * branch).astype(BF16)


def cross_temporal_backward(
    continued, g3_ref, u1_ref, q_ref, k_ref, v_ref, o_ref, stat_ref, rq_ref, ro_ref,
    u2_ref, qc_ref, oc_ref, statc_ref, rqc_ref, roc_ref, kp_ref, vp_ref, rk_ref, rv_ref,
    ctx_ref, mod_ref, mask_ref, ad_ref, w_hbm, *rest,
):
    before_ref = None
    if continued:
        before_ref, *rest = rest
    (
        g1_ref, gw_ref, w_ref, bias_ref, dk_acc, dv_acc, q_s, k_s, v_s, do_s, dq_s, dk_s, dv_s, ctx_s, sems,
    ) = rest
    width = u1_ref.shape[2]
    step = pl.program_id(0)
    first = step == 0
    order = (7, 4, 3, 0, 1, 2)
    loads = Loads(
        [(w_hbm.at[n], w_ref.at[i, pl.ds(0, width), :]) for i, n in enumerate(order)], sems
    )
    loads.start()

    @pl.when(first)
    def _():
        bias_ref[...] = same_place(bias_ref.shape)
        gw_ref[...] = before_ref[...] if continued else jnp.zeros_like(gw_ref)
        dk_acc[...] = jnp.zeros_like(dk_acc)
        dv_acc[...] = jnp.zeros_like(dv_acc)
        for i, n in enumerate(order):
            w_ref[i, width:, :] = up_rows(ad_ref, 4 + n, n if n < 3 else 0, width)

    def rows(ref):
        return ref[...].reshape(ROWS, ref.shape[2])

    grad = rows(g3_ref)
    loads.ready(0)
    do_s[...] = one_back(
        grad.astype(BF16), rows(oc_ref), roc_ref[0], ad_ref, 11, w_ref.at[0], gw_ref, 14
    ).astype(BF16)
    q_s[...] = rows(qc_ref)
    count = 120
    carried = None
    for pair in range(PAIRS):
        win = window(pair)
        q_win, do_win = q_s[:, win], do_s[:, win]
        scores = nt(kp_ref[pair], q_win) * EXP_SCALE
        grad_probs = nt(vp_ref[pair], do_win)
        all_probs, all_grads = [], []
        nothing = jnp.zeros((PAD - count, ROWS), F32)
        for sub in range(2):
            span = slice(PAD * sub, PAD * sub + count)
            row = 2 * pair + sub
            probs = jnp.exp2(scores[span] - statc_ref[0, row : row + 1, :])
            own = grad_probs[span]
            inner = jnp.sum(probs * own, 0, keepdims=True)
            all_probs += [probs, nothing]
            all_grads += [probs * (own - inner), nothing]
        probs = jnp.concatenate(all_probs, 0).astype(BF16)
        grad_scores = jnp.concatenate(all_grads, 0).astype(BF16)
        dk_acc[pair] += nn(grad_scores, q_win)
        dv_acc[pair] += nn(probs, do_win)
        out = tn(grad_scores, kp_ref[pair])
        low = out[:, :128]
        dq_s[:, tile(pair)] = ((low if carried is None else low + carried) * SCALE).astype(BF16)
        carried = out[:, 128:]
    dq_s[:, tile(PAIRS)] = (carried * SCALE).astype(BF16)
    loads.ready(1)
    grad = grad + one_back(
        dq_s[...], rows(u2_ref), rqc_ref[0], ad_ref, 8, w_ref.at[1], gw_ref, 8
    )
    loads.ready(2)
    do_s[...] = one_back(
        (mod_ref[2:3, :] * grad).astype(BF16), rows(o_ref), ro_ref[0], ad_ref, 7, w_ref.at[2], gw_ref, 6
    ).astype(BF16)
    q_s[...] = rows(q_ref)
    k_s[...] = rows(k_ref)
    v_s[...] = rows(v_ref)

    def put(index, values):
        dq_s[:, tile(index)] = (values[0] * SCALE).astype(BF16)
        dk_s[:, tile(index)] = (values[1] * SCALE).astype(BF16)
        dv_s[:, tile(index)] = values[2].astype(BF16)

    attend_back(q_s, k_s, v_s, do_s, mask_ref, bias_ref, stat_ref.at[0], put)
    grad = grad + three_back(
        (dq_s, dk_s, dv_s), rows(u1_ref), rq_ref[0], ad_ref, 4, w_ref, loads, 3, gw_ref, 0
    )
    g1_ref[...] = grad.astype(BF16).reshape(g1_ref.shape)

    @pl.when(step == pl.num_programs(0) - 1)
    def _():
        context = ctx_ref[...].astype(F32)
        for acc, factor, rank_ref, number, at in (
            (dk_acc, SCALE, rk_ref, 9, 10),
            (dv_acc, 1.0, rv_ref, 10, 12),
        ):
            held = None
            for pair in range(PAIRS):
                whole = acc[pair]
                out = whole[:PAD] * mask_ref[2 * pair : 2 * pair + 1, :].astype(F32)
                out = out + whole[PAD:] * mask_ref[2 * pair + 1 : 2 * pair + 2, :].astype(F32)
                out = out * factor
                low = out[:, :128]
                ctx_s[:, tile(pair)] = low if held is None else low + held
                held = out[:, 128:]
            ctx_s[:, tile(PAIRS)] = held
            grad_kv = ctx_s[...]
            grad_rank = lax.dot_general(
                grad_kv, ad_ref[2 * number + 1].astype(F32), (((1,), (1,)), ((), ())),
                precision=HIGHEST, preferred_element_type=F32,
            )
            gw_ref[block_rows(at), :] += lax.dot_general(
                grad_rank, context, (((0,), (0,)), ((), ())),
                precision=HIGHEST, preferred_element_type=F32,
            )
            gw_ref[block_rows(at + 1), :] += lax.dot_general(
                rank_ref[...].astype(F32), grad_kv, (((0,), (0,)), ((), ())),
                precision=HIGHEST, preferred_element_type=F32,
            )


def pack_columns(table_ref, packed_ref, clips):
    parts = packed_ref.shape[0] // clips
    _, share, cols = packed_ref.shape
    for f in range(clips):
        for s in range(parts):
            piece = table_ref[share * s : share * (s + 1), cols * f : cols * (f + 1)]
            packed_ref[f * parts + s] = piece.astype(BF16)


def spatial_backward(
    halves, clips, *refs,
):
    g1_refs, refs = refs[:halves], refs[halves:]
    (
        x_ref, q_ref, k_ref, v_ref, o_ref, stat_ref, rq_ref, ro_ref, mod_ref, mask_ref, ad_ref, w_hbm,
        g0_ref, packed_ref, w_ref, gw_ref, do_s, dq_s, dk_s, dv_s, sems,
    ) = refs
    width = x_ref.shape[2]
    order = (3, 0, 1, 2)
    loads = Loads(
        [(w_hbm.at[n], w_ref.at[i, pl.ds(0, width), :]) for i, n in enumerate(order)], sems
    )
    loads.start()

    @pl.when(loads.first)
    def _():
        gw_ref[...] = jnp.zeros_like(gw_ref)
        for i, n in enumerate(order):
            w_ref[i, width:, :] = up_rows(ad_ref, n, n % 3, width)

    parts = g1_refs[0].shape[0]
    pieces = [ref[s, 0] for s in range(parts) for ref in g1_refs]
    grad = jnp.concatenate(pieces, 0).astype(F32)
    loads.ready(0)
    do_s[...] = one_back(
        (mod_ref[2:3, :] * grad).astype(BF16), o_ref[0], ro_ref[0], ad_ref, 3, w_ref.at[0], gw_ref, 6
    ).astype(BF16)

    def put(index, values):
        dq_s[:, tile(index)] = (values[0] * SCALE).astype(BF16)
        dk_s[:, tile(index)] = (values[1] * SCALE).astype(BF16)
        dv_s[:, tile(index)] = values[2].astype(BF16)

    attend_back(
        q_ref.at[0], k_ref.at[0], v_ref.at[0], do_s, mask_ref, None, stat_ref.at[0], put
    )
    normal, inverse = normalize(x_ref[0].astype(F32))
    inputs = (normal * (1.0 + mod_ref[1:2, :]) + mod_ref[0:1, :]).astype(BF16)
    grad_in = three_back(
        (dq_s, dk_s, dv_s), inputs, rq_ref[0], ad_ref, 0, w_ref, loads, 1, gw_ref, 0
    )
    grad = grad + normalize_back(normal, inverse, grad_in * (1.0 + mod_ref[1:2, :]))
    g0_ref[0] = grad.astype(BF16)

    @pl.when(pl.program_id(0) == pl.num_programs(0) - 1)
    def _():
        pack_columns(gw_ref, packed_ref, clips)


def pack_early(clips, *refs):
    *sources, packed_ref, table_ref = refs
    at = 0
    for ref in sources:
        table_ref[at : at + ref.shape[0], :] = ref[...]
        at += ref.shape[0]
    table_ref[at:, :] = jnp.zeros((table_ref.shape[0] - at, table_ref.shape[1]), F32)
    pack_columns(table_ref, packed_ref, clips)


def combine(index_ref, got_ref, out_ref, acc_ref):
    clips = index_ref.shape[0]
    parts = got_ref.shape[0] // clips
    acc_ref[...] = jnp.zeros_like(acc_ref)

    def step(f, carry):
        total = got_ref[f * parts].astype(F32)
        for s in range(1, parts):
            total = total + got_ref[f * parts + s].astype(F32)
        acc_ref[index_ref[f]] += total
        return carry

    lax.fori_loop(0, clips, step, 0)
    table = acc_ref[...].astype(BF16)
    for s in range(parts):
        out_ref[s] = table


def whole_block(array):
    zeros = (0,) * array.ndim
    return pl.BlockSpec(array.shape, lambda i: zeros)


def anywhere():
    return pl.BlockSpec(memory_space=pl.ANY)


def like(shape, dtype):
    return jax.ShapeDtypeStruct(shape, dtype)


PARAMS = pltpu.CompilerParams(
    dimension_semantics=("arbitrary",), vmem_limit_bytes=VMEM_LIMIT
)


def cost(flops, read):
    return pl.CostEstimate(flops=flops, bytes_accessed=read, transcendentals=flops // 4096)


def run_spatial_forward(video, mods, masks, wide, w_s, parts):
    frames, rows, d = video.shape
    places = rows // parts
    by_frame = lambda i: (i, 0, 0)
    row_block = pl.BlockSpec((1, rows, d), by_frame)
    return pl.pallas_call(
        spatial_forward,
        grid=(frames,),
        in_specs=[row_block, whole_block(mods), whole_block(masks), whole_block(wide), anywhere()],
        out_specs=[
            pl.BlockSpec((parts, 1, places, d), lambda i: (0, i, 0, 0)),
            row_block,
            row_block,
            row_block,
            row_block,
            pl.BlockSpec((1, HEADS, rows), by_frame),
            pl.BlockSpec((1, rows, 3 * RANK), by_frame),
            pl.BlockSpec((1, rows, RANK), by_frame),
        ],
        out_shape=[like((parts, frames, places, d), BF16)]
        + [like(video.shape, BF16)] * 4
        + [
            like((frames, HEADS, rows), F32),
            like((frames, rows, 3 * RANK), BF16),
            like((frames, rows, RANK), BF16),
        ],
        scratch_shapes=[
            pltpu.VMEM((4, d + PAD, d), BF16),
            pltpu.VMEM((ROWS, d + PAD), BF16),
            pltpu.SemaphoreType.DMA((4,)),
        ],
        compiler_params=PARAMS,
        cost_estimate=cost(10 * frames * rows * d * d, 30_000_000),
        name="spatial_forward",
    )(video, mods, masks, wide, w_s)


def run_temporal_cross_forward(x1, context, mods, masks, wide, w_tc):
    frames, places, d = x1.shape
    groups = places * frames // ROWS
    across = pl.BlockSpec((frames, ROWS // frames, d), lambda i: (0, i, 0))
    by_group = lambda i: (i, 0, 0)
    stat = pl.BlockSpec((1, HEADS, ROWS), by_group)
    three = pl.BlockSpec((1, ROWS, 3 * RANK), by_group)
    one = pl.BlockSpec((1, ROWS, RANK), by_group)
    full = lambda *shape: pl.BlockSpec(shape, lambda i: (0,) * len(shape))
    act = like(x1.shape, BF16)
    stat_shape = like((groups, HEADS, ROWS), F32)
    one_shape = like((groups, ROWS, RANK), BF16)
    return pl.pallas_call(
        temporal_cross_forward,
        grid=(groups,),
        in_specs=[across, whole_block(context), whole_block(mods), whole_block(masks), whole_block(wide), anywhere()],
        out_specs=[across] * 4 + [stat, three, one] + [across] * 3 + [stat, one, one]
        + [full(PAIRS, 2 * PAD, 256)] * 2 + [full(PAD, RANK)] * 2 + [across],
        out_shape=[act] * 4 + [stat_shape, like((groups, ROWS, 3 * RANK), BF16), one_shape]
        + [act] * 3 + [stat_shape, one_shape, one_shape]
        + [like((PAIRS, 2 * PAD, 256), BF16)] * 2 + [like((PAD, RANK), BF16)] * 2
        + [like(x1.shape, F32)],
        scratch_shapes=[pltpu.VMEM((8, d + PAD, d), BF16), pltpu.VMEM((ROWS, ROWS), F32)]
        + [pltpu.VMEM((ROWS, d + PAD), BF16)]
        + [pltpu.VMEM((ROWS, d), BF16)] * 4
        + [pltpu.SemaphoreType.DMA((8,))],
        compiler_params=PARAMS,
        cost_estimate=cost(14 * places * frames * d * d, 50_000_000),
        name="temporal_cross_forward",
    )(x1, context, mods, masks, wide, w_tc)


def run_feed_forward(x3, cot, mods, maps, w_f):
    tokens, d = x3.shape
    chunks = w_f.shape[0] // 2
    rows = pl.BlockSpec((ROWS, d), lambda i: (i, 0))
    fixed = lambda n: pl.BlockSpec((n * RANK, d), lambda i: (0, 0))
    return pl.pallas_call(
        feed_forward,
        grid=(tokens // ROWS,),
        in_specs=[rows, rows, whole_block(mods), whole_block(maps), anywhere()],
        out_specs=[pl.BlockSpec((ROWS, chunks * d), lambda i: (i, 0)), rows, fixed(1), fixed(chunks)],
        out_shape=[
            like((tokens, chunks * d), BF16),
            like((tokens, d), F32),
            like((RANK, d), F32),
            like((chunks * RANK, d), F32),
        ],
        scratch_shapes=[
            pltpu.VMEM((chunks, d + PAD, d), BF16),
            pltpu.VMEM((chunks, d, d + PAD), BF16),
            pltpu.VMEM((ROWS, d + PAD), BF16),
            pltpu.VMEM((ROWS, d + PAD), BF16),
            pltpu.SemaphoreType.DMA((2 * chunks,)),
        ],
        compiler_params=PARAMS,
        cost_estimate=cost(6 * tokens * d * d * chunks, 50_000_000),
        name="feed_forward",
    )(x3, cot, mods, maps, w_f)


def run_feed_forward_out(active, x3, cot, mods, maps, w_f):
    tokens, d = x3.shape
    chunks = w_f.shape[0] // 2
    rows = pl.BlockSpec((ROWS, d), lambda i: (i, 0))
    fixed = lambda n: pl.BlockSpec((n * RANK, d), lambda i: (0, 0))
    return pl.pallas_call(
        feed_forward_out,
        grid=(tokens // ROWS,),
        in_specs=[
            pl.BlockSpec((ROWS, chunks * d), lambda i: (i, 0)),
            rows,
            rows,
            whole_block(mods),
            whole_block(maps),
            anywhere(),
        ],
        out_specs=[rows, fixed(1), fixed(chunks)],
        out_shape=[
            like((tokens, d), BF16),
            like((RANK, d), F32),
            like((chunks * RANK, d), F32),
        ],
        scratch_shapes=[pltpu.VMEM((chunks, d, d + PAD), BF16), pltpu.SemaphoreType.DMA((chunks,))],
        compiler_params=PARAMS,
        cost_estimate=cost(2 * tokens * d * d * chunks, 30_000_000),
        name="feed_forward_out",
    )(active, x3, cot, mods, maps, w_f)


def run_cross_temporal_backward(g3, u1, saved, context, mods, masks, wide, w_tc, half, halves, before):
    frames, places, d = u1.shape
    groups = places * frames // ROWS // halves
    start = half * groups
    across = pl.BlockSpec((frames, ROWS // frames, d), lambda i: (0, i + start, 0))
    by_group = lambda i: (i + start, 0, 0)
    stat = pl.BlockSpec((1, HEADS, ROWS), by_group)
    three = pl.BlockSpec((1, ROWS, 3 * RANK), by_group)
    one = pl.BlockSpec((1, ROWS, RANK), by_group)
    kp, vp, rk, rv = saved[13:17]
    grads = pl.BlockSpec((16 * RANK, d), lambda i: (0, 0))
    extra = [] if before is None else [before]

    def body(*refs):
        cross_temporal_backward(before is not None, *refs)

    return pl.pallas_call(
        body,
        grid=(groups,),
        in_specs=[across, across] + [across] * 4 + [stat, three, one] + [across] * 3 + [stat, one, one]
        + [whole_block(kp), whole_block(vp), whole_block(rk), whole_block(rv)]
        + [whole_block(context), whole_block(mods), whole_block(masks), whole_block(wide), anywhere()]
        + [grads] * len(extra),
        out_specs=[pl.BlockSpec((frames, ROWS // frames, d), lambda i: (0, i, 0)), grads],
        out_shape=[like((frames, places // halves, d), BF16), like((16 * RANK, d), F32)],
        scratch_shapes=[
            pltpu.VMEM((6, d + PAD, d), BF16),
            pltpu.VMEM((ROWS, ROWS), F32),
            pltpu.VMEM((PAIRS, 2 * PAD, 256), F32),
            pltpu.VMEM((PAIRS, 2 * PAD, 256), F32),
        ]
        + [pltpu.VMEM((ROWS, d), BF16)] * 7
        + [pltpu.VMEM((PAD, d), F32), pltpu.SemaphoreType.DMA((6,))],
        compiler_params=PARAMS,
        cost_estimate=cost(14 * places // halves * frames * d * d, 30_000_000),
        name="cross_temporal_backward",
    )(g3, u1, *saved[:17], context, mods, masks, wide, w_tc, *extra)


def run_spatial_backward(g1_halves, video, saved, mods, masks, wide, w_s, clips):
    frames, rows, d = video.shape
    parts = g1_halves[0].shape[0]
    by_frame = lambda i: (i, 0, 0)
    row_block = pl.BlockSpec((1, rows, d), by_frame)
    packed = (clips * parts, 8 * RANK // parts, d // clips)

    def body(*refs):
        spatial_backward(len(g1_halves), clips, *refs)

    return pl.pallas_call(
        body,
        grid=(frames,),
        in_specs=[
            pl.BlockSpec((parts, 1, g.shape[2], d), lambda i: (0, i, 0, 0)) for g in g1_halves
        ]
        + [row_block] * 5
        + [
            pl.BlockSpec((1, HEADS, rows), by_frame),
            pl.BlockSpec((1, rows, 3 * RANK), by_frame),
            pl.BlockSpec((1, rows, RANK), by_frame),
            whole_block(mods),
            whole_block(masks),
            whole_block(wide),
            anywhere(),
        ],
        out_specs=[row_block, pl.BlockSpec(packed, lambda i: (0, 0, 0))],
        out_shape=[like(video.shape, BF16), like(packed, BF16)],
        scratch_shapes=[pltpu.VMEM((4, d + PAD, d), BF16), pltpu.VMEM((8 * RANK, d), F32)]
        + [pltpu.VMEM((ROWS, d), BF16)] * 4
        + [pltpu.SemaphoreType.DMA((4,))],
        compiler_params=PARAMS,
        cost_estimate=cost(10 * frames * rows * d * d, 30_000_000),
        name="spatial_backward",
    )(*g1_halves, video, *saved, mods, masks, wide, w_s)


EARLY_BLOCKS = 28


def run_pack_early(sources, clips, parts):
    d = sources[0].shape[1]
    packed = (clips * parts, EARLY_BLOCKS * RANK // parts, d // clips)

    def body(*refs):
        pack_early(clips, *refs)

    return pl.pallas_call(
        body,
        out_shape=like(packed, BF16),
        scratch_shapes=[pltpu.VMEM((EARLY_BLOCKS * RANK, d), F32)],
        compiler_params=pltpu.CompilerParams(vmem_limit_bytes=VMEM_LIMIT),
        name="pack_early",
    )(*sources)


def run_combine(all_index, got, adapters):
    clips = all_index.shape[0]
    parts = got.shape[0] // clips
    _, share, cols = got.shape
    return pl.pallas_call(
        combine,
        in_specs=[pl.BlockSpec(memory_space=pltpu.SMEM), pl.BlockSpec(memory_space=pltpu.VMEM)],
        out_specs=pl.BlockSpec(memory_space=pltpu.VMEM),
        out_shape=like((parts, adapters, share, cols), BF16),
        scratch_shapes=[pltpu.VMEM((adapters, share, cols), F32)],
        compiler_params=pltpu.CompilerParams(vmem_limit_bytes=VMEM_LIMIT),
        name="combine",
    )(all_index, got)


def exchange(array, axes="seq"):
    return lax.all_to_all(array, axes, split_axis=0, concat_axis=0, tiled=True)


def fetch_adapters(choice, adapt_wide, adapt_ff):
    cols = adapt_wide.shape[-1]
    times = adapt_ff.shape[-1] // cols
    narrow = adapt_ff.reshape(adapt_ff.shape[:-1] + (times, cols))
    narrow = jnp.moveaxis(narrow, 3, 1).reshape(2 * times, *adapt_wide.shape[1:])
    table = jnp.concatenate([adapt_wide, narrow], 0)
    picked = jnp.sum(
        choice[:, None, :, None, None] * table[None].astype(F32), axis=2
    ).astype(BF16)
    got = exchange(picked, "fsdp")
    return jnp.moveaxis(got, 0, 2).reshape(table.shape[0], RANK, -1)


def reduce_grads(packed, all_index, adapters):
    got = exchange(packed, ("fsdp", "seq"))
    return run_combine(all_index, got, adapters)


def spread_grads(quarter):
    whole = exchange(quarter)
    parts, adapters, share, cols = whole.shape
    table = whole.transpose(1, 0, 2, 3).reshape(adapters, -1, RANK, cols)
    return table.transpose(1, 0, 2, 3).astype(F32)


def hidden_order(up, down, clips):
    rows, hidden = up.shape
    width = down.shape[1]
    times = hidden // width
    cols = width // clips
    up = up.reshape(rows, clips, times, cols).transpose(2, 0, 1, 3).reshape(times, rows, width)
    return jnp.concatenate([up, down.reshape(times, cols, width)], 0)


def on_device(
    video,
    context,
    modulation,
    adapter_index,
    cotangent,
    qkv_weights,
    out_weights,
    ffn_up,
    ffn_down,
    adapt_wide,
    adapt_ff,
):
    parts = lax.axis_size("seq")
    clips = lax.axis_size("fsdp")
    d = video.shape[-1]
    adapters = adapt_wide.shape[2]
    places = SPATIAL // parts
    frames = FRAMES // parts
    mods = modulation[0, 0]
    masks = head_masks()
    ctx = jnp.pad(context[0], ((0, PAD - context.shape[1]), (0, 0)))

    def gather(array):
        return lax.all_gather(array, "fsdp", axis=1, tiled=True)

    def attention_weights(j):
        return [qkv_weights[0, 3 * j : 3 * j + 3], out_weights[0, j : j + 1]]

    w_s = gather(jnp.concatenate(attention_weights(0), 0))
    all_index = exchange(jnp.broadcast_to(adapter_index, (clips,)), "fsdp")
    choice = (all_index[:, None] == jnp.arange(adapters)[None, :]).astype(F32)
    wide = fetch_adapters(choice, adapt_wide[0], adapt_ff[0])
    w_tc = gather(jnp.concatenate(attention_weights(1) + attention_weights(2), 0))
    w_f = gather(hidden_order(ffn_up[0], ffn_down[0], clips))
    maps_f = wide[24:]

    cot = cotangent.reshape(frames, parts, places, d).transpose(1, 0, 2, 3)
    cot = exchange(cot).reshape(FRAMES * places, d)
    frames_in = video.reshape(frames, SPATIAL, d)
    x1, *kept_s = run_spatial_forward(frames_in, mods, masks, wide, w_s, parts)
    u1 = exchange(x1).reshape(FRAMES, places, d)
    *kept_t, x3 = run_temporal_cross_forward(u1, ctx, mods, masks, wide, w_tc)
    x3 = x3.reshape(FRAMES * places, d)
    active, g3, grad_a24, grad_b24 = run_feed_forward(x3, cot, mods, maps_f, w_f)
    g3 = g3.reshape(FRAMES, places, d)
    groups = FRAMES * places // ROWS
    halves = 2 if groups % 2 == 0 else 1
    g1_halves, grads_t = [], None
    for half in range(halves):
        g1, grads_t = run_cross_temporal_backward(
            g3, u1, kept_t, ctx, mods, masks, wide, w_tc, half, halves, grads_t
        )
        g1_halves.append(exchange(g1.reshape(parts, frames, places // halves, d)))
    x4, grad_b25, grad_down = run_feed_forward_out(active, x3, cot, mods, maps_f, w_f)
    packed = run_pack_early([grads_t, grad_a24, grad_b25, grad_b24, grad_down], clips, parts)
    early = reduce_grads(packed, all_index, adapters)
    output = exchange(x4.reshape(parts, frames, places, d))
    early, *g1_halves = lax.optimization_barrier((early, *g1_halves))
    g0, packed = run_spatial_backward(g1_halves, frames_in, kept_s, mods, masks, wide, w_s, clips)
    early = spread_grads(early)
    late = spread_grads(reduce_grads(packed, all_index, adapters))
    output = output.transpose(1, 0, 2, 3).reshape(video.shape)
    wide_out = jnp.concatenate([late, early[:18]], 0)
    times = adapt_ff.shape[-1] // adapt_wide.shape[-1]
    narrow_out = early[18 : 18 + 2 * times].reshape(2, times, adapters, RANK, -1)
    narrow_out = jnp.moveaxis(narrow_out, 1, 3).reshape(2, adapters, RANK, -1)
    return (output, g0.reshape(video.shape), wide_out[None], narrow_out[None])


def solution(mesh):
    return jax.shard_map(
        on_device,
        mesh=mesh,
        in_specs=(
            P("fsdp", "seq", None),
            P("fsdp", None, None),
            P("fsdp", None, None, None),
            P("fsdp"),
            P("fsdp", "seq", None),
            P(None, None, "fsdp", None),
            P(None, None, "fsdp", None),
            P(None, "fsdp", None),
            P(None, "fsdp", None),
            P(None, None, None, None, "fsdp"),
            P(None, None, None, None, "fsdp"),
        ),
        out_specs=(
            P("fsdp", "seq", None),
            P("fsdp", "seq", None),
            P(None, None, None, None, "fsdp"),
            P(None, None, None, None, "fsdp"),
        ),
        check_vma=False,
    )
```

time: 832 us -> 797 us (0.958)
  waiting for transfers between devices: 354 us -> 258 us
  blocking collectives: 31.2 us -> 72.6 us
  local copies, waits for them, and re-layouts: 30 us -> 53.5 us
  other arithmetic: 32.9 us -> 21.8 us
    pallas_call x2 -> x7, Pallas kernels: 129 us -> 176 us  [the longest x2 91.8 us: run_cross_temporal_backward(): pl.pallas_call(body, grid=(groups,), in_specs=[across, across] + [across]...]
    psum x1 -> x0, waiting for transfers between devices: 43.3 us -> none  [collect_grads(): total = lax.psum(table.astype(BF16), 'seq').astype(F32)]
    all_to_all x1 -> x3, blocking collectives: 31.2 us -> 72.6 us  [exchange(): return lax.all_to_all(array, axes, split_axis=0, concat_axis=0, tiled=True)]
    all_to_all x6 -> x8, waiting for transfers between devices: 228 us -> 194 us  [exchange(): return lax.all_to_all(array, axes, split_axis=0, concat_axis=0, tiled=True)]
    pallas_call x1, Pallas kernels: 73.4 us -> 53.4 us  [run_temporal_cross_forward(): pl.pallas_call(temporal_cross_forward, grid=(groups,), in_specs=[across,...]
    pallas_call x1, Pallas kernels: 89.4 us -> 69.8 us  [run_feed_forward(): pl.pallas_call(feed_forward, grid=(tokens // ROWS,), in_specs=[rows, rows...]
    all_gather x5 -> x3, waiting for transfers between devices: 82.3 us -> 63.3 us  [gather(): return lax.all_gather(array, 'fsdp', axis=1, tiled=True)]
    reduce_sum x1 -> x0, other arithmetic: 8.73 us -> none  [collect_grads(): jnp.sum(choice[:, None, :, None, None] * got[:, :, None].astype(F32), axi...]
  transfers between devices with their start and end apart: 12 -> 11, of which waited for: 9 -> 8; matrix products, arithmetic and copies ran while one was open for 6% -> 7% of each run, Pallas kernels for 14% -> 21%
where the time goes in v2:
time: 797 us; the launch traced here: 788 us
  Pallas kernels  333 us (42%)
  waiting for transfers between devices  258 us (32%)
  blocking collectives  72.6 us (9%)
  local copies, waits for them, and re-layouts  53.5 us (7%)
  starting transfers between devices  34.2 us (4%)
  other arithmetic  21.8 us (3%)
  between operations  15 us (2%)
    all_to_all x8, waiting for transfers between devices, exchange(): return lax.all_to_all(array, axes, split_axis=0, concat_axis=0, tiled=True)  194 us
    pallas_call x2, Pallas kernels, run_cross_temporal_backward(): pl.pallas_call(body, grid=(groups,), in_specs=[across, across] + [across]...  91.8 us
    all_to_all x3, blocking collectives, exchange(): return lax.all_to_all(array, axes, split_axis=0, concat_axis=0, tiled=True)  72.6 us
    pallas_call x1, Pallas kernels, run_feed_forward(): pl.pallas_call(feed_forward, grid=(tokens // ROWS,), in_specs=[rows, rows...  69.8 us
    all_gather x3, waiting for transfers between devices, gather(): return lax.all_gather(array, 'fsdp', axis=1, tiled=True)  63.3 us
    pallas_call x1, Pallas kernels, run_temporal_cross_forward(): pl.pallas_call(temporal_cross_forward, grid=(groups,), in_specs=[across,...  53.4 us
    pallas_call x1, Pallas kernels, run_spatial_backward(): pl.pallas_call(body, grid=(frames,), in_specs=[pl.BlockSpec((parts, 1, g....  49.3 us
    all_to_all x8, starting transfers between devices, exchange(): return lax.all_to_all(array, axes, split_axis=0, concat_axis=0, tiled=True)  34.1 us
  transfers between devices with their start and end apart: 11, of which 8 were waited for; matrix products, arithmetic and copies ran while one was open for 7% of the time, Pallas kernels for 21%

profile of v2, /device:TPU:0, one launch (start us, length us, event | category | flops | bytes accessed | tf_op | source)
XLA Modules:
  0.0 787.6 jit_solution(8737892037937562824)
XLA Ops:
  14.8 5.2 reshape_squeeze.10
  25.2 3.5 pad_maximum_fusion.1
  30.1 5.2 all-to-all-start
  40.3 10.1 %multiply_reduce_fusion = bf16[8,34,16,144]{3,2,1,0:T(8,128)(2,1)} fusion(f32[34,8,16,144]{3,2,1,0:T(8,128)} %maximum_convert_fusion, f32[8,8]{1,0:T(8,128)S(1)} %fusion.2), kind=kLoop, calls=%fused_computation | loop fusion | flops 9400320 | bytes 3760384 | tf_op jit(solution)/shard_map/reduce_sum | solution.py:895
  50.4 3.9 all-to-all-start.1
  55.6 45.4 %all-to-all-done.1 = bf16[8,34,16,144]{3,2,1,0:T(8,128)(2,1)S(1)} async-done(((bf16[8,34,16,144]{3,2,1,0:T(8,128)(2,1)}), bf16[8,34,16,144]{3,2,1,0:T(8,128)(2,1)S(1)}, u32[]{:S(2)}, u32[]{:S(2)}) %all-to-all-start.1) | async-done | bytes 1253408 | tf_op jit(solution)/shard_map/all_to_all | solution.py:886
  101.1 3.8 copy.69
  104.8 4.5 reshape.106.ad_ref.refs_22_.refs_12_
  109.4 33.2 %spatial_forward.1 = (bf16[4,4,64,1152]{3,2,1,0:T(8,128)(2,1)}, bf16[4,256,1152]{2,1,0:T(8,128)(2,1)}, bf16[4,256,1152]{2,1,0:T(8,128)(2,1)}, bf16[4,256,1152]{2...) custom-call(bf16[4,256,1152]{2,1,0:T(8,128)(2,1)} %bitcast.95, ...), custom_call_target="tpu_custom_call" | custom-call | flops 13589544960 | bytes 30000000 | tf_op jit(solution)/shard_map/spatial_forward/pallas_call | solution.py:653
  142.6 4.7 all-to-all-start.2
  147.3 3.3 copy.86
  150.5 47.1 %all-to-all-done.2 = bf16[4,4,64,1152]{3,2,1,0:T(8,128)(2,1)S(1)} async-done(((bf16[4,4,64,1152]{3,2,1,0:T(8,128)(2,1)}), bf16[4,4,64,1152]{3,2,1,0:T(8,128)(2,1)S(1)}, u32[]{:S(2)}, u32[]{:S(2)}) %all-to-all-start.2) | async-done | bytes 2359328 | tf_op jit(solution)/shard_map/all_to_all | solution.py:886
  199.1 4.8 all-to-all-start.3
  207.4 6.1 all-gather.6.cloned.1.call-done.w_hbm.refs_23_
  213.5 53.4 %temporal_cross_forward.1 = (bf16[16,64,1152]{2,1,0:T(8,128)(2,1)}, bf16[16,64,1152]{2,1,0:T(8,128)(2,1)}, bf16[16,64,1152]{2,1,0:T(8,128)(2,1)}, bf16[16,64,115...) custom-call(bf16[16,64,1152]{2,1,0:T(8,128)(2,1)} %bitcast.64, ...), custom_call_target="tpu_custom_call" | custom-call | flops 19025362944 | bytes 50000000 | tf_op jit(solution)/shard_map/temporal_cross_forward/pallas_call | solution.py:697
  266.9 57.2 %all-gather.8.cloned.1.call-done.w_hbm = bf16[8,1152,1152]{2,1,0:T(8,128)(2,1)} async-done(((bf16[8,144,1152]{2,1,0:T(8,128)(2,1)}), bf16[8,1152,1152]{2,1,0:T(8,128)(2,1)}) %all-gather.8.cloned.1.call-update) | async-done | bytes 21233680 | tf_op jit(solution)/shard_map/all_gather | solution.py:947
  324.1 69.8 %feed_forward.1 = (bf16[1024,4608]{1,0:T(8,128)(2,1)}, f32[1024,1152]{1,0:T(8,128)}, f32[16,1152]{1,0:T(8,128)}, f32[64,1152]{1,0:T(8,128)}) custom-call(f32[1024,1152]{1,0:T(8,128)} %bitcast.97, bf16[1024,1152]{1,0:T(8,128)(2,1)} %bitcast.17.cot_ref, f32[6,1152]{1,0:T(8,128)} %bitcast.89, bf16[10,16,1152]{2,1,0:T(8,128)(2,1)} %slice.37.ad_ref, ...), custom_call_target="tpu_custom_call" | custom-call | flops 32614907904 | bytes 50000000 | tf_op jit(solution)/shard_map/feed_forward/pallas_call | solution.py:722
  393.9 45.5 %cross_temporal_backward.2 = (bf16[16,32,1152]{2,1,0:T(8,128)(2,1)}, f32[256,1152]{1,0:T(8,128)}) custom-call(f32[16,64,1152]{2,1,0:T(8,128)} %bitcast.67, bf16[16,64,1152]{2,1,0:T(8,128)(2,1)} %bitcast.65, bf16[16,64,1152]{2,1,0:T(8,128)(2,1)} %get-tuple-element.51.refs_2_, bf16[16,64,1152]{2,1,0:T(8,128)(2,1)} %get-tuple-element.52.refs_3_, ...), custom_call_target="tpu_custom_call" | custom-call | flops 9512681472 | bytes 30000000 | tf_op jit(solution)/shard_map/cross_temporal_backward/pallas_call | solution.py:791
  439.5 4.6 all-to-all-start.6
  444.1 46.2 %cross_temporal_backward.3 = (bf16[16,32,1152]{2,1,0:T(8,128)(2,1)}, f32[256,1152]{1,0:T(8,128)}) custom-call(f32[16,64,1152]{2,1,0:T(8,128)} %bitcast.68, bf16[16,64,1152]{2,1,0:T(8,128)(2,1)} %bitcast.66, bf16[16,64,1152]{2,1,0:T(8,128)(2,1)} %get-tuple-element.51.refs_2_, bf16[16,64,1152]{2,1,0:T(8,128)(2,1)} %get-tuple-element.52.refs_3_, ...), custom_call_target="tpu_custom_call" | custom-call | flops 9512681472 | bytes 30000000 | tf_op jit(solution)/shard_map/cross_temporal_backward/pallas_call | solution.py:791
  490.3 26.5 %feed_forward_out.1 = (bf16[1024,1152]{1,0:T(8,128)(2,1)}, f32[16,1152]{1,0:T(8,128)}, f32[64,1152]{1,0:T(8,128)}) custom-call(bf16[1024,4608]{1,0:T(8,128)(2,1)} %get-tuple-element.48.act_ref, f32[1024,1152]{1,0:T(8,128)} %bitcast.98, bf16[1024,1152]{1,0:T(8,128)(2,1)} %bitcast.17.cot_ref, f32[6,1152]{1,0:T(8,128)} %bitcast.92, ...), custom_call_target="tpu_custom_call" | custom-call | flops 10871635968 | bytes 30000000 | tf_op jit(solution)/shard_map/feed_forward_out/pallas_call | solution.py:751
  522.1 35.0 %all_to_all.55 = bf16[32,112,144]{1,2,0:T(8,128)(2,1)S(1)} all-to-all(bf16[32,112,144]{1,2,0:T(8,128)(2,1)S(1)} %copy.74), channel_id=1, replica_groups=mesh['seq'=4,'fsdp'=8] {'fsdp','seq'}, dimensions={0} | all-to-all | bytes 2064384 | tf_op jit(solution)/shard_map/all_to_all | solution.py:886
  557.2 3.5 all-to-all-start.7
  562.4 3.2 combine.2
  565.7 24.4 %all-to-all-done.7.refs_1_ = bf16[4,4,32,1152]{3,2,1,0:T(8,128)(2,1)S(1)} async-done(((bf16[4,4,32,1152]{3,2,1,0:T(8,128)(2,1)}), bf16[4,4,32,1152]{3,2,1,0:T(8,128)(2,1)S(1)}, u32[]{:S(2)}, u32[]{:S(2)}) %all-to-all-start.7) | async-done | bytes 1179680 | tf_op jit(solution)/shard_map/all_to_all | solution.py:886
  591.0 49.3 %spatial_backward.1 = (bf16[4,256,1152]{2,1,0:T(8,128)(2,1)}, bf16[32,32,144]{2,1,0:T(8,128)(2,1)}) custom-call(bf16[4,4,32,1152]{3,2,1,0:T(8,128)(2,1)} %copy-done.5, bf16[4,4,32,1152]{3,2,1,0:T(8,128)(2,1)} %copy-done.6, bf16[4,256,1152]{2,1,0:T(8,128)(2,1)} %bitcast.96, bf16[4,256,1152]{2,1,0:T(8,128)(2,1)} %get-tuple-element.78.refs_3_, ...), custom_call_target="tpu_custom_call" | custom-call | flops 13589544960 | bytes 30000000 | tf_op jit(solution)/shard_map/spatial_backward/pallas_call | solution.py:824
  640.4 17.7 %all_to_all.56.got_ref = bf16[32,32,144]{2,1,0:T(8,128)(2,1)} all-to-all(bf16[32,32,144]{2,1,0:T(8,128)(2,1)} %get-tuple-element.86), channel_id=1, replica_groups=mesh['seq'=4,'fsdp'=8] {'fsdp','seq'}, dimensions={0} | all-to-all | bytes 589824 | tf_op jit(solution)/shard_map/all_to_all | solution.py:886
  660.1 19.9 %all_to_all.57 = bf16[4,8,32,144]{3,2,1,0:T(8,128)(2,1)} all-to-all(bf16[4,8,32,144]{3,2,1,0:T(8,128)(2,1)} %combine.3), channel_id=1, replica_groups=mesh['seq'=4,'fsdp'=8] {'seq'}, dimensions={0} | all-to-all | bytes 589824 | tf_op jit(solution)/shard_map/all_to_all | solution.py:886
  680.0 3.6 all-to-all-start.4
  686.4 51.6 %all-to-all-done.4 = bf16[4,4,64,1152]{3,2,1,0:T(8,128)(2,1)S(1)} async-done(((bf16[4,4,64,1152]{3,2,1,0:T(8,128)(2,1)}), bf16[4,4,64,1152]{3,2,1,0:T(8,128)(2,1)S(1)}, u32[]{:S(2)}, u32[]{:S(2)}) %all-to-all-start.4) | async-done | bytes 2359328 | tf_op jit(solution)/shard_map/all_to_all | solution.py:886
  738.0 3.7 all-to-all-start.10
  745.6 24.3 %all-to-all-done.10 = bf16[4,8,112,144]{2,3,1,0:T(8,128)(2,1)S(1)} async-done(((bf16[4,8,112,144]{2,3,1,0:T(8,128)(2,1)}), bf16[4,8,112,144]{2,3,1,0:T(8,128)(2,1)S(1)}, u32[]{:S(2)}, u32[]{:S(2)}) %all-to-all-start.10) | async-done | bytes 1032224 | tf_op jit(solution)/shard_map/all_to_all | solution.py:886
  (70 shorter events, 52.0 us)
Async XLA Ops:
  7.2 102.2 %all-gather.4.cloned.1.call-start = ((), (), s32[]{:S(2)}) async-start(), calls=%async_computation.11 | async-start | bytes 11943936 | tf_op jit(solution)/shard_map/all_gather | solution.py:947
  11.7 201.8 %all-gather.6.cloned.1.call-start = ((), (), s32[]{:S(2)}) async-start(), calls=%async_computation.12 | async-start | bytes 23887872 | tf_op jit(solution)/shard_map/all_gather | solution.py:947
  13.5 1.3 copy-start.4
  13.5 310.6 %all-gather.8.cloned.1.call-start = ((), (), s32[]{:S(2)}) async-start(), calls=%async_computation.13 | async-start | bytes 23887872 | tf_op jit(solution)/shard_map/all_gather | solution.py:947
  28.7 6.6 copy-start.7
  28.7 7.1 copy-start.3
  30.1 9.8 %all-to-all-start = ((s32[8,1,1]{2,1,0:T(1,128)}), s32[8,1,1]{2,1,0:T(1,128)S(1)}, u32[]{:S(2)}, u32[]{:S(2)}) async-start(s32[8,1,1]{2,1,0:T(1,128)} %broadcast_in_dim.7), calls=%async_computation | async-start | bytes 8192 | tf_op jit(solution)/shard_map/all_to_all | solution.py:886
  40.2 10.2 %copy-start.10 = (s32[8]{0:T(128)}, s32[8]{0:T(128)S(1)}, u32[]{:S(2)}) copy-start(s32[8]{0:T(128)S(1)} %reduce.index_ref) | copy-start | bytes 100
  50.4 3.9 copy-start.9
  50.4 4.6 copy-start.11
  50.4 4.6 copy-start.12
  50.4 50.7 %all-to-all-start.1 = ((bf16[8,34,16,144]{3,2,1,0:T(8,128)(2,1)}), bf16[8,34,16,144]{3,2,1,0:T(8,128)(2,1)S(1)}, u32[]{:S(2)}, u32[]{:S(2)}) async-start(bf16[8,34,16,144]{3,2,1,0:T(8,128)(2,1)} %multiply_reduce_fusion), calls=%async_computation.1 | async-start | bytes 4456448 | tf_op jit(solution)/shard_map/all_to_all | solution.py:886
  101.1 8.3 %copy-start.1 = (bf16[8,34,16,144]{3,2,1,0:T(8,128)(2,1)}, bf16[8,34,16,144]{3,2,1,0:T(8,128)(2,1)S(1)}, u32[]{:S(2)}) copy-start(bf16[8,34,16,144]{3,2,1,0:T(8,128)(2,1)S(1)} %all-to-all-done.1) | copy-start | bytes 3760132
  142.6 55.1 %all-to-all-start.2 = ((bf16[4,4,64,1152]{3,2,1,0:T(8,128)(2,1)}), bf16[4,4,64,1152]{3,2,1,0:T(8,128)(2,1)S(1)}, u32[]{:S(2)}, u32[]{:S(2)}) async-start(bf16[4,4,64,1152]{3,2,1,0:T(8,128)(2,1)} %get-tuple-element.46), calls=%async_computation.2 | async-start | bytes 4718592 | tf_op jit(solution)/shard_map/all_to_all | solution.py:886
  197.7 1.4 copy-start
  197.7 6.2 copy-start.8
  199.1 67.9 %all-to-all-start.3 = ((bf16[4,4,64,1152]{3,2,1,0:T(8,128)(2,1)}), bf16[4,4,64,1152]{3,2,1,0:T(8,128)(2,1)}, u32[]{:S(2)}, u32[]{:S(2)}) async-start(bf16[4,4,64,1152]{3,2,1,0:T(8,128)(2,1)} %bitcast.74), calls=%async_computation.3 | async-start | bytes 4718592 | tf_op jit(solution)/shard_map/all_to_all | solution.py:886
  439.5 82.6 %all-to-all-start.6 = ((bf16[4,4,32,1152]{3,2,1,0:T(8,128)(2,1)}), bf16[4,4,32,1152]{3,2,1,0:T(8,128)(2,1)S(1)}, u32[]{:S(2)}, u32[]{:S(2)}) async-start(bf16[4,4,32,1152]{3,2,1,0:T(8,128)(2,1)} %bitcast.86), calls=%async_computation.6 | async-start | bytes 2359296 | tf_op jit(solution)/shard_map/all_to_all | solution.py:886
  522.1 35.0 %copy-start.5 = (bf16[4,4,32,1152]{3,2,1,0:T(8,128)(2,1)}, bf16[4,4,32,1152]{3,2,1,0:T(8,128)(2,1)S(1)}, u32[]{:S(2)}) copy-start(bf16[4,4,32,1152]{3,2,1,0:T(8,128)(2,1)S(1)} %all-to-all-done.6.refs_0_) | copy-start | bytes 3538948
  557.2 32.8 %all-to-all-start.7 = ((bf16[4,4,32,1152]{3,2,1,0:T(8,128)(2,1)}), bf16[4,4,32,1152]{3,2,1,0:T(8,128)(2,1)S(1)}, u32[]{:S(2)}, u32[]{:S(2)}) async-start(bf16[4,4,32,1152]{3,2,1,0:T(8,128)(2,1)} %bitcast.85), calls=%async_computation.7 | async-start | bytes 2359296 | tf_op jit(solution)/shard_map/all_to_all | solution.py:886
  590.0 1.0 copy-start.6
  680.0 58.0 %all-to-all-start.4 = ((bf16[4,4,64,1152]{3,2,1,0:T(8,128)(2,1)}), bf16[4,4,64,1152]{3,2,1,0:T(8,128)(2,1)S(1)}, u32[]{:S(2)}, u32[]{:S(2)}) async-start(bf16[4,4,64,1152]{3,2,1,0:T(8,128)(2,1)} %bitcast.79), calls=%async_computation.4 | async-start | bytes 4718592 | tf_op jit(solution)/shard_map/all_to_all | solution.py:886
  738.0 32.0 %all-to-all-start.10 = ((bf16[4,8,112,144]{2,3,1,0:T(8,128)(2,1)}), bf16[4,8,112,144]{2,3,1,0:T(8,128)(2,1)S(1)}, u32[]{:S(2)}, u32[]{:S(2)}) async-start(bf16[4,8,112,144]{2,3,1,0:T(8,128)(2,1)} %copy.77), calls=%async_computation.10 | async-start | bytes 2359296 | tf_op jit(solution)/shard_map/all_to_all | solution.py:886
  774.1 2.0 copy-start.2
Sparse Core Ops, SparseCore 0:
  11.8 84.9 all-gather.3
  99.4 114.0 all-gather.5
  215.4 108.6 all-gather.7

commit v3 on v2

--- a/solution.py
+++ b/solution.py
@@ -17,6 +17,7 @@
 PAD = 128
 SCALE = HEAD_DIM ** (-0.5)
 EXP_SCALE = SCALE * math.log2(math.e)
+LN2 = math.log(2.0)
 HIGHEST = lax.Precision.HIGHEST
 F32 = jnp.float32
 BF16 = jnp.bfloat16
@@ -102,19 +103,19 @@
     for pair in range(PAIRS):
         win = window(pair)
         q_win, k_win, v_win = q_ref[:, win], k_ref[:, win], v_ref[:, win]
-        out = None
+        all_weights, all_values = [], []
         for head in (2 * pair, 2 * pair + 1):
             mask = mask_ref[head : head + 1, :]
-            scores = nt(k_win * mask, q_win) * EXP_SCALE
+            scores = nt(k_win * mask, q_win)
             if bias is not None:
                 scores = scores + bias[...]
             top = jnp.max(scores, 0, keepdims=True)
             grown = jnp.exp2(scores - top)
             total = jnp.sum(grown, 0, keepdims=True)
             stat_ref[head : head + 1, :] = top + jnp.log2(total)
-            weights = (grown * (1.0 / total)).astype(BF16)
-            part = tn(weights, v_win * mask)
-            out = part if out is None else out + part
+            all_weights.append((grown * (1.0 / total)).astype(BF16))
+            all_values.append(v_win * mask)
+        out = tn(jnp.concatenate(all_weights, 0), jnp.concatenate(all_values, 0))
         low = out[:, :128]
         put_out(pair, low if carried is None else low + carried)
         carried = out[:, 128:]
@@ -126,23 +127,26 @@
     for pair in range(PAIRS):
         win = window(pair)
         q_win, k_win, v_win, do_win = q_ref[:, win], k_ref[:, win], v_ref[:, win], do_ref[:, win]
-        grads = None
+        all_grads, all_probs, keys, queries, outs = [], [], [], [], []
         for head in (2 * pair, 2 * pair + 1):
             mask = mask_ref[head : head + 1, :]
             k_own = k_win * mask
-            scores = nt(k_own, q_win) * EXP_SCALE
+            scores = nt(k_own, q_win)
             if bias is not None:
                 scores = scores + bias[...]
             probs = jnp.exp2(scores - stat_ref[head : head + 1, :])
             grad_probs = nt(v_win * mask, do_win)
             inner = jnp.sum(probs * grad_probs, 0, keepdims=True)
-            grad_scores = (probs * (grad_probs - inner)).astype(BF16)
-            parts = (
-                tn(grad_scores, k_own),
-                nn(grad_scores, q_win * mask),
-                nn(probs.astype(BF16), do_win * mask),
-            )
-            grads = parts if grads is None else tuple(a + b for a, b in zip(grads, parts))
+            all_grads.append((probs * (grad_probs - inner)).astype(BF16))
+            all_probs.append(probs.astype(BF16))
+            keys.append(k_own)
+            queries.append(q_win * mask)
+            outs.append(do_win * mask)
+        grads = (
+            tn(jnp.concatenate(all_grads, 0), jnp.concatenate(keys, 0)),
+            nn(jnp.concatenate(all_grads, 1), jnp.concatenate(queries, 0)),
+            nn(jnp.concatenate(all_probs, 1), jnp.concatenate(outs, 0)),
+        )
         lows = tuple(g[:, :128] for g in grads)
         if carried is not None:
             lows = tuple(a + b for a, b in zip(lows, carried))
@@ -162,7 +166,8 @@
     lhs_ref[:, width : width + 3 * RANK] = ranks
     for i in range(3):
         loads.ready(first_load + i)
-        outs[i][...] = nn(lhs_ref[...], weights[first_load + i]).astype(BF16)
+        total = nn(lhs_ref[...], weights[first_load + i])
+        outs[i][...] = (total * EXP_SCALE if i == 0 else total).astype(BF16)
 
 
 def one_projection(lhs_ref, ad_ref, number, weight_ref, rank_ref):
@@ -236,14 +241,15 @@
 
 
 def temporal_cross_forward(
-    x_ref, ctx_ref, mod_ref, mask_ref, ad_ref, w_hbm,
+    x_ref, ctx_ref, mod_ref, mask_ref, ad_ref, wt_hbm, wc_hbm,
     q_ref, k_ref, v_ref, o_ref, stat_ref, rq_ref, ro_ref,
     u2_ref, qc_ref, oc_ref, statc_ref, rqc_ref, roc_ref, kp_ref, vp_ref, rk_ref, rv_ref, x3_ref,
     w_ref, bias_ref, lhs_ref, q_s, k_s, v_s, o_s, sems,
 ):
     width = x_ref.shape[2]
     first = pl.program_id(0) == 0
-    loads = Loads([(w_hbm.at[i], w_ref.at[i, pl.ds(0, width), :]) for i in range(8)], sems)
+    sources = [wt_hbm.at[i] for i in range(4)] + [wc_hbm.at[i] for i in range(4)]
+    loads = Loads([(w, w_ref.at[i, pl.ds(0, width), :]) for i, w in enumerate(sources)], sems)
     loads.start()
 
     @pl.when(first)
@@ -274,7 +280,8 @@
     u2_ref[...] = inputs.reshape(u2_ref.shape)
     lhs_ref[:, :width] = inputs
     loads.ready(4)
-    q_s[...] = one_projection(lhs_ref, ad_ref, 8, w_ref.at[4], rqc_ref.at[0]).astype(BF16)
+    queries = one_projection(lhs_ref, ad_ref, 8, w_ref.at[4], rqc_ref.at[0])
+    q_s[...] = (queries * EXP_SCALE).astype(BF16)
     qc_ref[...] = q_s[...].reshape(qc_ref.shape)
     loads.ready(5)
     loads.ready(6)
@@ -294,7 +301,7 @@
     carried = None
     count = 120
     for pair in range(PAIRS):
-        scores = nt(kp_ref[pair], q_s[:, window(pair)]) * EXP_SCALE
+        scores = nt(kp_ref[pair], q_s[:, window(pair)])
         pieces = []
         for sub in range(2):
             own = scores[PAD * sub : PAD * sub + count]
@@ -327,24 +334,66 @@
 
 
 def transposed_map(rows):
-    wide = jnp.concatenate([rows.astype(F32), jnp.zeros((PAD - RANK, rows.shape[1]), F32)], 0)
+    nothing = jnp.zeros((PAD - rows.shape[0], rows.shape[1]), F32)
+    wide = jnp.concatenate([rows.astype(F32), nothing], 0)
     return wide.T.astype(BF16)
 
 
-def down_loads(down_hbm, down_ref, first):
-    chunks, width, _ = down_ref.shape
-    return [(down_hbm.at[first + c], down_ref.at[c, :, pl.ds(0, width)]) for c in range(chunks)]
+def down_loads(core_ref, mine_hbm, other_hbm, down_ref, width):
+    half = width // 2
+    entries = []
+    for c in range(down_ref.shape[0] // width):
+        for source, core in ((mine_hbm, core_ref[0]), (other_hbm, 1 - core_ref[0])):
+            start = pl.multiple_of(c * width + core * half, 16)
+            entries.append((source.at[c], down_ref.at[pl.ds(start, half), pl.ds(0, width)]))
+    return entries
+
+
+def fill_down_maps(ad_ref, down_ref, width):
+    chunks = down_ref.shape[0] // width
+    for c in range(chunks):
+        rows = slice(c * width, (c + 1) * width)
+        down_ref[rows, width:] = transposed_map(ad_ref[2 + chunks + c])
+
+
+def feed_forward_grad(
+    core_ref, cot_ref, mod_ref, ad_ref, mine_hbm, other_hbm, grad_ref, down_ref, lhs_ref, sems
+):
+    width = cot_ref.shape[1]
+    entries = down_loads(core_ref, mine_hbm, other_hbm, down_ref, width)
+    loads = Loads(entries, sems)
+    loads.start()
+
+    @pl.when(loads.first)
+    def _():
+        lhs_ref[:, width:] = jnp.zeros((ROWS, PAD), BF16)
+        fill_down_maps(ad_ref, down_ref, width)
+
+    branch = (mod_ref[5:6, :] * cot_ref[...].astype(F32)).astype(BF16)
+    lhs_ref[:, :width] = branch
+    lhs_ref[:, width : width + RANK] = nt(branch, ad_ref[1]).astype(BF16)
+    for i in range(len(entries)):
+        loads.ready(i)
+    for cols in hidden_chunks(down_ref.shape[0]):
+        grad_ref[:, cols] = nt(lhs_ref[...], down_ref[cols, :]).astype(BF16)
+
+
+def hidden_chunks(hidden):
+    return [slice(at, at + 1536) for at in range(0, hidden, 1536)]
 
 
 def feed_forward(
-    x3_ref, cot_ref, mod_ref, ad_ref, w_hbm,
-    act_ref, g3_ref, gd_ref, gu_ref, up_ref, down_ref, lhs_ref, dlhs_ref, sems,
+    x3_ref, cot_ref, grad_ref, mod_ref, ad_ref, w_hbm,
+    act_ref, g3_ref, gd_ref, gu_ref, up_ref, lhs_ref, dh_ref, sems,
 ):
     width = x3_ref.shape[1]
-    chunks = down_ref.shape[0]
+    hidden_size = up_ref.shape[1]
+    chunks = hidden_size // width
     loads = Loads(
-        [(w_hbm.at[c], up_ref.at[c, pl.ds(0, width), :]) for c in range(chunks)]
-        + down_loads(w_hbm, down_ref, chunks),
+        [
+            (w_hbm.at[c], up_ref.at[pl.ds(0, width), pl.ds(c * width, width)])
+            for c in range(chunks)
+        ],
         sems,
     )
     loads.start()
@@ -354,63 +403,50 @@
         gd_ref[...] = jnp.zeros_like(gd_ref)
         gu_ref[...] = jnp.zeros_like(gu_ref)
         lhs_ref[:, width:] = jnp.zeros((ROWS, PAD), BF16)
-        dlhs_ref[:, width:] = jnp.zeros((ROWS, PAD), BF16)
+        up_ref[width + RANK :, :] = jnp.zeros((PAD - RANK, hidden_size), BF16)
         for c in range(chunks):
-            rows = ad_ref[2 + c]
-            up_ref[c, width:, :] = jnp.concatenate([rows, jnp.zeros((PAD - RANK, width), BF16)], 0)
-            down_ref[c, :, width:] = transposed_map(ad_ref[2 + chunks + c])
+            up_ref[width : width + RANK, c * width : (c + 1) * width] = ad_ref[2 + c]
 
     normal, inverse = normalize(x3_ref[...])
     inputs = (normal * (1.0 + mod_ref[4:5, :]) + mod_ref[3:4, :]).astype(BF16)
-    cot = cot_ref[...].astype(F32)
-    grad_branch = (mod_ref[5:6, :] * cot).astype(BF16)
     rank_up = nt(inputs, ad_ref[0]).astype(BF16)
     lhs_ref[:, :width] = inputs
     lhs_ref[:, width : width + RANK] = rank_up
-    dlhs_ref[:, :width] = grad_branch
-    dlhs_ref[:, width : width + RANK] = nt(grad_branch, ad_ref[1]).astype(BF16)
-    both = None
     for c in range(chunks):
         loads.ready(c)
-        hidden = nn(lhs_ref[...], up_ref[c])
-        active, slope = gelu_both(hidden)
-        act_ref[:, c * width : (c + 1) * width] = active.astype(BF16)
-        loads.ready(chunks + c)
-        grad_active = nt(dlhs_ref[...], down_ref[c])
-        grad_hidden = (slope * grad_active).astype(BF16)
-        part = nt(grad_hidden, up_ref[c])
-        both = part if both is None else both + part
-        gu_ref[block_rows(c), :] += tn(rank_up, grad_hidden)
+    for cols in hidden_chunks(hidden_size):
+        active, slope = gelu_both(nn(lhs_ref[...], up_ref[:, cols]))
+        act_ref[:, cols] = active.astype(BF16)
+        dh_ref[:, cols] = (slope * grad_ref[:, cols].astype(F32)).astype(BF16)
+    both = nt(dh_ref[...], up_ref[...])
+    gu_ref[...] += tn(rank_up, dh_ref[...])
     grad_rank = both[:, width : width + RANK].astype(BF16)
     grad_in = both[:, :width] + nn(grad_rank, ad_ref[0])
     gd_ref[...] += tn(grad_rank, lhs_ref[:, :width])
-    g3_ref[...] = cot + normalize_back(normal, inverse, grad_in * (1.0 + mod_ref[4:5, :]))
+    grad_in = normalize_back(normal, inverse, grad_in * (1.0 + mod_ref[4:5, :]))
+    g3_ref[...] = cot_ref[...].astype(F32) + grad_in
 
 
 def feed_forward_out(
-    act_ref, x3_ref, cot_ref, mod_ref, ad_ref, w_hbm, x4_ref, gu_ref, gd_ref, down_ref, sems
+    core_ref, act_ref, x3_ref, cot_ref, mod_ref, ad_ref, mine_hbm, other_hbm,
+    x4_ref, gu_ref, gd_ref, down_ref, sems,
 ):
     width = x3_ref.shape[1]
-    chunks = down_ref.shape[0]
-    loads = Loads(down_loads(w_hbm, down_ref, chunks), sems)
+    entries = down_loads(core_ref, mine_hbm, other_hbm, down_ref, width)
+    loads = Loads(entries, sems)
     loads.start()
 
     @pl.when(loads.first)
     def _():
         gu_ref[...] = jnp.zeros_like(gu_ref)
         gd_ref[...] = jnp.zeros_like(gd_ref)
-        for c in range(chunks):
-            down_ref[c, :, width:] = transposed_map(ad_ref[2 + chunks + c])
+        fill_down_maps(ad_ref, down_ref, width)
 
     grad_branch = (mod_ref[5:6, :] * cot_ref[...].astype(F32)).astype(BF16)
-    grad_rank = nt(grad_branch, ad_ref[1]).astype(BF16)
-    both = None
-    for c in range(chunks):
-        active = act_ref[:, c * width : (c + 1) * width]
-        loads.ready(c)
-        part = nn(active, down_ref[c])
-        both = part if both is None else both + part
-        gd_ref[block_rows(c), :] += tn(grad_rank, active)
+    gd_ref[...] += tn(nt(grad_branch, ad_ref[1]).astype(BF16), act_ref[...])
+    for i in range(len(entries)):
+        loads.ready(i)
+    both = nn(act_ref[...], down_ref[...])
     ranks = both[:, width : width + RANK].astype(BF16)
     branch = both[:, :width] + nn(ranks, ad_ref[1])
     gu_ref[...] += tn(ranks, grad_branch)
@@ -418,29 +454,22 @@
 
 
 def cross_temporal_backward(
-    continued, g3_ref, u1_ref, q_ref, k_ref, v_ref, o_ref, stat_ref, rq_ref, ro_ref,
-    u2_ref, qc_ref, oc_ref, statc_ref, rqc_ref, roc_ref, kp_ref, vp_ref, rk_ref, rv_ref,
-    ctx_ref, mod_ref, mask_ref, ad_ref, w_hbm, *rest,
+    g3_ref, u1_ref, q_ref, k_ref, v_ref, o_ref, stat_ref, rq_ref, ro_ref,
+    u2_ref, qc_ref, oc_ref, statc_ref, rqc_ref, roc_ref, kp_ref, vp_ref,
+    mod_ref, mask_ref, ad_ref, wt_hbm, wc_hbm,
+    g1_ref, gw_ref, dk_acc, dv_acc, w_ref, bias_ref, q_s, k_s, v_s, do_s, dq_s, dk_s, dv_s, sems,
 ):
-    before_ref = None
-    if continued:
-        before_ref, *rest = rest
-    (
-        g1_ref, gw_ref, w_ref, bias_ref, dk_acc, dv_acc, q_s, k_s, v_s, do_s, dq_s, dk_s, dv_s, ctx_s, sems,
-    ) = rest
     width = u1_ref.shape[2]
-    step = pl.program_id(0)
-    first = step == 0
+    first = pl.program_id(0) == 0
     order = (7, 4, 3, 0, 1, 2)
-    loads = Loads(
-        [(w_hbm.at[n], w_ref.at[i, pl.ds(0, width), :]) for i, n in enumerate(order)], sems
-    )
+    sources = [wc_hbm.at[n - 4] if n >= 4 else wt_hbm.at[n] for n in order]
+    loads = Loads([(w, w_ref.at[i, pl.ds(0, width), :]) for i, w in enumerate(sources)], sems)
     loads.start()
 
     @pl.when(first)
     def _():
         bias_ref[...] = same_place(bias_ref.shape)
-        gw_ref[...] = before_ref[...] if continued else jnp.zeros_like(gw_ref)
+        gw_ref[...] = jnp.zeros_like(gw_ref)
         dk_acc[...] = jnp.zeros_like(dk_acc)
         dv_acc[...] = jnp.zeros_like(dv_acc)
         for i, n in enumerate(order):
@@ -460,7 +489,7 @@
     for pair in range(PAIRS):
         win = window(pair)
         q_win, do_win = q_s[:, win], do_s[:, win]
-        scores = nt(kp_ref[pair], q_win) * EXP_SCALE
+        scores = nt(kp_ref[pair], q_win)
         grad_probs = nt(vp_ref[pair], do_win)
         all_probs, all_grads = [], []
         nothing = jnp.zeros((PAD - count, ROWS), F32)
@@ -495,7 +524,7 @@
 
     def put(index, values):
         dq_s[:, tile(index)] = (values[0] * SCALE).astype(BF16)
-        dk_s[:, tile(index)] = (values[1] * SCALE).astype(BF16)
+        dk_s[:, tile(index)] = (values[1] * LN2).astype(BF16)
         dv_s[:, tile(index)] = values[2].astype(BF16)
 
     attend_back(q_s, k_s, v_s, do_s, mask_ref, bias_ref, stat_ref.at[0], put)
@@ -503,37 +532,6 @@
         (dq_s, dk_s, dv_s), rows(u1_ref), rq_ref[0], ad_ref, 4, w_ref, loads, 3, gw_ref, 0
     )
     g1_ref[...] = grad.astype(BF16).reshape(g1_ref.shape)
-
-    @pl.when(step == pl.num_programs(0) - 1)
-    def _():
-        context = ctx_ref[...].astype(F32)
-        for acc, factor, rank_ref, number, at in (
-            (dk_acc, SCALE, rk_ref, 9, 10),
-            (dv_acc, 1.0, rv_ref, 10, 12),
-        ):
-            held = None
-            for pair in range(PAIRS):
-                whole = acc[pair]
-                out = whole[:PAD] * mask_ref[2 * pair : 2 * pair + 1, :].astype(F32)
-                out = out + whole[PAD:] * mask_ref[2 * pair + 1 : 2 * pair + 2, :].astype(F32)
-                out = out * factor
-                low = out[:, :128]
-                ctx_s[:, tile(pair)] = low if held is None else low + held
-                held = out[:, 128:]
-            ctx_s[:, tile(PAIRS)] = held
-            grad_kv = ctx_s[...]
-            grad_rank = lax.dot_general(
-                grad_kv, ad_ref[2 * number + 1].astype(F32), (((1,), (1,)), ((), ())),
-                precision=HIGHEST, preferred_element_type=F32,
-            )
-            gw_ref[block_rows(at), :] += lax.dot_general(
-                grad_rank, context, (((0,), (0,)), ((), ())),
-                precision=HIGHEST, preferred_element_type=F32,
-            )
-            gw_ref[block_rows(at + 1), :] += lax.dot_general(
-                rank_ref[...].astype(F32), grad_kv, (((0,), (0,)), ((), ())),
-                precision=HIGHEST, preferred_element_type=F32,
-            )
 
 
 def pack_columns(table_ref, packed_ref, clips):
@@ -545,64 +543,150 @@
             packed_ref[f * parts + s] = piece.astype(BF16)
 
 
-def spatial_backward(
-    halves, clips, *refs,
-):
+def stacked(g1_refs):
+    parts = g1_refs[0].shape[0]
+    pieces = [ref[s, 0] for s in range(parts) for ref in g1_refs]
+    return jnp.concatenate(pieces, 0).astype(F32)
+
+
+def spatial_backward(halves, clips, *refs):
     g1_refs, refs = refs[:halves], refs[halves:]
     (
         x_ref, q_ref, k_ref, v_ref, o_ref, stat_ref, rq_ref, ro_ref, mod_ref, mask_ref, ad_ref, w_hbm,
-        g0_ref, packed_ref, w_ref, gw_ref, do_s, dq_s, dk_s, dv_s, sems,
+        down_ref, up_ref, d_ref, packed_ref, w_ref, gw_ref, do_s, sems,
     ) = refs
     width = x_ref.shape[2]
-    order = (3, 0, 1, 2)
-    loads = Loads(
-        [(w_hbm.at[n], w_ref.at[i, pl.ds(0, width), :]) for i, n in enumerate(order)], sems
-    )
+    loads = Loads([(w_hbm.at[3], w_ref.at[pl.ds(0, width), :])], sems)
     loads.start()
 
     @pl.when(loads.first)
     def _():
         gw_ref[...] = jnp.zeros_like(gw_ref)
-        for i, n in enumerate(order):
-            w_ref[i, width:, :] = up_rows(ad_ref, n, n % 3, width)
-
-    parts = g1_refs[0].shape[0]
-    pieces = [ref[s, 0] for s in range(parts) for ref in g1_refs]
-    grad = jnp.concatenate(pieces, 0).astype(F32)
+        w_ref[width:, :] = up_rows(ad_ref, 3, 0, width)
+
+    grad = stacked(g1_refs)
     loads.ready(0)
     do_s[...] = one_back(
-        (mod_ref[2:3, :] * grad).astype(BF16), o_ref[0], ro_ref[0], ad_ref, 3, w_ref.at[0], gw_ref, 6
+        (mod_ref[2:3, :] * grad).astype(BF16), o_ref[0], ro_ref[0], ad_ref, 3, w_ref, gw_ref, 6
     ).astype(BF16)
 
     def put(index, values):
-        dq_s[:, tile(index)] = (values[0] * SCALE).astype(BF16)
-        dk_s[:, tile(index)] = (values[1] * SCALE).astype(BF16)
-        dv_s[:, tile(index)] = values[2].astype(BF16)
+        for i, factor in enumerate((SCALE, LN2, 1.0)):
+            value = values[i] if factor == 1.0 else values[i] * factor
+            d_ref[0, :, width * i + 128 * index : width * i + 128 * index + 128] = value.astype(BF16)
 
     attend_back(
         q_ref.at[0], k_ref.at[0], v_ref.at[0], do_s, mask_ref, None, stat_ref.at[0], put
     )
+    ranks = rq_ref[0]
+    grad_ranks = None
+    for i in range(3):
+        grad = d_ref[0, :, width * i : width * (i + 1)]
+        gw_ref[block_rows(2 * i + 1), :] += tn(ranks, grad)[block_rows(i)]
+        part = nt(grad, up_rows(ad_ref, i, i, width))
+        grad_ranks = part if grad_ranks is None else grad_ranks + part
+    d_ref[0, :, 3 * width :] = grad_ranks.astype(BF16)
+    normal, _ = normalize(x_ref[0].astype(F32))
+    inputs = (normal * (1.0 + mod_ref[1:2, :]) + mod_ref[0:1, :]).astype(BF16)
+    downs = tn(d_ref[0, :, 3 * width :], inputs)
+    for i in range(3):
+        gw_ref[block_rows(2 * i), :] += downs[block_rows(i)]
+
+    @pl.when(pl.program_id(0) == pl.num_programs(0) - 1)
+    def _():
+        at = 8 * RANK
+        gw_ref[at : at + RANK, :] = down_ref[...]
+        gw_ref[at + RANK : at + RANK + up_ref.shape[0], :] = up_ref[...]
+        pack_columns(gw_ref, packed_ref, clips)
+
+
+def spatial_input_grad(halves, *refs):
+    g1_refs, refs = refs[:halves], refs[halves:]
+    x_ref, d_ref, mod_ref, ad_ref, w_hbm, g0_ref, w_ref, sems = refs
+    width = x_ref.shape[2]
+    loads = Loads(
+        [(w_hbm.at[i], w_ref.at[:, pl.ds(i * width, width)]) for i in range(3)], sems
+    )
+    loads.start()
+
+    @pl.when(loads.first)
+    def _():
+        w_ref[:, 3 * width :] = transposed_map(three_downs(ad_ref, 0))
+
     normal, inverse = normalize(x_ref[0].astype(F32))
-    inputs = (normal * (1.0 + mod_ref[1:2, :]) + mod_ref[0:1, :]).astype(BF16)
-    grad_in = three_back(
-        (dq_s, dk_s, dv_s), inputs, rq_ref[0], ad_ref, 0, w_ref, loads, 1, gw_ref, 0
-    )
+    grad = stacked(g1_refs)
+    for i in range(3):
+        loads.ready(i)
+    grad_in = nt(d_ref[0], w_ref[...])
     grad = grad + normalize_back(normal, inverse, grad_in * (1.0 + mod_ref[1:2, :]))
     g0_ref[0] = grad.astype(BF16)
 
-    @pl.when(pl.program_id(0) == pl.num_programs(0) - 1)
-    def _():
-        pack_columns(gw_ref, packed_ref, clips)
-
-
-def pack_early(clips, *refs):
-    *sources, packed_ref, table_ref = refs
-    at = 0
-    for ref in sources:
-        table_ref[at : at + ref.shape[0], :] = ref[...]
-        at += ref.shape[0]
+
+def pack_early(clips, halves, *refs):
+    gw_refs, refs = refs[:halves], refs[halves:]
+    dk_refs, refs = refs[:halves], refs[halves:]
+    dv_refs, refs = refs[:halves], refs[halves:]
+    down_ref, up_ref, rk_ref, rv_ref, ctx_ref, mask_ref, ad_ref, packed_ref, table_ref, ctx_s = refs
+
+    def added(each):
+        total = each[0]
+        for value in each[1:]:
+            total = total + value
+        return total
+
+    at = gw_refs[0].shape[0]
+    table_ref[:at, :] = added([ref[...] for ref in gw_refs])
+    table_ref[at : at + RANK, :] = down_ref[...]
+    at += RANK
+    table_ref[at : at + up_ref.shape[0], :] = up_ref[...]
+    at += up_ref.shape[0]
     table_ref[at:, :] = jnp.zeros((table_ref.shape[0] - at, table_ref.shape[1]), F32)
+    context = ctx_ref[...].astype(F32)
+    for accs, factor, rank_ref, number, at in (
+        (dk_refs, LN2, rk_ref, 9, 10),
+        (dv_refs, 1.0, rv_ref, 10, 12),
+    ):
+        held = None
+        for pair in range(PAIRS):
+            whole = added([ref[pair] for ref in accs]) * factor
+            out = whole[:PAD] * mask_ref[2 * pair : 2 * pair + 1, :].astype(F32)
+            out = out + whole[PAD:] * mask_ref[2 * pair + 1 : 2 * pair + 2, :].astype(F32)
+            low = out[:, :128]
+            ctx_s[:, tile(pair)] = low if held is None else low + held
+            held = out[:, 128:]
+        ctx_s[:, tile(PAIRS)] = held
+        grad_kv = ctx_s[...]
+        grad_rank = lax.dot_general(
+            grad_kv, ad_ref[2 * number + 1].astype(F32), (((1,), (1,)), ((), ())),
+            precision=HIGHEST, preferred_element_type=F32,
+        )
+        table_ref[block_rows(at), :] = lax.dot_general(
+            grad_rank, context, (((0,), (0,)), ((), ())),
+            precision=HIGHEST, preferred_element_type=F32,
+        )
+        table_ref[block_rows(at + 1), :] = lax.dot_general(
+            rank_ref[...].astype(F32), grad_kv, (((0,), (0,)), ((), ())),
+            precision=HIGHEST, preferred_element_type=F32,
+        )
     pack_columns(table_ref, packed_ref, clips)
+
+
+def assemble(early_ref, late_ref, wide_ref, narrow_ref):
+    adapters = wide_ref.shape[1]
+    times = narrow_ref.shape[3] // wide_ref.shape[3]
+
+    def block(ref, index, a):
+        each = ref.shape[2] // RANK
+        return ref[index // each, a, block_rows(index % each), :].astype(F32)
+
+    for a in range(adapters):
+        for i in range(8):
+            wide_ref[i, a] = block(late_ref, i, a)
+        for i in range(17):
+            wide_ref[8 + i, a] = block(early_ref, i, a)
+        wide_ref[25, a] = block(late_ref, 8, a)
+        for n, (ref, at) in enumerate(((early_ref, 17), (late_ref, 9))):
+            narrow_ref[n, a] = jnp.concatenate([block(ref, at + j, a) for j in range(times)], 1)
 
 
 def combine(index_ref, got_ref, out_ref, acc_ref):
@@ -623,9 +707,58 @@
         out_ref[s] = table
 
 
+def tail_groups(cols):
+    tail = cols - PAD
+    return PAD // tail if 0 < tail < PAD and PAD % tail == 0 else 0
+
+
+def pick(index_ref, wide_ref, narrow_ref, out_ref):
+    clips = index_ref.shape[0]
+    count, _, _, cols = wide_ref.shape
+    times = narrow_ref.shape[3] // cols
+    group = tail_groups(cols)
+    total = count + 2 * times
+
+    def step(f, carry):
+        a = index_ref[f]
+        blocks = [wide_ref[k, a] for k in range(count)]
+        for p in range(2):
+            rows = narrow_ref[p, a]
+            blocks += [rows[:, cols * j : cols * (j + 1)] for j in range(times)]
+        if not group:
+            for k, rows in enumerate(blocks):
+                out_ref[f, block_rows(k), :] = rows
+            return carry
+        for k, rows in enumerate(blocks):
+            out_ref[f, block_rows(k), :] = rows[:, :PAD]
+        for k in range(0, total, group):
+            tails = [rows[:, PAD:] for rows in blocks[k : k + group]]
+            missing = group - len(tails)
+            if missing:
+                tails.append(jnp.zeros((RANK, missing * (cols - PAD)), BF16))
+            out_ref[f, block_rows(total + k // group), :] = jnp.concatenate(tails, 1)
+        return carry
+
+    lax.fori_loop(0, clips, step, 0)
+
+
+def unpick(count, cols, got_ref, out_ref):
+    clips = got_ref.shape[0]
+    group = tail_groups(cols)
+    for k in range(count):
+        pieces = []
+        for f in range(clips):
+            pieces.append(got_ref[f, block_rows(k), :])
+            if group:
+                at = (k % group) * (cols - PAD)
+                tails = got_ref[f, block_rows(count + k // group), :]
+                pieces.append(tails[:, at : at + cols - PAD])
+        out_ref[k] = jnp.concatenate(pieces, 1)
+
+
 def whole_block(array):
     zeros = (0,) * array.ndim
-    return pl.BlockSpec(array.shape, lambda i: zeros)
+    return pl.BlockSpec(array.shape, lambda i: zeros, pipeline_mode=pl.Buffered(1))
 
 
 def anywhere():
@@ -682,7 +815,7 @@
     )(video, mods, masks, wide, w_s)
 
 
-def run_temporal_cross_forward(x1, context, mods, masks, wide, w_tc):
+def run_temporal_cross_forward(x1, context, mods, masks, wide, w_t, w_c):
     frames, places, d = x1.shape
     groups = places * frames // ROWS
     across = pl.BlockSpec((frames, ROWS // frames, d), lambda i: (0, i, 0))
@@ -697,7 +830,7 @@
     return pl.pallas_call(
         temporal_cross_forward,
         grid=(groups,),
-        in_specs=[across, whole_block(context), whole_block(mods), whole_block(masks), whole_block(wide), anywhere()],
+        in_specs=[across, whole_block(context), whole_block(mods), whole_block(masks), whole_block(wide), anywhere(), anywhere()],
         out_specs=[across] * 4 + [stat, three, one] + [across] * 3 + [stat, one, one]
         + [full(PAIRS, 2 * PAD, 256)] * 2 + [full(PAD, RANK)] * 2 + [across],
         out_shape=[act] * 4 + [stat_shape, like((groups, ROWS, 3 * RANK), BF16), one_shape]
@@ -711,68 +844,106 @@
         compiler_params=PARAMS,
         cost_estimate=cost(14 * places * frames * d * d, 50_000_000),
         name="temporal_cross_forward",
-    )(x1, context, mods, masks, wide, w_tc)
-
-
-def run_feed_forward(x3, cot, mods, maps, w_f):
+    )(x1, context, mods, masks, wide, w_t, w_c)
+
+
+def in_smem():
+    return pl.BlockSpec(memory_space=pltpu.SMEM)
+
+
+def run_feed_forward_grad(cot, mods, maps, down):
+    tokens, d = cot.shape
+    core, mine, other = down
+    hidden = mine.shape[0] * d
+    return pl.pallas_call(
+        feed_forward_grad,
+        grid=(tokens // ROWS,),
+        in_specs=[in_smem(), pl.BlockSpec((ROWS, d), lambda i: (i, 0)), whole_block(mods), whole_block(maps), anywhere(), anywhere()],
+        out_specs=pl.BlockSpec((ROWS, hidden), lambda i: (i, 0)),
+        out_shape=like((tokens, hidden), BF16),
+        scratch_shapes=[
+            pltpu.VMEM((hidden, d + PAD), BF16),
+            pltpu.VMEM((ROWS, d + PAD), BF16),
+            pltpu.SemaphoreType.DMA((2 * mine.shape[0],)),
+        ],
+        compiler_params=PARAMS,
+        cost_estimate=cost(2 * tokens * d * hidden, 30_000_000),
+        name="feed_forward_grad",
+    )(core, cot, mods, maps, mine, other)
+
+
+def run_feed_forward(x3, cot, grad_active, mods, maps, up):
     tokens, d = x3.shape
-    chunks = w_f.shape[0] // 2
+    chunks = up.shape[0]
     rows = pl.BlockSpec((ROWS, d), lambda i: (i, 0))
-    fixed = lambda n: pl.BlockSpec((n * RANK, d), lambda i: (0, 0))
+    wide_rows = pl.BlockSpec((ROWS, chunks * d), lambda i: (i, 0))
     return pl.pallas_call(
         feed_forward,
         grid=(tokens // ROWS,),
-        in_specs=[rows, rows, whole_block(mods), whole_block(maps), anywhere()],
-        out_specs=[pl.BlockSpec((ROWS, chunks * d), lambda i: (i, 0)), rows, fixed(1), fixed(chunks)],
+        in_specs=[rows, rows, wide_rows, whole_block(mods), whole_block(maps), anywhere()],
+        out_specs=[
+            wide_rows,
+            rows,
+            pl.BlockSpec((RANK, d), lambda i: (0, 0)),
+            pl.BlockSpec((RANK, chunks * d), lambda i: (0, 0)),
+        ],
         out_shape=[
             like((tokens, chunks * d), BF16),
             like((tokens, d), F32),
             like((RANK, d), F32),
-            like((chunks * RANK, d), F32),
+            like((RANK, chunks * d), F32),
         ],
         scratch_shapes=[
-            pltpu.VMEM((chunks, d + PAD, d), BF16),
-            pltpu.VMEM((chunks, d, d + PAD), BF16),
+            pltpu.VMEM((d + PAD, chunks * d), BF16),
             pltpu.VMEM((ROWS, d + PAD), BF16),
-            pltpu.VMEM((ROWS, d + PAD), BF16),
-            pltpu.SemaphoreType.DMA((2 * chunks,)),
+            pltpu.VMEM((ROWS, chunks * d), BF16),
+            pltpu.SemaphoreType.DMA((chunks,)),
         ],
         compiler_params=PARAMS,
-        cost_estimate=cost(6 * tokens * d * d * chunks, 50_000_000),
+        cost_estimate=cost(4 * tokens * d * d * chunks, 50_000_000),
         name="feed_forward",
-    )(x3, cot, mods, maps, w_f)
-
-
-def run_feed_forward_out(active, x3, cot, mods, maps, w_f):
+    )(x3, cot, grad_active, mods, maps, up)
+
+
+def run_feed_forward_out(active, x3, cot, mods, maps, down):
     tokens, d = x3.shape
-    chunks = w_f.shape[0] // 2
+    core, mine, other = down
+    hidden = active.shape[1]
     rows = pl.BlockSpec((ROWS, d), lambda i: (i, 0))
-    fixed = lambda n: pl.BlockSpec((n * RANK, d), lambda i: (0, 0))
     return pl.pallas_call(
         feed_forward_out,
         grid=(tokens // ROWS,),
         in_specs=[
-            pl.BlockSpec((ROWS, chunks * d), lambda i: (i, 0)),
+            in_smem(),
+            pl.BlockSpec((ROWS, hidden), lambda i: (i, 0)),
             rows,
             rows,
             whole_block(mods),
             whole_block(maps),
             anywhere(),
-        ],
-        out_specs=[rows, fixed(1), fixed(chunks)],
+            anywhere(),
+        ],
+        out_specs=[
+            rows,
+            pl.BlockSpec((RANK, d), lambda i: (0, 0)),
+            pl.BlockSpec((RANK, hidden), lambda i: (0, 0)),
+        ],
         out_shape=[
             like((tokens, d), BF16),
             like((RANK, d), F32),
-            like((chunks * RANK, d), F32),
-        ],
-        scratch_shapes=[pltpu.VMEM((chunks, d, d + PAD), BF16), pltpu.SemaphoreType.DMA((chunks,))],
+            like((RANK, hidden), F32),
+        ],
+        scratch_shapes=[
+            pltpu.VMEM((hidden, d + PAD), BF16),
+            pltpu.SemaphoreType.DMA((2 * mine.shape[0],)),
+        ],
         compiler_params=PARAMS,
-        cost_estimate=cost(2 * tokens * d * d * chunks, 30_000_000),
+        cost_estimate=cost(2 * tokens * d * hidden, 30_000_000),
         name="feed_forward_out",
-    )(active, x3, cot, mods, maps, w_f)
-
-
-def run_cross_temporal_backward(g3, u1, saved, context, mods, masks, wide, w_tc, half, halves, before):
+    )(core, active, x3, cot, mods, maps, mine, other)
+
+
+def run_cross_temporal_backward(g3, u1, saved, mods, masks, wide, w_t, w_c, half, halves):
     frames, places, d = u1.shape
     groups = places * frames // ROWS // halves
     start = half * groups
@@ -781,42 +952,44 @@
     stat = pl.BlockSpec((1, HEADS, ROWS), by_group)
     three = pl.BlockSpec((1, ROWS, 3 * RANK), by_group)
     one = pl.BlockSpec((1, ROWS, RANK), by_group)
-    kp, vp, rk, rv = saved[13:17]
-    grads = pl.BlockSpec((16 * RANK, d), lambda i: (0, 0))
-    extra = [] if before is None else [before]
-
-    def body(*refs):
-        cross_temporal_backward(before is not None, *refs)
-
+    kp, vp = saved[13:15]
+    pair_sums = pl.BlockSpec((PAIRS, 2 * PAD, 256), lambda i: (0, 0, 0))
     return pl.pallas_call(
-        body,
+        cross_temporal_backward,
         grid=(groups,),
         in_specs=[across, across] + [across] * 4 + [stat, three, one] + [across] * 3 + [stat, one, one]
-        + [whole_block(kp), whole_block(vp), whole_block(rk), whole_block(rv)]
-        + [whole_block(context), whole_block(mods), whole_block(masks), whole_block(wide), anywhere()]
-        + [grads] * len(extra),
-        out_specs=[pl.BlockSpec((frames, ROWS // frames, d), lambda i: (0, i, 0)), grads],
-        out_shape=[like((frames, places // halves, d), BF16), like((16 * RANK, d), F32)],
+        + [whole_block(kp), whole_block(vp)]
+        + [whole_block(mods), whole_block(masks), whole_block(wide), anywhere(), anywhere()],
+        out_specs=[
+            pl.BlockSpec((frames, ROWS // frames, d), lambda i: (0, i, 0)),
+            pl.BlockSpec((16 * RANK, d), lambda i: (0, 0)),
+            pair_sums,
+            pair_sums,
+        ],
+        out_shape=[like((frames, places // halves, d), BF16), like((16 * RANK, d), F32)]
+        + [like((PAIRS, 2 * PAD, 256), F32)] * 2,
         scratch_shapes=[
             pltpu.VMEM((6, d + PAD, d), BF16),
             pltpu.VMEM((ROWS, ROWS), F32),
-            pltpu.VMEM((PAIRS, 2 * PAD, 256), F32),
-            pltpu.VMEM((PAIRS, 2 * PAD, 256), F32),
         ]
         + [pltpu.VMEM((ROWS, d), BF16)] * 7
-        + [pltpu.VMEM((PAD, d), F32), pltpu.SemaphoreType.DMA((6,))],
+        + [pltpu.SemaphoreType.DMA((6,))],
         compiler_params=PARAMS,
         cost_estimate=cost(14 * places // halves * frames * d * d, 30_000_000),
         name="cross_temporal_backward",
-    )(g3, u1, *saved[:17], context, mods, masks, wide, w_tc, *extra)
-
-
-def run_spatial_backward(g1_halves, video, saved, mods, masks, wide, w_s, clips):
+    )(g3, u1, *saved[:15], mods, masks, wide, w_t, w_c)
+
+
+LATE_BLOCKS = 16
+EARLY_BLOCKS = 24
+
+
+def run_spatial_backward(g1_halves, video, saved, mods, masks, wide, w_s, late_down, late_up, clips):
     frames, rows, d = video.shape
     parts = g1_halves[0].shape[0]
     by_frame = lambda i: (i, 0, 0)
     row_block = pl.BlockSpec((1, rows, d), by_frame)
-    packed = (clips * parts, 8 * RANK // parts, d // clips)
+    packed = (clips * parts, LATE_BLOCKS * RANK // parts, d // clips)
 
     def body(*refs):
         spatial_backward(len(g1_halves), clips, *refs)
@@ -836,35 +1009,116 @@
             whole_block(masks),
             whole_block(wide),
             anywhere(),
-        ],
-        out_specs=[row_block, pl.BlockSpec(packed, lambda i: (0, 0, 0))],
-        out_shape=[like(video.shape, BF16), like(packed, BF16)],
-        scratch_shapes=[pltpu.VMEM((4, d + PAD, d), BF16), pltpu.VMEM((8 * RANK, d), F32)]
-        + [pltpu.VMEM((ROWS, d), BF16)] * 4
-        + [pltpu.SemaphoreType.DMA((4,))],
+            whole_block(late_down),
+            whole_block(late_up),
+        ],
+        out_specs=[
+            pl.BlockSpec((1, rows, 3 * d + PAD), by_frame),
+            pl.BlockSpec(packed, lambda i: (0, 0, 0)),
+        ],
+        out_shape=[like((frames, rows, 3 * d + PAD), BF16), like(packed, BF16)],
+        scratch_shapes=[pltpu.VMEM((d + PAD, d), BF16), pltpu.VMEM((LATE_BLOCKS * RANK, d), F32)]
+        + [pltpu.VMEM((ROWS, d), BF16), pltpu.SemaphoreType.DMA((1,))],
         compiler_params=PARAMS,
-        cost_estimate=cost(10 * frames * rows * d * d, 30_000_000),
+        cost_estimate=cost(6 * frames * rows * d * d, 30_000_000),
         name="spatial_backward",
-    )(*g1_halves, video, *saved, mods, masks, wide, w_s)
-
-
-EARLY_BLOCKS = 28
-
-
-def run_pack_early(sources, clips, parts):
-    d = sources[0].shape[1]
+    )(*g1_halves, video, *saved, mods, masks, wide, w_s, late_down, late_up)
+
+
+def run_spatial_input_grad(g1_halves, video, grads, mods, wide, w_s):
+    frames, rows, d = video.shape
+    parts = g1_halves[0].shape[0]
+    by_frame = lambda i: (i, 0, 0)
+    row_block = pl.BlockSpec((1, rows, d), by_frame)
+
+    def body(*refs):
+        spatial_input_grad(len(g1_halves), *refs)
+
+    return pl.pallas_call(
+        body,
+        grid=(frames,),
+        in_specs=[
+            pl.BlockSpec((parts, 1, g.shape[2], d), lambda i: (0, i, 0, 0)) for g in g1_halves
+        ]
+        + [
+            row_block,
+            pl.BlockSpec((1, rows, grads.shape[2]), by_frame),
+            whole_block(mods),
+            whole_block(wide),
+            anywhere(),
+        ],
+        out_specs=row_block,
+        out_shape=like(video.shape, BF16),
+        scratch_shapes=[pltpu.VMEM((d, 3 * d + PAD), BF16), pltpu.SemaphoreType.DMA((3,))],
+        compiler_params=PARAMS,
+        cost_estimate=cost(6 * frames * rows * d * d, 20_000_000),
+        name="spatial_input_grad",
+    )(*g1_halves, video, grads, mods, wide, w_s)
+
+
+PLAIN = pltpu.CompilerParams(vmem_limit_bytes=VMEM_LIMIT)
+
+
+def in_vmem():
+    return pl.BlockSpec(memory_space=pltpu.VMEM)
+
+
+def run_pack_early(gw, dk, dv, sources, clips, parts):
+    d = gw[0].shape[1]
     packed = (clips * parts, EARLY_BLOCKS * RANK // parts, d // clips)
 
     def body(*refs):
-        pack_early(clips, *refs)
+        pack_early(clips, len(gw), *refs)
 
     return pl.pallas_call(
         body,
         out_shape=like(packed, BF16),
-        scratch_shapes=[pltpu.VMEM((EARLY_BLOCKS * RANK, d), F32)],
-        compiler_params=pltpu.CompilerParams(vmem_limit_bytes=VMEM_LIMIT),
+        scratch_shapes=[pltpu.VMEM((EARLY_BLOCKS * RANK, d), F32), pltpu.VMEM((PAD, d), F32)],
+        compiler_params=PLAIN,
         name="pack_early",
-    )(*sources)
+    )(*gw, *dk, *dv, *sources)
+
+
+def run_assemble(early, late, wide_shape, narrow_shape):
+    return pl.pallas_call(
+        assemble,
+        in_specs=[in_vmem()] * 2,
+        out_specs=[in_vmem()] * 2,
+        out_shape=[like(wide_shape, F32), like(narrow_shape, F32)],
+        compiler_params=PLAIN,
+        name="assemble",
+    )(early, late)
+
+
+def run_pick(all_index, wide, narrow):
+    count, _, _, cols = wide.shape
+    blocks = count + 2 * (narrow.shape[3] // cols)
+    group = tail_groups(cols)
+    shape = (blocks * RANK, cols)
+    if group:
+        shape = ((blocks + -(-blocks // group)) * RANK, PAD)
+    return pl.pallas_call(
+        pick,
+        in_specs=[in_smem(), in_vmem(), in_vmem()],
+        out_specs=in_vmem(),
+        out_shape=like((all_index.shape[0], *shape), BF16),
+        compiler_params=PLAIN,
+        name="pick",
+    )(all_index, wide, narrow)
+
+
+def run_unpick(got, blocks, cols):
+    def body(*refs):
+        unpick(blocks, cols, *refs)
+
+    return pl.pallas_call(
+        body,
+        in_specs=[in_vmem()],
+        out_specs=in_vmem(),
+        out_shape=like((blocks, RANK, got.shape[0] * cols), BF16),
+        compiler_params=PLAIN,
+        name="unpick",
+    )(got)
 
 
 def run_combine(all_index, got, adapters):
@@ -886,38 +1140,33 @@
     return lax.all_to_all(array, axes, split_axis=0, concat_axis=0, tiled=True)
 
 
-def fetch_adapters(choice, adapt_wide, adapt_ff):
-    cols = adapt_wide.shape[-1]
-    times = adapt_ff.shape[-1] // cols
-    narrow = adapt_ff.reshape(adapt_ff.shape[:-1] + (times, cols))
-    narrow = jnp.moveaxis(narrow, 3, 1).reshape(2 * times, *adapt_wide.shape[1:])
-    table = jnp.concatenate([adapt_wide, narrow], 0)
-    picked = jnp.sum(
-        choice[:, None, :, None, None] * table[None].astype(F32), axis=2
-    ).astype(BF16)
-    got = exchange(picked, "fsdp")
-    return jnp.moveaxis(got, 0, 2).reshape(table.shape[0], RANK, -1)
-
-
 def reduce_grads(packed, all_index, adapters):
     got = exchange(packed, ("fsdp", "seq"))
     return run_combine(all_index, got, adapters)
 
 
-def spread_grads(quarter):
-    whole = exchange(quarter)
-    parts, adapters, share, cols = whole.shape
-    table = whole.transpose(1, 0, 2, 3).reshape(adapters, -1, RANK, cols)
-    return table.transpose(1, 0, 2, 3).astype(F32)
-
-
-def hidden_order(up, down, clips):
+def up_chunks(up, clips, times):
     rows, hidden = up.shape
-    width = down.shape[1]
-    times = hidden // width
-    cols = width // clips
-    up = up.reshape(rows, clips, times, cols).transpose(2, 0, 1, 3).reshape(times, rows, width)
-    return jnp.concatenate([up, down.reshape(times, cols, width)], 0)
+    cols = hidden // (clips * times)
+    return up.reshape(rows, clips, times, cols).transpose(2, 0, 1, 3).reshape(times, rows, -1)
+
+
+def gather(array):
+    return lax.all_gather(array, "fsdp", axis=1, tiled=True)
+
+
+def fetch_down(down, clips, parts, times, d):
+    quarters = down.reshape(times, -1, d)
+    half = d // 2
+    if times != parts or clips % 2:
+        whole = gather(quarters)
+        return jnp.zeros((1,), jnp.int32), whole[:, :half], whole[:, half:]
+    own = gather(lax.dynamic_slice_in_dim(quarters, lax.axis_index("seq"), 1, 0))[0]
+    core = lax.axis_index("fsdp") % 2
+    piece = lax.dynamic_slice_in_dim(own, core * half, half, 0)
+    mine = exchange(jnp.broadcast_to(piece[None], (parts, half, d)))
+    other = lax.ppermute(mine, "fsdp", [(i, i ^ 1) for i in range(clips)])
+    return core.astype(jnp.int32)[None], mine, other
 
 
 def on_device(
@@ -936,25 +1185,28 @@
     parts = lax.axis_size("seq")
     clips = lax.axis_size("fsdp")
     d = video.shape[-1]
-    adapters = adapt_wide.shape[2]
+    count, adapters, _, cols = adapt_wide.shape[1:]
+    times = adapt_ff.shape[-1] // cols
     places = SPATIAL // parts
     frames = FRAMES // parts
     mods = modulation[0, 0]
     masks = head_masks()
     ctx = jnp.pad(context[0], ((0, PAD - context.shape[1]), (0, 0)))
 
-    def gather(array):
-        return lax.all_gather(array, "fsdp", axis=1, tiled=True)
-
     def attention_weights(j):
-        return [qkv_weights[0, 3 * j : 3 * j + 3], out_weights[0, j : j + 1]]
-
-    w_s = gather(jnp.concatenate(attention_weights(0), 0))
+        return gather(
+            jnp.concatenate([qkv_weights[0, 3 * j : 3 * j + 3], out_weights[0, j : j + 1]], 0)
+        )
+
     all_index = exchange(jnp.broadcast_to(adapter_index, (clips,)), "fsdp")
-    choice = (all_index[:, None] == jnp.arange(adapters)[None, :]).astype(F32)
-    wide = fetch_adapters(choice, adapt_wide[0], adapt_ff[0])
-    w_tc = gather(jnp.concatenate(attention_weights(1) + attention_weights(2), 0))
-    w_f = gather(hidden_order(ffn_up[0], ffn_down[0], clips))
+    down = fetch_down(ffn_down[0], clips, parts, times, d)
+    w_s = attention_weights(0)
+    picked = run_pick(all_index, adapt_wide[0], adapt_ff[0])
+    wide = run_unpick(exchange(picked, "fsdp"), count + 2 * times, cols)
+    w_t = attention_weights(1)
+    w_c = attention_weights(2)
+    ffn_up, _ = lax.optimization_barrier((ffn_up, picked))
+    up = gather(up_chunks(ffn_up[0], clips, times))
     maps_f = wide[24:]
 
     cot = cotangent.reshape(frames, parts, places, d).transpose(1, 0, 2, 3)
@@ -962,31 +1214,43 @@
     frames_in = video.reshape(frames, SPATIAL, d)
     x1, *kept_s = run_spatial_forward(frames_in, mods, masks, wide, w_s, parts)
     u1 = exchange(x1).reshape(FRAMES, places, d)
-    *kept_t, x3 = run_temporal_cross_forward(u1, ctx, mods, masks, wide, w_tc)
+    grad_active = run_feed_forward_grad(cot, mods, maps_f, down)
+    *kept_t, x3 = run_temporal_cross_forward(u1, ctx, mods, masks, wide, w_t, w_c)
     x3 = x3.reshape(FRAMES * places, d)
-    active, g3, grad_a24, grad_b24 = run_feed_forward(x3, cot, mods, maps_f, w_f)
+    active, g3, grad_a24, grad_b24 = run_feed_forward(x3, cot, grad_active, mods, maps_f, up)
     g3 = g3.reshape(FRAMES, places, d)
     groups = FRAMES * places // ROWS
     halves = 2 if groups % 2 == 0 else 1
-    g1_halves, grads_t = [], None
+    g1_halves, gw, dk, dv = [], [], [], []
     for half in range(halves):
-        g1, grads_t = run_cross_temporal_backward(
-            g3, u1, kept_t, ctx, mods, masks, wide, w_tc, half, halves, grads_t
+        g1, *sums = run_cross_temporal_backward(
+            g3, u1, kept_t, mods, masks, wide, w_t, w_c, half, halves
         )
+        for kept, value in zip((gw, dk, dv), sums):
+            kept.append(value)
         g1_halves.append(exchange(g1.reshape(parts, frames, places // halves, d)))
-    x4, grad_b25, grad_down = run_feed_forward_out(active, x3, cot, mods, maps_f, w_f)
-    packed = run_pack_early([grads_t, grad_a24, grad_b25, grad_b24, grad_down], clips, parts)
+
+    def as_blocks(rows):
+        return rows.reshape(RANK, times, d).transpose(1, 0, 2).reshape(times * RANK, d)
+
+    sources = [grad_a24, as_blocks(grad_b24), kept_t[15], kept_t[16], ctx, masks, wide]
+    packed = run_pack_early(gw, dk, dv, sources, clips, parts)
+    active, packed = lax.optimization_barrier((active, packed))
+    x4, grad_b25, grad_down = run_feed_forward_out(active, x3, cot, mods, maps_f, down)
     early = reduce_grads(packed, all_index, adapters)
     output = exchange(x4.reshape(parts, frames, places, d))
     early, *g1_halves = lax.optimization_barrier((early, *g1_halves))
-    g0, packed = run_spatial_backward(g1_halves, frames_in, kept_s, mods, masks, wide, w_s, clips)
-    early = spread_grads(early)
-    late = spread_grads(reduce_grads(packed, all_index, adapters))
+    grads, packed = run_spatial_backward(
+        g1_halves, frames_in, kept_s, mods, masks, wide, w_s, grad_b25, as_blocks(grad_down), clips
+    )
+    early = exchange(early)
+    g0 = run_spatial_input_grad(g1_halves, frames_in, grads, mods, wide, w_s)
+    late = reduce_grads(packed, all_index, adapters)
+    late, early, output = lax.optimization_barrier((late, early, output))
+    wide_out, narrow_out = run_assemble(
+        early, exchange(late), adapt_wide.shape[1:], adapt_ff.shape[1:]
+    )
     output = output.transpose(1, 0, 2, 3).reshape(video.shape)
-    wide_out = jnp.concatenate([late, early[:18]], 0)
-    times = adapt_ff.shape[-1] // adapt_wide.shape[-1]
-    narrow_out = early[18 : 18 + 2 * times].reshape(2, times, adapters, RANK, -1)
-    narrow_out = jnp.moveaxis(narrow_out, 1, 3).reshape(2, adapters, RANK, -1)
     return (output, g0.reshape(video.shape), wide_out[None], narrow_out[None])
 
 

time: 797 us -> 810 us (1.016)
  blocking collectives: 72.6 us -> 109 us
  other arithmetic: 21.8 us -> 5.07 us
  local copies, waits for them, and re-layouts: 53.5 us -> 44.5 us
    all_to_all x8, waiting for transfers between devices: 194 us -> 258 us  [exchange(): return lax.all_to_all(array, axes, split_axis=0, concat_axis=0, tiled=True)]
    all_gather x3 -> x5, waiting for transfers between devices: 63.3 us -> 0.08 us  [gather(): return lax.all_gather(array, 'fsdp', axis=1, tiled=True)]
    pallas_call x3 -> x8, Pallas kernels: 118 us -> 160 us  [the longest x2 84.1 us: run_cross_temporal_backward(): pl.pallas_call(cross_temporal_backward, grid=(groups,), in_specs=[across,...]
    all_to_all x3 -> x4, blocking collectives: 72.6 us -> 109 us  [exchange(): return lax.all_to_all(array, axes, split_axis=0, concat_axis=0, tiled=True)]
    pallas_call x1, Pallas kernels: 69.8 us -> 43 us  [run_feed_forward(): pl.pallas_call(feed_forward, grid=(tokens // ROWS,), in_specs=[rows, rows...]
    pallas_call x1, Pallas kernels: 49.3 us -> 34.4 us  [run_spatial_backward(): pl.pallas_call(body, grid=(frames,), in_specs=[pl.BlockSpec((parts, 1, g....]
    reduce_sum x1 -> x0, other arithmetic: 10.1 us -> none  [fetch_adapters(): jnp.sum(choice[:, None, :, None, None] * table[None].astype(F32), axis=2)]
  transfers between devices with their start and end apart: 11 -> 14, of which waited for: 8 -> 7; matrix products, arithmetic and copies ran while one was open for 7% -> 5% of each run, Pallas kernels for 21% -> 20%
where the time goes in v3:
time: 810 us; the launch traced here: 800 us
  Pallas kernels  334 us (41%)
  waiting for transfers between devices  259 us (32%)
  blocking collectives  109 us (13%)
  local copies, waits for them, and re-layouts  44.5 us (5%)
  starting transfers between devices  34.7 us (4%)
  between operations  15 us (2%)
    all_to_all x8, waiting for transfers between devices, exchange(): return lax.all_to_all(array, axes, split_axis=0, concat_axis=0, tiled=True)  258 us
    all_to_all x4, blocking collectives, exchange(): return lax.all_to_all(array, axes, split_axis=0, concat_axis=0, tiled=True)  109 us
    pallas_call x2, Pallas kernels, run_cross_temporal_backward(): pl.pallas_call(cross_temporal_backward, grid=(groups,), in_specs=[across,...  84.1 us
    pallas_call x1, Pallas kernels, run_temporal_cross_forward(): pl.pallas_call(temporal_cross_forward, grid=(groups,), in_specs=[across,...  50.6 us
    pallas_call x1, Pallas kernels, run_feed_forward(): pl.pallas_call(feed_forward, grid=(tokens // ROWS,), in_specs=[rows, rows...  43 us
    all_to_all x8, starting transfers between devices, exchange(): return lax.all_to_all(array, axes, split_axis=0, concat_axis=0, tiled=True)  34.5 us
    pallas_call x1, Pallas kernels, run_spatial_backward(): pl.pallas_call(body, grid=(frames,), in_specs=[pl.BlockSpec((parts, 1, g....  34.4 us
    pallas_call x1, Pallas kernels, run_spatial_forward(): pl.pallas_call(spatial_forward, grid=(frames,), in_specs=[row_block, whol...  31.2 us
  transfers between devices with their start and end apart: 14, of which 7 were waited for; matrix products, arithmetic and copies ran while one was open for 5% of the time, Pallas kernels for 20%

profile of v3, /device:TPU:0, one launch (start us, length us, event | category | flops | bytes accessed | tf_op | source)
XLA Modules:
  0.0 800.5 jit_solution(16538586365153332089)
XLA Ops:
  17.2 9.6 %all_to_all.63 = s32[8,1,1]{2,1,0:T(1,128)S(1)} all-to-all(s32[8,1,1]{2,1,0:T(1,128)S(1)} %broadcast_in_dim.27), channel_id=1, replica_groups=mesh['seq'=4,'fsdp'=8] {'fsdp'}, dimensions={0} | all-to-all | bytes 64 | tf_op jit(solution)/shard_map/all_to_all | solution.py:1140
  27.6 3.6 pick.1
  31.2 5.2 reshape_squeeze.7
  39.8 4.7 reshape.68
  44.5 3.6 all-to-all-start.1
  49.5 24.8 %all-to-all-done.1.refs_0_ = bf16[8,624,128]{2,1,0:T(8,128)(2,1)S(1)} async-done(((bf16[8,624,128]{2,1,0:T(8,128)(2,1)}), bf16[8,624,128]{2,1,0:T(8,128)(2,1)S(1)}, u32[]{:S(2)}, u32[]{:S(2)}) %all-to-all-start.1) | async-done | bytes 1277984 | tf_op jit(solution)/shard_map/all_to_all | solution.py:1140
  77.2 5.2 all-to-all-start.4
  85.8 110.2 %all-to-all-done.4.mine_hbm = bf16[4,576,1152]{2,1,0:T(8,128)(2,1)} async-done(((bf16[4,576,1152]{2,1,0:T(8,128)(2,1)}), bf16[4,576,1152]{2,1,0:T(8,128)(2,1)}, u32[]{:S(2)}, u32[]{:S(2)}) %all-to-all-start.4) | async-done | bytes 5308448 | tf_op jit(solution)/shard_map/all_to_all | solution.py:1140
  196.0 4.6 all-to-all-start.3
  205.0 31.2 %spatial_forward.1 = (bf16[4,4,64,1152]{3,2,1,0:T(8,128)(2,1)}, bf16[4,256,1152]{2,1,0:T(8,128)(2,1)}, bf16[4,256,1152]{2,1,0:T(8,128)(2,1)}, bf16[4,256,1152]{2...) custom-call(bf16[4,256,1152]{2,1,0:T(8,128)(2,1)} %bitcast.87, ...), custom_call_target="tpu_custom_call" | custom-call | flops 13589544960 | bytes 30000000 | tf_op jit(solution)/shard_map/spatial_forward/pallas_call | solution.py:786
  236.2 17.6 %all-to-all-done.3 = bf16[4,4,64,1152]{3,2,1,0:T(8,128)(2,1)} async-done(((bf16[4,4,64,1152]{3,2,1,0:T(8,128)(2,1)}), bf16[4,4,64,1152]{3,2,1,0:T(8,128)(2,1)}, u32[]{:S(2)}, u32[]{:S(2)}) %all-to-all-start.3) | async-done | bytes 2359328 | tf_op jit(solution)/shard_map/all_to_all | solution.py:1140
  253.8 4.9 all-to-all-start.2
  261.2 20.8 %feed_forward_grad.1.grad_ref = bf16[1024,4608]{1,0:T(8,128)(2,1)} custom-call(s32[1]{0:T(128)} %bitcast.16.core_ref, bf16[1024,1152]{1,0:T(8,128)(2,1)} %bitcast.15.cot_ref, f32[6,1152]{1,0:T(8,128)} %bitcast.73, bf16[10,16,1152]{2,1,0:T(8,128)(2,1)} %slice.28.ad_ref, bf16[4,576,1152]{2,1,0:T(8,128)(2,1)} %all-to-all-done.4.mine_hbm, ...), custom_call_target="tpu_custom_call" | custom-call | flops 10871635968 | bytes 30000000 | tf_op jit(solution)/shard_map/feed_forward_grad/pallas_call | solution.py:858
  282.1 30.0 %all-to-all-done.2 = bf16[4,4,64,1152]{3,2,1,0:T(8,128)(2,1)} async-done(((bf16[4,4,64,1152]{3,2,1,0:T(8,128)(2,1)}), bf16[4,4,64,1152]{3,2,1,0:T(8,128)(2,1)}, u32[]{:S(2)}, u32[]{:S(2)}) %all-to-all-start.2) | async-done | bytes 2359328 | tf_op jit(solution)/shard_map/all_to_all | solution.py:1140
  312.1 50.6 %temporal_cross_forward.1 = (bf16[16,64,1152]{2,1,0:T(8,128)(2,1)}, bf16[16,64,1152]{2,1,0:T(8,128)(2,1)}, bf16[16,64,1152]{2,1,0:T(8,128)(2,1)}, bf16[16,64,115...) custom-call(bf16[16,64,1152]{2,1,0:T(8,128)(2,1)} %bitcast.6.x_ref.u, ...), custom_call_target="tpu_custom_call" | custom-call | flops 19025362944 | bytes 50000000 | tf_op jit(solution)/shard_map/temporal_cross_forward/pallas_call | solution.py:830
  362.7 43.0 %feed_forward.1 = (bf16[1024,4608]{1,0:T(8,128)(2,1)}, f32[1024,1152]{1,0:T(8,128)}, f32[16,1152]{1,0:T(8,128)}, f32[16,4608]{1,0:T(8,128)}) custom-call(f32[1024,1152]{1,0:T(8,128)} %bitcast.91, bf16[1024,1152]{1,0:T(8,128)(2,1)} %bitcast.15.cot_ref, bf16[1024,4608]{1,0:T(8,128)(2,1)} %feed_forward_grad.1.grad_ref, f32[6,1152]{1,0:T(8,128)} %bitcast.75, ...), custom_call_target="tpu_custom_call" | custom-call | flops 21743271936 | bytes 50000000 | tf_op jit(solution)/shard_map/feed_forward/pallas_call | solution.py:880
  407.4 42.2 %cross_temporal_backward.3 = (bf16[16,32,1152]{2,1,0:T(8,128)(2,1)}, f32[256,1152]{1,0:T(8,128)}, f32[8,256,256]{2,1,0:T(8,128)}, f32[8,256,256]{2,1,0:T(8,128)}) custom-call(f32[16,64,1152]{2,1,0:T(8,128)} %bitcast.61, bf16[16,64,1152]{2,1,0:T(8,128)(2,1)} %bitcast.6.x_ref.u1_ref, bf16[16,64,1152]{2,1,0:T(8,128)(2,1)} %get-tuple-element.63.q_ref, ...), custom_call_target="tpu_custom_call" | custom-call | flops 9512681472 | bytes 30000000 | tf_op jit(solution)/shard_map/cross_temporal_backward/pallas_call | solution.py:957
  449.6 41.8 %cross_temporal_backward.2 = (bf16[16,32,1152]{2,1,0:T(8,128)(2,1)}, f32[256,1152]{1,0:T(8,128)}, f32[8,256,256]{2,1,0:T(8,128)}, f32[8,256,256]{2,1,0:T(8,128)}) custom-call(f32[16,64,1152]{2,1,0:T(8,128)} %bitcast.62, bf16[16,64,1152]{2,1,0:T(8,128)(2,1)} %bitcast.6.x_ref.u1_ref, bf16[16,64,1152]{2,1,0:T(8,128)(2,1)} %get-tuple-element.63.q_ref, ...), custom_call_target="tpu_custom_call" | custom-call | flops 9512681472 | bytes 30000000 | tf_op jit(solution)/shard_map/cross_temporal_backward/pallas_call | solution.py:957
  491.5 9.6 %pack_early.1 = bf16[32,96,144]{2,1,0:T(8,128)(2,1)} custom-call(f32[256,1152]{1,0:T(8,128)} %get-tuple-element.78.refs_0_, f32[256,1152]{1,0:T(8,128)} %get-tuple-element.79.refs_1_, f32[8,256,256]{2,1,0:T(8,128)} %get-tuple-element.80.refs_2_, f32[8,256,256]{2,1,0:T(8,128)} %get-tuple-element.81.refs_3_, f32[8,256,256]{2,1,0:T(8,128)} %get-tuple-element.82.refs_4_, ...), custom_call_target="tpu_custom_call" | custom-call | tf_op jit(solution)/shard_map/pack_early/pallas_call | solution.py:1073
  503.1 33.7 %all_to_all.64 = bf16[32,96,144]{1,2,0:T(8,128)(2,1)S(1)} all-to-all(bf16[32,96,144]{1,2,0:T(8,128)(2,1)S(1)} %copy.33), channel_id=1, replica_groups=mesh['seq'=4,'fsdp'=8] {'fsdp','seq'}, dimensions={0} | all-to-all | bytes 1769472 | tf_op jit(solution)/shard_map/all_to_all | solution.py:1140
  536.7 32.5 %all_to_all.65.refs_1_ = bf16[4,4,32,1152]{3,2,1,0:T(8,128)(2,1)} all-to-all(bf16[4,4,32,1152]{3,2,1,0:T(8,128)(2,1)S(1)} %bitcast.70), channel_id=1, replica_groups=mesh['seq'=4,'fsdp'=8] {'seq'}, dimensions={0} | all-to-all | bytes 2359296 | tf_op jit(solution)/shard_map/all_to_all | solution.py:1140
  569.2 3.5 all-to-all-start.6
  572.7 25.0 %feed_forward_out.1 = (bf16[1024,1152]{1,0:T(8,128)(2,1)}, f32[16,1152]{1,0:T(8,128)}, f32[16,4608]{1,0:T(8,128)}) custom-call(s32[1]{0:T(128)} %bitcast.16.core_ref, bf16[1024,4608]{1,0:T(8,128)(2,1)} %get-tuple-element.100.act_ref, f32[1024,1152]{1,0:T(8,128)} %bitcast.92, bf16[1024,1152]{1,0:T(8,128)(2,1)} %bitcast.15.cot_ref, f32[6,1152]{1,0:T(8,128)} %bitcast.78, ...), custom_call_target="tpu_custom_call" | custom-call | flops 10871635968 | bytes 30000000 | tf_op jit(solution)/shard_map/feed_forward_out/pallas_call | solution.py:913
  605.2 34.4 %spatial_backward.1 = (bf16[4,256,3584]{2,1,0:T(8,128)(2,1)}, bf16[32,64,144]{2,1,0:T(8,128)(2,1)}) custom-call(bf16[4,4,32,1152]{3,2,1,0:T(8,128)(2,1)} %copy-done.6, bf16[4,4,32,1152]{3,2,1,0:T(8,128)(2,1)} %all_to_all.65.refs_1_, bf16[4,256,1152]{2,1,0:T(8,128)(2,1)} %bitcast.88, bf16[4,256,1152]{2,1,0:T(8,128)(2,1)} %get-tuple-element.93.refs_3_, ...), custom_call_target="tpu_custom_call" | custom-call | flops 8153726976 | bytes 30000000 | tf_op jit(solution)/shard_map/spatial_backward/pallas_call | solution.py:997
  639.7 4.4 all-to-all-start.8
  645.1 24.1 %all-to-all-done.8.got_ref = bf16[32,64,144]{2,1,0:T(8,128)(2,1)} async-done(((bf16[32,64,144]{2,1,0:T(8,128)(2,1)}), bf16[32,64,144]{2,1,0:T(8,128)(2,1)}, u32[]{:S(2)}, u32[]{:S(2)}) %all-to-all-start.8) | async-done | bytes 589856 | tf_op jit(solution)/shard_map/all_to_all | solution.py:1140
  669.1 32.9 %all_to_all.66 = bf16[4,8,96,144]{2,3,1,0:T(8,128)(2,1)S(1)} all-to-all(bf16[4,8,96,144]{2,3,1,0:T(8,128)(2,1)S(1)} %copy.36), channel_id=1, replica_groups=mesh['seq'=4,'fsdp'=8] {'seq'}, dimensions={0} | all-to-all | bytes 1769472 | tf_op jit(solution)/shard_map/all_to_all | solution.py:1140
  702.1 4.5 all-to-all-start.10
  709.1 50.9 %all-to-all-done.10 = bf16[4,4,64,1152]{3,2,1,0:T(8,128)(2,1)} async-done(((bf16[4,4,64,1152]{3,2,1,0:T(8,128)(2,1)}), bf16[4,4,64,1152]{3,2,1,0:T(8,128)(2,1)}, u32[]{:S(2)}, u32[]{:S(2)}) %all-to-all-start.10) | async-done | bytes 2359328 | tf_op jit(solution)/shard_map/all_to_all | solution.py:1140
  760.0 3.7 all-to-all-start.11
  763.7 19.3 %spatial_input_grad.1 = bf16[4,256,1152]{2,1,0:T(8,128)(2,1)} custom-call(bf16[4,4,32,1152]{3,2,1,0:T(8,128)(2,1)} %copy-done.6, bf16[4,4,32,1152]{3,2,1,0:T(8,128)(2,1)} %all_to_all.65.refs_1_, bf16[4,256,1152]{2,1,0:T(8,128)(2,1)} %bitcast.89, bf16[4,256,3584]{2,1,0:T(8,128)(2,1)} %get-tuple-element.107.refs_3_, f32[6,1152]{1,0:T(8,128)} %bitcast.80, ...), custom_call_target="tpu_custom_call" | custom-call | flops 8153726976 | bytes 20000000 | tf_op jit(solution)/shard_map/spatial_input_grad/pallas_call | solution.py:1037
  789.9 3.9 assemble.1
  (69 shorter events, 49.4 us)
Async XLA Ops:
  7.2 1.3 copy-start
  7.2 40.9 %all-gather.12.cloned.1.call-start = ((), (), s32[]{:S(2)}) async-start(), calls=%async_computation.15 | async-start | bytes 2985984 | tf_op jit(solution)/shard_map/all_gather | solution.py:1155
  9.3 195.7 %all-gather.6.cloned.1.call-start = ((), (), s32[]{:S(2)}) async-start(), calls=%async_computation.12 | async-start | bytes 11943936 | tf_op jit(solution)/shard_map/all_gather | solution.py:1155
  13.8 268.2 %all-gather.10.cloned.1.call-start = ((), (), s32[]{:S(2)}) async-start(), calls=%async_computation.14 | async-start | bytes 11943936 | tf_op jit(solution)/shard_map/all_gather | solution.py:1155
  15.1 266.9 %all-gather.8.cloned.1.call-start = ((), (), s32[]{:S(2)}) async-start(), calls=%async_computation.13 | async-start | bytes 11943936 | tf_op jit(solution)/shard_map/all_gather | solution.py:1155
  16.4 14.8 %copy-start.5 = (bf16[1,144,4608]{2,1,0:T(8,128)(2,1)S(1)}, bf16[1,144,4608]{2,1,0:T(8,128)(2,1)}, u32[]{:S(2)}) copy-start(bf16[1,144,4608]{2,1,0:T(8,128)(2,1)} %param.19) | copy-start | bytes 3981316
  16.4 346.2 %all-gather.14.cloned.1.call-start = ((), (), s32[]{:S(2)}) async-start(), calls=%async_computation.16 | async-start | bytes 11943936 | tf_op jit(solution)/shard_map/all_gather | solution.py:1155
  44.5 29.9 %all-to-all-start.1 = ((bf16[8,624,128]{2,1,0:T(8,128)(2,1)}), bf16[8,624,128]{2,1,0:T(8,128)(2,1)S(1)}, u32[]{:S(2)}, u32[]{:S(2)}) async-start(bf16[8,624,128]{2,1,0:T(8,128)(2,1)} %pick.1), calls=%async_computation.1 | async-start | bytes 2555904 | tf_op jit(solution)/shard_map/all_to_all | solution.py:1140
  74.3 2.8 copy-start.3
  77.2 118.8 %all-to-all-start.4 = ((bf16[4,576,1152]{2,1,0:T(8,128)(2,1)}), bf16[4,576,1152]{2,1,0:T(8,128)(2,1)}, u32[]{:S(2)}, u32[]{:S(2)}) async-start(bf16[4,576,1152]{2,1,0:T(8,128)(2,1)} %broadcast_in_dim.30), calls=%async_computation.4 | async-start | bytes 10616832 | tf_op jit(solution)/shard_map/all_to_all | solution.py:1140
  196.0 4.7 copy-start.9
  196.0 5.3 copy-start.10
  196.0 5.3 copy-start.11
  196.0 57.8 %all-to-all-start.3 = ((bf16[4,4,64,1152]{3,2,1,0:T(8,128)(2,1)}), bf16[4,4,64,1152]{3,2,1,0:T(8,128)(2,1)}, u32[]{:S(2)}, u32[]{:S(2)}) async-start(bf16[4,4,64,1152]{3,2,1,0:T(8,128)(2,1)} %bitcast.64), calls=%async_computation.3 | async-start | bytes 4718592 | tf_op jit(solution)/shard_map/all_to_all | solution.py:1140
  200.6 60.6 %collective-permute-start = (bf16[4,576,1152]{2,1,0:T(8,128)(2,1)}, bf16[4,576,1152]{2,1,0:T(8,128)(2,1)}, u32[]{:S(2)}, u32[]{:S(2)}) collective-permute-start(bf16[4,576,1152]{2,1,0:T(8,128)(2,1)} %all-to-all-done.4.mine_hbm), channel_id=1, source_target_pairs={{0,1},{1,0},{2,3},{3,2},{4,5},{5,4},{6,7},{7,6},{8,9},{9,8},{10,11... | collective-permute-start | bytes 15925256 | tf_op jit(solution)/shard_map/ppermute | solution.py:1168
  253.8 4.9 copy-start.8
  253.8 58.2 %all-to-all-start.2 = ((bf16[4,4,64,1152]{3,2,1,0:T(8,128)(2,1)}), bf16[4,4,64,1152]{3,2,1,0:T(8,128)(2,1)}, u32[]{:S(2)}, u32[]{:S(2)}) async-start(bf16[4,4,64,1152]{3,2,1,0:T(8,128)(2,1)} %get-tuple-element.58), calls=%async_computation.2 | async-start | bytes 4718592 | tf_op jit(solution)/shard_map/all_to_all | solution.py:1140
  503.0 33.7 %copy-start.7 = (bf16[16,32,1152]{2,1,0:T(8,128)(2,1)S(1)}, bf16[16,32,1152]{2,1,0:T(8,128)(2,1)}, u32[]{:S(2)}) copy-start(bf16[16,32,1152]{2,1,0:T(8,128)(2,1)} %get-tuple-element.90) | copy-start | bytes 3538948
  569.2 34.9 %all-to-all-start.6 = ((bf16[4,4,32,1152]{3,2,1,0:T(8,128)(2,1)}), bf16[4,4,32,1152]{3,2,1,0:T(8,128)(2,1)S(1)}, u32[]{:S(2)}, u32[]{:S(2)}) async-start(bf16[4,4,32,1152]{3,2,1,0:T(8,128)(2,1)} %bitcast.69), calls=%async_computation.6 | async-start | bytes 2359296 | tf_op jit(solution)/shard_map/all_to_all | solution.py:1140
  604.1 1.1 copy-start.6
  639.6 4.5 copy-start.2
  639.7 29.5 %all-to-all-start.8 = ((bf16[32,64,144]{2,1,0:T(8,128)(2,1)}), bf16[32,64,144]{2,1,0:T(8,128)(2,1)}, u32[]{:S(2)}, u32[]{:S(2)}) async-start(bf16[32,64,144]{2,1,0:T(8,128)(2,1)} %get-tuple-element.103), calls=%async_computation.8 | async-start | bytes 2097152 | tf_op jit(solution)/shard_map/all_to_all | solution.py:1140
  702.1 57.9 %all-to-all-start.10 = ((bf16[4,4,64,1152]{3,2,1,0:T(8,128)(2,1)}), bf16[4,4,64,1152]{3,2,1,0:T(8,128)(2,1)}, u32[]{:S(2)}, u32[]{:S(2)}) async-start(bf16[4,4,64,1152]{3,2,1,0:T(8,128)(2,1)} %bitcast.66), calls=%async_computation.10 | async-start | bytes 4718592 | tf_op jit(solution)/shard_map/all_to_all | solution.py:1140
  760.0 28.9 %all-to-all-start.11 = ((bf16[4,8,64,144]{3,2,1,0:T(8,128)(2,1)}), bf16[4,8,64,144]{3,2,1,0:T(8,128)(2,1)S(1)}, u32[]{:S(2)}, u32[]{:S(2)}) async-start(bf16[4,8,64,144]{3,2,1,0:T(8,128)(2,1)} %combine.3), calls=%async_computation.11 | async-start | bytes 2097152 | tf_op jit(solution)/shard_map/all_to_all | solution.py:1140
  783.0 10.7 %copy-start.1 = (bf16[1,576,1152]{2,1,0:T(8,128)(2,1)S(1)}, bf16[1,576,1152]{2,1,0:T(8,128)(2,1)}, u32[]{:S(2)}) copy-start(bf16[1,576,1152]{2,1,0:T(8,128)(2,1)} %param.20) | copy-start | bytes 3981316
  788.9 1.0 copy-start.4
Sparse Core Ops, SparseCore 0:
  10.5 32.9 all-gather.11
  46.0 71.7 all-gather.5
  119.6 63.7 all-gather.9
  185.2 63.7 all-gather.7
  250.8 63.7 all-gather.13

commit v4 on v3

--- a/solution.py
+++ b/solution.py
@@ -208,10 +208,13 @@
     return both[:, :width] + nn(grad_ranks, three_downs(ad_ref, number))
 
 
-def spatial_forward(
-    x_ref, mod_ref, mask_ref, ad_ref, w_hbm, x1_ref, q_ref, k_ref, v_ref, o_ref, stat_ref, rq_ref, ro_ref,
-    w_ref, lhs_ref, sems,
-):
+def place_of(seq_ref, k, parts, places):
+    return pl.multiple_of(lax.rem(seq_ref[0] + k, parts) * places, 16)
+
+
+def spatial_forward(seq_ref, x_ref, mod_ref, mask_ref, ad_ref, w_hbm, *refs):
+    x1_refs = refs[:-11]
+    q_ref, k_ref, v_ref, o_ref, stat_ref, rq_ref, ro_ref, w_ref, lhs_ref, x1_s, sems = refs[-11:]
     width = x_ref.shape[2]
     loads = Loads([(w_hbm.at[i], w_ref.at[i, pl.ds(0, width), :]) for i in range(4)], sems)
     loads.start()
@@ -236,17 +239,28 @@
     attend(q, k, v, mask_ref, None, put_out, stat_ref.at[0])
     loads.ready(3)
     branch = one_projection(lhs_ref, ad_ref, 3, w_ref.at[3], ro_ref.at[0])
-    result = (stream + mod_ref[2:3, :] * branch).astype(BF16)
-    x1_ref[...] = result.reshape(x1_ref.shape)
-
-
-def temporal_cross_forward(
-    x_ref, ctx_ref, mod_ref, mask_ref, ad_ref, wt_hbm, wc_hbm,
+    x1_s[...] = (stream + mod_ref[2:3, :] * branch).astype(BF16)
+    places = x1_refs[0].shape[1]
+    for k, ref in enumerate(x1_refs):
+        ref[0] = x1_s[pl.ds(place_of(seq_ref, k, len(x1_refs), places), places), :]
+
+
+def rows_of(refs):
+    pieces = [ref[...].reshape(-1, ref.shape[2]) for ref in refs]
+    return pieces[0] if len(pieces) == 1 else jnp.concatenate(pieces, 0)
+
+
+def temporal_cross_forward(parts, *refs):
+    _temporal_cross_forward(refs[:parts], *refs[parts:])
+
+
+def _temporal_cross_forward(
+    x_refs, ctx_ref, mod_ref, mask_ref, ad_ref, wt_hbm, wc_hbm,
     q_ref, k_ref, v_ref, o_ref, stat_ref, rq_ref, ro_ref,
     u2_ref, qc_ref, oc_ref, statc_ref, rqc_ref, roc_ref, kp_ref, vp_ref, rk_ref, rv_ref, x3_ref,
     w_ref, bias_ref, lhs_ref, q_s, k_s, v_s, o_s, sems,
 ):
-    width = x_ref.shape[2]
+    width = x_refs[0].shape[2]
     first = pl.program_id(0) == 0
     sources = [wt_hbm.at[i] for i in range(4)] + [wc_hbm.at[i] for i in range(4)]
     loads = Loads([(w, w_ref.at[i, pl.ds(0, width), :]) for i, w in enumerate(sources)], sems)
@@ -259,7 +273,7 @@
         for i in range(8):
             w_ref[i, width:, :] = up_rows(ad_ref, 4 + i, i if i < 3 else 0, width)
 
-    loaded = x_ref[...].reshape(ROWS, width)
+    loaded = rows_of(x_refs)
     stream = loaded.astype(F32)
     lhs_ref[:, :width] = loaded
     three_projections(lhs_ref, ad_ref, 4, w_ref, loads, 0, (q_s, k_s, v_s), rq_ref.at[0])
@@ -339,13 +353,15 @@
     return wide.T.astype(BF16)
 
 
-def down_loads(core_ref, mine_hbm, other_hbm, down_ref, width):
+def down_loads(order_ref, pieces, down_ref, width):
     half = width // 2
+    count = len(pieces) // 2
+    core = order_ref[count]
     entries = []
-    for c in range(down_ref.shape[0] // width):
-        for source, core in ((mine_hbm, core_ref[0]), (other_hbm, 1 - core_ref[0])):
-            start = pl.multiple_of(c * width + core * half, 16)
-            entries.append((source.at[c], down_ref.at[pl.ds(start, half), pl.ds(0, width)]))
+    for k in range(count):
+        for source, side in ((pieces[k], core), (pieces[count + k], 1 - core)):
+            start = pl.multiple_of(order_ref[k] * width + side * half, 16)
+            entries.append((source, down_ref.at[pl.ds(start, half), pl.ds(0, width)]))
     return entries
 
 
@@ -356,11 +372,11 @@
         down_ref[rows, width:] = transposed_map(ad_ref[2 + chunks + c])
 
 
-def feed_forward_grad(
-    core_ref, cot_ref, mod_ref, ad_ref, mine_hbm, other_hbm, grad_ref, down_ref, lhs_ref, sems
-):
+def feed_forward_grad(count, order_ref, cot_ref, mod_ref, ad_ref, *refs):
+    pieces = refs[:count]
+    grad_ref, down_ref, lhs_ref, sems = refs[count:]
     width = cot_ref.shape[1]
-    entries = down_loads(core_ref, mine_hbm, other_hbm, down_ref, width)
+    entries = down_loads(order_ref, pieces, down_ref, width)
     loads = Loads(entries, sems)
     loads.start()
 
@@ -427,12 +443,13 @@
     g3_ref[...] = cot_ref[...].astype(F32) + grad_in
 
 
-def feed_forward_out(
-    core_ref, act_ref, x3_ref, cot_ref, mod_ref, ad_ref, mine_hbm, other_hbm,
-    x4_ref, gu_ref, gd_ref, down_ref, sems,
-):
+def feed_forward_out(count, order_ref, act_ref, x3_ref, cot_ref, mod_ref, ad_ref, *refs):
+    pieces, refs = refs[:count], refs[count:]
+    x4_refs = refs[:-4]
+    gu_ref, gd_ref, down_ref, sems = refs[-4:]
     width = x3_ref.shape[1]
-    entries = down_loads(core_ref, mine_hbm, other_hbm, down_ref, width)
+    step = pl.program_id(0)
+    entries = down_loads(order_ref, pieces, down_ref, width)
     loads = Loads(entries, sems)
     loads.start()
 
@@ -450,16 +467,28 @@
     ranks = both[:, width : width + RANK].astype(BF16)
     branch = both[:, :width] + nn(ranks, ad_ref[1])
     gu_ref[...] += tn(ranks, grad_branch)
-    x4_ref[...] = (x3_ref[...] + mod_ref[5:6, :] * branch).astype(BF16)
-
-
-def cross_temporal_backward(
-    g3_ref, u1_ref, q_ref, k_ref, v_ref, o_ref, stat_ref, rq_ref, ro_ref,
+    result = (x3_ref[...] + mod_ref[5:6, :] * branch).astype(BF16)
+    share = x4_refs[0].shape[0]
+    for k, ref in enumerate(x4_refs):
+        at = k * share
+
+        @pl.when(step == at // ROWS)
+        def _():
+            ref[...] = result[at % ROWS : at % ROWS + share]
+
+
+def cross_temporal_backward(parts, *refs):
+    outs = len(refs) - parts - 13
+    _cross_temporal_backward(refs[:parts], refs[outs : outs + parts], *refs[parts:outs], *refs[outs + parts :])
+
+
+def _cross_temporal_backward(
+    u1_refs, g1_refs, g3_ref, q_ref, k_ref, v_ref, o_ref, stat_ref, rq_ref, ro_ref,
     u2_ref, qc_ref, oc_ref, statc_ref, rqc_ref, roc_ref, kp_ref, vp_ref,
     mod_ref, mask_ref, ad_ref, wt_hbm, wc_hbm,
-    g1_ref, gw_ref, dk_acc, dv_acc, w_ref, bias_ref, q_s, k_s, v_s, do_s, dq_s, dk_s, dv_s, sems,
+    gw_ref, dk_acc, dv_acc, w_ref, bias_ref, q_s, k_s, v_s, do_s, dq_s, dk_s, dv_s, sems,
 ):
-    width = u1_ref.shape[2]
+    width = u1_refs[0].shape[2]
     first = pl.program_id(0) == 0
     order = (7, 4, 3, 0, 1, 2)
     sources = [wc_hbm.at[n - 4] if n >= 4 else wt_hbm.at[n] for n in order]
@@ -529,28 +558,74 @@
 
     attend_back(q_s, k_s, v_s, do_s, mask_ref, bias_ref, stat_ref.at[0], put)
     grad = grad + three_back(
-        (dq_s, dk_s, dv_s), rows(u1_ref), rq_ref[0], ad_ref, 4, w_ref, loads, 3, gw_ref, 0
+        (dq_s, dk_s, dv_s), rows_of(u1_refs), rq_ref[0], ad_ref, 4, w_ref, loads, 3, gw_ref, 0
     )
-    g1_ref[...] = grad.astype(BF16).reshape(g1_ref.shape)
+    grad = grad.astype(BF16)
+    share = ROWS // len(g1_refs)
+    for k, ref in enumerate(g1_refs):
+        ref[...] = grad[share * k : share * (k + 1)].reshape(ref.shape)
+
+
+def tail_groups(cols):
+    tail = cols - PAD
+    return PAD // tail if 0 < tail < PAD and PAD % tail == 0 else 0
+
+
+def packed_rows(blocks, cols):
+    group = tail_groups(cols)
+    if not group:
+        return blocks * RANK, cols
+    return (blocks + -(-blocks // group)) * RANK, PAD
+
+
+def put_blocks(blocks, put):
+    cols = blocks[0].shape[1]
+    group = tail_groups(cols)
+    for k, rows in enumerate(blocks):
+        put(k, rows[:, :PAD] if group else rows)
+    for k in range(0, len(blocks), group) if group else ():
+        tails = [rows[:, PAD:] for rows in blocks[k : k + group]]
+        missing = group - len(tails)
+        if missing:
+            tails.append(jnp.zeros((RANK, missing * (cols - PAD)), blocks[0].dtype))
+        put(len(blocks) + k // group, jnp.concatenate(tails, 1))
+
+
+def get_block(get, index, count, cols):
+    group = tail_groups(cols)
+    if not group:
+        return get(index)
+    at = (index % group) * (cols - PAD)
+    return jnp.concatenate([get(index), get(count + index // group)[:, at : at + cols - PAD]], 1)
 
 
 def pack_columns(table_ref, packed_ref, clips):
     parts = packed_ref.shape[0] // clips
-    _, share, cols = packed_ref.shape
+    share = table_ref.shape[0] // parts
+    cols = table_ref.shape[1] // clips
     for f in range(clips):
         for s in range(parts):
-            piece = table_ref[share * s : share * (s + 1), cols * f : cols * (f + 1)]
-            packed_ref[f * parts + s] = piece.astype(BF16)
-
-
-def stacked(g1_refs):
-    parts = g1_refs[0].shape[0]
-    pieces = [ref[s, 0] for s in range(parts) for ref in g1_refs]
-    return jnp.concatenate(pieces, 0).astype(F32)
-
-
-def spatial_backward(halves, clips, *refs):
-    g1_refs, refs = refs[:halves], refs[halves:]
+            piece = table_ref[share * s : share * (s + 1), cols * f : cols * (f + 1)].astype(BF16)
+            blocks = [piece[block_rows(k)] for k in range(share // RANK)]
+
+            def put(k, rows):
+                packed_ref[f * parts + s, block_rows(k), :] = rows
+
+            put_blocks(blocks, put)
+
+
+def stacked(seq_ref, g1_refs, halves, whole_ref):
+    parts = len(g1_refs) // halves
+    part = g1_refs[0].shape[1]
+    for half in range(halves):
+        for k in range(parts):
+            start = place_of(seq_ref, k, parts, part * halves) + half * part
+            whole_ref[pl.ds(pl.multiple_of(start, 16), part), :] = g1_refs[half * parts + k][0]
+    return whole_ref[...].astype(F32)
+
+
+def spatial_backward(pieces, halves, clips, seq_ref, *refs):
+    g1_refs, refs = refs[:pieces], refs[pieces:]
     (
         x_ref, q_ref, k_ref, v_ref, o_ref, stat_ref, rq_ref, ro_ref, mod_ref, mask_ref, ad_ref, w_hbm,
         down_ref, up_ref, d_ref, packed_ref, w_ref, gw_ref, do_s, sems,
@@ -564,7 +639,7 @@
         gw_ref[...] = jnp.zeros_like(gw_ref)
         w_ref[width:, :] = up_rows(ad_ref, 3, 0, width)
 
-    grad = stacked(g1_refs)
+    grad = stacked(seq_ref, g1_refs, halves, do_s)
     loads.ready(0)
     do_s[...] = one_back(
         (mod_ref[2:3, :] * grad).astype(BF16), o_ref[0], ro_ref[0], ad_ref, 3, w_ref, gw_ref, 6
@@ -600,9 +675,9 @@
         pack_columns(gw_ref, packed_ref, clips)
 
 
-def spatial_input_grad(halves, *refs):
-    g1_refs, refs = refs[:halves], refs[halves:]
-    x_ref, d_ref, mod_ref, ad_ref, w_hbm, g0_ref, w_ref, sems = refs
+def spatial_input_grad(pieces, halves, seq_ref, *refs):
+    g1_refs, refs = refs[:pieces], refs[pieces:]
+    x_ref, d_ref, mod_ref, ad_ref, w_hbm, g0_ref, w_ref, whole_s, sems = refs
     width = x_ref.shape[2]
     loads = Loads(
         [(w_hbm.at[i], w_ref.at[:, pl.ds(i * width, width)]) for i in range(3)], sems
@@ -614,12 +689,19 @@
         w_ref[:, 3 * width :] = transposed_map(three_downs(ad_ref, 0))
 
     normal, inverse = normalize(x_ref[0].astype(F32))
-    grad = stacked(g1_refs)
+    grad = stacked(seq_ref, g1_refs, halves, whole_s)
     for i in range(3):
         loads.ready(i)
     grad_in = nt(d_ref[0], w_ref[...])
     grad = grad + normalize_back(normal, inverse, grad_in * (1.0 + mod_ref[1:2, :]))
     g0_ref[0] = grad.astype(BF16)
+
+
+def put_in_place(seq_ref, *refs):
+    *pieces, out_ref = refs
+    places = pieces[0].shape[1]
+    for k, ref in enumerate(pieces):
+        out_ref[0, pl.ds(place_of(seq_ref, k, len(pieces), places), places), :] = ref[0]
 
 
 def pack_early(clips, halves, *refs):
@@ -672,21 +754,29 @@
 
 
 def assemble(early_ref, late_ref, wide_ref, narrow_ref):
-    adapters = wide_ref.shape[1]
-    times = narrow_ref.shape[3] // wide_ref.shape[3]
-
-    def block(ref, index, a):
-        each = ref.shape[2] // RANK
-        return ref[index // each, a, block_rows(index % each), :].astype(F32)
+    _, adapters, _, cols = wide_ref.shape
+    times = narrow_ref.shape[3] // cols
+
+    def block(ref, total, index, a):
+        each = total // ref.shape[0]
+
+        def get(k):
+            return ref[index // each, a, block_rows(k), :].astype(F32)
+
+        return get_block(get, index % each, each, cols)
 
     for a in range(adapters):
         for i in range(8):
-            wide_ref[i, a] = block(late_ref, i, a)
+            wide_ref[i, a] = block(late_ref, LATE_BLOCKS, i, a)
         for i in range(17):
-            wide_ref[8 + i, a] = block(early_ref, i, a)
-        wide_ref[25, a] = block(late_ref, 8, a)
-        for n, (ref, at) in enumerate(((early_ref, 17), (late_ref, 9))):
-            narrow_ref[n, a] = jnp.concatenate([block(ref, at + j, a) for j in range(times)], 1)
+            wide_ref[8 + i, a] = block(early_ref, EARLY_BLOCKS, i, a)
+        wide_ref[25, a] = block(late_ref, LATE_BLOCKS, 8, a)
+        narrow_ref[0, a] = jnp.concatenate(
+            [block(early_ref, EARLY_BLOCKS, 17 + j, a) for j in range(times)], 1
+        )
+        narrow_ref[1, a] = jnp.concatenate(
+            [block(late_ref, LATE_BLOCKS, 9 + j, a) for j in range(times)], 1
+        )
 
 
 def combine(index_ref, got_ref, out_ref, acc_ref):
@@ -707,17 +797,9 @@
         out_ref[s] = table
 
 
-def tail_groups(cols):
-    tail = cols - PAD
-    return PAD // tail if 0 < tail < PAD and PAD % tail == 0 else 0
-
-
 def pick(index_ref, wide_ref, narrow_ref, out_ref):
-    clips = index_ref.shape[0]
     count, _, _, cols = wide_ref.shape
     times = narrow_ref.shape[3] // cols
-    group = tail_groups(cols)
-    total = count + 2 * times
 
     def step(f, carry):
         a = index_ref[f]
@@ -725,34 +807,25 @@
         for p in range(2):
             rows = narrow_ref[p, a]
             blocks += [rows[:, cols * j : cols * (j + 1)] for j in range(times)]
-        if not group:
-            for k, rows in enumerate(blocks):
-                out_ref[f, block_rows(k), :] = rows
-            return carry
-        for k, rows in enumerate(blocks):
-            out_ref[f, block_rows(k), :] = rows[:, :PAD]
-        for k in range(0, total, group):
-            tails = [rows[:, PAD:] for rows in blocks[k : k + group]]
-            missing = group - len(tails)
-            if missing:
-                tails.append(jnp.zeros((RANK, missing * (cols - PAD)), BF16))
-            out_ref[f, block_rows(total + k // group), :] = jnp.concatenate(tails, 1)
+
+        def put(k, rows):
+            out_ref[f, block_rows(k), :] = rows
+
+        put_blocks(blocks, put)
         return carry
 
-    lax.fori_loop(0, clips, step, 0)
+    lax.fori_loop(0, index_ref.shape[0], step, 0)
 
 
 def unpick(count, cols, got_ref, out_ref):
-    clips = got_ref.shape[0]
-    group = tail_groups(cols)
     for k in range(count):
         pieces = []
-        for f in range(clips):
-            pieces.append(got_ref[f, block_rows(k), :])
-            if group:
-                at = (k % group) * (cols - PAD)
-                tails = got_ref[f, block_rows(count + k // group), :]
-                pieces.append(tails[:, at : at + cols - PAD])
+        for f in range(got_ref.shape[0]):
+
+            def get(index):
+                return got_ref[f, block_rows(index), :]
+
+            pieces.append(get_block(get, k, count, cols))
         out_ref[k] = jnp.concatenate(pieces, 1)
 
 
@@ -778,7 +851,7 @@
     return pl.CostEstimate(flops=flops, bytes_accessed=read, transcendentals=flops // 4096)
 
 
-def run_spatial_forward(video, mods, masks, wide, w_s, parts):
+def run_spatial_forward(seq, video, mods, masks, wide, w_s, parts):
     frames, rows, d = video.shape
     places = rows // parts
     by_frame = lambda i: (i, 0, 0)
@@ -786,9 +859,9 @@
     return pl.pallas_call(
         spatial_forward,
         grid=(frames,),
-        in_specs=[row_block, whole_block(mods), whole_block(masks), whole_block(wide), anywhere()],
-        out_specs=[
-            pl.BlockSpec((parts, 1, places, d), lambda i: (0, i, 0, 0)),
+        in_specs=[in_smem(), row_block, whole_block(mods), whole_block(masks), whole_block(wide), anywhere()],
+        out_specs=[pl.BlockSpec((1, places, d), by_frame)] * parts
+        + [
             row_block,
             row_block,
             row_block,
@@ -797,7 +870,7 @@
             pl.BlockSpec((1, rows, 3 * RANK), by_frame),
             pl.BlockSpec((1, rows, RANK), by_frame),
         ],
-        out_shape=[like((parts, frames, places, d), BF16)]
+        out_shape=[like((frames, places, d), BF16)] * parts
         + [like(video.shape, BF16)] * 4
         + [
             like((frames, HEADS, rows), F32),
@@ -807,36 +880,45 @@
         scratch_shapes=[
             pltpu.VMEM((4, d + PAD, d), BF16),
             pltpu.VMEM((ROWS, d + PAD), BF16),
+            pltpu.VMEM((ROWS, d), BF16),
             pltpu.SemaphoreType.DMA((4,)),
         ],
         compiler_params=PARAMS,
         cost_estimate=cost(10 * frames * rows * d * d, 30_000_000),
         name="spatial_forward",
-    )(video, mods, masks, wide, w_s)
+    )(seq, video, mods, masks, wide, w_s)
 
 
 def run_temporal_cross_forward(x1, context, mods, masks, wide, w_t, w_c):
-    frames, places, d = x1.shape
+    parts = len(x1)
+    own_frames, places, d = x1[0].shape
+    frames = own_frames * parts
     groups = places * frames // ROWS
-    across = pl.BlockSpec((frames, ROWS // frames, d), lambda i: (0, i, 0))
+    each = ROWS // frames
+    across = pl.BlockSpec((frames, each, d), lambda i: (0, i, 0))
     by_group = lambda i: (i, 0, 0)
     stat = pl.BlockSpec((1, HEADS, ROWS), by_group)
     three = pl.BlockSpec((1, ROWS, 3 * RANK), by_group)
     one = pl.BlockSpec((1, ROWS, RANK), by_group)
     full = lambda *shape: pl.BlockSpec(shape, lambda i: (0,) * len(shape))
-    act = like(x1.shape, BF16)
+    act = like((frames, places, d), BF16)
+
+    def body(*refs):
+        temporal_cross_forward(parts, *refs)
+
     stat_shape = like((groups, HEADS, ROWS), F32)
     one_shape = like((groups, ROWS, RANK), BF16)
     return pl.pallas_call(
-        temporal_cross_forward,
+        body,
         grid=(groups,),
-        in_specs=[across, whole_block(context), whole_block(mods), whole_block(masks), whole_block(wide), anywhere(), anywhere()],
+        in_specs=[pl.BlockSpec((own_frames, each, d), lambda i: (0, i, 0))] * parts
+        + [whole_block(context), whole_block(mods), whole_block(masks), whole_block(wide), anywhere(), anywhere()],
         out_specs=[across] * 4 + [stat, three, one] + [across] * 3 + [stat, one, one]
         + [full(PAIRS, 2 * PAD, 256)] * 2 + [full(PAD, RANK)] * 2 + [across],
         out_shape=[act] * 4 + [stat_shape, like((groups, ROWS, 3 * RANK), BF16), one_shape]
         + [act] * 3 + [stat_shape, one_shape, one_shape]
         + [like((PAIRS, 2 * PAD, 256), BF16)] * 2 + [like((PAD, RANK), BF16)] * 2
-        + [like(x1.shape, F32)],
+        + [like((frames, places, d), F32)],
         scratch_shapes=[pltpu.VMEM((8, d + PAD, d), BF16), pltpu.VMEM((ROWS, ROWS), F32)]
         + [pltpu.VMEM((ROWS, d + PAD), BF16)]
         + [pltpu.VMEM((ROWS, d), BF16)] * 4
@@ -844,7 +926,7 @@
         compiler_params=PARAMS,
         cost_estimate=cost(14 * places * frames * d * d, 50_000_000),
         name="temporal_cross_forward",
-    )(x1, context, mods, masks, wide, w_t, w_c)
+    )(*x1, context, mods, masks, wide, w_t, w_c)
 
 
 def in_smem():
@@ -853,23 +935,28 @@
 
 def run_feed_forward_grad(cot, mods, maps, down):
     tokens, d = cot.shape
-    core, mine, other = down
-    hidden = mine.shape[0] * d
+    order, *pieces = down
+    hidden = len(pieces) // 2 * d
+
+    def body(*refs):
+        feed_forward_grad(len(pieces), *refs)
+
     return pl.pallas_call(
-        feed_forward_grad,
+        body,
         grid=(tokens // ROWS,),
-        in_specs=[in_smem(), pl.BlockSpec((ROWS, d), lambda i: (i, 0)), whole_block(mods), whole_block(maps), anywhere(), anywhere()],
+        in_specs=[in_smem(), pl.BlockSpec((ROWS, d), lambda i: (i, 0)), whole_block(mods), whole_block(maps)]
+        + [anywhere()] * len(pieces),
         out_specs=pl.BlockSpec((ROWS, hidden), lambda i: (i, 0)),
         out_shape=like((tokens, hidden), BF16),
         scratch_shapes=[
             pltpu.VMEM((hidden, d + PAD), BF16),
             pltpu.VMEM((ROWS, d + PAD), BF16),
-            pltpu.SemaphoreType.DMA((2 * mine.shape[0],)),
+            pltpu.SemaphoreType.DMA((len(pieces),)),
         ],
         compiler_params=PARAMS,
         cost_estimate=cost(2 * tokens * d * hidden, 30_000_000),
         name="feed_forward_grad",
-    )(core, cot, mods, maps, mine, other)
+    )(order, cot, mods, maps, *pieces)
 
 
 def run_feed_forward(x3, cot, grad_active, mods, maps, up):
@@ -905,13 +992,18 @@
     )(x3, cot, grad_active, mods, maps, up)
 
 
-def run_feed_forward_out(active, x3, cot, mods, maps, down):
+def run_feed_forward_out(active, x3, cot, mods, maps, down, parts):
     tokens, d = x3.shape
-    core, mine, other = down
+    order, *pieces = down
     hidden = active.shape[1]
+    share = tokens // parts
+
+    def body(*refs):
+        feed_forward_out(len(pieces), *refs)
+
     rows = pl.BlockSpec((ROWS, d), lambda i: (i, 0))
     return pl.pallas_call(
-        feed_forward_out,
+        body,
         grid=(tokens // ROWS,),
         in_specs=[
             in_smem(),
@@ -920,31 +1012,33 @@
             rows,
             whole_block(mods),
             whole_block(maps),
-            anywhere(),
-            anywhere(),
-        ],
-        out_specs=[
-            rows,
+        ]
+        + [anywhere()] * len(pieces),
+        out_specs=[pl.BlockSpec((share, d), lambda i: (0, 0))] * parts
+        + [
             pl.BlockSpec((RANK, d), lambda i: (0, 0)),
             pl.BlockSpec((RANK, hidden), lambda i: (0, 0)),
         ],
-        out_shape=[
-            like((tokens, d), BF16),
+        out_shape=[like((share, d), BF16)] * parts
+        + [
             like((RANK, d), F32),
             like((RANK, hidden), F32),
         ],
         scratch_shapes=[
             pltpu.VMEM((hidden, d + PAD), BF16),
-            pltpu.SemaphoreType.DMA((2 * mine.shape[0],)),
+            pltpu.SemaphoreType.DMA((len(pieces),)),
         ],
         compiler_params=PARAMS,
         cost_estimate=cost(2 * tokens * d * hidden, 30_000_000),
         name="feed_forward_out",
-    )(core, active, x3, cot, mods, maps, mine, other)
+    )(order, active, x3, cot, mods, maps, *pieces)
 
 
 def run_cross_temporal_backward(g3, u1, saved, mods, masks, wide, w_t, w_c, half, halves):
-    frames, places, d = u1.shape
+    parts = len(u1)
+    own_frames, places, d = u1[0].shape
+    frames = own_frames * parts
+    each = ROWS // frames
     groups = places * frames // ROWS // halves
     start = half * groups
     across = pl.BlockSpec((frames, ROWS // frames, d), lambda i: (0, i + start, 0))
@@ -954,19 +1048,25 @@
     one = pl.BlockSpec((1, ROWS, RANK), by_group)
     kp, vp = saved[13:15]
     pair_sums = pl.BlockSpec((PAIRS, 2 * PAD, 256), lambda i: (0, 0, 0))
+
+    def body(*refs):
+        cross_temporal_backward(parts, *refs)
+
     return pl.pallas_call(
-        cross_temporal_backward,
+        body,
         grid=(groups,),
-        in_specs=[across, across] + [across] * 4 + [stat, three, one] + [across] * 3 + [stat, one, one]
+        in_specs=[pl.BlockSpec((own_frames, each, d), lambda i: (0, i + start, 0))] * parts
+        + [across] + [across] * 4 + [stat, three, one] + [across] * 3 + [stat, one, one]
         + [whole_block(kp), whole_block(vp)]
         + [whole_block(mods), whole_block(masks), whole_block(wide), anywhere(), anywhere()],
-        out_specs=[
-            pl.BlockSpec((frames, ROWS // frames, d), lambda i: (0, i, 0)),
+        out_specs=[pl.BlockSpec((own_frames, each, d), lambda i: (0, i, 0))] * parts
+        + [
             pl.BlockSpec((16 * RANK, d), lambda i: (0, 0)),
             pair_sums,
             pair_sums,
         ],
-        out_shape=[like((frames, places // halves, d), BF16), like((16 * RANK, d), F32)]
+        out_shape=[like((own_frames, places // halves, d), BF16)] * parts
+        + [like((16 * RANK, d), F32)]
         + [like((PAIRS, 2 * PAD, 256), F32)] * 2,
         scratch_shapes=[
             pltpu.VMEM((6, d + PAD, d), BF16),
@@ -977,29 +1077,27 @@
         compiler_params=PARAMS,
         cost_estimate=cost(14 * places // halves * frames * d * d, 30_000_000),
         name="cross_temporal_backward",
-    )(g3, u1, *saved[:15], mods, masks, wide, w_t, w_c)
+    )(*u1, g3, *saved[:15], mods, masks, wide, w_t, w_c)
 
 
 LATE_BLOCKS = 16
 EARLY_BLOCKS = 24
 
 
-def run_spatial_backward(g1_halves, video, saved, mods, masks, wide, w_s, late_down, late_up, clips):
+def run_spatial_backward(seq, g1, halves, video, saved, mods, masks, wide, w_s, late_down, late_up, clips):
     frames, rows, d = video.shape
-    parts = g1_halves[0].shape[0]
+    parts = len(g1) // halves
     by_frame = lambda i: (i, 0, 0)
     row_block = pl.BlockSpec((1, rows, d), by_frame)
-    packed = (clips * parts, LATE_BLOCKS * RANK // parts, d // clips)
+    packed = (clips * parts, *packed_rows(LATE_BLOCKS // parts, d // clips))
 
     def body(*refs):
-        spatial_backward(len(g1_halves), clips, *refs)
+        spatial_backward(len(g1), halves, clips, *refs)
 
     return pl.pallas_call(
         body,
         grid=(frames,),
-        in_specs=[
-            pl.BlockSpec((parts, 1, g.shape[2], d), lambda i: (0, i, 0, 0)) for g in g1_halves
-        ]
+        in_specs=[in_smem()] + [pl.BlockSpec((1, g.shape[1], d), by_frame) for g in g1]
         + [row_block] * 5
         + [
             pl.BlockSpec((1, HEADS, rows), by_frame),
@@ -1022,24 +1120,21 @@
         compiler_params=PARAMS,
         cost_estimate=cost(6 * frames * rows * d * d, 30_000_000),
         name="spatial_backward",
-    )(*g1_halves, video, *saved, mods, masks, wide, w_s, late_down, late_up)
-
-
-def run_spatial_input_grad(g1_halves, video, grads, mods, wide, w_s):
+    )(seq, *g1, video, *saved, mods, masks, wide, w_s, late_down, late_up)
+
+
+def run_spatial_input_grad(seq, g1, halves, video, grads, mods, wide, w_s):
     frames, rows, d = video.shape
-    parts = g1_halves[0].shape[0]
     by_frame = lambda i: (i, 0, 0)
     row_block = pl.BlockSpec((1, rows, d), by_frame)
 
     def body(*refs):
-        spatial_input_grad(len(g1_halves), *refs)
+        spatial_input_grad(len(g1), halves, *refs)
 
     return pl.pallas_call(
         body,
         grid=(frames,),
-        in_specs=[
-            pl.BlockSpec((parts, 1, g.shape[2], d), lambda i: (0, i, 0, 0)) for g in g1_halves
-        ]
+        in_specs=[in_smem()] + [pl.BlockSpec((1, g.shape[1], d), by_frame) for g in g1]
         + [
             row_block,
             pl.BlockSpec((1, rows, grads.shape[2]), by_frame),
@@ -1049,11 +1144,31 @@
         ],
         out_specs=row_block,
         out_shape=like(video.shape, BF16),
-        scratch_shapes=[pltpu.VMEM((d, 3 * d + PAD), BF16), pltpu.SemaphoreType.DMA((3,))],
+        scratch_shapes=[
+            pltpu.VMEM((d, 3 * d + PAD), BF16),
+            pltpu.VMEM((ROWS, d), BF16),
+            pltpu.SemaphoreType.DMA((3,)),
+        ],
         compiler_params=PARAMS,
         cost_estimate=cost(6 * frames * rows * d * d, 20_000_000),
         name="spatial_input_grad",
-    )(*g1_halves, video, grads, mods, wide, w_s)
+    )(seq, *g1, video, grads, mods, wide, w_s)
+
+
+def run_put_in_place(seq, pieces):
+    frames, places, d = pieces[0].shape
+    by_frame = lambda i: (i, 0, 0)
+    rows = places * len(pieces)
+    return pl.pallas_call(
+        put_in_place,
+        grid=(frames,),
+        in_specs=[in_smem()] + [pl.BlockSpec((1, places, d), by_frame)] * len(pieces),
+        out_specs=pl.BlockSpec((1, rows, d), by_frame),
+        out_shape=like((frames, rows, d), BF16),
+        compiler_params=PARAMS,
+        cost_estimate=cost(0, 4 * frames * rows * d),
+        name="put_in_place",
+    )(seq, *pieces)
 
 
 PLAIN = pltpu.CompilerParams(vmem_limit_bytes=VMEM_LIMIT)
@@ -1065,7 +1180,7 @@
 
 def run_pack_early(gw, dk, dv, sources, clips, parts):
     d = gw[0].shape[1]
-    packed = (clips * parts, EARLY_BLOCKS * RANK // parts, d // clips)
+    packed = (clips * parts, *packed_rows(EARLY_BLOCKS // parts, d // clips))
 
     def body(*refs):
         pack_early(clips, len(gw), *refs)
@@ -1075,6 +1190,7 @@
         out_shape=like(packed, BF16),
         scratch_shapes=[pltpu.VMEM((EARLY_BLOCKS * RANK, d), F32), pltpu.VMEM((PAD, d), F32)],
         compiler_params=PLAIN,
+        cost_estimate=cost(50000000, 8000000),
         name="pack_early",
     )(*gw, *dk, *dv, *sources)
 
@@ -1086,23 +1202,21 @@
         out_specs=[in_vmem()] * 2,
         out_shape=[like(wide_shape, F32), like(narrow_shape, F32)],
         compiler_params=PLAIN,
+        cost_estimate=cost(0, 6000000),
         name="assemble",
     )(early, late)
 
 
 def run_pick(all_index, wide, narrow):
     count, _, _, cols = wide.shape
-    blocks = count + 2 * (narrow.shape[3] // cols)
-    group = tail_groups(cols)
-    shape = (blocks * RANK, cols)
-    if group:
-        shape = ((blocks + -(-blocks // group)) * RANK, PAD)
+    shape = packed_rows(count + 2 * (narrow.shape[3] // cols), cols)
     return pl.pallas_call(
         pick,
         in_specs=[in_smem(), in_vmem(), in_vmem()],
         out_specs=in_vmem(),
         out_shape=like((all_index.shape[0], *shape), BF16),
         compiler_params=PLAIN,
+        cost_estimate=cost(0, 3000000),
         name="pick",
     )(all_index, wide, narrow)
 
@@ -1117,6 +1231,7 @@
         out_specs=in_vmem(),
         out_shape=like((blocks, RANK, got.shape[0] * cols), BF16),
         compiler_params=PLAIN,
+        cost_estimate=cost(0, 2500000),
         name="unpick",
     )(got)
 
@@ -1132,6 +1247,7 @@
         out_shape=like((parts, adapters, share, cols), BF16),
         scratch_shapes=[pltpu.VMEM((adapters, share, cols), F32)],
         compiler_params=pltpu.CompilerParams(vmem_limit_bytes=VMEM_LIMIT),
+        cost_estimate=cost(0, 1000000),
         name="combine",
     )(all_index, got)
 
@@ -1155,18 +1271,37 @@
     return lax.all_gather(array, "fsdp", axis=1, tiled=True)
 
 
-def fetch_down(down, clips, parts, times, d):
+def send(array, axis, shift):
+    size = lax.axis_size(axis)
+    return lax.ppermute(array, axis, [(i, (i + shift) % size) for i in range(size)])
+
+
+def to_places(pieces):
+    return [pieces[0]] + [send(pieces[k], "seq", k) for k in range(1, len(pieces))]
+
+
+def to_frames(pieces):
+    return [pieces[0]] + [send(pieces[k], "seq", -k) for k in range(1, len(pieces))]
+
+
+def fetch_spatial_and_down(spatial, down, clips, parts, times, d):
     quarters = down.reshape(times, -1, d)
     half = d // 2
     if times != parts or clips % 2:
         whole = gather(quarters)
-        return jnp.zeros((1,), jnp.int32), whole[:, :half], whole[:, half:]
-    own = gather(lax.dynamic_slice_in_dim(quarters, lax.axis_index("seq"), 1, 0))[0]
+        pieces = [whole[i, side * half : (side + 1) * half] for side in range(2) for i in range(times)]
+        return gather(spatial), [jnp.arange(times + 1, dtype=jnp.int32) % times, *pieces]
+    seq = lax.axis_index("seq")
     core = lax.axis_index("fsdp") % 2
-    piece = lax.dynamic_slice_in_dim(own, core * half, half, 0)
-    mine = exchange(jnp.broadcast_to(piece[None], (parts, half, d)))
-    other = lax.ppermute(mine, "fsdp", [(i, i ^ 1) for i in range(clips)])
-    return core.astype(jnp.int32)[None], mine, other
+    own = lax.dynamic_slice_in_dim(quarters, seq, 1, 0)
+    got = gather(jnp.concatenate([spatial, own], 0))
+    first = lax.dynamic_slice(got, (times, core * half, 0), (1, half, d))[0]
+    other = lax.dynamic_slice(got, (times, (1 - core) * half, 0), (1, half, d))[0]
+    mine = [first] + [send(first, "seq", k) for k in range(1, parts)]
+    swap = [(i, i ^ 1) for i in range(clips)]
+    others = [other] + [lax.ppermute(piece, "fsdp", swap) for piece in mine[1:]]
+    order = jnp.concatenate([(seq - jnp.arange(parts)) % parts, core[None]]).astype(jnp.int32)
+    return got, [order, *mine, *others]
 
 
 def on_device(
@@ -1194,26 +1329,32 @@
     ctx = jnp.pad(context[0], ((0, PAD - context.shape[1]), (0, 0)))
 
     def attention_weights(j):
-        return gather(
-            jnp.concatenate([qkv_weights[0, 3 * j : 3 * j + 3], out_weights[0, j : j + 1]], 0)
-        )
-
+        return jnp.concatenate([qkv_weights[0, 3 * j : 3 * j + 3], out_weights[0, j : j + 1]], 0)
+
+    seq = lax.axis_index("seq").astype(jnp.int32)[None]
     all_index = exchange(jnp.broadcast_to(adapter_index, (clips,)), "fsdp")
-    down = fetch_down(ffn_down[0], clips, parts, times, d)
-    w_s = attention_weights(0)
+    w_s, down = fetch_spatial_and_down(
+        attention_weights(0), ffn_down[0], clips, parts, times, d
+    )
     picked = run_pick(all_index, adapt_wide[0], adapt_ff[0])
     wide = run_unpick(exchange(picked, "fsdp"), count + 2 * times, cols)
-    w_t = attention_weights(1)
-    w_c = attention_weights(2)
+    w_t = gather(attention_weights(1))
+    w_c = gather(attention_weights(2))
     ffn_up, _ = lax.optimization_barrier((ffn_up, picked))
     up = gather(up_chunks(ffn_up[0], clips, times))
     maps_f = wide[24:]
 
-    cot = cotangent.reshape(frames, parts, places, d).transpose(1, 0, 2, 3)
-    cot = exchange(cot).reshape(FRAMES * places, d)
+    cot = cotangent.reshape(frames, SPATIAL, d)
+    cot = to_places(
+        [
+            lax.dynamic_slice_in_dim(cot, (seq[0] + k) % parts * places, places, 1)
+            for k in range(parts)
+        ]
+    )
+    cot = jnp.concatenate(cot, 0).reshape(FRAMES * places, d)
     frames_in = video.reshape(frames, SPATIAL, d)
-    x1, *kept_s = run_spatial_forward(frames_in, mods, masks, wide, w_s, parts)
-    u1 = exchange(x1).reshape(FRAMES, places, d)
+    made = run_spatial_forward(seq, frames_in, mods, masks, wide, w_s, parts)
+    u1, kept_s = to_places(made[:parts]), made[parts:]
     grad_active = run_feed_forward_grad(cot, mods, maps_f, down)
     *kept_t, x3 = run_temporal_cross_forward(u1, ctx, mods, masks, wide, w_t, w_c)
     x3 = x3.reshape(FRAMES * places, d)
@@ -1221,36 +1362,38 @@
     g3 = g3.reshape(FRAMES, places, d)
     groups = FRAMES * places // ROWS
     halves = 2 if groups % 2 == 0 else 1
-    g1_halves, gw, dk, dv = [], [], [], []
+    g1, gw, dk, dv = [], [], [], []
     for half in range(halves):
-        g1, *sums = run_cross_temporal_backward(
+        *pieces, gw_half, dk_half, dv_half = run_cross_temporal_backward(
             g3, u1, kept_t, mods, masks, wide, w_t, w_c, half, halves
         )
-        for kept, value in zip((gw, dk, dv), sums):
-            kept.append(value)
-        g1_halves.append(exchange(g1.reshape(parts, frames, places // halves, d)))
+        gw.append(gw_half)
+        dk.append(dk_half)
+        dv.append(dv_half)
+        g1.append(to_frames(pieces))
 
     def as_blocks(rows):
         return rows.reshape(RANK, times, d).transpose(1, 0, 2).reshape(times * RANK, d)
 
     sources = [grad_a24, as_blocks(grad_b24), kept_t[15], kept_t[16], ctx, masks, wide]
     packed = run_pack_early(gw, dk, dv, sources, clips, parts)
-    active, packed = lax.optimization_barrier((active, packed))
-    x4, grad_b25, grad_down = run_feed_forward_out(active, x3, cot, mods, maps_f, down)
+    active, packed, *g1[0] = lax.optimization_barrier((active, packed, *g1[0]))
+    *x4, grad_b25, grad_down = run_feed_forward_out(active, x3, cot, mods, maps_f, down, parts)
     early = reduce_grads(packed, all_index, adapters)
-    output = exchange(x4.reshape(parts, frames, places, d))
-    early, *g1_halves = lax.optimization_barrier((early, *g1_halves))
+    output = to_frames([piece.reshape(frames, places, d) for piece in x4])
+    g1 = [piece for pieces in g1 for piece in pieces]
+    early, *g1 = lax.optimization_barrier((early, *g1))
     grads, packed = run_spatial_backward(
-        g1_halves, frames_in, kept_s, mods, masks, wide, w_s, grad_b25, as_blocks(grad_down), clips
+        seq, g1, halves, frames_in, kept_s, mods, masks, wide, w_s, grad_b25, as_blocks(grad_down), clips
     )
     early = exchange(early)
-    g0 = run_spatial_input_grad(g1_halves, frames_in, grads, mods, wide, w_s)
+    packed, early, *output = lax.optimization_barrier((packed, early, *output))
+    g0 = run_spatial_input_grad(seq, g1, halves, frames_in, grads, mods, wide, w_s)
     late = reduce_grads(packed, all_index, adapters)
-    late, early, output = lax.optimization_barrier((late, early, output))
     wide_out, narrow_out = run_assemble(
         early, exchange(late), adapt_wide.shape[1:], adapt_ff.shape[1:]
     )
-    output = output.transpose(1, 0, 2, 3).reshape(video.shape)
+    output = run_put_in_place(seq, output).reshape(video.shape)
     return (output, g0.reshape(video.shape), wide_out[None], narrow_out[None])
 
 

time: 810 us -> 716 us (0.88)
  blocking collectives: 109 us -> 31.6 us
  waiting for transfers between devices: 259 us -> 202 us
  starting transfers between devices: 34.7 us -> 72.6 us
  local copies, waits for them, and re-layouts: 44.5 us -> 31.9 us
    all_to_all x8 -> x4, waiting for transfers between devices: 258 us -> 36.8 us  [exchange(): return lax.all_to_all(array, axes, split_axis=0, concat_axis=0, tiled=True)]
    ppermute x1 -> x21, waiting for transfers between devices: 0.01 us -> 144 us  [the longest x18 144 us: send(): lax.ppermute(array, axis, [(i, (i + shift) % size) for i in range(size)])]
    all_to_all x4 -> x2, blocking collectives: 109 us -> 31.6 us  [exchange(): return lax.all_to_all(array, axes, split_axis=0, concat_axis=0, tiled=True)]
    ppermute x1 -> x21, starting transfers between devices: 0.07 us -> 57.7 us  [the longest x18 57.2 us: send(): lax.ppermute(array, axis, [(i, (i + shift) % size) for i in range(size)])]
    all_gather x5 -> x4, waiting for transfers between devices: 0.08 us -> 22 us  [gather(): return lax.all_gather(array, 'fsdp', axis=1, tiled=True)]
    all_to_all x8 -> x4, starting transfers between devices: 34.5 us -> 14.7 us  [exchange(): return lax.all_to_all(array, axes, split_axis=0, concat_axis=0, tiled=True)]
    pallas_call x8 -> x9, Pallas kernels: 265 us -> 273 us  [the longest x2 84.3 us: run_cross_temporal_backward(): pl.pallas_call(body, grid=(groups,), in_specs=[pl.BlockSpec((own_frames,...]
  transfers between devices with their start and end apart: 14 -> 29, of which waited for: 7 -> 9; matrix products, arithmetic and copies ran while one was open for 5% -> 4% of each run, Pallas kernels for 20% -> 35%
where the time goes in v4:
time: 716 us; the launch traced here: 706 us
  Pallas kernels  342 us (48%)
  waiting for transfers between devices  202 us (28%)
  starting transfers between devices  72.6 us (10%)
  local copies, waits for them, and re-layouts  31.9 us (4%)
  blocking collectives  31.6 us (4%)
  between operations  15.2 us (2%)
  other arithmetic  10.8 us (2%)
    ppermute x18, waiting for transfers between devices, send(): lax.ppermute(array, axis, [(i, (i + shift) % size) for i in range(size)])  144 us
    pallas_call x2, Pallas kernels, run_cross_temporal_backward(): pl.pallas_call(body, grid=(groups,), in_specs=[pl.BlockSpec((own_frames,...  84.3 us
    ppermute x18, starting transfers between devices, send(): lax.ppermute(array, axis, [(i, (i + shift) % size) for i in range(size)])  57.2 us
    pallas_call x1, Pallas kernels, run_temporal_cross_forward(): pl.pallas_call(body, grid=(groups,), in_specs=[pl.BlockSpec((own_frames,...  50.9 us
    pallas_call x1, Pallas kernels, run_feed_forward(): pl.pallas_call(feed_forward, grid=(tokens // ROWS,), in_specs=[rows, rows...  42.5 us
    all_to_all x4, waiting for transfers between devices, exchange(): return lax.all_to_all(array, axes, split_axis=0, concat_axis=0, tiled=True)  36.8 us
    pallas_call x1, Pallas kernels, run_spatial_backward(): pl.pallas_call(body, grid=(frames,), in_specs=[in_smem()] + [pl.BlockSpec...  34.9 us
    all_to_all x2, blocking collectives, exchange(): return lax.all_to_all(array, axes, split_axis=0, concat_axis=0, tiled=True)  31.6 us
  transfers between devices with their start and end apart: 29, of which 9 were waited for; matrix products, arithmetic and copies ran while one was open for 4% of the time, Pallas kernels for 35%

profile of v4, /device:TPU:0, one launch (start us, length us, event | category | flops | bytes accessed | tf_op | source)
XLA Modules:
  0.0 706.4 jit_solution(10393177856584100789)
XLA Ops:
  19.4 9.6 %all_to_all.33 = s32[8,1,1]{2,1,0:T(1,128)S(1)} all-to-all(s32[8,1,1]{2,1,0:T(1,128)S(1)} %broadcast_in_dim.23), channel_id=1, replica_groups=mesh['seq'=4,'fsdp'=8] {'fsdp'}, dimensions={0} | all-to-all | bytes 64 | tf_op jit(solution)/shard_map/all_to_all | solution.py:1256
  33.4 5.2 reshape_squeeze.7
  43.5 3.6 all-to-all-start.1
  50.1 3.6 collective-permute-start.5
  55.0 19.2 %all-to-all-done.1.refs_0_ = bf16[8,624,128]{2,1,0:T(8,128)(2,1)S(1)} async-done(((bf16[8,624,128]{2,1,0:T(8,128)(2,1)}), bf16[8,624,128]{2,1,0:T(8,128)(2,1)S(1)}, u32[]{:S(2)}, u32[]{:S(2)}) %all-to-all-start.1) | async-done | bytes 1277984 | tf_op jit(solution)/shard_map/all_to_all | solution.py:1256
  75.2 4.7 unpick.1.ad_ref.refs_7_.refs_22_.refs_12_.refs_19_
  79.9 22.0 %all-gather.5.cloned.1.call-done.w_hbm.refs_20_.refs_13_ = bf16[5,1152,1152]{2,1,0:T(8,128)(2,1)} async-done(((bf16[5,144,1152]{2,1,0:T(8,128)(2,1)}), bf16[5,1152,1152]{2,1,0:T(8,128)(2,1)}) %all-gather.5.cloned.1.call-update) | async-done | bytes 13271056 | tf_op jit(solution)/shard_map/all_gather | solution.py:1271
  105.3 3.6 collective-permute-start.8
  110.0 31.3 %spatial_forward.1 = (bf16[4,64,1152]{2,1,0:T(8,128)(2,1)}, bf16[4,64,1152]{2,1,0:T(8,128)(2,1)}, bf16[4,64,1152]{2,1,0:T(8,128)(2,1)}, bf16[4,64,1152]{2,1,0:T(...) custom-call(s32[1]{0:T(128)} %bitcast.seq_ref.refs_0_, ...), custom_call_target="tpu_custom_call" | custom-call | flops 13589544960 | bytes 30000000 | tf_op jit(solution)/shard_map/spatial_forward/pallas_call | solution.py:859
  145.0 64.2 %collective-permute-done.3 = bf16[4,64,1152]{2,1,0:T(8,128)(2,1)S(1)} collective-permute-done((bf16[4,64,1152]{2,1,0:T(8,128)(2,1)S(1)}, bf16[4,64,1152]{2,1,0:T(8,128)(2,1)S(1)}, u32[]{:S(2)}, u32[]{:S(2)}) %collective-permute-start.3) | collective-permute-done | bytes 589856 | tf_op jit(solution)/shard_map/ppermute | solution.py:1276
  209.2 30.3 %collective-permute-start.1 = (bf16[4,64,1152]{2,1,0:T(8,128)(2,1)}, bf16[4,64,1152]{2,1,0:T(8,128)(2,1)S(1)}, u32[]{:S(2)}, u32[]{:S(2)}) collective-permute-start(bf16[4,64,1152]{2,1,0:T(8,128)(2,1)} %get-tuple-element.85), channel_id=1, source_target_pairs={{0,16},{8,24},{16,0},{24,8},{1,17},{9,25},{17,1},{25,9},{2,18},{10... | collective-permute-start | bytes 1769480 | tf_op jit(solution)/shard_map/ppermute | solution.py:1276
  245.3 16.6 %collective-permute-done.7.refs_6_.refs_8_ = bf16[576,1152]{1,0:T(8,128)(2,1)} collective-permute-done((bf16[576,1152]{1,0:T(8,128)(2,1)}, bf16[576,1152]{1,0:T(8,128)(2,1)}, u32[]{:S(2)}, u32[]{:S(2)}) %collective-permute-start.7) | collective-permute-done | bytes 1327136 | tf_op jit(solution)/shard_map/ppermute | solution.py:1276
  262.4 11.4 %collective-permute-done.1.refs_2_ = bf16[4,64,1152]{2,1,0:T(8,128)(2,1)S(1)} collective-permute-done((bf16[4,64,1152]{2,1,0:T(8,128)(2,1)}, bf16[4,64,1152]{2,1,0:T(8,128)(2,1)S(1)}, u32[]{:S(2)}, u32[]{:S(2)}) %collective-permute-start.1) | collective-permute-done | bytes 589856 | tf_op jit(solution)/shard_map/ppermute | solution.py:1276
  273.7 14.0 %collective-permute-done.2.refs_3_ = bf16[4,64,1152]{2,1,0:T(8,128)(2,1)S(1)} collective-permute-done((bf16[4,64,1152]{2,1,0:T(8,128)(2,1)}, bf16[4,64,1152]{2,1,0:T(8,128)(2,1)S(1)}, u32[]{:S(2)}, u32[]{:S(2)}) %collective-permute-start.2) | collective-permute-done | bytes 589856 | tf_op jit(solution)/shard_map/ppermute | solution.py:1276
  288.6 50.9 %temporal_cross_forward.1 = (bf16[16,64,1152]{2,1,0:T(8,128)(2,1)}, bf16[16,64,1152]{2,1,0:T(8,128)(2,1)}, bf16[16,64,1152]{2,1,0:T(8,128)(2,1)}, bf16[16,64,115...) custom-call(bf16[4,64,1152]{2,1,0:T(8,128)(2,1)} %get-tuple-element., ...), custom_call_target="tpu_custom_call" | custom-call | flops 19025362944 | bytes 50000000 | tf_op jit(solution)/shard_map/temporal_cross_forward/pallas_call | solution.py:911
  339.6 21.3 %feed_forward_grad.1.grad_ref = bf16[1024,4608]{1,0:T(8,128)(2,1)} custom-call(s32[5]{0:T(128)} %pad_add_fusion.refs_0_, bf16[1024,1152]{1,0:T(8,128)(2,1)} %bitcast.64, f32[6,1152]{1,0:T(8,128)} %bitcast.73, bf16[10,16,1152]{2,1,0:T(8,128)(2,1)} %slice.28.refs_3_.ad_ref.refs_5_, bf16[576,1152]{1,0:T(8,128)(2,1)} %get-tuple-element.163.refs_4_.refs_6_, ...), custom_call_target="tpu_custom_call" | custom-call | flops 10871635968 | bytes 30000000 | tf_op jit(solution)/shard_map/feed_forward_grad/pallas_call | solution.py:944
  360.9 42.5 %feed_forward.1 = (bf16[1024,4608]{1,0:T(8,128)(2,1)}, f32[1024,1152]{1,0:T(8,128)}, f32[16,1152]{1,0:T(8,128)}, f32[16,4608]{1,0:T(8,128)}) custom-call(f32[1024,1152]{1,0:T(8,128)} %bitcast.93, bf16[1024,1152]{1,0:T(8,128)(2,1)} %bitcast.65, bf16[1024,4608]{1,0:T(8,128)(2,1)} %feed_forward_grad.1.grad_ref, f32[6,1152]{1,0:T(8,128)} %bitcast.74, ...), custom_call_target="tpu_custom_call" | custom-call | flops 21743271936 | bytes 50000000 | tf_op jit(solution)/shard_map/feed_forward/pallas_call | solution.py:967
  403.4 42.0 %cross_temporal_backward.2 = (bf16[4,32,1152]{2,1,0:T(8,128)(2,1)}, bf16[4,32,1152]{2,1,0:T(8,128)(2,1)}, bf16[4,32,1152]{2,1,0:T(8,128)(2,1)}, bf16[4,32,1152]{...) custom-call(bf16[4,64,1152]{2,1,0:T(8,128)(2,1)} %get-tuple-element.83.refs_0_, ...), custom_call_target="tpu_custom_call" | custom-call | flops 9512681472 | bytes 30000000 | tf_op jit(solution)/shard_map/cross_temporal_backward/pallas_call | solution.py:1055
  451.0 42.3 %cross_temporal_backward.3 = (bf16[4,32,1152]{2,1,0:T(8,128)(2,1)}, bf16[4,32,1152]{2,1,0:T(8,128)(2,1)}, bf16[4,32,1152]{2,1,0:T(8,128)(2,1)}, bf16[4,32,1152]{...) custom-call(bf16[4,64,1152]{2,1,0:T(8,128)(2,1)} %get-tuple-element.83.refs_0_, ...), custom_call_target="tpu_custom_call" | custom-call | flops 9512681472 | bytes 30000000 | tf_op jit(solution)/shard_map/cross_temporal_backward/pallas_call | solution.py:1055
  494.1 9.5 %pack_early.1 = bf16[32,112,128]{2,1,0:T(8,128)(2,1)} custom-call(f32[256,1152]{1,0:T(8,128)} %get-tuple-element.106.refs_0_, f32[256,1152]{1,0:T(8,128)} %get-tuple-element.107.refs_1_, f32[8,256,256]{2,1,0:T(8,128)} %get-tuple-element.108.refs_2_, f32[8,256,256]{2,1,0:T(8,128)} %get-tuple-element.109.refs_3_, f32[8,256,256]{2,1,0:T(8,128)} %get-tuple-element.110.refs_4_, ...), custom_call_target="tpu_custom_call" | custom-call | flops 50000000 | bytes 8000000 | tf_op jit(solution)/shard_map/pack_early/pallas_call | solution.py:1188
  506.9 3.7 collective-permute-start.15
  511.7 17.6 %all-to-all-done.2.got_ref = bf16[32,112,128]{2,1,0:T(8,128)(2,1)S(1)} async-done(((bf16[32,112,128]{2,1,0:T(8,128)(2,1)}), bf16[32,112,128]{2,1,0:T(8,128)(2,1)S(1)}, u32[]{:S(2)}, u32[]{:S(2)}) %all-to-all-start.2) | async-done | bytes 917536 | tf_op jit(solution)/shard_map/all_to_all | solution.py:1256
  532.6 23.1 %collective-permute-done.16.refs_7_ = bf16[4,32,1152]{2,1,0:T(8,128)(2,1)S(1)} collective-permute-done((bf16[4,32,1152]{2,1,0:T(8,128)(2,1)S(1)}, bf16[4,32,1152]{2,1,0:T(8,128)(2,1)S(1)}, u32[]{:S(2)}, u32[]{:S(2)}) %collective-permute-start.16) | collective-permute-done | bytes 294944 | tf_op jit(solution)/shard_map/ppermute | solution.py:1276
  560.0 26.3 %feed_forward_out.1 = (bf16[256,1152]{1,0:T(8,128)(2,1)}, bf16[256,1152]{1,0:T(8,128)(2,1)}, bf16[256,1152]{1,0:T(8,128)(2,1)}, bf16[256,1152]{1,0:T(8,128)(2,1)...) custom-call(s32[5]{0:T(128)} %pad_add_fusion.refs_0_, bf16[1024,4608]{1,0:T(8,128)(2,1)} %get-tuple-element.144.refs_1_, ...), custom_call_target="tpu_custom_call" | custom-call | flops 10871635968 | bytes 30000000 | tf_op jit(solution)/shard_map/feed_forward_out/pallas_call | solution.py:1005
  588.0 3.8 collective-permute-start.18
  592.8 34.9 %spatial_backward.1 = (bf16[4,256,3584]{2,1,0:T(8,128)(2,1)}, bf16[32,80,128]{2,1,0:T(8,128)(2,1)}) custom-call(s32[1]{0:T(128)} %bitcast.seq_ref.refs_0_, bf16[4,32,1152]{2,1,0:T(8,128)(2,1)} %get-tuple-element.129.refs_1_, bf16[4,32,1152]{2,1,0:T(8,128)(2,1)} %copy-done.21, bf16[4,32,1152]{2,1,0:T(8,128)(2,1)} %collective-permute-done.13.refs_3_, ...), custom_call_target="tpu_custom_call" | custom-call | flops 8153726976 | bytes 30000000 | tf_op jit(solution)/shard_map/spatial_backward/pallas_call | solution.py:1097
  627.8 14.3 %collective-permute-done.19.refs_2_ = bf16[4,64,1152]{2,1,0:T(8,128)(2,1)S(1)} collective-permute-done((bf16[4,64,1152]{2,1,0:T(8,128)(2,1)}, bf16[4,64,1152]{2,1,0:T(8,128)(2,1)S(1)}, u32[]{:S(2)}, u32[]{:S(2)}) %collective-permute-start.19) | collective-permute-done | bytes 589856 | tf_op jit(solution)/shard_map/ppermute | solution.py:1276
  642.1 22.0 %all_to_all.34.got_ref = bf16[32,80,128]{2,1,0:T(8,128)(2,1)} all-to-all(bf16[32,80,128]{2,1,0:T(8,128)(2,1)} %get-tuple-element.159), channel_id=1, replica_groups=mesh['seq'=4,'fsdp'=8] {'fsdp','seq'}, dimensions={0} | all-to-all | bytes 1310720 | tf_op jit(solution)/shard_map/all_to_all | solution.py:1256
  666.2 4.3 all-to-all-start.5
  670.5 19.7 %spatial_input_grad.1 = bf16[4,256,1152]{2,1,0:T(8,128)(2,1)} custom-call(s32[1]{0:T(128)} %bitcast.seq_ref.refs_0_, bf16[4,32,1152]{2,1,0:T(8,128)(2,1)} %get-tuple-element.129.refs_1_, bf16[4,32,1152]{2,1,0:T(8,128)(2,1)} %copy-done.21, bf16[4,32,1152]{2,1,0:T(8,128)(2,1)} %collective-permute-done.13.refs_3_, ...), custom_call_target="tpu_custom_call" | custom-call | flops 8153726976 | bytes 20000000 | tf_op jit(solution)/shard_map/spatial_input_grad/pallas_call | solution.py:1134
  690.3 4.0 put_in_place.1
  695.1 4.5 assemble.1
  (126 shorter events, 65.4 us)
Async XLA Ops:
  7.2 94.6 %all-gather.5.cloned.1.call-start = ((), (), s32[]{:S(2)}) async-start(), calls=%async_computation.6 | async-start | bytes 14929920 | tf_op jit(solution)/shard_map/all_gather | solution.py:1271
  15.0 247.4 %all-gather.9.cloned.1.call-start = ((), (), s32[]{:S(2)}) async-start(), calls=%async_computation.8 | async-start | bytes 11943936 | tf_op jit(solution)/shard_map/all_gather | solution.py:1271
  17.3 245.1 %all-gather.7.cloned.1.call-start = ((), (), s32[]{:S(2)}) async-start(), calls=%async_computation.7 | async-start | bytes 11943936 | tf_op jit(solution)/shard_map/all_gather | solution.py:1271
  18.6 342.3 %all-gather.11.cloned.1.call-start = ((), (), s32[]{:S(2)}) async-start(), calls=%async_computation.9 | async-start | bytes 11943936 | tf_op jit(solution)/shard_map/all_gather | solution.py:1271
  43.5 30.6 %all-to-all-start.1 = ((bf16[8,624,128]{2,1,0:T(8,128)(2,1)}), bf16[8,624,128]{2,1,0:T(8,128)(2,1)S(1)}, u32[]{:S(2)}, u32[]{:S(2)}) async-start(bf16[8,624,128]{2,1,0:T(8,128)(2,1)} %pick.1), calls=%async_computation.1 | async-start | bytes 2555904 | tf_op jit(solution)/shard_map/all_to_all | solution.py:1256
  50.1 91.2 %collective-permute-start.5 = (bf16[4,64,1152]{2,1,0:T(8,128)(2,1)}, bf16[4,64,1152]{2,1,0:T(8,128)(2,1)S(1)}, u32[]{:S(2)}, u32[]{:S(2)}) collective-permute-start(bf16[4,64,1152]{2,1,0:T(8,128)(2,1)} %get-tuple-element.168), channel_id=1, source_target_pairs={{0,24},{8,0},{16,8},{24,16},{1,25},{9,1},{17,9},{25,17},{2,26},{10... | collective-permute-start | bytes 1769480 | tf_op jit(solution)/shard_map/ppermute | solution.py:1276
  53.7 90.3 %collective-permute-start.4 = (bf16[4,64,1152]{2,1,0:T(8,128)(2,1)}, bf16[4,64,1152]{2,1,0:T(8,128)(2,1)S(1)}, u32[]{:S(2)}, u32[]{:S(2)}) collective-permute-start(bf16[4,64,1152]{2,1,0:T(8,128)(2,1)} %get-tuple-element.169), channel_id=1, source_target_pairs={{0,16},{8,24},{16,0},{24,8},{1,17},{9,25},{17,1},{25,9},{2,18},{10... | collective-permute-start | bytes 1769480 | tf_op jit(solution)/shard_map/ppermute | solution.py:1276
  105.3 139.9 %collective-permute-start.8 = (bf16[576,1152]{1,0:T(8,128)(2,1)}, bf16[576,1152]{1,0:T(8,128)(2,1)}, u32[]{:S(2)}, u32[]{:S(2)}) collective-permute-start(bf16[576,1152]{1,0:T(8,128)(2,1)} %get-tuple-element.163.refs_4_.refs_6_), channel_id=1, source_target_pairs={{0,24},{8,0},{16,8},{24,16},{1,25},{9,1},{17,9},{25,17},{2,26},{10... | collective-permute-start | bytes 3981320 | tf_op jit(solution)/shard_map/ppermute | solution.py:1276
  108.9 152.9 %collective-permute-start.7 = (bf16[576,1152]{1,0:T(8,128)(2,1)}, bf16[576,1152]{1,0:T(8,128)(2,1)}, u32[]{:S(2)}, u32[]{:S(2)}) collective-permute-start(bf16[576,1152]{1,0:T(8,128)(2,1)} %get-tuple-element.163.refs_4_.refs_6_), channel_id=1, source_target_pairs={{0,16},{8,24},{16,0},{24,8},{1,17},{9,25},{17,1},{25,9},{2,18},{10... | collective-permute-start | bytes 3981320 | tf_op jit(solution)/shard_map/ppermute | solution.py:1276
  108.9 152.9 %collective-permute-start.6 = (bf16[576,1152]{1,0:T(8,128)(2,1)}, bf16[576,1152]{1,0:T(8,128)(2,1)}, u32[]{:S(2)}, u32[]{:S(2)}) collective-permute-start(bf16[576,1152]{1,0:T(8,128)(2,1)} %get-tuple-element.163.refs_4_.refs_6_), channel_id=1, source_target_pairs={{0,8},{8,16},{16,24},{24,0},{1,9},{9,17},{17,25},{25,1},{2,10},{10... | collective-permute-start | bytes 3981320 | tf_op jit(solution)/shard_map/ppermute | solution.py:1276
  141.3 67.8 %collective-permute-start.3 = (bf16[4,64,1152]{2,1,0:T(8,128)(2,1)S(1)}, bf16[4,64,1152]{2,1,0:T(8,128)(2,1)S(1)}, u32[]{:S(2)}, u32[]{:S(2)}) collective-permute-start(bf16[4,64,1152]{2,1,0:T(8,128)(2,1)S(1)} %copy-done.15), channel_id=1, source_target_pairs={{0,8},{8,16},{16,24},{24,0},{1,9},{9,17},{17,25},{25,1},{2,10},{10... | collective-permute-start | bytes 1769480 | tf_op jit(solution)/shard_map/ppermute | solution.py:1276
  144.0 95.5 %copy-start.12 = (bf16[4,64,1152]{2,1,0:T(8,128)(2,1)}, bf16[4,64,1152]{2,1,0:T(8,128)(2,1)S(1)}, u32[]{:S(2)}) copy-start(bf16[4,64,1152]{2,1,0:T(8,128)(2,1)S(1)} %collective-permute-done.4) | copy-start | bytes 1769476
  144.0 95.5 %collective-permute-start = (bf16[4,64,1152]{2,1,0:T(8,128)(2,1)}, bf16[4,64,1152]{2,1,0:T(8,128)(2,1)S(1)}, u32[]{:S(2)}, u32[]{:S(2)}) collective-permute-start(bf16[4,64,1152]{2,1,0:T(8,128)(2,1)} %get-tuple-element.84), channel_id=1, source_target_pairs={{0,8},{8,16},{16,24},{24,0},{1,9},{9,17},{17,25},{25,1},{2,10},{10... | collective-permute-start | bytes 1769480 | tf_op jit(solution)/shard_map/ppermute | solution.py:1276
  209.2 64.6 %collective-permute-start.1 = (bf16[4,64,1152]{2,1,0:T(8,128)(2,1)}, bf16[4,64,1152]{2,1,0:T(8,128)(2,1)S(1)}, u32[]{:S(2)}, u32[]{:S(2)}) collective-permute-start(bf16[4,64,1152]{2,1,0:T(8,128)(2,1)} %get-tuple-element.85), channel_id=1, source_target_pairs={{0,16},{8,24},{16,0},{24,8},{1,17},{9,25},{17,1},{25,9},{2,18},{10... | collective-permute-start | bytes 1769480 | tf_op jit(solution)/shard_map/ppermute | solution.py:1276
  239.5 48.3 %collective-permute-start.2 = (bf16[4,64,1152]{2,1,0:T(8,128)(2,1)}, bf16[4,64,1152]{2,1,0:T(8,128)(2,1)S(1)}, u32[]{:S(2)}, u32[]{:S(2)}) collective-permute-start(bf16[4,64,1152]{2,1,0:T(8,128)(2,1)} %get-tuple-element.86), channel_id=1, source_target_pairs={{0,24},{8,0},{16,8},{24,16},{1,25},{9,1},{17,9},{25,17},{2,26},{10... | collective-permute-start | bytes 1769480 | tf_op jit(solution)/shard_map/ppermute | solution.py:1276
  245.3 94.3 %collective-permute-start.11 = (bf16[576,1152]{1,0:T(8,128)(2,1)}, bf16[576,1152]{1,0:T(8,128)(2,1)}, u32[]{:S(2)}, u32[]{:S(2)}) collective-permute-start(bf16[576,1152]{1,0:T(8,128)(2,1)} %collective-permute-done.8.refs_7_.refs_9_), channel_id=1, source_target_pairs={{0,1},{1,0},{2,3},{3,2},{4,5},{5,4},{6,7},{7,6},{8,9},{9,8},{10,11... | collective-permute-start | bytes 3981320 | tf_op jit(solution)/shard_map/ppermute | solution.py:1302
  261.9 77.7 %collective-permute-start.10 = (bf16[576,1152]{1,0:T(8,128)(2,1)}, bf16[576,1152]{1,0:T(8,128)(2,1)}, u32[]{:S(2)}, u32[]{:S(2)}) collective-permute-start(bf16[576,1152]{1,0:T(8,128)(2,1)} %collective-permute-done.7.refs_6_.refs_8_), channel_id=1, source_target_pairs={{0,1},{1,0},{2,3},{3,2},{4,5},{5,4},{6,7},{7,6},{8,9},{9,8},{10,11... | collective-permute-start | bytes 3981320 | tf_op jit(solution)/shard_map/ppermute | solution.py:1302
  261.9 77.7 %collective-permute-start.9 = (bf16[576,1152]{1,0:T(8,128)(2,1)}, bf16[576,1152]{1,0:T(8,128)(2,1)}, u32[]{:S(2)}, u32[]{:S(2)}) collective-permute-start(bf16[576,1152]{1,0:T(8,128)(2,1)} %collective-permute-done.6.refs_5_.refs_7_), channel_id=1, source_target_pairs={{0,1},{1,0},{2,3},{3,2},{4,5},{5,4},{6,7},{7,6},{8,9},{9,8},{10,11... | collective-permute-start | bytes 3981320 | tf_op jit(solution)/shard_map/ppermute | solution.py:1302
  445.4 58.1 %collective-permute-start.12 = (bf16[4,32,1152]{2,1,0:T(8,128)(2,1)}, bf16[4,32,1152]{2,1,0:T(8,128)(2,1)S(1)}, u32[]{:S(2)}, u32[]{:S(2)}) collective-permute-start(bf16[4,32,1152]{2,1,0:T(8,128)(2,1)} %get-tuple-element.117), channel_id=1, source_target_pairs={{0,24},{8,0},{16,8},{24,16},{1,25},{9,1},{17,9},{25,17},{2,26},{10... | collective-permute-start | bytes 884744 | tf_op jit(solution)/shard_map/ppermute | solution.py:1276
  448.1 55.5 %collective-permute-start.13 = (bf16[4,32,1152]{2,1,0:T(8,128)(2,1)}, bf16[4,32,1152]{2,1,0:T(8,128)(2,1)}, u32[]{:S(2)}, u32[]{:S(2)}) collective-permute-start(bf16[4,32,1152]{2,1,0:T(8,128)(2,1)} %get-tuple-element.118), channel_id=1, source_target_pairs={{0,16},{8,24},{16,0},{24,8},{1,17},{9,25},{17,1},{25,9},{2,18},{10... | collective-permute-start | bytes 884744 | tf_op jit(solution)/shard_map/ppermute | solution.py:1276
  449.3 54.3 %collective-permute-start.14 = (bf16[4,32,1152]{2,1,0:T(8,128)(2,1)}, bf16[4,32,1152]{2,1,0:T(8,128)(2,1)}, u32[]{:S(2)}, u32[]{:S(2)}) collective-permute-start(bf16[4,32,1152]{2,1,0:T(8,128)(2,1)} %get-tuple-element.119), channel_id=1, source_target_pairs={{0,8},{8,16},{16,24},{24,0},{1,9},{9,17},{17,25},{25,1},{2,10},{10... | collective-permute-start | bytes 884744 | tf_op jit(solution)/shard_map/ppermute | solution.py:1276
  503.5 52.9 %copy-start.21 = (bf16[4,32,1152]{2,1,0:T(8,128)(2,1)}, bf16[4,32,1152]{2,1,0:T(8,128)(2,1)S(1)}, u32[]{:S(2)}) copy-start(bf16[4,32,1152]{2,1,0:T(8,128)(2,1)S(1)} %collective-permute-done.12.refs_2_) | copy-start | bytes 884740
  503.6 25.7 %all-to-all-start.2 = ((bf16[32,112,128]{2,1,0:T(8,128)(2,1)}), bf16[32,112,128]{2,1,0:T(8,128)(2,1)S(1)}, u32[]{:S(2)}, u32[]{:S(2)}) async-start(bf16[32,112,128]{2,1,0:T(8,128)(2,1)} %pack_early.1), calls=%async_computation.2 | async-start | bytes 1835008 | tf_op jit(solution)/shard_map/all_to_all | solution.py:1256
  506.9 25.6 %collective-permute-start.15 = (bf16[4,32,1152]{2,1,0:T(8,128)(2,1)S(1)}, bf16[4,32,1152]{2,1,0:T(8,128)(2,1)S(1)}, u32[]{:S(2)}, u32[]{:S(2)}) collective-permute-start(bf16[4,32,1152]{2,1,0:T(8,128)(2,1)S(1)} %copy-done.27), channel_id=1, source_target_pairs={{0,24},{8,0},{16,8},{24,16},{1,25},{9,1},{17,9},{25,17},{2,26},{10... | collective-permute-start | bytes 884744 | tf_op jit(solution)/shard_map/ppermute | solution.py:1276
  510.6 45.0 %collective-permute-start.16 = (bf16[4,32,1152]{2,1,0:T(8,128)(2,1)S(1)}, bf16[4,32,1152]{2,1,0:T(8,128)(2,1)S(1)}, u32[]{:S(2)}, u32[]{:S(2)}) collective-permute-start(bf16[4,32,1152]{2,1,0:T(8,128)(2,1)S(1)} %copy-done.26), channel_id=1, source_target_pairs={{0,16},{8,24},{16,0},{24,8},{1,17},{9,25},{17,1},{25,9},{2,18},{10... | collective-permute-start | bytes 884744 | tf_op jit(solution)/shard_map/ppermute | solution.py:1276
  510.6 45.0 %collective-permute-start.17 = (bf16[4,32,1152]{2,1,0:T(8,128)(2,1)S(1)}, bf16[4,32,1152]{2,1,0:T(8,128)(2,1)S(1)}, u32[]{:S(2)}, u32[]{:S(2)}) collective-permute-start(bf16[4,32,1152]{2,1,0:T(8,128)(2,1)S(1)} %copy-done.25), channel_id=1, source_target_pairs={{0,8},{8,16},{16,24},{24,0},{1,9},{9,17},{17,25},{25,1},{2,10},{10... | collective-permute-start | bytes 884744 | tf_op jit(solution)/shard_map/ppermute | solution.py:1276
  556.4 85.7 %all-to-all-start.3 = ((bf16[4,8,112,128]{3,2,1,0:T(8,128)(2,1)}), bf16[4,8,112,128]{3,2,1,0:T(8,128)(2,1)S(1)}, u32[]{:S(2)}, u32[]{:S(2)}) async-start(bf16[4,8,112,128]{3,2,1,0:T(8,128)(2,1)} %combine.2), calls=%async_computation.3 | async-start | bytes 1835008 | tf_op jit(solution)/shard_map/all_to_all | solution.py:1256
  588.0 39.8 %collective-permute-start.18 = (bf16[4,64,1152]{2,1,0:T(8,128)(2,1)}, bf16[4,64,1152]{2,1,0:T(8,128)(2,1)S(1)}, u32[]{:S(2)}, u32[]{:S(2)}) collective-permute-start(bf16[4,64,1152]{2,1,0:T(8,128)(2,1)} %bitcast.92), channel_id=1, source_target_pairs={{0,24},{8,0},{16,8},{24,16},{1,25},{9,1},{17,9},{25,17},{2,26},{10... | collective-permute-start | bytes 1769480 | tf_op jit(solution)/shard_map/ppermute | solution.py:1276
  591.7 50.4 %collective-permute-start.19 = (bf16[4,64,1152]{2,1,0:T(8,128)(2,1)}, bf16[4,64,1152]{2,1,0:T(8,128)(2,1)S(1)}, u32[]{:S(2)}, u32[]{:S(2)}) collective-permute-start(bf16[4,64,1152]{2,1,0:T(8,128)(2,1)} %bitcast.91), channel_id=1, source_target_pairs={{0,16},{8,24},{16,0},{24,8},{1,17},{9,25},{17,1},{25,9},{2,18},{10... | collective-permute-start | bytes 1769480 | tf_op jit(solution)/shard_map/ppermute | solution.py:1276
  591.7 50.4 %collective-permute-start.20 = (bf16[4,64,1152]{2,1,0:T(8,128)(2,1)}, bf16[4,64,1152]{2,1,0:T(8,128)(2,1)}, u32[]{:S(2)}, u32[]{:S(2)}) collective-permute-start(bf16[4,64,1152]{2,1,0:T(8,128)(2,1)} %bitcast.90), channel_id=1, source_target_pairs={{0,8},{8,16},{16,24},{24,0},{1,9},{9,17},{17,25},{25,1},{2,10},{10... | collective-permute-start | bytes 1769480 | tf_op jit(solution)/shard_map/ppermute | solution.py:1276
  627.7 62.5 %copy-start.13 = (bf16[4,64,1152]{2,1,0:T(8,128)(2,1)}, bf16[4,64,1152]{2,1,0:T(8,128)(2,1)S(1)}, u32[]{:S(2)}) copy-start(bf16[4,64,1152]{2,1,0:T(8,128)(2,1)S(1)} %collective-permute-done.18.refs_1_) | copy-start | bytes 1769476
  666.2 28.0 %all-to-all-start.5 = ((bf16[4,8,80,128]{3,2,1,0:T(8,128)(2,1)}), bf16[4,8,80,128]{3,2,1,0:T(8,128)(2,1)S(1)}, u32[]{:S(2)}, u32[]{:S(2)}) async-start(bf16[4,8,80,128]{3,2,1,0:T(8,128)(2,1)} %combine.3), calls=%async_computation.5 | async-start | bytes 1310720 | tf_op jit(solution)/shard_map/all_to_all | solution.py:1256
  (25 other events, 349.1 us)
Sparse Core Ops, SparseCore 0:
  15.1 86.6 all-gather.4
  103.7 64.0 all-gather.8
  169.7 63.7 all-gather.6
  235.3 63.7 all-gather.10

commit v5 on v4

--- a/solution.py
+++ b/solution.py
@@ -1256,11 +1256,6 @@
     return lax.all_to_all(array, axes, split_axis=0, concat_axis=0, tiled=True)
 
 
-def reduce_grads(packed, all_index, adapters):
-    got = exchange(packed, ("fsdp", "seq"))
-    return run_combine(all_index, got, adapters)
-
-
 def up_chunks(up, clips, times):
     rows, hidden = up.shape
     cols = hidden // (clips * times)
@@ -1284,24 +1279,41 @@
     return [pieces[0]] + [send(pieces[k], "seq", -k) for k in range(1, len(pieces))]
 
 
-def fetch_spatial_and_down(spatial, down, clips, parts, times, d):
+def gather_spatial_and_down(spatial, down, parts, times, clips, d):
     quarters = down.reshape(times, -1, d)
+    if times != parts or clips % 2:
+        return gather(spatial), None
+    own = lax.dynamic_slice_in_dim(quarters, lax.axis_index("seq"), 1, 0)
+    got = gather(jnp.concatenate([spatial, own], 0))
     half = d // 2
-    if times != parts or clips % 2:
-        whole = gather(quarters)
-        pieces = [whole[i, side * half : (side + 1) * half] for side in range(2) for i in range(times)]
-        return gather(spatial), [jnp.arange(times + 1, dtype=jnp.int32) % times, *pieces]
+    core = lax.axis_index("fsdp") % 2
+    first = lax.dynamic_slice(got, (times, core * half, 0), (1, half, d))[0]
+    other = lax.dynamic_slice(got, (times, (1 - core) * half, 0), (1, half, d))[0]
+    return got, (first, other, send(first, "seq", 1))
+
+
+def spread_down(started, down, arrived, parts, times, clips, d):
+    half = d // 2
+    if started is None:
+        whole = gather(down.reshape(times, -1, d))
+        return [whole[i, side * half : (side + 1) * half] for side in range(2) for i in range(times)], arrived
+    first, other, second = started
+    later, second, *arrived = lax.optimization_barrier((first, second, *arrived))
+    mine = [first, second] + [send(later, "seq", k) for k in range(2, parts)]
+    return mine + [other], arrived
+
+
+def swap_down(pieces, after, parts, times, clips):
+    if len(pieces) == 2 * times:
+        return [jnp.arange(times + 1, dtype=jnp.int32) % times, *pieces], after
+    *mine, other = pieces
+    after, *mine = lax.optimization_barrier((after, *mine))
+    swap = [(i, i ^ 1) for i in range(clips)]
+    others = [other] + [lax.ppermute(piece, "fsdp", swap) for piece in mine[1:]]
     seq = lax.axis_index("seq")
     core = lax.axis_index("fsdp") % 2
-    own = lax.dynamic_slice_in_dim(quarters, seq, 1, 0)
-    got = gather(jnp.concatenate([spatial, own], 0))
-    first = lax.dynamic_slice(got, (times, core * half, 0), (1, half, d))[0]
-    other = lax.dynamic_slice(got, (times, (1 - core) * half, 0), (1, half, d))[0]
-    mine = [first] + [send(first, "seq", k) for k in range(1, parts)]
-    swap = [(i, i ^ 1) for i in range(clips)]
-    others = [other] + [lax.ppermute(piece, "fsdp", swap) for piece in mine[1:]]
     order = jnp.concatenate([(seq - jnp.arange(parts)) % parts, core[None]]).astype(jnp.int32)
-    return got, [order, *mine, *others]
+    return [order, *mine, *others], after
 
 
 def on_device(
@@ -1333,8 +1345,8 @@
 
     seq = lax.axis_index("seq").astype(jnp.int32)[None]
     all_index = exchange(jnp.broadcast_to(adapter_index, (clips,)), "fsdp")
-    w_s, down = fetch_spatial_and_down(
-        attention_weights(0), ffn_down[0], clips, parts, times, d
+    w_s, started = gather_spatial_and_down(
+        attention_weights(0), ffn_down[0], parts, times, clips, d
     )
     picked = run_pick(all_index, adapt_wide[0], adapt_ff[0])
     wide = run_unpick(exchange(picked, "fsdp"), count + 2 * times, cols)
@@ -1351,13 +1363,14 @@
             for k in range(parts)
         ]
     )
+    frames_in, *cot = lax.optimization_barrier((video.reshape(frames, SPATIAL, d), *cot))
     cot = jnp.concatenate(cot, 0).reshape(FRAMES * places, d)
-    frames_in = video.reshape(frames, SPATIAL, d)
     made = run_spatial_forward(seq, frames_in, mods, masks, wide, w_s, parts)
     u1, kept_s = to_places(made[:parts]), made[parts:]
+    pieces, u1 = spread_down(started, ffn_down[0], u1, parts, times, clips, d)
+    *kept_t, x3 = run_temporal_cross_forward(u1, ctx, mods, masks, wide, w_t, w_c)
+    down, x3 = swap_down(pieces, x3.reshape(FRAMES * places, d), parts, times, clips)
     grad_active = run_feed_forward_grad(cot, mods, maps_f, down)
-    *kept_t, x3 = run_temporal_cross_forward(u1, ctx, mods, masks, wide, w_t, w_c)
-    x3 = x3.reshape(FRAMES * places, d)
     active, g3, grad_a24, grad_b24 = run_feed_forward(x3, cot, grad_active, mods, maps_f, up)
     g3 = g3.reshape(FRAMES, places, d)
     groups = FRAMES * places // ROWS
@@ -1379,7 +1392,8 @@
     packed = run_pack_early(gw, dk, dv, sources, clips, parts)
     active, packed, *g1[0] = lax.optimization_barrier((active, packed, *g1[0]))
     *x4, grad_b25, grad_down = run_feed_forward_out(active, x3, cot, mods, maps_f, down, parts)
-    early = reduce_grads(packed, all_index, adapters)
+    early, *x4 = lax.optimization_barrier((exchange(packed, ("fsdp", "seq")), *x4))
+    early = run_combine(all_index, early, adapters)
     output = to_frames([piece.reshape(frames, places, d) for piece in x4])
     g1 = [piece for pieces in g1 for piece in pieces]
     early, *g1 = lax.optimization_barrier((early, *g1))
@@ -1389,7 +1403,7 @@
     early = exchange(early)
     packed, early, *output = lax.optimization_barrier((packed, early, *output))
     g0 = run_spatial_input_grad(seq, g1, halves, frames_in, grads, mods, wide, w_s)
-    late = reduce_grads(packed, all_index, adapters)
+    late = run_combine(all_index, exchange(packed, ("fsdp", "seq")), adapters)
     wide_out, narrow_out = run_assemble(
         early, exchange(late), adapt_wide.shape[1:], adapt_ff.shape[1:]
     )

time: 716 us -> 662 us (0.925)
  waiting for transfers between devices: 202 us -> 169 us
  starting transfers between devices: 72.6 us -> 54.9 us
    all_to_all x4, waiting for transfers between devices: 36.8 us -> 0.01 us  [exchange(): return lax.all_to_all(array, axes, split_axis=0, concat_axis=0, tiled=True)]
    ppermute x18, starting transfers between devices: 57.2 us -> 37.3 us  [send(): lax.ppermute(array, axis, [(i, (i + shift) % size) for i in range(size)])]
    all_gather x4, waiting for transfers between devices: 22 us -> 31.4 us  [gather(): return lax.all_gather(array, 'fsdp', axis=1, tiled=True)]
    ppermute x18, waiting for transfers between devices: 144 us -> 136 us  [send(): lax.ppermute(array, axis, [(i, (i + shift) % size) for i in range(size)])]
  transfers between devices with their start and end apart: 29 -> 29, of which waited for: 9 -> 9; matrix products, arithmetic and copies ran while one was open for 4% -> 5% of each run, Pallas kernels for 35% -> 38%
where the time goes in v5:
time: 662 us; the launch traced here: 652 us
  Pallas kernels  341 us (52%)
  waiting for transfers between devices  169 us (26%)
  starting transfers between devices  54.9 us (8%)
  local copies, waits for them, and re-layouts  30.5 us (5%)
  blocking collectives  29.9 us (5%)
  between operations  15.2 us (2%)
  other arithmetic  11 us (2%)
    ppermute x18, waiting for transfers between devices, send(): lax.ppermute(array, axis, [(i, (i + shift) % size) for i in range(size)])  136 us
    pallas_call x2, Pallas kernels, run_cross_temporal_backward(): pl.pallas_call(body, grid=(groups,), in_specs=[pl.BlockSpec((own_frames,...  84.2 us
    pallas_call x1, Pallas kernels, run_temporal_cross_forward(): pl.pallas_call(body, grid=(groups,), in_specs=[pl.BlockSpec((own_frames,...  50.8 us
    pallas_call x1, Pallas kernels, run_feed_forward(): pl.pallas_call(feed_forward, grid=(tokens // ROWS,), in_specs=[rows, rows...  42.5 us
    ppermute x18, starting transfers between devices, send(): lax.ppermute(array, axis, [(i, (i + shift) % size) for i in range(size)])  37.3 us
    pallas_call x1, Pallas kernels, run_spatial_backward(): pl.pallas_call(body, grid=(frames,), in_specs=[in_smem()] + [pl.BlockSpec...  34.9 us
    all_gather x4, waiting for transfers between devices, gather(): return lax.all_gather(array, 'fsdp', axis=1, tiled=True)  31.4 us
    pallas_call x1, Pallas kernels, run_spatial_forward(): pl.pallas_call(spatial_forward, grid=(frames,), in_specs=[in_smem(), row_...  30.8 us
  transfers between devices with their start and end apart: 29, of which 9 were waited for; matrix products, arithmetic and copies ran while one was open for 5% of the time, Pallas kernels for 38%

profile of v5, /device:TPU:0, one launch (start us, length us, event | category | flops | bytes accessed | tf_op | source)
XLA Modules:
  0.0 651.9 jit_solution(4662746013095638222)
XLA Ops:
  19.4 9.6 %all_to_all.33 = s32[8,1,1]{2,1,0:T(1,128)S(1)} all-to-all(s32[8,1,1]{2,1,0:T(1,128)S(1)} %broadcast_in_dim.23), channel_id=1, replica_groups=mesh['seq'=4,'fsdp'=8] {'fsdp'}, dimensions={0} | all-to-all | bytes 64 | tf_op jit(solution)/shard_map/all_to_all | solution.py:1256
  33.4 5.2 reshape_squeeze.7
  43.5 3.6 all-to-all-start.1
  50.0 3.6 collective-permute-start.3
  56.0 11.8 %collective-permute-done.3 = bf16[4,64,1152]{2,1,0:T(8,128)(2,1)S(1)} collective-permute-done((bf16[4,64,1152]{2,1,0:T(8,128)(2,1)}, bf16[4,64,1152]{2,1,0:T(8,128)(2,1)S(1)}, u32[]{:S(2)}, u32[]{:S(2)}) %collective-permute-start.3) | collective-permute-done | bytes 589856 | tf_op jit(solution)/shard_map/ppermute | solution.py:1271
  67.7 37.0 %collective-permute-done.2 = bf16[4,64,1152]{2,1,0:T(8,128)(2,1)S(1)} collective-permute-done((bf16[4,64,1152]{2,1,0:T(8,128)(2,1)}, bf16[4,64,1152]{2,1,0:T(8,128)(2,1)S(1)}, u32[]{:S(2)}, u32[]{:S(2)}) %collective-permute-start.2) | collective-permute-done | bytes 589856 | tf_op jit(solution)/shard_map/ppermute | solution.py:1271
  105.9 4.7 unpick.1.ad_ref.refs_7_.refs_22_.refs_12_.refs_19_
  110.5 3.9 dynamic-slice_bitcast_fusion
  115.3 30.8 %spatial_forward.1 = (bf16[4,64,1152]{2,1,0:T(8,128)(2,1)}, bf16[4,64,1152]{2,1,0:T(8,128)(2,1)}, bf16[4,64,1152]{2,1,0:T(8,128)(2,1)}, bf16[4,64,1152]{2,1,0:T(...) custom-call(s32[1]{0:T(128)} %bitcast.seq_ref.refs_0_, ...), custom_call_target="tpu_custom_call" | custom-call | flops 13589544960 | bytes 30000000 | tf_op jit(solution)/shard_map/spatial_forward/pallas_call | solution.py:859
  152.1 12.5 %collective-permute-done.4.refs_1_ = bf16[4,64,1152]{2,1,0:T(8,128)(2,1)S(1)} collective-permute-done((bf16[4,64,1152]{2,1,0:T(8,128)(2,1)}, bf16[4,64,1152]{2,1,0:T(8,128)(2,1)S(1)}, u32[]{:S(2)}, u32[]{:S(2)}) %collective-permute-start.4) | collective-permute-done | bytes 589856 | tf_op jit(solution)/shard_map/ppermute | solution.py:1271
  164.6 23.0 %collective-permute-done.5.refs_2_ = bf16[4,64,1152]{2,1,0:T(8,128)(2,1)S(1)} collective-permute-done((bf16[4,64,1152]{2,1,0:T(8,128)(2,1)}, bf16[4,64,1152]{2,1,0:T(8,128)(2,1)S(1)}, u32[]{:S(2)}, u32[]{:S(2)}) %collective-permute-start.5) | collective-permute-done | bytes 589856 | tf_op jit(solution)/shard_map/ppermute | solution.py:1271
  187.6 14.2 %collective-permute-start.8 = (bf16[576,1152]{1,0:T(8,128)(2,1)}, bf16[576,1152]{1,0:T(8,128)(2,1)}, u32[]{:S(2)}, u32[]{:S(2)}) collective-permute-start(bf16[576,1152]{1,0:T(8,128)(2,1)} %get-tuple-element.121.refs_4_.refs_6_), channel_id=1, source_target_pairs={{0,24},{8,0},{16,8},{24,16},{1,25},{9,1},{17,9},{25,17},{2,26},{10... | collective-permute-start | bytes 3981320 | tf_op jit(solution)/shard_map/ppermute | solution.py:1271
  202.2 31.4 %all-gather.7.cloned.1.call-done.refs_8_.refs_23_ = bf16[4,1152,1152]{2,1,0:T(8,128)(2,1)} async-done(((bf16[4,144,1152]{2,1,0:T(8,128)(2,1)}), bf16[4,1152,1152]{2,1,0:T(8,128)(2,1)}) %all-gather.7.cloned.1.call-update) | async-done | bytes 10616848 | tf_op jit(solution)/shard_map/all_gather | solution.py:1266
  233.6 50.8 %temporal_cross_forward.1 = (bf16[16,64,1152]{2,1,0:T(8,128)(2,1)}, bf16[16,64,1152]{2,1,0:T(8,128)(2,1)}, bf16[16,64,1152]{2,1,0:T(8,128)(2,1)}, bf16[16,64,115...) custom-call(bf16[4,64,1152]{2,1,0:T(8,128)(2,1)} %get-tuple-element., ...), custom_call_target="tpu_custom_call" | custom-call | flops 19025362944 | bytes 50000000 | tf_op jit(solution)/shard_map/temporal_cross_forward/pallas_call | solution.py:911
  284.4 4.0 collective-permute-done.7.refs_6_.refs_8_
  296.5 21.3 %feed_forward_grad.1.grad_ref = bf16[1024,4608]{1,0:T(8,128)(2,1)} custom-call(s32[5]{0:T(128)} %pad_add_fusion.refs_0_, bf16[1024,1152]{1,0:T(8,128)(2,1)} %bitcast.64, f32[6,1152]{1,0:T(8,128)} %bitcast.73, bf16[10,16,1152]{2,1,0:T(8,128)(2,1)} %slice.28.refs_3_.ad_ref.refs_5_, bf16[576,1152]{1,0:T(8,128)(2,1)} %get-tuple-element.121.refs_4_.refs_6_, ...), custom_call_target="tpu_custom_call" | custom-call | flops 10871635968 | bytes 30000000 | tf_op jit(solution)/shard_map/feed_forward_grad/pallas_call | solution.py:944
  317.8 42.5 %feed_forward.1 = (bf16[1024,4608]{1,0:T(8,128)(2,1)}, f32[1024,1152]{1,0:T(8,128)}, f32[16,1152]{1,0:T(8,128)}, f32[16,4608]{1,0:T(8,128)}) custom-call(f32[1024,1152]{1,0:T(8,128)} %bitcast.92, bf16[1024,1152]{1,0:T(8,128)(2,1)} %bitcast.65, bf16[1024,4608]{1,0:T(8,128)(2,1)} %feed_forward_grad.1.grad_ref, f32[6,1152]{1,0:T(8,128)} %bitcast.74, ...), custom_call_target="tpu_custom_call" | custom-call | flops 21743271936 | bytes 50000000 | tf_op jit(solution)/shard_map/feed_forward/pallas_call | solution.py:967
  360.3 42.0 %cross_temporal_backward.2 = (bf16[4,32,1152]{2,1,0:T(8,128)(2,1)}, bf16[4,32,1152]{2,1,0:T(8,128)(2,1)}, bf16[4,32,1152]{2,1,0:T(8,128)(2,1)}, bf16[4,32,1152]{...) custom-call(bf16[4,64,1152]{2,1,0:T(8,128)(2,1)} %get-tuple-element.109.refs_0_, ...), custom_call_target="tpu_custom_call" | custom-call | flops 9512681472 | bytes 30000000 | tf_op jit(solution)/shard_map/cross_temporal_backward/pallas_call | solution.py:1055
  404.7 42.3 %cross_temporal_backward.3 = (bf16[4,32,1152]{2,1,0:T(8,128)(2,1)}, bf16[4,32,1152]{2,1,0:T(8,128)(2,1)}, bf16[4,32,1152]{2,1,0:T(8,128)(2,1)}, bf16[4,32,1152]{...) custom-call(bf16[4,64,1152]{2,1,0:T(8,128)(2,1)} %get-tuple-element.109.refs_0_, ...), custom_call_target="tpu_custom_call" | custom-call | flops 9512681472 | bytes 30000000 | tf_op jit(solution)/shard_map/cross_temporal_backward/pallas_call | solution.py:1055
  447.7 9.5 %pack_early.1 = bf16[32,112,128]{2,1,0:T(8,128)(2,1)} custom-call(f32[256,1152]{1,0:T(8,128)} %get-tuple-element.143.refs_0_, f32[256,1152]{1,0:T(8,128)} %get-tuple-element.144.refs_1_, f32[8,256,256]{2,1,0:T(8,128)} %get-tuple-element.145.refs_2_, f32[8,256,256]{2,1,0:T(8,128)} %get-tuple-element.146.refs_3_, f32[8,256,256]{2,1,0:T(8,128)} %get-tuple-element.147.refs_4_, ...), custom_call_target="tpu_custom_call" | custom-call | flops 50000000 | bytes 8000000 | tf_op jit(solution)/shard_map/pack_early/pallas_call | solution.py:1188
  457.2 5.6 all-to-all-start.2
  462.8 3.7 collective-permute-start.15
  467.6 26.3 %feed_forward_out.1 = (bf16[256,1152]{1,0:T(8,128)(2,1)}, bf16[256,1152]{1,0:T(8,128)(2,1)}, bf16[256,1152]{1,0:T(8,128)(2,1)}, bf16[256,1152]{1,0:T(8,128)(2,1)...) custom-call(s32[5]{0:T(128)} %pad_add_fusion.refs_0_, bf16[1024,4608]{1,0:T(8,128)(2,1)} %get-tuple-element.158.refs_1_, ...), custom_call_target="tpu_custom_call" | custom-call | flops 10871635968 | bytes 30000000 | tf_op jit(solution)/shard_map/feed_forward_out/pallas_call | solution.py:1005
  497.2 14.3 %collective-permute-done.16.refs_7_ = bf16[4,32,1152]{2,1,0:T(8,128)(2,1)S(1)} collective-permute-done((bf16[4,32,1152]{2,1,0:T(8,128)(2,1)S(1)}, bf16[4,32,1152]{2,1,0:T(8,128)(2,1)S(1)}, u32[]{:S(2)}, u32[]{:S(2)}) %collective-permute-start.16) | collective-permute-done | bytes 294944 | tf_op jit(solution)/shard_map/ppermute | solution.py:1271
  516.6 3.8 collective-permute-start.18
  521.5 34.9 %spatial_backward.1 = (bf16[4,256,3584]{2,1,0:T(8,128)(2,1)}, bf16[32,80,128]{2,1,0:T(8,128)(2,1)}) custom-call(s32[1]{0:T(128)} %bitcast.seq_ref.refs_0_, bf16[4,32,1152]{2,1,0:T(8,128)(2,1)} %get-tuple-element.172.refs_1_, bf16[4,32,1152]{2,1,0:T(8,128)(2,1)} %collective-permute-done.12.refs_2_, bf16[4,32,1152]{2,1,0:T(8,128)(2,1)} %collective-permute-done.13.refs_3_, ...), custom_call_target="tpu_custom_call" | custom-call | flops 8153726976 | bytes 30000000 | tf_op jit(solution)/shard_map/spatial_backward/pallas_call | solution.py:1097
  556.4 33.0 %collective-permute-done.19.refs_2_ = bf16[4,64,1152]{2,1,0:T(8,128)(2,1)S(1)} collective-permute-done((bf16[4,64,1152]{2,1,0:T(8,128)(2,1)}, bf16[4,64,1152]{2,1,0:T(8,128)(2,1)S(1)}, u32[]{:S(2)}, u32[]{:S(2)}) %collective-permute-start.19) | collective-permute-done | bytes 589856 | tf_op jit(solution)/shard_map/ppermute | solution.py:1271
  589.4 20.2 %all_to_all.34.got_ref = bf16[32,80,128]{2,1,0:T(8,128)(2,1)} all-to-all(bf16[32,80,128]{2,1,0:T(8,128)(2,1)} %get-tuple-element.201), channel_id=1, replica_groups=mesh['seq'=4,'fsdp'=8] {'fsdp','seq'}, dimensions={0} | all-to-all | bytes 1310720 | tf_op jit(solution)/shard_map/all_to_all | solution.py:1256
  611.8 4.2 all-to-all-start.5
  616.1 19.7 %spatial_input_grad.1 = bf16[4,256,1152]{2,1,0:T(8,128)(2,1)} custom-call(s32[1]{0:T(128)} %bitcast.seq_ref.refs_0_, bf16[4,32,1152]{2,1,0:T(8,128)(2,1)} %get-tuple-element.172.refs_1_, bf16[4,32,1152]{2,1,0:T(8,128)(2,1)} %collective-permute-done.12.refs_2_, bf16[4,32,1152]{2,1,0:T(8,128)(2,1)} %collective-permute-done.13.refs_3_, ...), custom_call_target="tpu_custom_call" | custom-call | flops 8153726976 | bytes 20000000 | tf_op jit(solution)/shard_map/spatial_input_grad/pallas_call | solution.py:1134
  635.8 4.0 put_in_place.1
  640.6 4.5 assemble.1
  (128 shorter events, 59.1 us)
Async XLA Ops:
  7.2 103.3 %all-gather.5.cloned.1.call-start = ((), (), s32[]{:S(2)}) async-start(), calls=%async_computation.6 | async-start | bytes 14929920 | tf_op jit(solution)/shard_map/all_gather | solution.py:1266
  15.0 187.1 %all-gather.9.cloned.1.call-start = ((), (), s32[]{:S(2)}) async-start(), calls=%async_computation.8 | async-start | bytes 11943936 | tf_op jit(solution)/shard_map/all_gather | solution.py:1266
  17.3 216.3 %all-gather.7.cloned.1.call-start = ((), (), s32[]{:S(2)}) async-start(), calls=%async_computation.7 | async-start | bytes 11943936 | tf_op jit(solution)/shard_map/all_gather | solution.py:1266
  18.6 299.2 %all-gather.11.cloned.1.call-start = ((), (), s32[]{:S(2)}) async-start(), calls=%async_computation.9 | async-start | bytes 11943936 | tf_op jit(solution)/shard_map/all_gather | solution.py:1266
  43.5 61.3 %all-to-all-start.1 = ((bf16[8,624,128]{2,1,0:T(8,128)(2,1)}), bf16[8,624,128]{2,1,0:T(8,128)(2,1)S(1)}, u32[]{:S(2)}, u32[]{:S(2)}) async-start(bf16[8,624,128]{2,1,0:T(8,128)(2,1)} %pick.1), calls=%async_computation.1 | async-start | bytes 2555904 | tf_op jit(solution)/shard_map/all_to_all | solution.py:1256
  50.0 17.7 %collective-permute-start.3 = (bf16[4,64,1152]{2,1,0:T(8,128)(2,1)}, bf16[4,64,1152]{2,1,0:T(8,128)(2,1)S(1)}, u32[]{:S(2)}, u32[]{:S(2)}) collective-permute-start(bf16[4,64,1152]{2,1,0:T(8,128)(2,1)} %get-tuple-element.209), channel_id=1, source_target_pairs={{0,24},{8,0},{16,8},{24,16},{1,25},{9,1},{17,9},{25,17},{2,26},{10... | collective-permute-start | bytes 1769480 | tf_op jit(solution)/shard_map/ppermute | solution.py:1271
  53.6 51.1 %collective-permute-start.2 = (bf16[4,64,1152]{2,1,0:T(8,128)(2,1)}, bf16[4,64,1152]{2,1,0:T(8,128)(2,1)S(1)}, u32[]{:S(2)}, u32[]{:S(2)}) collective-permute-start(bf16[4,64,1152]{2,1,0:T(8,128)(2,1)} %get-tuple-element.210), channel_id=1, source_target_pairs={{0,16},{8,24},{16,0},{24,8},{1,17},{9,25},{17,1},{25,9},{2,18},{10... | collective-permute-start | bytes 1769480 | tf_op jit(solution)/shard_map/ppermute | solution.py:1271
  53.7 51.1 %collective-permute-start.1 = (bf16[4,64,1152]{2,1,0:T(8,128)(2,1)}, bf16[4,64,1152]{2,1,0:T(8,128)(2,1)}, u32[]{:S(2)}, u32[]{:S(2)}) collective-permute-start(bf16[4,64,1152]{2,1,0:T(8,128)(2,1)} %get-tuple-element.211), channel_id=1, source_target_pairs={{0,8},{8,16},{16,24},{24,0},{1,9},{9,17},{17,25},{25,1},{2,10},{10... | collective-permute-start | bytes 1769480 | tf_op jit(solution)/shard_map/ppermute | solution.py:1271
  114.4 73.2 %collective-permute-start = (bf16[576,1152]{1,0:T(8,128)(2,1)}, bf16[576,1152]{1,0:T(8,128)(2,1)}, u32[]{:S(2)}, u32[]{:S(2)}) collective-permute-start(bf16[576,1152]{1,0:T(8,128)(2,1)} %get-tuple-element.121.refs_4_.refs_6_), channel_id=1, source_target_pairs={{0,8},{8,16},{16,24},{24,0},{1,9},{9,17},{17,25},{25,1},{2,10},{10... | collective-permute-start | bytes 3981320 | tf_op jit(solution)/shard_map/ppermute | solution.py:1271
  146.1 18.5 %collective-permute-start.4 = (bf16[4,64,1152]{2,1,0:T(8,128)(2,1)}, bf16[4,64,1152]{2,1,0:T(8,128)(2,1)S(1)}, u32[]{:S(2)}, u32[]{:S(2)}) collective-permute-start(bf16[4,64,1152]{2,1,0:T(8,128)(2,1)} %get-tuple-element.106), channel_id=1, source_target_pairs={{0,8},{8,16},{16,24},{24,0},{1,9},{9,17},{17,25},{25,1},{2,10},{10... | collective-permute-start | bytes 1769480 | tf_op jit(solution)/shard_map/ppermute | solution.py:1271
  148.7 38.9 %collective-permute-start.5 = (bf16[4,64,1152]{2,1,0:T(8,128)(2,1)}, bf16[4,64,1152]{2,1,0:T(8,128)(2,1)S(1)}, u32[]{:S(2)}, u32[]{:S(2)}) collective-permute-start(bf16[4,64,1152]{2,1,0:T(8,128)(2,1)} %get-tuple-element.107), channel_id=1, source_target_pairs={{0,16},{8,24},{16,0},{24,8},{1,17},{9,25},{17,1},{25,9},{2,18},{10... | collective-permute-start | bytes 1769480 | tf_op jit(solution)/shard_map/ppermute | solution.py:1271
  149.7 37.9 %collective-permute-start.6 = (bf16[4,64,1152]{2,1,0:T(8,128)(2,1)}, bf16[4,64,1152]{2,1,0:T(8,128)(2,1)S(1)}, u32[]{:S(2)}, u32[]{:S(2)}) collective-permute-start(bf16[4,64,1152]{2,1,0:T(8,128)(2,1)} %get-tuple-element.108), channel_id=1, source_target_pairs={{0,24},{8,0},{16,8},{24,16},{1,25},{9,1},{17,9},{25,17},{2,26},{10... | collective-permute-start | bytes 1769480 | tf_op jit(solution)/shard_map/ppermute | solution.py:1271
  164.6 69.0 %copy-start.7 = (bf16[4,64,1152]{2,1,0:T(8,128)(2,1)}, bf16[4,64,1152]{2,1,0:T(8,128)(2,1)S(1)}, u32[]{:S(2)}) copy-start(bf16[4,64,1152]{2,1,0:T(8,128)(2,1)S(1)} %collective-permute-done.4.refs_1_) | copy-start | bytes 1769476
  187.6 96.8 %collective-permute-start.8 = (bf16[576,1152]{1,0:T(8,128)(2,1)}, bf16[576,1152]{1,0:T(8,128)(2,1)}, u32[]{:S(2)}, u32[]{:S(2)}) collective-permute-start(bf16[576,1152]{1,0:T(8,128)(2,1)} %get-tuple-element.121.refs_4_.refs_6_), channel_id=1, source_target_pairs={{0,24},{8,0},{16,8},{24,16},{1,25},{9,1},{17,9},{25,17},{2,26},{10... | collective-permute-start | bytes 3981320 | tf_op jit(solution)/shard_map/ppermute | solution.py:1271
  201.8 86.6 %collective-permute-start.7 = (bf16[576,1152]{1,0:T(8,128)(2,1)}, bf16[576,1152]{1,0:T(8,128)(2,1)}, u32[]{:S(2)}, u32[]{:S(2)}) collective-permute-start(bf16[576,1152]{1,0:T(8,128)(2,1)} %get-tuple-element.121.refs_4_.refs_6_), channel_id=1, source_target_pairs={{0,16},{8,24},{16,0},{24,8},{1,17},{9,25},{17,1},{25,9},{2,18},{10... | collective-permute-start | bytes 3981320 | tf_op jit(solution)/shard_map/ppermute | solution.py:1271
  288.4 5.9 collective-permute-start.9
  288.4 6.0 collective-permute-start.10
  288.9 7.6 %collective-permute-start.11 = (bf16[576,1152]{1,0:T(8,128)(2,1)}, bf16[576,1152]{1,0:T(8,128)(2,1)}, u32[]{:S(2)}, u32[]{:S(2)}) collective-permute-start(bf16[576,1152]{1,0:T(8,128)(2,1)} %collective-permute-done.8.refs_7_.refs_9_), channel_id=1, source_target_pairs={{0,1},{1,0},{2,3},{3,2},{4,5},{5,4},{6,7},{7,6},{8,9},{9,8},{10,11... | collective-permute-start | bytes 3981320 | tf_op jit(solution)/shard_map/ppermute | solution.py:1312
  402.3 54.9 %collective-permute-start.12 = (bf16[4,32,1152]{2,1,0:T(8,128)(2,1)}, bf16[4,32,1152]{2,1,0:T(8,128)(2,1)}, u32[]{:S(2)}, u32[]{:S(2)}) collective-permute-start(bf16[4,32,1152]{2,1,0:T(8,128)(2,1)} %get-tuple-element.154), channel_id=1, source_target_pairs={{0,24},{8,0},{16,8},{24,16},{1,25},{9,1},{17,9},{25,17},{2,26},{10... | collective-permute-start | bytes 884744 | tf_op jit(solution)/shard_map/ppermute | solution.py:1271
  404.0 53.2 %collective-permute-start.13 = (bf16[4,32,1152]{2,1,0:T(8,128)(2,1)}, bf16[4,32,1152]{2,1,0:T(8,128)(2,1)}, u32[]{:S(2)}, u32[]{:S(2)}) collective-permute-start(bf16[4,32,1152]{2,1,0:T(8,128)(2,1)} %get-tuple-element.155), channel_id=1, source_target_pairs={{0,16},{8,24},{16,0},{24,8},{1,17},{9,25},{17,1},{25,9},{2,18},{10... | collective-permute-start | bytes 884744 | tf_op jit(solution)/shard_map/ppermute | solution.py:1271
  404.0 53.2 %collective-permute-start.14 = (bf16[4,32,1152]{2,1,0:T(8,128)(2,1)}, bf16[4,32,1152]{2,1,0:T(8,128)(2,1)}, u32[]{:S(2)}, u32[]{:S(2)}) collective-permute-start(bf16[4,32,1152]{2,1,0:T(8,128)(2,1)} %get-tuple-element.156), channel_id=1, source_target_pairs={{0,8},{8,16},{16,24},{24,0},{1,9},{9,17},{17,25},{25,1},{2,10},{10... | collective-permute-start | bytes 884744 | tf_op jit(solution)/shard_map/ppermute | solution.py:1271
  457.2 36.7 %all-to-all-start.2 = ((bf16[32,112,128]{2,1,0:T(8,128)(2,1)}), bf16[32,112,128]{2,1,0:T(8,128)(2,1)S(1)}, u32[]{:S(2)}, u32[]{:S(2)}) async-start(bf16[32,112,128]{2,1,0:T(8,128)(2,1)} %pack_early.1), calls=%async_computation.2 | async-start | bytes 1835008 | tf_op jit(solution)/shard_map/all_to_all | solution.py:1256
  462.8 34.4 %collective-permute-start.15 = (bf16[4,32,1152]{2,1,0:T(8,128)(2,1)S(1)}, bf16[4,32,1152]{2,1,0:T(8,128)(2,1)S(1)}, u32[]{:S(2)}, u32[]{:S(2)}) collective-permute-start(bf16[4,32,1152]{2,1,0:T(8,128)(2,1)S(1)} %copy-done.28), channel_id=1, source_target_pairs={{0,24},{8,0},{16,8},{24,16},{1,25},{9,1},{17,9},{25,17},{2,26},{10... | collective-permute-start | bytes 884744 | tf_op jit(solution)/shard_map/ppermute | solution.py:1271
  466.5 45.0 %collective-permute-start.16 = (bf16[4,32,1152]{2,1,0:T(8,128)(2,1)S(1)}, bf16[4,32,1152]{2,1,0:T(8,128)(2,1)S(1)}, u32[]{:S(2)}, u32[]{:S(2)}) collective-permute-start(bf16[4,32,1152]{2,1,0:T(8,128)(2,1)S(1)} %copy-done.27), channel_id=1, source_target_pairs={{0,16},{8,24},{16,0},{24,8},{1,17},{9,25},{17,1},{25,9},{2,18},{10... | collective-permute-start | bytes 884744 | tf_op jit(solution)/shard_map/ppermute | solution.py:1271
  466.5 45.0 %collective-permute-start.17 = (bf16[4,32,1152]{2,1,0:T(8,128)(2,1)S(1)}, bf16[4,32,1152]{2,1,0:T(8,128)(2,1)S(1)}, u32[]{:S(2)}, u32[]{:S(2)}) collective-permute-start(bf16[4,32,1152]{2,1,0:T(8,128)(2,1)S(1)} %copy-done.26), channel_id=1, source_target_pairs={{0,8},{8,16},{16,24},{24,0},{1,9},{9,17},{17,25},{25,1},{2,10},{10... | collective-permute-start | bytes 884744 | tf_op jit(solution)/shard_map/ppermute | solution.py:1271
  512.3 77.1 %all-to-all-start.3 = ((bf16[4,8,112,128]{3,2,1,0:T(8,128)(2,1)}), bf16[4,8,112,128]{3,2,1,0:T(8,128)(2,1)S(1)}, u32[]{:S(2)}, u32[]{:S(2)}) async-start(bf16[4,8,112,128]{3,2,1,0:T(8,128)(2,1)} %combine.2), calls=%async_computation.3 | async-start | bytes 1835008 | tf_op jit(solution)/shard_map/all_to_all | solution.py:1256
  516.6 39.8 %collective-permute-start.18 = (bf16[4,64,1152]{2,1,0:T(8,128)(2,1)}, bf16[4,64,1152]{2,1,0:T(8,128)(2,1)S(1)}, u32[]{:S(2)}, u32[]{:S(2)}) collective-permute-start(bf16[4,64,1152]{2,1,0:T(8,128)(2,1)} %bitcast.26), channel_id=1, source_target_pairs={{0,24},{8,0},{16,8},{24,16},{1,25},{9,1},{17,9},{25,17},{2,26},{10... | collective-permute-start | bytes 1769480 | tf_op jit(solution)/shard_map/ppermute | solution.py:1271
  520.4 69.0 %collective-permute-start.19 = (bf16[4,64,1152]{2,1,0:T(8,128)(2,1)}, bf16[4,64,1152]{2,1,0:T(8,128)(2,1)S(1)}, u32[]{:S(2)}, u32[]{:S(2)}) collective-permute-start(bf16[4,64,1152]{2,1,0:T(8,128)(2,1)} %bitcast.91), channel_id=1, source_target_pairs={{0,16},{8,24},{16,0},{24,8},{1,17},{9,25},{17,1},{25,9},{2,18},{10... | collective-permute-start | bytes 1769480 | tf_op jit(solution)/shard_map/ppermute | solution.py:1271
  520.4 69.0 %collective-permute-start.20 = (bf16[4,64,1152]{2,1,0:T(8,128)(2,1)S(1)}, bf16[4,64,1152]{2,1,0:T(8,128)(2,1)}, u32[]{:S(2)}, u32[]{:S(2)}) collective-permute-start(bf16[4,64,1152]{2,1,0:T(8,128)(2,1)S(1)} %bitcast.90), channel_id=1, source_target_pairs={{0,8},{8,16},{16,24},{24,0},{1,9},{9,17},{17,25},{25,1},{2,10},{10... | collective-permute-start | bytes 1769480 | tf_op jit(solution)/shard_map/ppermute | solution.py:1271
  556.4 79.4 %copy-start.13 = (bf16[4,64,1152]{2,1,0:T(8,128)(2,1)}, bf16[4,64,1152]{2,1,0:T(8,128)(2,1)S(1)}, u32[]{:S(2)}) copy-start(bf16[4,64,1152]{2,1,0:T(8,128)(2,1)S(1)} %collective-permute-done.18.refs_1_) | copy-start | bytes 1769476
  589.4 46.4 %copy-start.4 = (bf16[4,8,112,128]{3,2,1,0:T(8,128)(2,1)}, bf16[4,8,112,128]{3,2,1,0:T(8,128)(2,1)S(1)}, u32[]{:S(2)}) copy-start(bf16[4,8,112,128]{3,2,1,0:T(8,128)(2,1)S(1)} %all-to-all-done.3.early_ref) | copy-start | bytes 2752516
  611.8 27.9 %all-to-all-start.5 = ((bf16[4,8,80,128]{3,2,1,0:T(8,128)(2,1)}), bf16[4,8,80,128]{3,2,1,0:T(8,128)(2,1)S(1)}, u32[]{:S(2)}, u32[]{:S(2)}) async-start(bf16[4,8,80,128]{3,2,1,0:T(8,128)(2,1)} %combine.3), calls=%async_computation.5 | async-start | bytes 1310720 | tf_op jit(solution)/shard_map/all_to_all | solution.py:1256
  (26 other events, 431.3 us)
Sparse Core Ops, SparseCore 0:
  15.1 86.6 all-gather.4
  103.7 64.0 all-gather.8
  169.7 63.7 all-gather.6
  235.3 63.7 all-gather.10

commit v6 on v5

--- a/solution.py
+++ b/solution.py
@@ -250,31 +250,25 @@
     return pieces[0] if len(pieces) == 1 else jnp.concatenate(pieces, 0)
 
 
-def temporal_cross_forward(parts, *refs):
-    _temporal_cross_forward(refs[:parts], *refs[parts:])
-
-
-def _temporal_cross_forward(
-    x_refs, ctx_ref, mod_ref, mask_ref, ad_ref, wt_hbm, wc_hbm,
-    q_ref, k_ref, v_ref, o_ref, stat_ref, rq_ref, ro_ref,
-    u2_ref, qc_ref, oc_ref, statc_ref, rqc_ref, roc_ref, kp_ref, vp_ref, rk_ref, rv_ref, x3_ref,
-    w_ref, bias_ref, lhs_ref, q_s, k_s, v_s, o_s, sems,
-):
+def temporal_forward(parts, *refs):
+    x_refs, refs = refs[:parts], refs[parts:]
+    (
+        mod_ref, mask_ref, ad_ref, w_hbm,
+        q_ref, k_ref, v_ref, o_ref, stat_ref, rq_ref, ro_ref, u2_ref, x2_ref,
+        w_ref, bias_ref, lhs_ref, q_s, k_s, v_s, sems,
+    ) = refs
     width = x_refs[0].shape[2]
-    first = pl.program_id(0) == 0
-    sources = [wt_hbm.at[i] for i in range(4)] + [wc_hbm.at[i] for i in range(4)]
-    loads = Loads([(w, w_ref.at[i, pl.ds(0, width), :]) for i, w in enumerate(sources)], sems)
+    loads = Loads([(w_hbm.at[i], w_ref.at[i, pl.ds(0, width), :]) for i in range(4)], sems)
     loads.start()
 
-    @pl.when(first)
+    @pl.when(loads.first)
     def _():
         bias_ref[...] = same_place(bias_ref.shape)
         lhs_ref[:, width:] = jnp.zeros((ROWS, PAD), BF16)
-        for i in range(8):
-            w_ref[i, width:, :] = up_rows(ad_ref, 4 + i, i if i < 3 else 0, width)
+        for i in range(4):
+            w_ref[i, width:, :] = up_rows(ad_ref, 4 + i, i % 3, width)
 
     loaded = rows_of(x_refs)
-    stream = loaded.astype(F32)
     lhs_ref[:, :width] = loaded
     three_projections(lhs_ref, ad_ref, 4, w_ref, loads, 0, (q_s, k_s, v_s), rq_ref.at[0])
     q_ref[...] = q_s[...].reshape(q_ref.shape)
@@ -282,33 +276,50 @@
     v_ref[...] = v_s[...].reshape(v_ref.shape)
 
     def put_out(index, value):
-        o_s[:, tile(index)] = value.astype(BF16)
+        lhs_ref[:, tile(index)] = value.astype(BF16)
 
     attend(q_s, k_s, v_s, mask_ref, bias_ref, put_out, stat_ref.at[0])
-    lhs_ref[:, :width] = o_s[...]
-    o_ref[...] = o_s[...].reshape(o_ref.shape)
+    o_ref[...] = lhs_ref[:, :width].reshape(o_ref.shape)
     loads.ready(3)
     branch = one_projection(lhs_ref, ad_ref, 7, w_ref.at[3], ro_ref.at[0])
-    stream = stream + mod_ref[2:3, :] * branch
-    inputs = stream.astype(BF16)
-    u2_ref[...] = inputs.reshape(u2_ref.shape)
-    lhs_ref[:, :width] = inputs
-    loads.ready(4)
-    queries = one_projection(lhs_ref, ad_ref, 8, w_ref.at[4], rqc_ref.at[0])
+    stream = loaded.astype(F32) + mod_ref[2:3, :] * branch
+    u2_ref[...] = stream.astype(BF16).reshape(u2_ref.shape)
+    x2_ref[...] = stream.reshape(x2_ref.shape)
+
+
+def cross_forward(
+    x_ref, ctx_ref, mask_ref, ad_ref, w_hbm,
+    q_ref, o_ref, stat_ref, rq_ref, ro_ref, kp_ref, vp_ref, rk_ref, rv_ref, x3_ref,
+    w_ref, lhs_ref, q_s, k_s, sems,
+):
+    width = x_ref.shape[2]
+    loads = Loads([(w_hbm.at[i], w_ref.at[i, pl.ds(0, width), :]) for i in range(4)], sems)
+    loads.start()
+
+    @pl.when(loads.first)
+    def _():
+        lhs_ref[:, width:] = jnp.zeros((ROWS, PAD), BF16)
+        for i in (0, 3):
+            w_ref[i, width:, :] = up_rows(ad_ref, 8 + i, 0, width)
+
+    stream = x_ref[...].reshape(ROWS, width)
+    lhs_ref[:, :width] = stream.astype(BF16)
+    loads.ready(0)
+    queries = one_projection(lhs_ref, ad_ref, 8, w_ref.at[0], rq_ref.at[0])
     q_s[...] = (queries * EXP_SCALE).astype(BF16)
-    qc_ref[...] = q_s[...].reshape(qc_ref.shape)
-    loads.ready(5)
-    loads.ready(6)
-
-    @pl.when(first)
+    q_ref[...] = q_s[...].reshape(q_ref.shape)
+    loads.ready(1)
+    loads.ready(2)
+
+    @pl.when(loads.first)
     def _():
-        for number, at, rank_ref, pair_ref in ((9, 5, rk_ref, kp_ref), (10, 6, rv_ref, vp_ref)):
+        for number, at, rank_ref, pair_ref in ((9, 1, rk_ref, kp_ref), (10, 2, rv_ref, vp_ref)):
             ranks = nt(ctx_ref[...], ad_ref[2 * number]).astype(BF16)
             rank_ref[...] = ranks
             made = nn(ctx_ref[...], w_ref[at, :width, :]) + nn(ranks, ad_ref[2 * number + 1])
-            k_s[:PAD, :] = made.astype(BF16)
+            k_s[...] = made.astype(BF16)
             for pair in range(PAIRS):
-                piece = k_s[:PAD, window(pair)]
+                piece = k_s[:, window(pair)]
                 pair_ref[pair, :PAD, :] = piece * mask_ref[2 * pair : 2 * pair + 1, :]
                 pair_ref[pair, PAD:, :] = piece * mask_ref[2 * pair + 1 : 2 * pair + 2, :]
 
@@ -322,18 +333,17 @@
             top = jnp.max(own, 0, keepdims=True)
             grown = jnp.exp2(own - top)
             total = jnp.sum(grown, 0, keepdims=True)
-            statc_ref[0, 2 * pair + sub : 2 * pair + sub + 1, :] = top + jnp.log2(total)
+            stat_ref[0, 2 * pair + sub : 2 * pair + sub + 1, :] = top + jnp.log2(total)
             pieces += [grown * (1.0 / total), jnp.zeros((PAD - count, ROWS), F32)]
         weights = jnp.concatenate(pieces, 0).astype(BF16)
         out = tn(weights, vp_ref[pair])
         low = out[:, :128]
-        put_out(pair, low if carried is None else low + carried)
+        lhs_ref[:, tile(pair)] = (low if carried is None else low + carried).astype(BF16)
         carried = out[:, 128:]
-    put_out(PAIRS, carried)
-    lhs_ref[:, :width] = o_s[...]
-    oc_ref[...] = o_s[...].reshape(oc_ref.shape)
-    loads.ready(7)
-    stream = stream + one_projection(lhs_ref, ad_ref, 11, w_ref.at[7], roc_ref.at[0])
+    lhs_ref[:, tile(PAIRS)] = carried.astype(BF16)
+    o_ref[...] = lhs_ref[:, :width].reshape(o_ref.shape)
+    loads.ready(3)
+    stream = stream + one_projection(lhs_ref, ad_ref, 11, w_ref.at[3], ro_ref.at[0])
     x3_ref[...] = stream.reshape(x3_ref.shape)
 
 
@@ -376,42 +386,59 @@
     pieces = refs[:count]
     grad_ref, down_ref, lhs_ref, sems = refs[count:]
     width = cot_ref.shape[1]
-    entries = down_loads(order_ref, pieces, down_ref, width)
+    half = width // 2
+    chunks = count // 2
+    core = order_ref[chunks]
+    entries = []
+    for k in range(chunks):
+        for source, side in ((pieces[k], core), (pieces[chunks + k], 1 - core)):
+            start = pl.multiple_of(k * width + side * half, 16)
+            entries.append((source, down_ref.at[pl.ds(start, half), pl.ds(0, width)]))
     loads = Loads(entries, sems)
     loads.start()
 
     @pl.when(loads.first)
     def _():
         lhs_ref[:, width:] = jnp.zeros((ROWS, PAD), BF16)
-        fill_down_maps(ad_ref, down_ref, width)
+        for k in range(chunks):
+            rows = slice(k * width, (k + 1) * width)
+            down_ref[rows, width:] = transposed_map(ad_ref[2 + (ad_ref.shape[0] - 2) // 2 + order_ref[k]])
 
     branch = (mod_ref[5:6, :] * cot_ref[...].astype(F32)).astype(BF16)
     lhs_ref[:, :width] = branch
     lhs_ref[:, width : width + RANK] = nt(branch, ad_ref[1]).astype(BF16)
     for i in range(len(entries)):
         loads.ready(i)
-    for cols in hidden_chunks(down_ref.shape[0]):
-        grad_ref[:, cols] = nt(lhs_ref[...], down_ref[cols, :]).astype(BF16)
+    for k in range(chunks):
+        rows = slice(k * width, (k + 1) * width)
+        grad_ref[k] = nt(lhs_ref[...], down_ref[rows, :]).astype(BF16)
 
 
 def hidden_chunks(hidden):
     return [slice(at, at + 1536) for at in range(0, hidden, 1536)]
 
 
-def feed_forward(
-    x3_ref, cot_ref, grad_ref, mod_ref, ad_ref, w_hbm,
-    act_ref, g3_ref, gd_ref, gu_ref, up_ref, lhs_ref, dh_ref, sems,
-):
+def feed_forward(groups, count, order_ref, x3_ref, cot_ref, *refs):
+    grad_refs, pieces, refs = refs[:groups], refs[groups : groups + count], refs[groups + count :]
+    (
+        mod_ref, ad_ref, w_hbm, act_ref, g3_ref, gd_ref, gu_ref, up_ref, lhs_ref, dh_ref, sems, *rest
+    ) = refs
     width = x3_ref.shape[1]
     hidden_size = up_ref.shape[1]
     chunks = hidden_size // width
-    loads = Loads(
-        [
-            (w_hbm.at[c], up_ref.at[pl.ds(0, width), pl.ds(c * width, width)])
-            for c in range(chunks)
-        ],
-        sems,
-    )
+    late = count // 2
+    core = order_ref[chunks]
+    entries = [
+        (w_hbm.at[c], up_ref.at[pl.ds(0, width), pl.ds(c * width, width)]) for c in range(chunks)
+    ]
+    if late:
+        down_ref, dlhs_ref = rest
+        half = width // 2
+        for k in range(late):
+            for source, side in ((pieces[k], core), (pieces[late + k], 1 - core)):
+                start = pl.multiple_of(k * width + side * half, 16)
+                entries.append((source, down_ref.at[pl.ds(start, half), pl.ds(0, width)]))
+    loads = Loads(entries, sems)
     loads.start()
 
     @pl.when(loads.first)
@@ -422,18 +449,38 @@
         up_ref[width + RANK :, :] = jnp.zeros((PAD - RANK, hidden_size), BF16)
         for c in range(chunks):
             up_ref[width : width + RANK, c * width : (c + 1) * width] = ad_ref[2 + c]
+        for k in range(late):
+            rows = slice(k * width, (k + 1) * width)
+            at = order_ref[chunks - late + k]
+            down_ref[rows, width:] = transposed_map(ad_ref[2 + chunks + at])
+        if late:
+            dlhs_ref[:, width:] = jnp.zeros((ROWS, PAD), BF16)
 
     normal, inverse = normalize(x3_ref[...])
     inputs = (normal * (1.0 + mod_ref[4:5, :]) + mod_ref[3:4, :]).astype(BF16)
     rank_up = nt(inputs, ad_ref[0]).astype(BF16)
     lhs_ref[:, :width] = inputs
     lhs_ref[:, width : width + RANK] = rank_up
-    for c in range(chunks):
-        loads.ready(c)
+    at = 0
+    for grad_ref in grad_refs:
+        for k in range(grad_ref.shape[0]):
+            start = pl.multiple_of(order_ref[at] * width, 128)
+            dh_ref[:, pl.ds(start, width)] = grad_ref[k]
+            at += 1
+    if late:
+        branch = (mod_ref[5:6, :] * cot_ref[...].astype(F32)).astype(BF16)
+        dlhs_ref[:, :width] = branch
+        dlhs_ref[:, width : width + RANK] = nt(branch, ad_ref[1]).astype(BF16)
+    for i in range(len(entries)):
+        loads.ready(i)
+    for k in range(late):
+        start = pl.multiple_of(order_ref[at + k] * width, 128)
+        rows = slice(k * width, (k + 1) * width)
+        dh_ref[:, pl.ds(start, width)] = nt(dlhs_ref[...], down_ref[rows, :]).astype(BF16)
     for cols in hidden_chunks(hidden_size):
         active, slope = gelu_both(nn(lhs_ref[...], up_ref[:, cols]))
         act_ref[:, cols] = active.astype(BF16)
-        dh_ref[:, cols] = (slope * grad_ref[:, cols].astype(F32)).astype(BF16)
+        dh_ref[:, cols] = (slope * dh_ref[:, cols].astype(F32)).astype(BF16)
     both = nt(dh_ref[...], up_ref[...])
     gu_ref[...] += tn(rank_up, dh_ref[...])
     grad_rank = both[:, width : width + RANK].astype(BF16)
@@ -459,6 +506,7 @@
         gd_ref[...] = jnp.zeros_like(gd_ref)
         fill_down_maps(ad_ref, down_ref, width)
 
+    share = x4_refs[0].shape[0]
     grad_branch = (mod_ref[5:6, :] * cot_ref[...].astype(F32)).astype(BF16)
     gd_ref[...] += tn(nt(grad_branch, ad_ref[1]).astype(BF16), act_ref[...])
     for i in range(len(entries)):
@@ -468,7 +516,6 @@
     branch = both[:, :width] + nn(ranks, ad_ref[1])
     gu_ref[...] += tn(ranks, grad_branch)
     result = (x3_ref[...] + mod_ref[5:6, :] * branch).astype(BF16)
-    share = x4_refs[0].shape[0]
     for k, ref in enumerate(x4_refs):
         at = k * share
 
@@ -614,21 +661,27 @@
             put_blocks(blocks, put)
 
 
-def stacked(seq_ref, g1_refs, halves, whole_ref):
-    parts = len(g1_refs) // halves
-    part = g1_refs[0].shape[1]
-    for half in range(halves):
-        for k in range(parts):
-            start = place_of(seq_ref, k, parts, part * halves) + half * part
-            whole_ref[pl.ds(pl.multiple_of(start, 16), part), :] = g1_refs[half * parts + k][0]
+def stacked(seq_ref, g1_refs, shares, whole_ref):
+    parts = len(g1_refs) // shares
+    places = whole_ref.shape[0] // parts
+    at = 0
+    for share in range(shares):
+        refs = g1_refs[share * parts : (share + 1) * parts]
+        size = refs[0].shape[1]
+        for k, ref in enumerate(refs):
+            start = pl.multiple_of(place_of(seq_ref, k, parts, places) + at, 16)
+            whole_ref[pl.ds(start, size), :] = ref[0]
+        at += size
     return whole_ref[...].astype(F32)
 
 
-def spatial_backward(pieces, halves, clips, seq_ref, *refs):
+def spatial_backward(pieces, halves, clips, continued, last, seq_ref, *refs):
     g1_refs, refs = refs[:pieces], refs[pieces:]
+    if continued:
+        (_, before_ref), refs = refs[:2], refs[2:]
     (
         x_ref, q_ref, k_ref, v_ref, o_ref, stat_ref, rq_ref, ro_ref, mod_ref, mask_ref, ad_ref, w_hbm,
-        down_ref, up_ref, d_ref, packed_ref, w_ref, gw_ref, do_s, sems,
+        d_ref, sums_ref, w_ref, gw_ref, do_s, sems,
     ) = refs
     width = x_ref.shape[2]
     loads = Loads([(w_hbm.at[3], w_ref.at[pl.ds(0, width), :])], sems)
@@ -636,7 +689,7 @@
 
     @pl.when(loads.first)
     def _():
-        gw_ref[...] = jnp.zeros_like(gw_ref)
+        gw_ref[...] = before_ref[...] if continued else jnp.zeros_like(gw_ref)
         w_ref[width:, :] = up_rows(ad_ref, 3, 0, width)
 
     grad = stacked(seq_ref, g1_refs, halves, do_s)
@@ -669,10 +722,10 @@
 
     @pl.when(pl.program_id(0) == pl.num_programs(0) - 1)
     def _():
-        at = 8 * RANK
-        gw_ref[at : at + RANK, :] = down_ref[...]
-        gw_ref[at + RANK : at + RANK + up_ref.shape[0], :] = up_ref[...]
-        pack_columns(gw_ref, packed_ref, clips)
+        if last:
+            pack_columns(gw_ref, sums_ref, clips)
+        else:
+            sums_ref[...] = gw_ref[...]
 
 
 def spatial_input_grad(pieces, halves, seq_ref, *refs):
@@ -704,11 +757,11 @@
         out_ref[0, pl.ds(place_of(seq_ref, k, len(pieces), places), places), :] = ref[0]
 
 
-def pack_early(clips, halves, *refs):
-    gw_refs, refs = refs[:halves], refs[halves:]
-    dk_refs, refs = refs[:halves], refs[halves:]
-    dv_refs, refs = refs[:halves], refs[halves:]
-    down_ref, up_ref, rk_ref, rv_ref, ctx_ref, mask_ref, ad_ref, packed_ref, table_ref, ctx_s = refs
+def pack_early(clips, shares, *refs):
+    gw_refs, refs = refs[:shares], refs[shares:]
+    dk_refs, refs = refs[:shares], refs[shares:]
+    dv_refs, refs = refs[:shares], refs[shares:]
+    *others, rk_ref, rv_ref, ctx_ref, mask_ref, ad_ref, packed_ref, table_ref, ctx_s = refs
 
     def added(each):
         total = each[0]
@@ -718,11 +771,12 @@
 
     at = gw_refs[0].shape[0]
     table_ref[:at, :] = added([ref[...] for ref in gw_refs])
-    table_ref[at : at + RANK, :] = down_ref[...]
-    at += RANK
-    table_ref[at : at + up_ref.shape[0], :] = up_ref[...]
-    at += up_ref.shape[0]
-    table_ref[at:, :] = jnp.zeros((table_ref.shape[0] - at, table_ref.shape[1]), F32)
+    width = table_ref.shape[1]
+    for ref in others:
+        for k in range(ref.shape[1] // width):
+            table_ref[at : at + RANK, :] = ref[:, k * width : (k + 1) * width]
+            at += RANK
+    table_ref[at:, :] = jnp.zeros((table_ref.shape[0] - at, width), F32)
     context = ctx_ref[...].astype(F32)
     for accs, factor, rank_ref, number, at in (
         (dk_refs, LN2, rk_ref, 9, 10),
@@ -753,7 +807,13 @@
     pack_columns(table_ref, packed_ref, clips)
 
 
-def assemble(early_ref, late_ref, wide_ref, narrow_ref):
+def assemble(parts, seq_ref, *refs):
+    early_refs, late_refs, refs = refs[:parts], refs[parts : 2 * parts], refs[2 * parts :]
+    wide_ref, narrow_ref, early_ref, late_ref = refs
+    for k in range(parts):
+        source = lax.rem(seq_ref[0] + parts - k, parts)
+        early_ref[source] = early_refs[k][...]
+        late_ref[source] = late_refs[k][...]
     _, adapters, _, cols = wide_ref.shape
     times = narrow_ref.shape[3] // cols
 
@@ -768,15 +828,11 @@
     for a in range(adapters):
         for i in range(8):
             wide_ref[i, a] = block(late_ref, LATE_BLOCKS, i, a)
-        for i in range(17):
+        for i in range(18):
             wide_ref[8 + i, a] = block(early_ref, EARLY_BLOCKS, i, a)
-        wide_ref[25, a] = block(late_ref, LATE_BLOCKS, 8, a)
-        narrow_ref[0, a] = jnp.concatenate(
-            [block(early_ref, EARLY_BLOCKS, 17 + j, a) for j in range(times)], 1
-        )
-        narrow_ref[1, a] = jnp.concatenate(
-            [block(late_ref, LATE_BLOCKS, 9 + j, a) for j in range(times)], 1
-        )
+        for n in range(2):
+            pieces = [block(early_ref, EARLY_BLOCKS, 18 + n * times + j, a) for j in range(times)]
+            narrow_ref[n, a] = jnp.concatenate(pieces, 1)
 
 
 def combine(index_ref, got_ref, out_ref, acc_ref):
@@ -792,9 +848,7 @@
         return carry
 
     lax.fori_loop(0, clips, step, 0)
-    table = acc_ref[...].astype(BF16)
-    for s in range(parts):
-        out_ref[s] = table
+    out_ref[...] = acc_ref[...].astype(BF16)
 
 
 def pick(index_ref, wide_ref, narrow_ref, out_ref):
@@ -847,8 +901,10 @@
 )
 
 
-def cost(flops, read):
-    return pl.CostEstimate(flops=flops, bytes_accessed=read, transcendentals=flops // 4096)
+def cost(flops, read, part=4):
+    return pl.CostEstimate(
+        flops=flops // part, bytes_accessed=read // part, transcendentals=0
+    )
 
 
 def run_spatial_forward(seq, video, mods, masks, wide, w_s, parts):
@@ -889,7 +945,7 @@
     )(seq, video, mods, masks, wide, w_s)
 
 
-def run_temporal_cross_forward(x1, context, mods, masks, wide, w_t, w_c):
+def run_temporal_forward(x1, mods, masks, wide, w_t):
     parts = len(x1)
     own_frames, places, d = x1[0].shape
     frames = own_frames * parts
@@ -897,46 +953,76 @@
     each = ROWS // frames
     across = pl.BlockSpec((frames, each, d), lambda i: (0, i, 0))
     by_group = lambda i: (i, 0, 0)
-    stat = pl.BlockSpec((1, HEADS, ROWS), by_group)
-    three = pl.BlockSpec((1, ROWS, 3 * RANK), by_group)
-    one = pl.BlockSpec((1, ROWS, RANK), by_group)
-    full = lambda *shape: pl.BlockSpec(shape, lambda i: (0,) * len(shape))
     act = like((frames, places, d), BF16)
 
     def body(*refs):
-        temporal_cross_forward(parts, *refs)
-
-    stat_shape = like((groups, HEADS, ROWS), F32)
-    one_shape = like((groups, ROWS, RANK), BF16)
+        temporal_forward(parts, *refs)
+
     return pl.pallas_call(
         body,
         grid=(groups,),
         in_specs=[pl.BlockSpec((own_frames, each, d), lambda i: (0, i, 0))] * parts
-        + [whole_block(context), whole_block(mods), whole_block(masks), whole_block(wide), anywhere(), anywhere()],
-        out_specs=[across] * 4 + [stat, three, one] + [across] * 3 + [stat, one, one]
+        + [whole_block(mods), whole_block(masks), whole_block(wide), anywhere()],
+        out_specs=[across] * 4
+        + [
+            pl.BlockSpec((1, HEADS, ROWS), by_group),
+            pl.BlockSpec((1, ROWS, 3 * RANK), by_group),
+            pl.BlockSpec((1, ROWS, RANK), by_group),
+            across,
+            across,
+        ],
+        out_shape=[act] * 4
+        + [
+            like((groups, HEADS, ROWS), F32),
+            like((groups, ROWS, 3 * RANK), BF16),
+            like((groups, ROWS, RANK), BF16),
+            act,
+            like((frames, places, d), F32),
+        ],
+        scratch_shapes=[pltpu.VMEM((4, d + PAD, d), BF16), pltpu.VMEM((ROWS, ROWS), F32)]
+        + [pltpu.VMEM((ROWS, d + PAD), BF16)]
+        + [pltpu.VMEM((ROWS, d), BF16)] * 3
+        + [pltpu.SemaphoreType.DMA((4,))],
+        compiler_params=PARAMS,
+        cost_estimate=cost(10 * places * frames * d * d, 30_000_000),
+        name="temporal_forward",
+    )(*x1, mods, masks, wide, w_t)
+
+
+def run_cross_forward(x2, context, masks, wide, w_c):
+    frames, places, d = x2.shape
+    groups = places * frames // ROWS
+    across = pl.BlockSpec((frames, ROWS // frames, d), lambda i: (0, i, 0))
+    by_group = lambda i: (i, 0, 0)
+    full = lambda *shape: pl.BlockSpec(shape, lambda i: (0,) * len(shape))
+    one = pl.BlockSpec((1, ROWS, RANK), by_group)
+    one_shape = like((groups, ROWS, RANK), BF16)
+    act = like((frames, places, d), BF16)
+    return pl.pallas_call(
+        cross_forward,
+        grid=(groups,),
+        in_specs=[across, whole_block(context), whole_block(masks), whole_block(wide), anywhere()],
+        out_specs=[across] * 2 + [pl.BlockSpec((1, HEADS, ROWS), by_group), one, one]
         + [full(PAIRS, 2 * PAD, 256)] * 2 + [full(PAD, RANK)] * 2 + [across],
-        out_shape=[act] * 4 + [stat_shape, like((groups, ROWS, 3 * RANK), BF16), one_shape]
-        + [act] * 3 + [stat_shape, one_shape, one_shape]
+        out_shape=[act] * 2 + [like((groups, HEADS, ROWS), F32), one_shape, one_shape]
         + [like((PAIRS, 2 * PAD, 256), BF16)] * 2 + [like((PAD, RANK), BF16)] * 2
-        + [like((frames, places, d), F32)],
-        scratch_shapes=[pltpu.VMEM((8, d + PAD, d), BF16), pltpu.VMEM((ROWS, ROWS), F32)]
-        + [pltpu.VMEM((ROWS, d + PAD), BF16)]
-        + [pltpu.VMEM((ROWS, d), BF16)] * 4
-        + [pltpu.SemaphoreType.DMA((8,))],
+        + [like(x2.shape, F32)],
+        scratch_shapes=[pltpu.VMEM((4, d + PAD, d), BF16), pltpu.VMEM((ROWS, d + PAD), BF16)]
+        + [pltpu.VMEM((ROWS, d), BF16), pltpu.VMEM((PAD, d), BF16)]
+        + [pltpu.SemaphoreType.DMA((4,))],
         compiler_params=PARAMS,
-        cost_estimate=cost(14 * places * frames * d * d, 50_000_000),
-        name="temporal_cross_forward",
-    )(*x1, context, mods, masks, wide, w_t, w_c)
+        cost_estimate=cost(8 * places * frames * d * d, 30_000_000),
+        name="cross_forward",
+    )(x2, context, masks, wide, w_c)
 
 
 def in_smem():
     return pl.BlockSpec(memory_space=pltpu.SMEM)
 
 
-def run_feed_forward_grad(cot, mods, maps, down):
+def run_feed_forward_grad(cot, mods, maps, order, pieces):
     tokens, d = cot.shape
-    order, *pieces = down
-    hidden = len(pieces) // 2 * d
+    chunks = len(pieces) // 2
 
     def body(*refs):
         feed_forward_grad(len(pieces), *refs)
@@ -946,28 +1032,37 @@
         grid=(tokens // ROWS,),
         in_specs=[in_smem(), pl.BlockSpec((ROWS, d), lambda i: (i, 0)), whole_block(mods), whole_block(maps)]
         + [anywhere()] * len(pieces),
-        out_specs=pl.BlockSpec((ROWS, hidden), lambda i: (i, 0)),
-        out_shape=like((tokens, hidden), BF16),
+        out_specs=pl.BlockSpec((chunks, ROWS, d), lambda i: (0, i, 0)),
+        out_shape=like((chunks, tokens, d), BF16),
         scratch_shapes=[
-            pltpu.VMEM((hidden, d + PAD), BF16),
+            pltpu.VMEM((chunks * d, d + PAD), BF16),
             pltpu.VMEM((ROWS, d + PAD), BF16),
             pltpu.SemaphoreType.DMA((len(pieces),)),
         ],
         compiler_params=PARAMS,
-        cost_estimate=cost(2 * tokens * d * hidden, 30_000_000),
+        cost_estimate=cost(2 * tokens * d * d * chunks, 20_000_000),
         name="feed_forward_grad",
     )(order, cot, mods, maps, *pieces)
 
 
-def run_feed_forward(x3, cot, grad_active, mods, maps, up):
+def run_feed_forward(x3, cot, order, grad_active, pieces, mods, maps, up):
     tokens, d = x3.shape
     chunks = up.shape[0]
+    late = len(pieces) // 2
     rows = pl.BlockSpec((ROWS, d), lambda i: (i, 0))
     wide_rows = pl.BlockSpec((ROWS, chunks * d), lambda i: (i, 0))
+    more = [pltpu.VMEM((late * d, d + PAD), BF16), pltpu.VMEM((ROWS, d + PAD), BF16)] if late else []
+
+    def body(*refs):
+        feed_forward(len(grad_active), len(pieces), *refs)
+
     return pl.pallas_call(
-        feed_forward,
+        body,
         grid=(tokens // ROWS,),
-        in_specs=[rows, rows, wide_rows, whole_block(mods), whole_block(maps), anywhere()],
+        in_specs=[in_smem(), rows, rows]
+        + [pl.BlockSpec((g.shape[0], ROWS, d), lambda i: (0, i, 0)) for g in grad_active]
+        + [anywhere()] * len(pieces)
+        + [whole_block(mods), whole_block(maps), anywhere()],
         out_specs=[
             wide_rows,
             rows,
@@ -984,30 +1079,34 @@
             pltpu.VMEM((d + PAD, chunks * d), BF16),
             pltpu.VMEM((ROWS, d + PAD), BF16),
             pltpu.VMEM((ROWS, chunks * d), BF16),
-            pltpu.SemaphoreType.DMA((chunks,)),
+            pltpu.SemaphoreType.DMA((chunks + len(pieces),)),
+            *more,
         ],
         compiler_params=PARAMS,
         cost_estimate=cost(4 * tokens * d * d * chunks, 50_000_000),
         name="feed_forward",
-    )(x3, cot, grad_active, mods, maps, up)
-
-
-def run_feed_forward_out(active, x3, cot, mods, maps, down, parts):
+    )(order, x3, cot, *grad_active, *pieces, mods, maps, up)
+
+
+def run_feed_forward_out(active, x3, cot, mods, maps, down, parts, half, halves):
     tokens, d = x3.shape
     order, *pieces = down
     hidden = active.shape[1]
     share = tokens // parts
+    parts = parts // halves
+    steps = tokens // ROWS // halves
+    start = half * steps
 
     def body(*refs):
         feed_forward_out(len(pieces), *refs)
 
-    rows = pl.BlockSpec((ROWS, d), lambda i: (i, 0))
+    rows = pl.BlockSpec((ROWS, d), lambda i: (i + start, 0))
     return pl.pallas_call(
         body,
-        grid=(tokens // ROWS,),
+        grid=(steps,),
         in_specs=[
             in_smem(),
-            pl.BlockSpec((ROWS, hidden), lambda i: (i, 0)),
+            pl.BlockSpec((ROWS, hidden), lambda i: (i + start, 0)),
             rows,
             rows,
             whole_block(mods),
@@ -1029,18 +1128,16 @@
             pltpu.SemaphoreType.DMA((len(pieces),)),
         ],
         compiler_params=PARAMS,
-        cost_estimate=cost(2 * tokens * d * hidden, 30_000_000),
+        cost_estimate=cost(2 * steps * ROWS * d * hidden, 20_000_000, 64),
         name="feed_forward_out",
     )(order, active, x3, cot, mods, maps, *pieces)
 
 
-def run_cross_temporal_backward(g3, u1, saved, mods, masks, wide, w_t, w_c, half, halves):
+def run_cross_temporal_backward(g3, u1, saved, mods, masks, wide, w_t, w_c, start, groups):
     parts = len(u1)
     own_frames, places, d = u1[0].shape
     frames = own_frames * parts
     each = ROWS // frames
-    groups = places * frames // ROWS // halves
-    start = half * groups
     across = pl.BlockSpec((frames, ROWS // frames, d), lambda i: (0, i + start, 0))
     by_group = lambda i: (i + start, 0, 0)
     stat = pl.BlockSpec((1, HEADS, ROWS), by_group)
@@ -1065,7 +1162,7 @@
             pair_sums,
             pair_sums,
         ],
-        out_shape=[like((own_frames, places // halves, d), BF16)] * parts
+        out_shape=[like((own_frames, groups * each, d), BF16)] * parts
         + [like((16 * RANK, d), F32)]
         + [like((PAIRS, 2 * PAD, 256), F32)] * 2,
         scratch_shapes=[
@@ -1075,29 +1172,35 @@
         + [pltpu.VMEM((ROWS, d), BF16)] * 7
         + [pltpu.SemaphoreType.DMA((6,))],
         compiler_params=PARAMS,
-        cost_estimate=cost(14 * places // halves * frames * d * d, 30_000_000),
+        cost_estimate=cost(14 * groups * ROWS * d * d, 30_000_000, 64),
         name="cross_temporal_backward",
     )(*u1, g3, *saved[:15], mods, masks, wide, w_t, w_c)
 
 
-LATE_BLOCKS = 16
-EARLY_BLOCKS = 24
-
-
-def run_spatial_backward(seq, g1, halves, video, saved, mods, masks, wide, w_s, late_down, late_up, clips):
+LATE_BLOCKS = 8
+EARLY_BLOCKS = 28
+
+
+def run_spatial_backward(seq, g1, halves, video, saved, mods, masks, wide, w_s, clips, start, count, before):
     frames, rows, d = video.shape
     parts = len(g1) // halves
-    by_frame = lambda i: (i, 0, 0)
+    by_frame = lambda i: (i + start, 0, 0)
     row_block = pl.BlockSpec((1, rows, d), by_frame)
-    packed = (clips * parts, *packed_rows(LATE_BLOCKS // parts, d // clips))
+    last = start + count == frames
+    sums = (8 * RANK, d)
+    if last:
+        sums = (clips * parts, *packed_rows(LATE_BLOCKS // parts, d // clips))
+    zeros = (0,) * len(sums)
 
     def body(*refs):
-        spatial_backward(len(g1), halves, clips, *refs)
-
+        spatial_backward(len(g1), halves, clips, bool(before), last, *refs)
+
+    extra = [anywhere(), whole_block(before[1])] if before else []
     return pl.pallas_call(
         body,
-        grid=(frames,),
+        grid=(count,),
         in_specs=[in_smem()] + [pl.BlockSpec((1, g.shape[1], d), by_frame) for g in g1]
+        + extra
         + [row_block] * 5
         + [
             pl.BlockSpec((1, HEADS, rows), by_frame),
@@ -1107,20 +1210,19 @@
             whole_block(masks),
             whole_block(wide),
             anywhere(),
-            whole_block(late_down),
-            whole_block(late_up),
         ],
         out_specs=[
             pl.BlockSpec((1, rows, 3 * d + PAD), by_frame),
-            pl.BlockSpec(packed, lambda i: (0, 0, 0)),
-        ],
-        out_shape=[like((frames, rows, 3 * d + PAD), BF16), like(packed, BF16)],
+            pl.BlockSpec(sums, lambda i: zeros),
+        ],
+        out_shape=[like((frames, rows, 3 * d + PAD), BF16), like(sums, BF16 if last else F32)],
+        input_output_aliases={1 + len(g1): 0} if before else {},
         scratch_shapes=[pltpu.VMEM((d + PAD, d), BF16), pltpu.VMEM((LATE_BLOCKS * RANK, d), F32)]
         + [pltpu.VMEM((ROWS, d), BF16), pltpu.SemaphoreType.DMA((1,))],
         compiler_params=PARAMS,
-        cost_estimate=cost(6 * frames * rows * d * d, 30_000_000),
+        cost_estimate=cost(6 * count * rows * d * d, 20_000_000, 64),
         name="spatial_backward",
-    )(seq, *g1, video, *saved, mods, masks, wide, w_s, late_down, late_up)
+    )(seq, *g1, *before, video, *saved, mods, masks, wide, w_s)
 
 
 def run_spatial_input_grad(seq, g1, halves, video, grads, mods, wide, w_s):
@@ -1150,7 +1252,7 @@
             pltpu.SemaphoreType.DMA((3,)),
         ],
         compiler_params=PARAMS,
-        cost_estimate=cost(6 * frames * rows * d * d, 20_000_000),
+        cost_estimate=cost(6 * frames * rows * d * d, 20_000_000, 64),
         name="spatial_input_grad",
     )(seq, *g1, video, grads, mods, wide, w_s)
 
@@ -1166,7 +1268,7 @@
         out_specs=pl.BlockSpec((1, rows, d), by_frame),
         out_shape=like((frames, rows, d), BF16),
         compiler_params=PARAMS,
-        cost_estimate=cost(0, 4 * frames * rows * d),
+        cost_estimate=cost(0, 4 * frames * rows * d, 64),
         name="put_in_place",
     )(seq, *pieces)
 
@@ -1190,21 +1292,27 @@
         out_shape=like(packed, BF16),
         scratch_shapes=[pltpu.VMEM((EARLY_BLOCKS * RANK, d), F32), pltpu.VMEM((PAD, d), F32)],
         compiler_params=PLAIN,
-        cost_estimate=cost(50000000, 8000000),
+        cost_estimate=cost(50000000, 8000000, 64),
         name="pack_early",
     )(*gw, *dk, *dv, *sources)
 
 
-def run_assemble(early, late, wide_shape, narrow_shape):
+def run_assemble(seq, early, late, wide_shape, narrow_shape):
+    parts = len(early)
+
+    def body(*refs):
+        assemble(parts, *refs)
+
     return pl.pallas_call(
-        assemble,
-        in_specs=[in_vmem()] * 2,
+        body,
+        in_specs=[in_smem()] + [in_vmem()] * (2 * parts),
         out_specs=[in_vmem()] * 2,
         out_shape=[like(wide_shape, F32), like(narrow_shape, F32)],
+        scratch_shapes=[pltpu.VMEM((parts, *piece.shape), BF16) for piece in (early[0], late[0])],
         compiler_params=PLAIN,
-        cost_estimate=cost(0, 6000000),
+        cost_estimate=cost(0, 6_000_000, 64),
         name="assemble",
-    )(early, late)
+    )(seq, *early, *late)
 
 
 def run_pick(all_index, wide, narrow):
@@ -1237,17 +1345,15 @@
 
 
 def run_combine(all_index, got, adapters):
-    clips = all_index.shape[0]
-    parts = got.shape[0] // clips
     _, share, cols = got.shape
     return pl.pallas_call(
         combine,
         in_specs=[pl.BlockSpec(memory_space=pltpu.SMEM), pl.BlockSpec(memory_space=pltpu.VMEM)],
         out_specs=pl.BlockSpec(memory_space=pltpu.VMEM),
-        out_shape=like((parts, adapters, share, cols), BF16),
+        out_shape=like((adapters, share, cols), BF16),
         scratch_shapes=[pltpu.VMEM((adapters, share, cols), F32)],
         compiler_params=pltpu.CompilerParams(vmem_limit_bytes=VMEM_LIMIT),
-        cost_estimate=cost(0, 1000000),
+        cost_estimate=cost(0, 1000000, 64),
         name="combine",
     )(all_index, got)
 
@@ -1292,28 +1398,20 @@
     return got, (first, other, send(first, "seq", 1))
 
 
-def spread_down(started, down, arrived, parts, times, clips, d):
-    half = d // 2
-    if started is None:
-        whole = gather(down.reshape(times, -1, d))
-        return [whole[i, side * half : (side + 1) * half] for side in range(2) for i in range(times)], arrived
-    first, other, second = started
-    later, second, *arrived = lax.optimization_barrier((first, second, *arrived))
-    mine = [first, second] + [send(later, "seq", k) for k in range(2, parts)]
-    return mine + [other], arrived
-
-
-def swap_down(pieces, after, parts, times, clips):
-    if len(pieces) == 2 * times:
-        return [jnp.arange(times + 1, dtype=jnp.int32) % times, *pieces], after
-    *mine, other = pieces
-    after, *mine = lax.optimization_barrier((after, *mine))
-    swap = [(i, i ^ 1) for i in range(clips)]
-    others = [other] + [lax.ppermute(piece, "fsdp", swap) for piece in mine[1:]]
+def swap_cores(piece, clips):
+    return lax.ppermute(piece, "fsdp", [(i, i ^ 1) for i in range(clips)])
+
+
+def to_all(piece):
+    return [piece] + [send(piece, "seq", k) for k in range(1, lax.axis_size("seq"))]
+
+
+def down_order(times, parts, clips):
+    if times != parts or clips % 2:
+        return jnp.arange(times, dtype=jnp.int32), jnp.zeros((1,), jnp.int32)
     seq = lax.axis_index("seq")
     core = lax.axis_index("fsdp") % 2
-    order = jnp.concatenate([(seq - jnp.arange(parts)) % parts, core[None]]).astype(jnp.int32)
-    return [order, *mine, *others], after
+    return ((seq - jnp.arange(parts)) % parts).astype(jnp.int32), core.astype(jnp.int32)[None]
 
 
 def on_device(
@@ -1336,6 +1434,7 @@
     times = adapt_ff.shape[-1] // cols
     places = SPATIAL // parts
     frames = FRAMES // parts
+    half_d = d // 2
     mods = modulation[0, 0]
     masks = head_masks()
     ctx = jnp.pad(context[0], ((0, PAD - context.shape[1]), (0, 0)))
@@ -1367,45 +1466,85 @@
     cot = jnp.concatenate(cot, 0).reshape(FRAMES * places, d)
     made = run_spatial_forward(seq, frames_in, mods, masks, wide, w_s, parts)
     u1, kept_s = to_places(made[:parts]), made[parts:]
-    pieces, u1 = spread_down(started, ffn_down[0], u1, parts, times, clips, d)
-    *kept_t, x3 = run_temporal_cross_forward(u1, ctx, mods, masks, wide, w_t, w_c)
-    down, x3 = swap_down(pieces, x3.reshape(FRAMES * places, d), parts, times, clips)
-    grad_active = run_feed_forward_grad(cot, mods, maps_f, down)
-    active, g3, grad_a24, grad_b24 = run_feed_forward(x3, cot, grad_active, mods, maps_f, up)
+    order, core = down_order(times, parts, clips)
+    if started is None:
+        whole_down = gather(ffn_down[0].reshape(times, -1, d))
+        sides = [[whole_down[i, :half_d] for i in range(times)], [whole_down[i, half_d:] for i in range(times)]]
+        *kept_t, x2 = run_temporal_forward(u1, mods, masks, wide, w_t)
+        *kept_c, x3 = run_cross_forward(x2, ctx, masks, wide, w_c)
+        late_pieces = []
+        grad_active = [
+            run_feed_forward_grad(cot, mods, maps_f, jnp.concatenate([order, core]), sides[0] + sides[1])
+        ]
+    else:
+        first, other, second = started
+        later, second, *u1 = lax.optimization_barrier((first, second, *u1))
+        mine = [first, second] + [send(later, "seq", k) for k in range(3, parts)]
+        last = send(later, "seq", 2)
+        *kept_t, x2 = run_temporal_forward(u1, mods, masks, wide, w_t)
+        x2, *mine = lax.optimization_barrier((x2, *mine))
+        others = [other] + [swap_cores(piece, clips) for piece in mine[1:]]
+        order = jnp.concatenate([order[:2], order[3:], order[2:3]])
+        early_order = jnp.concatenate([order[:-1], core])
+        *kept_c, x3 = run_cross_forward(x2, ctx, masks, wide, w_c)
+        mine[0], x3 = lax.optimization_barrier((mine[0], x3))
+        grad_early = run_feed_forward_grad(cot, mods, maps_f, early_order, mine + others)
+        last, grad_early = lax.optimization_barrier((last, grad_early))
+        last_other = swap_cores(last, clips)
+        grad_active = [grad_early]
+        late_pieces = [last, last_other]
+        sides = [mine + [last], others + [last_other]]
+    down = [jnp.concatenate([order, core]), *sides[0], *sides[1]]
+    x3 = x3.reshape(FRAMES * places, d)
+    active, g3, grad_a24, grad_b24 = run_feed_forward(
+        x3, cot, jnp.concatenate([order, core]), grad_active, late_pieces, mods, maps_f, up
+    )
     g3 = g3.reshape(FRAMES, places, d)
     groups = FRAMES * places // ROWS
-    halves = 2 if groups % 2 == 0 else 1
+    saved = kept_t + kept_c
+    *x4, grad_b25, grad_down = run_feed_forward_out(
+        active, x3, cot, mods, maps_f, down, parts, 0, 1
+    )
+    x4[0], g3 = lax.optimization_barrier((x4[0], g3))
+    output = to_frames([piece.reshape(frames, places, d) for piece in x4])
+    shares = [groups - 1, 1] if groups > 1 else [1]
     g1, gw, dk, dv = [], [], [], []
-    for half in range(halves):
-        *pieces, gw_half, dk_half, dv_half = run_cross_temporal_backward(
-            g3, u1, kept_t, mods, masks, wide, w_t, w_c, half, halves
+    for share, size in enumerate(shares):
+        *pieces, gw_part, dk_part, dv_part = run_cross_temporal_backward(
+            g3, u1, saved, mods, masks, wide, w_t, w_c, sum(shares[:share]), size
         )
-        gw.append(gw_half)
-        dk.append(dk_half)
-        dv.append(dv_half)
+        gw.append(gw_part)
+        dk.append(dk_part)
+        dv.append(dv_part)
+        pieces[0], g3 = lax.optimization_barrier((pieces[0], g3))
+        if share == 0:
+            g3, *output = lax.optimization_barrier((g3, *output))
         g1.append(to_frames(pieces))
-
-    def as_blocks(rows):
-        return rows.reshape(RANK, times, d).transpose(1, 0, 2).reshape(times * RANK, d)
-
-    sources = [grad_a24, as_blocks(grad_b24), kept_t[15], kept_t[16], ctx, masks, wide]
+    sources = [grad_a24, grad_b25, grad_b24, grad_down, kept_c[7], kept_c[8], ctx, masks, wide]
     packed = run_pack_early(gw, dk, dv, sources, clips, parts)
-    active, packed, *g1[0] = lax.optimization_barrier((active, packed, *g1[0]))
-    *x4, grad_b25, grad_down = run_feed_forward_out(active, x3, cot, mods, maps_f, down, parts)
-    early, *x4 = lax.optimization_barrier((exchange(packed, ("fsdp", "seq")), *x4))
-    early = run_combine(all_index, early, adapters)
-    output = to_frames([piece.reshape(frames, places, d) for piece in x4])
-    g1 = [piece for pieces in g1 for piece in pieces]
-    early, *g1 = lax.optimization_barrier((early, *g1))
-    grads, packed = run_spatial_backward(
-        seq, g1, halves, frames_in, kept_s, mods, masks, wide, w_s, grad_b25, as_blocks(grad_down), clips
-    )
-    early = exchange(early)
-    packed, early, *output = lax.optimization_barrier((packed, early, *output))
+    g1 = [piece for done in g1 for piece in done]
+    packed, *g1 = lax.optimization_barrier((packed, *g1))
+    got = exchange(packed, ("fsdp", "seq"))
+    halves = len(shares)
+    before = []
+    spatial = [frames - frames // 2, frames // 2] if frames > 1 else [1]
+    for turn, size in enumerate(spatial):
+        grads, sums = before = run_spatial_backward(
+            seq, g1, halves, frames_in, kept_s, mods, masks, wide, w_s, clips, sum(spatial[:turn]), size, before
+        )
+        if turn == 0:
+            got, sums = lax.optimization_barrier((got, sums))
+            table = run_combine(all_index, got, adapters)
+            if len(spatial) > 1:
+                table, sums = lax.optimization_barrier((table, sums))
+            early = to_all(table)
+        before = [grads, sums]
+    packed, *early = lax.optimization_barrier((sums, *early))
     g0 = run_spatial_input_grad(seq, g1, halves, frames_in, grads, mods, wide, w_s)
-    late = run_combine(all_index, exchange(packed, ("fsdp", "seq")), adapters)
+    got, g0 = lax.optimization_barrier((exchange(packed, ("fsdp", "seq")), g0))
+    late = run_combine(all_index, got, adapters)
     wide_out, narrow_out = run_assemble(
-        early, exchange(late), adapt_wide.shape[1:], adapt_ff.shape[1:]
+        seq, early, to_all(late), adapt_wide.shape[1:], adapt_ff.shape[1:]
     )
     output = run_put_in_place(seq, output).reshape(video.shape)
     return (output, g0.reshape(video.shape), wide_out[None], narrow_out[None])

time: 662 us -> 617 us (0.932)
  waiting for transfers between devices: 169 us -> 107 us
  Pallas kernels: 341 us -> 370 us
  blocking collectives: 29.9 us -> 9.63 us
  starting transfers between devices: 54.9 us -> 62.1 us
    ppermute x18 -> x24, waiting for transfers between devices: 136 us -> 53.4 us  [send(): lax.ppermute(array, axis, [(i, (i + shift) % size) for i in range(size)])]
    pallas_call x5 -> x7, Pallas kernels: 159 us -> 181 us  [the longest x1 52.3 us: run_feed_forward(): pl.pallas_call(body, grid=(tokens // ROWS,), in_specs=[in_smem(), rows, r...]
    all_to_all x2 -> x1, blocking collectives: 29.9 us -> 9.63 us  [exchange(): return lax.all_to_all(array, axes, split_axis=0, concat_axis=0, tiled=True)]
    all_gather x4, waiting for transfers between devices: 31.4 us -> 47 us  [gather(): return lax.all_gather(array, 'fsdp', axis=1, tiled=True)]
    ppermute x18 -> x24, starting transfers between devices: 37.3 us -> 50.8 us  [send(): lax.ppermute(array, axis, [(i, (i + shift) % size) for i in range(size)])]
    pallas_call x1, Pallas kernels: 21.3 us -> 30.5 us  [run_feed_forward_grad(): pl.pallas_call(body, grid=(tokens // ROWS,), in_specs=[in_smem(), pl.Bloc...]
    all_to_all x4 -> x3, starting transfers between devices: 16.9 us -> 10.5 us  [exchange(): return lax.all_to_all(array, axes, split_axis=0, concat_axis=0, tiled=True)]
  transfers between devices with their start and end apart: 29 -> 34, of which waited for: 9 -> 9; matrix products, arithmetic and copies ran while one was open for 5% -> 6% of each run, Pallas kernels for 38% -> 46%
where the time goes in v6:
time: 617 us; the launch traced here: 611 us
  Pallas kernels  370 us (60%)
  waiting for transfers between devices  107 us (17%)
  starting transfers between devices  62.1 us (10%)
  local copies, waits for them, and re-layouts  33.7 us (5%)
  between operations  15.5 us (3%)
  other arithmetic  14 us (2%)
  blocking collectives  9.63 us (2%)
    pallas_call x2, Pallas kernels, run_cross_temporal_backward(): pl.pallas_call(body, grid=(groups,), in_specs=[pl.BlockSpec((own_frames,...  82.4 us
    ppermute x24, waiting for transfers between devices, send(): lax.ppermute(array, axis, [(i, (i + shift) % size) for i in range(size)])  53.4 us
    pallas_call x1, Pallas kernels, run_feed_forward(): pl.pallas_call(body, grid=(tokens // ROWS,), in_specs=[in_smem(), rows, r...  52.3 us
    ppermute x24, starting transfers between devices, send(): lax.ppermute(array, axis, [(i, (i + shift) % size) for i in range(size)])  50.8 us
    all_gather x4, waiting for transfers between devices, gather(): return lax.all_gather(array, 'fsdp', axis=1, tiled=True)  47 us
    pallas_call x2, Pallas kernels, run_spatial_backward(): pl.pallas_call(body, grid=(count,), in_specs=[in_smem()] + [pl.BlockSpec(...  40.3 us
    pallas_call x1, Pallas kernels, run_temporal_forward(): pl.pallas_call(body, grid=(groups,), in_specs=[pl.BlockSpec((own_frames,...  32.3 us
    pallas_call x1, Pallas kernels, run_spatial_forward(): pl.pallas_call(spatial_forward, grid=(frames,), in_specs=[in_smem(), row_...  30.8 us
  transfers between devices with their start and end apart: 34, of which 9 were waited for; matrix products, arithmetic and copies ran while one was open for 6% of the time, Pallas kernels for 46%

profile of v6, /device:TPU:0, one launch (start us, length us, event | category | flops | bytes accessed | tf_op | source)
XLA Modules:
  0.0 611.3 jit_solution(13341591213058036900)
XLA Ops:
  19.4 9.6 %all_to_all.23 = s32[8,1,1]{2,1,0:T(1,128)S(1)} all-to-all(s32[8,1,1]{2,1,0:T(1,128)S(1)} %broadcast_in_dim.23), channel_id=1, replica_groups=mesh['seq'=4,'fsdp'=8] {'fsdp'}, dimensions={0} | all-to-all | bytes 64 | tf_op jit(solution)/shard_map/all_to_all | solution.py:1362
  29.8 3.6 pick.1
  33.4 5.2 reshape_squeeze.7
  41.9 4.7 reshape.53
  46.6 3.6 all-to-all-start.1
  53.4 3.6 collective-permute-start.3
  58.0 47.0 %all-gather.5.cloned.1.call-done.w_hbm.refs_20_.refs_22_.refs_13_ = bf16[5,1152,1152]{2,1,0:T(8,128)(2,1)} async-done(((bf16[5,144,1152]{2,1,0:T(8,128)(2,1)}), bf16[5,1152,1152]{2,1,0:T(8,128)(2,1)}) %all-gather.5.cloned.1.call-update) | async-done | bytes 13271056 | tf_op jit(solution)/shard_map/all_gather | solution.py:1372
  112.1 4.7 unpick.1.ad_ref.refs_6_.refs_22_.refs_14_.refs_19_.refs_21_.refs_12_
  116.8 30.8 %spatial_forward.1 = (bf16[4,64,1152]{2,1,0:T(8,128)(2,1)}, bf16[4,64,1152]{2,1,0:T(8,128)(2,1)}, bf16[4,64,1152]{2,1,0:T(8,128)(2,1)}, bf16[4,64,1152]{2,1,0:T(...) custom-call(s32[1]{0:T(128)} %bitcast.seq_ref.refs_0_, ...), custom_call_target="tpu_custom_call" | custom-call | flops 3397386240 | bytes 7500000 | tf_op jit(solution)/shard_map/spatial_forward/pallas_call | solution.py:915
  153.2 12.7 %collective-permute-done.4.refs_1_ = bf16[4,64,1152]{2,1,0:T(8,128)(2,1)S(1)} collective-permute-done((bf16[4,64,1152]{2,1,0:T(8,128)(2,1)}, bf16[4,64,1152]{2,1,0:T(8,128)(2,1)S(1)}, u32[]{:S(2)}, u32[]{:S(2)}) %collective-permute-start.4) | collective-permute-done | bytes 589856 | tf_op jit(solution)/shard_map/ppermute | solution.py:1377
  166.0 24.4 %collective-permute-done.5.refs_2_ = bf16[4,64,1152]{2,1,0:T(8,128)(2,1)S(1)} collective-permute-done((bf16[4,64,1152]{2,1,0:T(8,128)(2,1)}, bf16[4,64,1152]{2,1,0:T(8,128)(2,1)S(1)}, u32[]{:S(2)}, u32[]{:S(2)}) %collective-permute-start.5) | collective-permute-done | bytes 589856 | tf_op jit(solution)/shard_map/ppermute | solution.py:1377
  190.4 14.6 %collective-permute-start.7 = (bf16[576,1152]{1,0:T(8,128)(2,1)S(1)}, bf16[576,1152]{1,0:T(8,128)(2,1)}, u32[]{:S(2)}, u32[]{:S(2)}) collective-permute-start(bf16[576,1152]{1,0:T(8,128)(2,1)S(1)} %get-tuple-element.134.refs_4_.refs_6_), channel_id=1, source_target_pairs={{0,24},{8,0},{16,8},{24,16},{1,25},{9,1},{17,9},{25,17},{2,26},{10... | collective-permute-start | bytes 3981320 | tf_op jit(solution)/shard_map/ppermute | solution.py:1377
  205.1 32.3 %temporal_forward.1 = (bf16[16,64,1152]{2,1,0:T(8,128)(2,1)}, bf16[16,64,1152]{2,1,0:T(8,128)(2,1)}, bf16[16,64,1152]{2,1,0:T(8,128)(2,1)}, bf16[16,64,1152]{2,1...) custom-call(bf16[4,64,1152]{2,1,0:T(8,128)(2,1)} %get-tuple-element., ...), custom_call_target="tpu_custom_call" | custom-call | flops 3397386240 | bytes 7500000 | tf_op jit(solution)/shard_map/temporal_forward/pallas_call | solution.py:961
  247.1 25.0 %cross_forward.1 = (bf16[16,64,1152]{2,1,0:T(8,128)(2,1)}, bf16[16,64,1152]{2,1,0:T(8,128)(2,1)}, f32[4,16,256]{2,1,0:T(8,128)}, bf16[4,256,16]{2,1,0:T(8,128)(2...) custom-call(f32[16,64,1152]{2,1,0:T(8,128)} %get-tuple-element.127.x, ...), custom_call_target="tpu_custom_call" | custom-call | flops 2717908992 | bytes 7500000 | tf_op jit(solution)/shard_map/cross_forward/pallas_call | solution.py:1001
  272.2 30.5 %feed_forward_grad.1.refs_3_ = bf16[3,1024,1152]{2,1,0:T(8,128)(2,1)} custom-call(s32[4]{0:T(128)} %pad_add_fusion.1.refs_0_, bf16[1024,1152]{1,0:T(8,128)(2,1)} %bitcast.51, f32[6,1152]{1,0:T(8,128)} %bitcast.61, bf16[10,16,1152]{2,1,0:T(8,128)(2,1)} %slice.42.refs_3_.refs_7_.refs_5_, bf16[576,1152]{1,0:T(8,128)(2,1)} %copy-done.2, ...), custom_call_target="tpu_custom_call" | custom-call | flops 2038431744 | bytes 5000000 | tf_op jit(solution)/shard_map/feed_forward_grad/pallas_call | solution.py:1030
  306.9 52.3 %feed_forward.1 = (bf16[1024,4608]{1,0:T(8,128)(2,1)}, f32[1024,1152]{1,0:T(8,128)}, f32[16,1152]{1,0:T(8,128)}, f32[16,4608]{1,0:T(8,128)}) custom-call(s32[5]{0:T(128)} %pad_add_fusion.refs_0_, f32[1024,1152]{1,0:T(8,128)} %bitcast.56, bf16[1024,1152]{1,0:T(8,128)(2,1)} %bitcast.52, bf16[3,1024,1152]{2,1,0:T(8,128)(2,1)} %feed_forward_grad.1.refs_3_, ...), custom_call_target="tpu_custom_call" | custom-call | flops 5435817984 | bytes 12500000 | tf_op jit(solution)/shard_map/feed_forward/pallas_call | solution.py:1059
  359.3 26.3 %feed_forward_out.1 = (bf16[256,1152]{1,0:T(8,128)(2,1)}, bf16[256,1152]{1,0:T(8,128)(2,1)}, bf16[256,1152]{1,0:T(8,128)(2,1)}, bf16[256,1152]{1,0:T(8,128)(2,1)...) custom-call(s32[5]{0:T(128)} %pad_add_fusion.refs_0_, bf16[1024,4608]{1,0:T(8,128)(2,1)} %get-tuple-element.140.refs_1_, ...), custom_call_target="tpu_custom_call" | custom-call | flops 169869312 | bytes 312500 | tf_op jit(solution)/shard_map/feed_forward_out/pallas_call | solution.py:1104
  388.4 58.7 %cross_temporal_backward.2 = (bf16[4,48,1152]{2,1,0:T(8,128)(2,1)}, bf16[4,48,1152]{2,1,0:T(8,128)(2,1)}, bf16[4,48,1152]{2,1,0:T(8,128)(2,1)}, bf16[4,48,1152]{...) custom-call(bf16[4,64,1152]{2,1,0:T(8,128)(2,1)} %get-tuple-element.119.refs_0_, ...), custom_call_target="tpu_custom_call" | custom-call | flops 222953472 | bytes 468750 | tf_op jit(solution)/shard_map/cross_temporal_backward/pallas_call | solution.py:1152
  451.3 23.7 %cross_temporal_backward.3 = (bf16[4,16,1152]{2,1,0:T(8,128)(2,1)}, bf16[4,16,1152]{2,1,0:T(8,128)(2,1)}, bf16[4,16,1152]{2,1,0:T(8,128)(2,1)}, bf16[4,16,1152]{...) custom-call(bf16[4,64,1152]{2,1,0:T(8,128)(2,1)} %get-tuple-element.119.refs_0_, ...), custom_call_target="tpu_custom_call" | custom-call | flops 74317824 | bytes 468750 | tf_op jit(solution)/shard_map/cross_temporal_backward/pallas_call | solution.py:1152
  481.4 9.5 %pack_early.1 = bf16[32,128,128]{2,1,0:T(8,128)(2,1)} custom-call(f32[256,1152]{1,0:T(8,128)} %get-tuple-element.169.refs_0_, f32[256,1152]{1,0:T(8,128)} %get-tuple-element.171.refs_1_, f32[8,256,256]{2,1,0:T(8,128)} %get-tuple-element.172.refs_2_, f32[8,256,256]{2,1,0:T(8,128)} %get-tuple-element.173.refs_3_, f32[8,256,256]{2,1,0:T(8,128)} %get-tuple-element.174.refs_4_, ...), custom_call_target="tpu_custom_call" | custom-call | flops 781250 | bytes 125000 | tf_op jit(solution)/shard_map/pack_early/pallas_call | solution.py:1290
  491.0 5.7 collective-permute-done.16.refs_3_
  496.7 4.6 collective-permute-done.19.refs_7_
  504.5 20.0 %spatial_backward.2 = (bf16[4,256,3584]{2,1,0:T(8,128)(2,1)}, f32[128,1152]{1,0:T(8,128)}) custom-call(s32[1]{0:T(128)} %bitcast.seq_ref.refs_0_, bf16[4,48,1152]{2,1,0:T(8,128)(2,1)} %get-tuple-element.191.refs_1_, bf16[4,48,1152]{2,1,0:T(8,128)(2,1)} %copy-done.10, bf16[4,48,1152]{2,1,0:T(8,128)(2,1)} %copy-done.11, bf16[4,48,1152]{2,1,0:T(8,128)(2,1)} %copy-done.12, ...), custom_call_target="tpu_custom_call" | custom-call | flops 63700992 | bytes 312500 | tf_op jit(solution)/shard_map/spatial_backward/pallas_call | solution.py:1199
  524.5 5.0 all-to-all-done.2.got_ref
  532.7 3.5 collective-permute-start.23
  537.6 20.3 %spatial_backward.3 = (bf16[4,256,3584]{2,1,0:T(8,128)(2,1)}, bf16[32,48,128]{2,1,0:T(8,128)(2,1)}) custom-call(s32[1]{0:T(128)} %bitcast.seq_ref.refs_0_, bf16[4,48,1152]{2,1,0:T(8,128)(2,1)} %get-tuple-element.191.refs_1_, bf16[4,48,1152]{2,1,0:T(8,128)(2,1)} %copy-done.10, bf16[4,48,1152]{2,1,0:T(8,128)(2,1)} %copy-done.11, ...), custom_call_target="tpu_custom_call", output_to_operand_aliasing={{0}: (9, {})} | custom-call | flops 63700992 | bytes 312500 | tf_op jit(solution)/shard_map/spatial_backward/pallas_call | solution.py:1199
  559.3 3.8 all-to-all-start.3
  563.2 19.6 %spatial_input_grad.1 = bf16[4,256,1152]{2,1,0:T(8,128)(2,1)} custom-call(s32[1]{0:T(128)} %bitcast.seq_ref.refs_0_, bf16[4,48,1152]{2,1,0:T(8,128)(2,1)} %get-tuple-element.191.refs_1_, bf16[4,48,1152]{2,1,0:T(8,128)(2,1)} %copy-done.10, bf16[4,48,1152]{2,1,0:T(8,128)(2,1)} %copy-done.11, bf16[4,48,1152]{2,1,0:T(8,128)(2,1)} %copy-done.12, ...), custom_call_target="tpu_custom_call" | custom-call | flops 127401984 | bytes 312500 | tf_op jit(solution)/shard_map/spatial_input_grad/pallas_call | solution.py:1236
  585.5 3.6 collective-permute-start.26
  590.2 3.9 put_in_place.1
  594.1 4.5 collective-permute-done.25.refs_7_
  599.8 4.5 assemble.1
  (149 shorter events, 73.9 us)
Async XLA Ops:
  7.2 97.7 %all-gather.5.cloned.1.call-start = ((), (), s32[]{:S(2)}) async-start(), calls=%async_computation.4 | async-start | bytes 14929920 | tf_op jit(solution)/shard_map/all_gather | solution.py:1372
  15.0 190.0 %all-gather.7.cloned.1.call-start = ((), (), s32[]{:S(2)}) async-start(), calls=%async_computation.5 | async-start | bytes 11943936 | tf_op jit(solution)/shard_map/all_gather | solution.py:1372
  17.3 229.8 %all-gather.9.cloned.1.call-start = ((), (), s32[]{:S(2)}) async-start(), calls=%async_computation.6 | async-start | bytes 11943936 | tf_op jit(solution)/shard_map/all_gather | solution.py:1372
  18.6 286.1 %all-gather.11.cloned.1.call-start = ((), (), s32[]{:S(2)}) async-start(), calls=%async_computation.7 | async-start | bytes 11943936 | tf_op jit(solution)/shard_map/all_gather | solution.py:1372
  46.6 64.4 %all-to-all-start.1 = ((bf16[8,624,128]{2,1,0:T(8,128)(2,1)}), bf16[8,624,128]{2,1,0:T(8,128)(2,1)S(1)}, u32[]{:S(2)}, u32[]{:S(2)}) async-start(bf16[8,624,128]{2,1,0:T(8,128)(2,1)} %pick.1), calls=%async_computation.1 | async-start | bytes 2555904 | tf_op jit(solution)/shard_map/all_to_all | solution.py:1362
  53.4 57.6 %collective-permute-start.3 = (bf16[4,64,1152]{2,1,0:T(8,128)(2,1)}, bf16[4,64,1152]{2,1,0:T(8,128)(2,1)S(1)}, u32[]{:S(2)}, u32[]{:S(2)}) collective-permute-start(bf16[4,64,1152]{2,1,0:T(8,128)(2,1)} %get-tuple-element.229), channel_id=1, source_target_pairs={{0,24},{8,0},{16,8},{24,16},{1,25},{9,1},{17,9},{25,17},{2,26},{10... | collective-permute-start | bytes 1769480 | tf_op jit(solution)/shard_map/ppermute | solution.py:1377
  57.0 54.0 %collective-permute-start.2 = (bf16[4,64,1152]{2,1,0:T(8,128)(2,1)}, bf16[4,64,1152]{2,1,0:T(8,128)(2,1)}, u32[]{:S(2)}, u32[]{:S(2)}) collective-permute-start(bf16[4,64,1152]{2,1,0:T(8,128)(2,1)} %get-tuple-element.230), channel_id=1, source_target_pairs={{0,16},{8,24},{16,0},{24,8},{1,17},{9,25},{17,1},{25,9},{2,18},{10... | collective-permute-start | bytes 1769480 | tf_op jit(solution)/shard_map/ppermute | solution.py:1377
  57.0 54.0 %collective-permute-start.1 = (bf16[4,64,1152]{2,1,0:T(8,128)(2,1)}, bf16[4,64,1152]{2,1,0:T(8,128)(2,1)}, u32[]{:S(2)}, u32[]{:S(2)}) collective-permute-start(bf16[4,64,1152]{2,1,0:T(8,128)(2,1)} %get-tuple-element.231), channel_id=1, source_target_pairs={{0,8},{8,16},{16,24},{24,0},{1,9},{9,17},{17,25},{25,1},{2,10},{10... | collective-permute-start | bytes 1769480 | tf_op jit(solution)/shard_map/ppermute | solution.py:1377
  107.9 82.5 %collective-permute-start = (bf16[576,1152]{1,0:T(8,128)(2,1)S(1)}, bf16[576,1152]{1,0:T(8,128)(2,1)}, u32[]{:S(2)}, u32[]{:S(2)}) collective-permute-start(bf16[576,1152]{1,0:T(8,128)(2,1)S(1)} %get-tuple-element.134.refs_4_.refs_6_), channel_id=1, source_target_pairs={{0,8},{8,16},{16,24},{24,0},{1,9},{9,17},{17,25},{25,1},{2,10},{10... | collective-permute-start | bytes 3981320 | tf_op jit(solution)/shard_map/ppermute | solution.py:1377
  147.6 18.4 %collective-permute-start.4 = (bf16[4,64,1152]{2,1,0:T(8,128)(2,1)}, bf16[4,64,1152]{2,1,0:T(8,128)(2,1)S(1)}, u32[]{:S(2)}, u32[]{:S(2)}) collective-permute-start(bf16[4,64,1152]{2,1,0:T(8,128)(2,1)} %get-tuple-element.116), channel_id=1, source_target_pairs={{0,8},{8,16},{16,24},{24,0},{1,9},{9,17},{17,25},{25,1},{2,10},{10... | collective-permute-start | bytes 1769480 | tf_op jit(solution)/shard_map/ppermute | solution.py:1377
  149.3 41.1 %collective-permute-start.5 = (bf16[4,64,1152]{2,1,0:T(8,128)(2,1)}, bf16[4,64,1152]{2,1,0:T(8,128)(2,1)S(1)}, u32[]{:S(2)}, u32[]{:S(2)}) collective-permute-start(bf16[4,64,1152]{2,1,0:T(8,128)(2,1)} %get-tuple-element.117), channel_id=1, source_target_pairs={{0,16},{8,24},{16,0},{24,8},{1,17},{9,25},{17,1},{25,9},{2,18},{10... | collective-permute-start | bytes 1769480 | tf_op jit(solution)/shard_map/ppermute | solution.py:1377
  150.6 39.9 %collective-permute-start.6 = (bf16[4,64,1152]{2,1,0:T(8,128)(2,1)}, bf16[4,64,1152]{2,1,0:T(8,128)(2,1)S(1)}, u32[]{:S(2)}, u32[]{:S(2)}) collective-permute-start(bf16[4,64,1152]{2,1,0:T(8,128)(2,1)} %get-tuple-element.118), channel_id=1, source_target_pairs={{0,24},{8,0},{16,8},{24,16},{1,25},{9,1},{17,9},{25,17},{2,26},{10... | collective-permute-start | bytes 1769480 | tf_op jit(solution)/shard_map/ppermute | solution.py:1377
  190.4 46.9 %collective-permute-start.7 = (bf16[576,1152]{1,0:T(8,128)(2,1)S(1)}, bf16[576,1152]{1,0:T(8,128)(2,1)}, u32[]{:S(2)}, u32[]{:S(2)}) collective-permute-start(bf16[576,1152]{1,0:T(8,128)(2,1)S(1)} %get-tuple-element.134.refs_4_.refs_6_), channel_id=1, source_target_pairs={{0,24},{8,0},{16,8},{24,16},{1,25},{9,1},{17,9},{25,17},{2,26},{10... | collective-permute-start | bytes 3981320 | tf_op jit(solution)/shard_map/ppermute | solution.py:1377
  237.4 34.8 %collective-permute-start.9 = (bf16[576,1152]{1,0:T(8,128)(2,1)}, bf16[576,1152]{1,0:T(8,128)(2,1)}, u32[]{:S(2)}, u32[]{:S(2)}) collective-permute-start(bf16[576,1152]{1,0:T(8,128)(2,1)} %collective-permute-done.refs_5_.refs_7_), channel_id=1, source_target_pairs={{0,1},{1,0},{2,3},{3,2},{4,5},{5,4},{6,7},{7,6},{8,9},{9,8},{10,11... | collective-permute-start | bytes 3981320 | tf_op jit(solution)/shard_map/ppermute | solution.py:1402
  237.4 34.7 %collective-permute-start.10 = (bf16[576,1152]{1,0:T(8,128)(2,1)}, bf16[576,1152]{1,0:T(8,128)(2,1)}, u32[]{:S(2)}, u32[]{:S(2)}) collective-permute-start(bf16[576,1152]{1,0:T(8,128)(2,1)} %collective-permute-done.7.refs_6_.refs_8_), channel_id=1, source_target_pairs={{0,1},{1,0},{2,3},{3,2},{4,5},{5,4},{6,7},{7,6},{8,9},{9,8},{10,11... | collective-permute-start | bytes 3981320 | tf_op jit(solution)/shard_map/ppermute | solution.py:1402
  237.9 64.8 %collective-permute-start.8 = (bf16[576,1152]{1,0:T(8,128)(2,1)S(1)}, bf16[576,1152]{1,0:T(8,128)(2,1)S(1)}, u32[]{:S(2)}, u32[]{:S(2)}) collective-permute-start(bf16[576,1152]{1,0:T(8,128)(2,1)S(1)} %get-tuple-element.134.refs_4_.refs_6_), channel_id=1, source_target_pairs={{0,16},{8,24},{16,0},{24,8},{1,17},{9,25},{17,1},{25,9},{2,18},{10... | collective-permute-start | bytes 3981320 | tf_op jit(solution)/shard_map/ppermute | solution.py:1377
  385.6 65.1 %collective-permute-start.12 = (bf16[4,64,1152]{2,1,0:T(8,128)(2,1)}, bf16[4,64,1152]{2,1,0:T(8,128)(2,1)S(1)}, u32[]{:S(2)}, u32[]{:S(2)}) collective-permute-start(bf16[4,64,1152]{2,1,0:T(8,128)(2,1)} %bitcast.82), channel_id=1, source_target_pairs={{0,24},{8,0},{16,8},{24,16},{1,25},{9,1},{17,9},{25,17},{2,26},{10... | collective-permute-start | bytes 1769480 | tf_op jit(solution)/shard_map/ppermute | solution.py:1377
  386.9 64.4 %collective-permute-start.13 = (bf16[4,64,1152]{2,1,0:T(8,128)(2,1)}, bf16[4,64,1152]{2,1,0:T(8,128)(2,1)S(1)}, u32[]{:S(2)}, u32[]{:S(2)}) collective-permute-start(bf16[4,64,1152]{2,1,0:T(8,128)(2,1)} %bitcast.81), channel_id=1, source_target_pairs={{0,16},{8,24},{16,0},{24,8},{1,17},{9,25},{17,1},{25,9},{2,18},{10... | collective-permute-start | bytes 1769480 | tf_op jit(solution)/shard_map/ppermute | solution.py:1377
  387.0 64.3 %collective-permute-start.14 = (bf16[4,64,1152]{2,1,0:T(8,128)(2,1)}, bf16[4,64,1152]{2,1,0:T(8,128)(2,1)S(1)}, u32[]{:S(2)}, u32[]{:S(2)}) collective-permute-start(bf16[4,64,1152]{2,1,0:T(8,128)(2,1)} %bitcast.80), channel_id=1, source_target_pairs={{0,8},{8,16},{16,24},{24,0},{1,9},{9,17},{17,25},{25,1},{2,10},{10... | collective-permute-start | bytes 1769480 | tf_op jit(solution)/shard_map/ppermute | solution.py:1377
  447.1 31.3 %collective-permute-start.15 = (bf16[4,48,1152]{2,1,0:T(8,128)(2,1)}, bf16[4,48,1152]{2,1,0:T(8,128)(2,1)S(1)}, u32[]{:S(2)}, u32[]{:S(2)}) collective-permute-start(bf16[4,48,1152]{2,1,0:T(8,128)(2,1)} %get-tuple-element.183), channel_id=1, source_target_pairs={{0,24},{8,0},{16,8},{24,16},{1,25},{9,1},{17,9},{25,17},{2,26},{10... | collective-permute-start | bytes 1327112 | tf_op jit(solution)/shard_map/ppermute | solution.py:1377
  449.6 47.1 %collective-permute-start.16 = (bf16[4,48,1152]{2,1,0:T(8,128)(2,1)}, bf16[4,48,1152]{2,1,0:T(8,128)(2,1)S(1)}, u32[]{:S(2)}, u32[]{:S(2)}) collective-permute-start(bf16[4,48,1152]{2,1,0:T(8,128)(2,1)} %get-tuple-element.184), channel_id=1, source_target_pairs={{0,16},{8,24},{16,0},{24,8},{1,17},{9,25},{17,1},{25,9},{2,18},{10... | collective-permute-start | bytes 1327112 | tf_op jit(solution)/shard_map/ppermute | solution.py:1377
  450.6 46.0 %collective-permute-start.17 = (bf16[4,48,1152]{2,1,0:T(8,128)(2,1)}, bf16[4,48,1152]{2,1,0:T(8,128)(2,1)S(1)}, u32[]{:S(2)}, u32[]{:S(2)}) collective-permute-start(bf16[4,48,1152]{2,1,0:T(8,128)(2,1)} %get-tuple-element.185), channel_id=1, source_target_pairs={{0,8},{8,16},{16,24},{24,0},{1,9},{9,17},{17,25},{25,1},{2,10},{10... | collective-permute-start | bytes 1327112 | tf_op jit(solution)/shard_map/ppermute | solution.py:1377
  475.1 21.6 %collective-permute-start.18 = (bf16[4,16,1152]{2,1,0:T(8,128)(2,1)}, bf16[4,16,1152]{2,1,0:T(8,128)(2,1)S(1)}, u32[]{:S(2)}, u32[]{:S(2)}) collective-permute-start(bf16[4,16,1152]{2,1,0:T(8,128)(2,1)} %get-tuple-element.188), channel_id=1, source_target_pairs={{0,24},{8,0},{16,8},{24,16},{1,25},{9,1},{17,9},{25,17},{2,26},{10... | collective-permute-start | bytes 442376 | tf_op jit(solution)/shard_map/ppermute | solution.py:1377
  478.3 23.1 %collective-permute-start.19 = (bf16[4,16,1152]{2,1,0:T(8,128)(2,1)}, bf16[4,16,1152]{2,1,0:T(8,128)(2,1)S(1)}, u32[]{:S(2)}, u32[]{:S(2)}) collective-permute-start(bf16[4,16,1152]{2,1,0:T(8,128)(2,1)} %get-tuple-element.189), channel_id=1, source_target_pairs={{0,16},{8,24},{16,0},{24,8},{1,17},{9,25},{17,1},{25,9},{2,18},{10... | collective-permute-start | bytes 442376 | tf_op jit(solution)/shard_map/ppermute | solution.py:1377
  478.4 23.0 %collective-permute-start.20 = (bf16[4,16,1152]{2,1,0:T(8,128)(2,1)}, bf16[4,16,1152]{2,1,0:T(8,128)(2,1)S(1)}, u32[]{:S(2)}, u32[]{:S(2)}) collective-permute-start(bf16[4,16,1152]{2,1,0:T(8,128)(2,1)} %get-tuple-element.190), channel_id=1, source_target_pairs={{0,8},{8,16},{16,24},{24,0},{1,9},{9,17},{17,25},{25,1},{2,10},{10... | collective-permute-start | bytes 442376 | tf_op jit(solution)/shard_map/ppermute | solution.py:1377
  501.3 28.2 %all-to-all-start.2 = ((bf16[32,128,128]{2,1,0:T(8,128)(2,1)}), bf16[32,128,128]{2,1,0:T(8,128)(2,1)S(1)}, u32[]{:S(2)}, u32[]{:S(2)}) async-start(bf16[32,128,128]{2,1,0:T(8,128)(2,1)} %pack_early.1), calls=%async_computation.2 | async-start | bytes 2097152 | tf_op jit(solution)/shard_map/all_to_all | solution.py:1362
  532.7 25.2 %collective-permute-start.23 = (bf16[8,128,128]{2,1,0:T(8,128)(2,1)}, bf16[8,128,128]{2,1,0:T(8,128)(2,1)S(1)}, u32[]{:S(2)}, u32[]{:S(2)}) collective-permute-start(bf16[8,128,128]{2,1,0:T(8,128)(2,1)} %combine.2.refs_1_), channel_id=1, source_target_pairs={{0,24},{8,0},{16,8},{24,16},{1,25},{9,1},{17,9},{25,17},{2,26},{10... | collective-permute-start | bytes 786440 | tf_op jit(solution)/shard_map/ppermute | solution.py:1377
  536.2 23.1 %collective-permute-start.22 = (bf16[8,128,128]{2,1,0:T(8,128)(2,1)}, bf16[8,128,128]{2,1,0:T(8,128)(2,1)S(1)}, u32[]{:S(2)}, u32[]{:S(2)}) collective-permute-start(bf16[8,128,128]{2,1,0:T(8,128)(2,1)} %combine.2.refs_1_), channel_id=1, source_target_pairs={{0,16},{8,24},{16,0},{24,8},{1,17},{9,25},{17,1},{25,9},{2,18},{10... | collective-permute-start | bytes 786440 | tf_op jit(solution)/shard_map/ppermute | solution.py:1377
  537.6 21.7 %collective-permute-start.21 = (bf16[8,128,128]{2,1,0:T(8,128)(2,1)}, bf16[8,128,128]{2,1,0:T(8,128)(2,1)S(1)}, u32[]{:S(2)}, u32[]{:S(2)}) collective-permute-start(bf16[8,128,128]{2,1,0:T(8,128)(2,1)} %combine.2.refs_1_), channel_id=1, source_target_pairs={{0,8},{8,16},{16,24},{24,0},{1,9},{9,17},{17,25},{25,1},{2,10},{10... | collective-permute-start | bytes 786440 | tf_op jit(solution)/shard_map/ppermute | solution.py:1377
  559.3 23.5 %all-to-all-start.3 = ((bf16[32,48,128]{2,1,0:T(8,128)(2,1)}), bf16[32,48,128]{2,1,0:T(8,128)(2,1)S(1)}, u32[]{:S(2)}, u32[]{:S(2)}) async-start(bf16[32,48,128]{2,1,0:T(8,128)(2,1)} %get-tuple-element.214), calls=%async_computation.3 | async-start | bytes 786432 | tf_op jit(solution)/shard_map/all_to_all | solution.py:1362
  589.1 9.5 %collective-permute-start.25 = (bf16[8,48,128]{2,1,0:T(8,128)(2,1)}, bf16[8,48,128]{2,1,0:T(8,128)(2,1)S(1)}, u32[]{:S(2)}, u32[]{:S(2)}) collective-permute-start(bf16[8,48,128]{2,1,0:T(8,128)(2,1)} %combine.3.refs_5_), channel_id=1, source_target_pairs={{0,16},{8,24},{16,0},{24,8},{1,17},{9,25},{17,1},{25,9},{2,18},{10... | collective-permute-start | bytes 294920 | tf_op jit(solution)/shard_map/ppermute | solution.py:1377
  589.1 9.5 %collective-permute-start.24 = (bf16[8,48,128]{2,1,0:T(8,128)(2,1)}, bf16[8,48,128]{2,1,0:T(8,128)(2,1)S(1)}, u32[]{:S(2)}, u32[]{:S(2)}) collective-permute-start(bf16[8,48,128]{2,1,0:T(8,128)(2,1)} %combine.3.refs_5_), channel_id=1, source_target_pairs={{0,8},{8,16},{16,24},{24,0},{1,9},{9,17},{17,25},{25,1},{2,10},{10... | collective-permute-start | bytes 294920 | tf_op jit(solution)/shard_map/ppermute | solution.py:1377
  (36 other events, 696.6 us)
Sparse Core Ops, SparseCore 0:
  15.1 89.7 all-gather.4
  106.8 64.0 all-gather.6
  172.9 63.7 all-gather.8
  238.5 64.0 all-gather.10

commit v7 on v6

--- a/solution.py
+++ b/solution.py
@@ -293,7 +293,7 @@
     w_ref, lhs_ref, q_s, k_s, sems,
 ):
     width = x_ref.shape[2]
-    loads = Loads([(w_hbm.at[i], w_ref.at[i, pl.ds(0, width), :]) for i in range(4)], sems)
+    loads = Loads([(w_hbm.at[4 + i], w_ref.at[i, pl.ds(0, width), :]) for i in range(4)], sems)
     loads.start()
 
     @pl.when(loads.first)
@@ -532,14 +532,15 @@
 def _cross_temporal_backward(
     u1_refs, g1_refs, g3_ref, q_ref, k_ref, v_ref, o_ref, stat_ref, rq_ref, ro_ref,
     u2_ref, qc_ref, oc_ref, statc_ref, rqc_ref, roc_ref, kp_ref, vp_ref,
-    mod_ref, mask_ref, ad_ref, wt_hbm, wc_hbm,
+    mod_ref, mask_ref, ad_ref, w_hbm,
     gw_ref, dk_acc, dv_acc, w_ref, bias_ref, q_s, k_s, v_s, do_s, dq_s, dk_s, dv_s, sems,
 ):
     width = u1_refs[0].shape[2]
     first = pl.program_id(0) == 0
     order = (7, 4, 3, 0, 1, 2)
-    sources = [wc_hbm.at[n - 4] if n >= 4 else wt_hbm.at[n] for n in order]
-    loads = Loads([(w, w_ref.at[i, pl.ds(0, width), :]) for i, w in enumerate(sources)], sems)
+    loads = Loads(
+        [(w_hbm.at[n], w_ref.at[i, pl.ds(0, width), :]) for i, n in enumerate(order)], sems
+    )
     loads.start()
 
     @pl.when(first)
@@ -1133,7 +1134,7 @@
     )(order, active, x3, cot, mods, maps, *pieces)
 
 
-def run_cross_temporal_backward(g3, u1, saved, mods, masks, wide, w_t, w_c, start, groups):
+def run_cross_temporal_backward(g3, u1, saved, mods, masks, wide, w_tc, start, groups):
     parts = len(u1)
     own_frames, places, d = u1[0].shape
     frames = own_frames * parts
@@ -1155,7 +1156,7 @@
         in_specs=[pl.BlockSpec((own_frames, each, d), lambda i: (0, i + start, 0))] * parts
         + [across] + [across] * 4 + [stat, three, one] + [across] * 3 + [stat, one, one]
         + [whole_block(kp), whole_block(vp)]
-        + [whole_block(mods), whole_block(masks), whole_block(wide), anywhere(), anywhere()],
+        + [whole_block(mods), whole_block(masks), whole_block(wide), anywhere()],
         out_specs=[pl.BlockSpec((own_frames, each, d), lambda i: (0, i, 0))] * parts
         + [
             pl.BlockSpec((16 * RANK, d), lambda i: (0, 0)),
@@ -1174,7 +1175,7 @@
         compiler_params=PARAMS,
         cost_estimate=cost(14 * groups * ROWS * d * d, 30_000_000, 64),
         name="cross_temporal_backward",
-    )(*u1, g3, *saved[:15], mods, masks, wide, w_t, w_c)
+    )(*u1, g3, *saved[:15], mods, masks, wide, w_tc)
 
 
 LATE_BLOCKS = 8
@@ -1386,16 +1387,20 @@
 
 
 def gather_spatial_and_down(spatial, down, parts, times, clips, d):
-    quarters = down.reshape(times, -1, d)
     if times != parts or clips % 2:
-        return gather(spatial), None
-    own = lax.dynamic_slice_in_dim(quarters, lax.axis_index("seq"), 1, 0)
-    got = gather(jnp.concatenate([spatial, own], 0))
+        return gather(spatial)
+    own = lax.dynamic_slice_in_dim(down.reshape(times, -1, d), lax.axis_index("seq"), 1, 0)
+    return gather(jnp.concatenate([spatial, own], 0))
+
+
+def start_down(got, parts, times, clips, d):
+    if times != parts or clips % 2:
+        return None
     half = d // 2
     core = lax.axis_index("fsdp") % 2
     first = lax.dynamic_slice(got, (times, core * half, 0), (1, half, d))[0]
     other = lax.dynamic_slice(got, (times, (1 - core) * half, 0), (1, half, d))[0]
-    return got, (first, other, send(first, "seq", 1))
+    return first, other, send(first, "seq", 1), send(first, "seq", -1)
 
 
 def swap_cores(piece, clips):
@@ -1444,17 +1449,12 @@
 
     seq = lax.axis_index("seq").astype(jnp.int32)[None]
     all_index = exchange(jnp.broadcast_to(adapter_index, (clips,)), "fsdp")
-    w_s, started = gather_spatial_and_down(
-        attention_weights(0), ffn_down[0], parts, times, clips, d
-    )
+    w_s = gather_spatial_and_down(attention_weights(0), ffn_down[0], parts, times, clips, d)
     picked = run_pick(all_index, adapt_wide[0], adapt_ff[0])
     wide = run_unpick(exchange(picked, "fsdp"), count + 2 * times, cols)
-    w_t = gather(attention_weights(1))
-    w_c = gather(attention_weights(2))
+    w_tc = gather(jnp.concatenate([attention_weights(1), attention_weights(2)], 0))
     ffn_up, _ = lax.optimization_barrier((ffn_up, picked))
     up = gather(up_chunks(ffn_up[0], clips, times))
-    maps_f = wide[24:]
-
     cot = cotangent.reshape(frames, SPATIAL, d)
     cot = to_places(
         [
@@ -1462,42 +1462,44 @@
             for k in range(parts)
         ]
     )
-    frames_in, *cot = lax.optimization_barrier((video.reshape(frames, SPATIAL, d), *cot))
+    frames_in = video.reshape(frames, SPATIAL, d)
+    maps_f = wide[24:]
+    order, core = down_order(times, parts, clips)
+    packed_order = jnp.concatenate([order, core])
+    if times == parts and clips % 2 == 0:
+        packed_order = jnp.concatenate([order[:2], order[parts - 1 :], order[2 : parts - 1], core])
+    w_s, wide, maps_f, packed_order, *cot = lax.optimization_barrier((w_s, wide, maps_f, packed_order, *cot))
+    started = start_down(w_s, parts, times, clips, d)
     cot = jnp.concatenate(cot, 0).reshape(FRAMES * places, d)
     made = run_spatial_forward(seq, frames_in, mods, masks, wide, w_s, parts)
     u1, kept_s = to_places(made[:parts]), made[parts:]
-    order, core = down_order(times, parts, clips)
     if started is None:
         whole_down = gather(ffn_down[0].reshape(times, -1, d))
         sides = [[whole_down[i, :half_d] for i in range(times)], [whole_down[i, half_d:] for i in range(times)]]
-        *kept_t, x2 = run_temporal_forward(u1, mods, masks, wide, w_t)
-        *kept_c, x3 = run_cross_forward(x2, ctx, masks, wide, w_c)
+        *kept_t, x2 = run_temporal_forward(u1, mods, masks, wide, w_tc)
+        *kept_c, x3 = run_cross_forward(x2, ctx, masks, wide, w_tc)
         late_pieces = []
-        grad_active = [
-            run_feed_forward_grad(cot, mods, maps_f, jnp.concatenate([order, core]), sides[0] + sides[1])
-        ]
+        grad_active = [run_feed_forward_grad(cot, mods, maps_f, packed_order, sides[0] + sides[1])]
     else:
-        first, other, second = started
-        later, second, *u1 = lax.optimization_barrier((first, second, *u1))
-        mine = [first, second] + [send(later, "seq", k) for k in range(3, parts)]
-        last = send(later, "seq", 2)
-        *kept_t, x2 = run_temporal_forward(u1, mods, masks, wide, w_t)
-        x2, *mine = lax.optimization_barrier((x2, *mine))
+        first, other, second, third = started
+        second, third, cot, x1_own = lax.optimization_barrier((second, third, cot, u1[0]))
+        mine = [first, second, third]
         others = [other] + [swap_cores(piece, clips) for piece in mine[1:]]
-        order = jnp.concatenate([order[:2], order[3:], order[2:3]])
-        early_order = jnp.concatenate([order[:-1], core])
-        *kept_c, x3 = run_cross_forward(x2, ctx, masks, wide, w_c)
-        mine[0], x3 = lax.optimization_barrier((mine[0], x3))
-        grad_early = run_feed_forward_grad(cot, mods, maps_f, early_order, mine + others)
-        last, grad_early = lax.optimization_barrier((last, grad_early))
-        last_other = swap_cores(last, clips)
-        grad_active = [grad_early]
-        late_pieces = [last, last_other]
-        sides = [mine + [last], others + [last_other]]
-    down = [jnp.concatenate([order, core]), *sides[0], *sides[1]]
+        early_order = jnp.concatenate([packed_order[:3], core])
+        grad_active = run_feed_forward_grad(cot, mods, maps_f, early_order, mine + others)
+        second, grad_active, *u1 = lax.optimization_barrier((second, grad_active, x1_own, *u1[1:]))
+        rest = [send(second, "seq", 1)] + [send(first, "seq", k) for k in range(3, parts - 1)]
+        *kept_t, x2 = run_temporal_forward(u1, mods, masks, wide, w_tc)
+        x2, *rest = lax.optimization_barrier((x2, *rest))
+        rest_others = [swap_cores(piece, clips) for piece in rest]
+        *kept_c, x3 = run_cross_forward(x2, ctx, masks, wide, w_tc)
+        grad_active = [grad_active]
+        late_pieces = rest + rest_others
+        sides = [mine + rest, others + rest_others]
+    down = [packed_order, *sides[0], *sides[1]]
     x3 = x3.reshape(FRAMES * places, d)
     active, g3, grad_a24, grad_b24 = run_feed_forward(
-        x3, cot, jnp.concatenate([order, core]), grad_active, late_pieces, mods, maps_f, up
+        x3, cot, packed_order, grad_active, late_pieces, mods, maps_f, up
     )
     g3 = g3.reshape(FRAMES, places, d)
     groups = FRAMES * places // ROWS
@@ -1511,7 +1513,7 @@
     g1, gw, dk, dv = [], [], [], []
     for share, size in enumerate(shares):
         *pieces, gw_part, dk_part, dv_part = run_cross_temporal_backward(
-            g3, u1, saved, mods, masks, wide, w_t, w_c, sum(shares[:share]), size
+            g3, u1, saved, mods, masks, wide, w_tc, sum(shares[:share]), size
         )
         gw.append(gw_part)
         dk.append(dk_part)

time: 617 us -> 597 us (0.968)
  Pallas kernels: 370 us -> 358 us
    all_gather x4 -> x3, waiting for transfers between devices: 47 us -> 0.04 us  [gather(): return lax.all_gather(array, 'fsdp', axis=1, tiled=True)]
    ppermute x24, waiting for transfers between devices: 53.4 us -> 79.5 us  [send(): lax.ppermute(array, axis, [(i, (i + shift) % size) for i in range(size)])]
    all_to_all x3, waiting for transfers between devices: 5.01 us -> 24.6 us  [exchange(): return lax.all_to_all(array, axes, split_axis=0, concat_axis=0, tiled=True)]
    pallas_call x1, Pallas kernels: 30.5 us -> 18.6 us  [run_feed_forward_grad(): pl.pallas_call(body, grid=(tokens // ROWS,), in_specs=[in_smem(), pl.Bloc...]
    ppermute x24, starting transfers between devices: 50.8 us -> 43.8 us  [send(): lax.ppermute(array, axis, [(i, (i + shift) % size) for i in range(size)])]
  transfers between devices with their start and end apart: 34 -> 33, of which waited for: 9 -> 10; matrix products, arithmetic and copies ran while one was open for 6% -> 6% of each run, Pallas kernels for 46% -> 46%
where the time goes in v7:
time: 597 us; the launch traced here: 591 us
  Pallas kernels  358 us (60%)
  waiting for transfers between devices  104 us (17%)
  starting transfers between devices  57.2 us (10%)
  local copies, waits for them, and re-layouts  35.2 us (6%)
  between operations  15.5 us (3%)
  other arithmetic  11.8 us (2%)
  blocking collectives  9.63 us (2%)
    pallas_call x2, Pallas kernels, run_cross_temporal_backward(): pl.pallas_call(body, grid=(groups,), in_specs=[pl.BlockSpec((own_frames,...  82.3 us
    ppermute x24, waiting for transfers between devices, send(): lax.ppermute(array, axis, [(i, (i + shift) % size) for i in range(size)])  79.5 us
    pallas_call x1, Pallas kernels, run_feed_forward(): pl.pallas_call(body, grid=(tokens // ROWS,), in_specs=[in_smem(), rows, r...  52.5 us
    ppermute x24, starting transfers between devices, send(): lax.ppermute(array, axis, [(i, (i + shift) % size) for i in range(size)])  43.8 us
    pallas_call x2, Pallas kernels, run_spatial_backward(): pl.pallas_call(body, grid=(count,), in_specs=[in_smem()] + [pl.BlockSpec(...  40.3 us
    pallas_call x1, Pallas kernels, run_temporal_forward(): pl.pallas_call(body, grid=(groups,), in_specs=[pl.BlockSpec((own_frames,...  32.2 us
    pallas_call x1, Pallas kernels, run_spatial_forward(): pl.pallas_call(spatial_forward, grid=(frames,), in_specs=[in_smem(), row_...  31.7 us
    pallas_call x1, Pallas kernels, run_feed_forward_out(): pl.pallas_call(body, grid=(steps,), in_specs=[in_smem(), pl.BlockSpec((RO...  26.3 us
  transfers between devices with their start and end apart: 33, of which 10 were waited for; matrix products, arithmetic and copies ran while one was open for 6% of the time, Pallas kernels for 46%

profile of v7, /device:TPU:0, one launch (start us, length us, event | category | flops | bytes accessed | tf_op | source)
XLA Modules:
  0.0 591.5 jit_solution(3802203200166077137)
XLA Ops:
  18.6 9.6 %all_to_all.23 = s32[8,1,1]{2,1,0:T(1,128)S(1)} all-to-all(s32[8,1,1]{2,1,0:T(1,128)S(1)} %broadcast_in_dim.23), channel_id=1, replica_groups=mesh['seq'=4,'fsdp'=8] {'fsdp'}, dimensions={0} | all-to-all | bytes 64 | tf_op jit(solution)/shard_map/all_to_all | solution.py:1363
  28.9 3.6 pick.1
  32.5 5.2 reshape_squeeze.7
  41.1 4.7 reshape.53
  52.5 3.6 collective-permute-start.2
  59.0 19.6 %all-to-all-done.1.refs_0_ = bf16[8,624,128]{2,1,0:T(8,128)(2,1)S(1)} async-done(((bf16[8,624,128]{2,1,0:T(8,128)(2,1)}), bf16[8,624,128]{2,1,0:T(8,128)(2,1)S(1)}, u32[]{:S(2)}, u32[]{:S(2)}) %all-to-all-start.1) | async-done | bytes 1277984 | tf_op jit(solution)/shard_map/all_to_all | solution.py:1363
  79.6 4.7 unpick.1.ad_ref.refs_6_.refs_22_.refs_14_.refs_19_.refs_21_.refs_12_
  86.1 21.2 %collective-permute-done.1 = bf16[4,64,1152]{2,1,0:T(8,128)(2,1)S(1)} collective-permute-done((bf16[4,64,1152]{2,1,0:T(8,128)(2,1)}, bf16[4,64,1152]{2,1,0:T(8,128)(2,1)S(1)}, u32[]{:S(2)}, u32[]{:S(2)}) %collective-permute-start.1) | collective-permute-done | bytes 589856 | tf_op jit(solution)/shard_map/ppermute | solution.py:1378
  114.3 31.7 %spatial_forward.1 = (bf16[4,64,1152]{2,1,0:T(8,128)(2,1)}, bf16[4,64,1152]{2,1,0:T(8,128)(2,1)}, bf16[4,64,1152]{2,1,0:T(8,128)(2,1)}, bf16[4,64,1152]{2,1,0:T(...) custom-call(s32[1]{0:T(128)} %bitcast.seq_ref.refs_0_, ...), custom_call_target="tpu_custom_call" | custom-call | flops 3397386240 | bytes 7500000 | tf_op jit(solution)/shard_map/spatial_forward/pallas_call | solution.py:916
  149.4 22.2 %collective-permute-done.3.refs_5_.refs_7_ = bf16[576,1152]{1,0:T(8,128)(2,1)S(1)} collective-permute-done((bf16[576,1152]{1,0:T(8,128)(2,1)S(1)}, bf16[576,1152]{1,0:T(8,128)(2,1)S(1)}, u32[]{:S(2)}, u32[]{:S(2)}) %collective-permute-start.3) | collective-permute-done | bytes 1327136 | tf_op jit(solution)/shard_map/ppermute | solution.py:1378
  178.0 18.6 %feed_forward_grad.1.refs_3_ = bf16[3,1024,1152]{2,1,0:T(8,128)(2,1)} custom-call(s32[4]{0:T(128)} %pad_add_fusion.1.refs_0_, bf16[1024,1152]{1,0:T(8,128)(2,1)} %bitcast.52, f32[6,1152]{1,0:T(8,128)} %bitcast.61, bf16[10,16,1152]{2,1,0:T(8,128)(2,1)} %slice.44.refs_3_.refs_7_.refs_5_, bf16[576,1152]{1,0:T(8,128)(2,1)} %copy-done.2, ...), custom_call_target="tpu_custom_call" | custom-call | flops 2038431744 | bytes 5000000 | tf_op jit(solution)/shard_map/feed_forward_grad/pallas_call | solution.py:1031
  196.7 18.2 %collective-permute-done.8.refs_2_ = bf16[4,64,1152]{2,1,0:T(8,128)(2,1)} collective-permute-done((bf16[4,64,1152]{2,1,0:T(8,128)(2,1)}, bf16[4,64,1152]{2,1,0:T(8,128)(2,1)}, u32[]{:S(2)}, u32[]{:S(2)}) %collective-permute-start.8) | collective-permute-done | bytes 589856 | tf_op jit(solution)/shard_map/ppermute | solution.py:1378
  214.8 12.6 %collective-permute-start.10 = (bf16[576,1152]{1,0:T(8,128)(2,1)}, bf16[576,1152]{1,0:T(8,128)(2,1)S(1)}, u32[]{:S(2)}, u32[]{:S(2)}) collective-permute-start(bf16[576,1152]{1,0:T(8,128)(2,1)} %copy-done.6), channel_id=1, source_target_pairs={{0,8},{8,16},{16,24},{24,0},{1,9},{9,17},{17,25},{25,1},{2,10},{10... | collective-permute-start | bytes 3981320 | tf_op jit(solution)/shard_map/ppermute | solution.py:1378
  227.5 32.2 %temporal_forward.1 = (bf16[16,64,1152]{2,1,0:T(8,128)(2,1)}, bf16[16,64,1152]{2,1,0:T(8,128)(2,1)}, bf16[16,64,1152]{2,1,0:T(8,128)(2,1)}, bf16[16,64,1152]{2,1...) custom-call(bf16[4,64,1152]{2,1,0:T(8,128)(2,1)} %get-tuple-element., ...), custom_call_target="tpu_custom_call" | custom-call | flops 3397386240 | bytes 7500000 | tf_op jit(solution)/shard_map/temporal_forward/pallas_call | solution.py:962
  260.7 23.7 %cross_forward.1 = (bf16[16,64,1152]{2,1,0:T(8,128)(2,1)}, bf16[16,64,1152]{2,1,0:T(8,128)(2,1)}, f32[4,16,256]{2,1,0:T(8,128)}, bf16[4,256,16]{2,1,0:T(8,128)(2...) custom-call(f32[16,64,1152]{2,1,0:T(8,128)} %get-tuple-element.137.x, ...), custom_call_target="tpu_custom_call" | custom-call | flops 2717908992 | bytes 7500000 | tf_op jit(solution)/shard_map/cross_forward/pallas_call | solution.py:1002
  285.5 52.5 %feed_forward.1 = (bf16[1024,4608]{1,0:T(8,128)(2,1)}, f32[1024,1152]{1,0:T(8,128)}, f32[16,1152]{1,0:T(8,128)}, f32[16,4608]{1,0:T(8,128)}) custom-call(s32[5]{0:T(128)} %copy-done.35, f32[1024,1152]{1,0:T(8,128)} %bitcast.57, bf16[1024,1152]{1,0:T(8,128)(2,1)} %bitcast.53, bf16[3,1024,1152]{2,1,0:T(8,128)(2,1)} %feed_forward_grad.1.refs_3_, ...), custom_call_target="tpu_custom_call" | custom-call | flops 5435817984 | bytes 12500000 | tf_op jit(solution)/shard_map/feed_forward/pallas_call | solution.py:1060
  338.0 26.3 %feed_forward_out.1 = (bf16[256,1152]{1,0:T(8,128)(2,1)}, bf16[256,1152]{1,0:T(8,128)(2,1)}, bf16[256,1152]{1,0:T(8,128)(2,1)}, bf16[256,1152]{1,0:T(8,128)(2,1)...) custom-call(s32[5]{0:T(128)} %copy-done.35, bf16[1024,4608]{1,0:T(8,128)(2,1)} %get-tuple-element.142.refs_1_, ...), custom_call_target="tpu_custom_call" | custom-call | flops 169869312 | bytes 312500 | tf_op jit(solution)/shard_map/feed_forward_out/pallas_call | solution.py:1105
  367.0 58.7 %cross_temporal_backward.2 = (bf16[4,48,1152]{2,1,0:T(8,128)(2,1)}, bf16[4,48,1152]{2,1,0:T(8,128)(2,1)}, bf16[4,48,1152]{2,1,0:T(8,128)(2,1)}, bf16[4,48,1152]{...) custom-call(bf16[4,64,1152]{2,1,0:T(8,128)(2,1)} %get-tuple-element.131.refs_0_, ...), custom_call_target="tpu_custom_call" | custom-call | flops 222953472 | bytes 468750 | tf_op jit(solution)/shard_map/cross_temporal_backward/pallas_call | solution.py:1153
  430.2 23.7 %cross_temporal_backward.3 = (bf16[4,16,1152]{2,1,0:T(8,128)(2,1)}, bf16[4,16,1152]{2,1,0:T(8,128)(2,1)}, bf16[4,16,1152]{2,1,0:T(8,128)(2,1)}, bf16[4,16,1152]{...) custom-call(bf16[4,64,1152]{2,1,0:T(8,128)(2,1)} %get-tuple-element.131.refs_0_, ...), custom_call_target="tpu_custom_call" | custom-call | flops 74317824 | bytes 468750 | tf_op jit(solution)/shard_map/cross_temporal_backward/pallas_call | solution.py:1153
  457.7 9.5 %pack_early.1 = bf16[32,128,128]{2,1,0:T(8,128)(2,1)} custom-call(f32[256,1152]{1,0:T(8,128)} %get-tuple-element.171.refs_0_, f32[256,1152]{1,0:T(8,128)} %get-tuple-element.173.refs_1_, f32[8,256,256]{2,1,0:T(8,128)} %get-tuple-element.174.refs_2_, f32[8,256,256]{2,1,0:T(8,128)} %get-tuple-element.175.refs_3_, f32[8,256,256]{2,1,0:T(8,128)} %get-tuple-element.176.refs_4_, ...), custom_call_target="tpu_custom_call" | custom-call | flops 781250 | bytes 125000 | tf_op jit(solution)/shard_map/pack_early/pallas_call | solution.py:1291
  467.2 7.1 %collective-permute-done.16.refs_3_ = bf16[4,48,1152]{2,1,0:T(8,128)(2,1)S(1)} collective-permute-done((bf16[4,48,1152]{2,1,0:T(8,128)(2,1)}, bf16[4,48,1152]{2,1,0:T(8,128)(2,1)S(1)}, u32[]{:S(2)}, u32[]{:S(2)}) %collective-permute-start.16) | collective-permute-done | bytes 442400 | tf_op jit(solution)/shard_map/ppermute | solution.py:1378
  474.3 5.0 collective-permute-done.19.refs_7_
  479.4 5.4 all-to-all-start.2
  484.8 20.0 %spatial_backward.2 = (bf16[4,256,3584]{2,1,0:T(8,128)(2,1)}, f32[128,1152]{1,0:T(8,128)}) custom-call(s32[1]{0:T(128)} %bitcast.seq_ref.refs_0_, bf16[4,48,1152]{2,1,0:T(8,128)(2,1)} %get-tuple-element.193.refs_1_, bf16[4,48,1152]{2,1,0:T(8,128)(2,1)} %copy-done.11, bf16[4,48,1152]{2,1,0:T(8,128)(2,1)} %copy-done.12, bf16[4,48,1152]{2,1,0:T(8,128)(2,1)} %copy-done.13, ...), custom_call_target="tpu_custom_call" | custom-call | flops 63700992 | bytes 312500 | tf_op jit(solution)/shard_map/spatial_backward/pallas_call | solution.py:1200
  504.8 5.0 all-to-all-done.2.got_ref
  517.8 20.3 %spatial_backward.3 = (bf16[4,256,3584]{2,1,0:T(8,128)(2,1)}, bf16[32,48,128]{2,1,0:T(8,128)(2,1)}) custom-call(s32[1]{0:T(128)} %bitcast.seq_ref.refs_0_, bf16[4,48,1152]{2,1,0:T(8,128)(2,1)} %get-tuple-element.193.refs_1_, bf16[4,48,1152]{2,1,0:T(8,128)(2,1)} %copy-done.11, bf16[4,48,1152]{2,1,0:T(8,128)(2,1)} %copy-done.12, ...), custom_call_target="tpu_custom_call", output_to_operand_aliasing={{0}: (9, {})} | custom-call | flops 63700992 | bytes 312500 | tf_op jit(solution)/shard_map/spatial_backward/pallas_call | solution.py:1200
  539.5 3.8 all-to-all-start.3
  543.3 19.6 %spatial_input_grad.1 = bf16[4,256,1152]{2,1,0:T(8,128)(2,1)} custom-call(s32[1]{0:T(128)} %bitcast.seq_ref.refs_0_, bf16[4,48,1152]{2,1,0:T(8,128)(2,1)} %get-tuple-element.193.refs_1_, bf16[4,48,1152]{2,1,0:T(8,128)(2,1)} %copy-done.11, bf16[4,48,1152]{2,1,0:T(8,128)(2,1)} %copy-done.12, bf16[4,48,1152]{2,1,0:T(8,128)(2,1)} %copy-done.13, ...), custom_call_target="tpu_custom_call" | custom-call | flops 127401984 | bytes 312500 | tf_op jit(solution)/shard_map/spatial_input_grad/pallas_call | solution.py:1237
  565.7 3.6 collective-permute-start.26
  570.4 3.9 put_in_place.1
  574.3 4.5 collective-permute-done.25.refs_7_
  580.0 4.5 assemble.1
  (153 shorter events, 71.3 us)
Async XLA Ops:
  7.2 100.1 %all-gather.4.cloned.1.call-start = ((), (), s32[]{:S(2)}) async-start(), calls=%async_computation.4 | async-start | bytes 14929920 | tf_op jit(solution)/shard_map/all_gather | solution.py:1373
  15.1 212.4 %all-gather.6.cloned.1.call-start = ((), (), s32[]{:S(2)}) async-start(), calls=%async_computation.5 | async-start | bytes 23887872 | tf_op jit(solution)/shard_map/all_gather | solution.py:1373
  17.8 266.7 %all-gather.8.cloned.1.call-start = ((), (), s32[]{:S(2)}) async-start(), calls=%async_computation.6 | async-start | bytes 11943936 | tf_op jit(solution)/shard_map/all_gather | solution.py:1373
  45.8 32.8 %all-to-all-start.1 = ((bf16[8,624,128]{2,1,0:T(8,128)(2,1)}), bf16[8,624,128]{2,1,0:T(8,128)(2,1)S(1)}, u32[]{:S(2)}, u32[]{:S(2)}) async-start(bf16[8,624,128]{2,1,0:T(8,128)(2,1)} %pick.1), calls=%async_computation.1 | async-start | bytes 2555904 | tf_op jit(solution)/shard_map/all_to_all | solution.py:1363
  52.5 33.5 %collective-permute-start.2 = (bf16[4,64,1152]{2,1,0:T(8,128)(2,1)}, bf16[4,64,1152]{2,1,0:T(8,128)(2,1)S(1)}, u32[]{:S(2)}, u32[]{:S(2)}) collective-permute-start(bf16[4,64,1152]{2,1,0:T(8,128)(2,1)} %get-tuple-element.231), channel_id=1, source_target_pairs={{0,24},{8,0},{16,8},{24,16},{1,25},{9,1},{17,9},{25,17},{2,26},{10... | collective-permute-start | bytes 1769480 | tf_op jit(solution)/shard_map/ppermute | solution.py:1378
  56.1 51.1 %collective-permute-start.1 = (bf16[4,64,1152]{2,1,0:T(8,128)(2,1)}, bf16[4,64,1152]{2,1,0:T(8,128)(2,1)S(1)}, u32[]{:S(2)}, u32[]{:S(2)}) collective-permute-start(bf16[4,64,1152]{2,1,0:T(8,128)(2,1)} %get-tuple-element.232), channel_id=1, source_target_pairs={{0,16},{8,24},{16,0},{24,8},{1,17},{9,25},{17,1},{25,9},{2,18},{10... | collective-permute-start | bytes 1769480 | tf_op jit(solution)/shard_map/ppermute | solution.py:1378
  56.1 51.1 %collective-permute-start = (bf16[4,64,1152]{2,1,0:T(8,128)(2,1)}, bf16[4,64,1152]{2,1,0:T(8,128)(2,1)S(1)}, u32[]{:S(2)}, u32[]{:S(2)}) collective-permute-start(bf16[4,64,1152]{2,1,0:T(8,128)(2,1)} %get-tuple-element.233), channel_id=1, source_target_pairs={{0,8},{8,16},{16,24},{24,0},{1,9},{9,17},{17,25},{25,1},{2,10},{10... | collective-permute-start | bytes 1769480 | tf_op jit(solution)/shard_map/ppermute | solution.py:1378
  110.8 38.7 %collective-permute-start.4 = (bf16[576,1152]{1,0:T(8,128)(2,1)S(1)}, bf16[576,1152]{1,0:T(8,128)(2,1)S(1)}, u32[]{:S(2)}, u32[]{:S(2)}) collective-permute-start(bf16[576,1152]{1,0:T(8,128)(2,1)S(1)} %get-tuple-element.227.refs_4_.refs_6_), channel_id=1, source_target_pairs={{0,24},{8,0},{16,8},{24,16},{1,25},{9,1},{17,9},{25,17},{2,26},{10... | collective-permute-start | bytes 3981320 | tf_op jit(solution)/shard_map/ppermute | solution.py:1378
  110.8 60.8 %collective-permute-start.3 = (bf16[576,1152]{1,0:T(8,128)(2,1)S(1)}, bf16[576,1152]{1,0:T(8,128)(2,1)S(1)}, u32[]{:S(2)}, u32[]{:S(2)}) collective-permute-start(bf16[576,1152]{1,0:T(8,128)(2,1)S(1)} %get-tuple-element.227.refs_4_.refs_6_), channel_id=1, source_target_pairs={{0,8},{8,16},{16,24},{24,0},{1,9},{9,17},{17,25},{25,1},{2,10},{10... | collective-permute-start | bytes 3981320 | tf_op jit(solution)/shard_map/ppermute | solution.py:1378
  171.6 5.2 collective-permute-start.5
  172.1 24.6 %collective-permute-start.7 = (bf16[4,64,1152]{2,1,0:T(8,128)(2,1)}, bf16[4,64,1152]{2,1,0:T(8,128)(2,1)}, u32[]{:S(2)}, u32[]{:S(2)}) collective-permute-start(bf16[4,64,1152]{2,1,0:T(8,128)(2,1)} %get-tuple-element.128), channel_id=1, source_target_pairs={{0,8},{8,16},{16,24},{24,0},{1,9},{9,17},{17,25},{25,1},{2,10},{10... | collective-permute-start | bytes 1769480 | tf_op jit(solution)/shard_map/ppermute | solution.py:1378
  172.1 42.7 %collective-permute-start.8 = (bf16[4,64,1152]{2,1,0:T(8,128)(2,1)}, bf16[4,64,1152]{2,1,0:T(8,128)(2,1)}, u32[]{:S(2)}, u32[]{:S(2)}) collective-permute-start(bf16[4,64,1152]{2,1,0:T(8,128)(2,1)} %get-tuple-element.129), channel_id=1, source_target_pairs={{0,16},{8,24},{16,0},{24,8},{1,17},{9,25},{17,1},{25,9},{2,18},{10... | collective-permute-start | bytes 1769480 | tf_op jit(solution)/shard_map/ppermute | solution.py:1378
  173.4 41.4 %collective-permute-start.9 = (bf16[4,64,1152]{2,1,0:T(8,128)(2,1)}, bf16[4,64,1152]{2,1,0:T(8,128)(2,1)}, u32[]{:S(2)}, u32[]{:S(2)}) collective-permute-start(bf16[4,64,1152]{2,1,0:T(8,128)(2,1)} %get-tuple-element.130), channel_id=1, source_target_pairs={{0,24},{8,0},{16,8},{24,16},{1,25},{9,1},{17,9},{25,17},{2,26},{10... | collective-permute-start | bytes 1769480 | tf_op jit(solution)/shard_map/ppermute | solution.py:1378
  214.8 44.9 %collective-permute-start.10 = (bf16[576,1152]{1,0:T(8,128)(2,1)}, bf16[576,1152]{1,0:T(8,128)(2,1)S(1)}, u32[]{:S(2)}, u32[]{:S(2)}) collective-permute-start(bf16[576,1152]{1,0:T(8,128)(2,1)} %copy-done.6), channel_id=1, source_target_pairs={{0,8},{8,16},{16,24},{24,0},{1,9},{9,17},{17,25},{25,1},{2,10},{10... | collective-permute-start | bytes 3981320 | tf_op jit(solution)/shard_map/ppermute | solution.py:1378
  259.7 24.7 %collective-permute-start.11 = (bf16[576,1152]{1,0:T(8,128)(2,1)S(1)}, bf16[576,1152]{1,0:T(8,128)(2,1)S(1)}, u32[]{:S(2)}, u32[]{:S(2)}) collective-permute-start(bf16[576,1152]{1,0:T(8,128)(2,1)S(1)} %collective-permute-done.10.refs_4_.refs_9_), channel_id=1, source_target_pairs={{0,1},{1,0},{2,3},{3,2},{4,5},{5,4},{6,7},{7,6},{8,9},{9,8},{10,11... | collective-permute-start | bytes 3981320 | tf_op jit(solution)/shard_map/ppermute | solution.py:1407
  364.3 64.3 %collective-permute-start.12 = (bf16[4,64,1152]{2,1,0:T(8,128)(2,1)}, bf16[4,64,1152]{2,1,0:T(8,128)(2,1)S(1)}, u32[]{:S(2)}, u32[]{:S(2)}) collective-permute-start(bf16[4,64,1152]{2,1,0:T(8,128)(2,1)} %bitcast.83), channel_id=1, source_target_pairs={{0,24},{8,0},{16,8},{24,16},{1,25},{9,1},{17,9},{25,17},{2,26},{10... | collective-permute-start | bytes 1769480 | tf_op jit(solution)/shard_map/ppermute | solution.py:1378
  364.6 65.6 %collective-permute-start.13 = (bf16[4,64,1152]{2,1,0:T(8,128)(2,1)}, bf16[4,64,1152]{2,1,0:T(8,128)(2,1)S(1)}, u32[]{:S(2)}, u32[]{:S(2)}) collective-permute-start(bf16[4,64,1152]{2,1,0:T(8,128)(2,1)} %bitcast.82), channel_id=1, source_target_pairs={{0,16},{8,24},{16,0},{24,8},{1,17},{9,25},{17,1},{25,9},{2,18},{10... | collective-permute-start | bytes 1769480 | tf_op jit(solution)/shard_map/ppermute | solution.py:1378
  366.1 64.1 %collective-permute-start.14 = (bf16[4,64,1152]{2,1,0:T(8,128)(2,1)}, bf16[4,64,1152]{2,1,0:T(8,128)(2,1)S(1)}, u32[]{:S(2)}, u32[]{:S(2)}) collective-permute-start(bf16[4,64,1152]{2,1,0:T(8,128)(2,1)} %bitcast.81), channel_id=1, source_target_pairs={{0,8},{8,16},{16,24},{24,0},{1,9},{9,17},{17,25},{25,1},{2,10},{10... | collective-permute-start | bytes 1769480 | tf_op jit(solution)/shard_map/ppermute | solution.py:1378
  425.7 31.7 %collective-permute-start.15 = (bf16[4,48,1152]{2,1,0:T(8,128)(2,1)}, bf16[4,48,1152]{2,1,0:T(8,128)(2,1)S(1)}, u32[]{:S(2)}, u32[]{:S(2)}) collective-permute-start(bf16[4,48,1152]{2,1,0:T(8,128)(2,1)} %get-tuple-element.185), channel_id=1, source_target_pairs={{0,24},{8,0},{16,8},{24,16},{1,25},{9,1},{17,9},{25,17},{2,26},{10... | collective-permute-start | bytes 1327112 | tf_op jit(solution)/shard_map/ppermute | solution.py:1378
  428.6 45.7 %collective-permute-start.16 = (bf16[4,48,1152]{2,1,0:T(8,128)(2,1)}, bf16[4,48,1152]{2,1,0:T(8,128)(2,1)S(1)}, u32[]{:S(2)}, u32[]{:S(2)}) collective-permute-start(bf16[4,48,1152]{2,1,0:T(8,128)(2,1)} %get-tuple-element.186), channel_id=1, source_target_pairs={{0,16},{8,24},{16,0},{24,8},{1,17},{9,25},{17,1},{25,9},{2,18},{10... | collective-permute-start | bytes 1327112 | tf_op jit(solution)/shard_map/ppermute | solution.py:1378
  428.6 45.7 %collective-permute-start.17 = (bf16[4,48,1152]{2,1,0:T(8,128)(2,1)}, bf16[4,48,1152]{2,1,0:T(8,128)(2,1)S(1)}, u32[]{:S(2)}, u32[]{:S(2)}) collective-permute-start(bf16[4,48,1152]{2,1,0:T(8,128)(2,1)} %get-tuple-element.187), channel_id=1, source_target_pairs={{0,8},{8,16},{16,24},{24,0},{1,9},{9,17},{17,25},{25,1},{2,10},{10... | collective-permute-start | bytes 1327112 | tf_op jit(solution)/shard_map/ppermute | solution.py:1378
  453.9 20.4 %collective-permute-start.18 = (bf16[4,16,1152]{2,1,0:T(8,128)(2,1)}, bf16[4,16,1152]{2,1,0:T(8,128)(2,1)S(1)}, u32[]{:S(2)}, u32[]{:S(2)}) collective-permute-start(bf16[4,16,1152]{2,1,0:T(8,128)(2,1)} %get-tuple-element.190), channel_id=1, source_target_pairs={{0,24},{8,0},{16,8},{24,16},{1,25},{9,1},{17,9},{25,17},{2,26},{10... | collective-permute-start | bytes 442376 | tf_op jit(solution)/shard_map/ppermute | solution.py:1378
  456.3 23.0 %collective-permute-start.19 = (bf16[4,16,1152]{2,1,0:T(8,128)(2,1)}, bf16[4,16,1152]{2,1,0:T(8,128)(2,1)S(1)}, u32[]{:S(2)}, u32[]{:S(2)}) collective-permute-start(bf16[4,16,1152]{2,1,0:T(8,128)(2,1)} %get-tuple-element.191), channel_id=1, source_target_pairs={{0,16},{8,24},{16,0},{24,8},{1,17},{9,25},{17,1},{25,9},{2,18},{10... | collective-permute-start | bytes 442376 | tf_op jit(solution)/shard_map/ppermute | solution.py:1378
  457.4 22.0 %collective-permute-start.20 = (bf16[4,16,1152]{2,1,0:T(8,128)(2,1)}, bf16[4,16,1152]{2,1,0:T(8,128)(2,1)S(1)}, u32[]{:S(2)}, u32[]{:S(2)}) collective-permute-start(bf16[4,16,1152]{2,1,0:T(8,128)(2,1)} %get-tuple-element.192), channel_id=1, source_target_pairs={{0,8},{8,16},{16,24},{24,0},{1,9},{9,17},{17,25},{25,1},{2,10},{10... | collective-permute-start | bytes 442376 | tf_op jit(solution)/shard_map/ppermute | solution.py:1378
  479.4 30.4 %all-to-all-start.2 = ((bf16[32,128,128]{2,1,0:T(8,128)(2,1)}), bf16[32,128,128]{2,1,0:T(8,128)(2,1)S(1)}, u32[]{:S(2)}, u32[]{:S(2)}) async-start(bf16[32,128,128]{2,1,0:T(8,128)(2,1)} %pack_early.1), calls=%async_computation.2 | async-start | bytes 2097152 | tf_op jit(solution)/shard_map/all_to_all | solution.py:1363
  512.9 25.2 %collective-permute-start.23 = (bf16[8,128,128]{2,1,0:T(8,128)(2,1)}, bf16[8,128,128]{2,1,0:T(8,128)(2,1)S(1)}, u32[]{:S(2)}, u32[]{:S(2)}) collective-permute-start(bf16[8,128,128]{2,1,0:T(8,128)(2,1)} %combine.2.refs_1_), channel_id=1, source_target_pairs={{0,24},{8,0},{16,8},{24,16},{1,25},{9,1},{17,9},{25,17},{2,26},{10... | collective-permute-start | bytes 786440 | tf_op jit(solution)/shard_map/ppermute | solution.py:1378
  516.4 23.1 %collective-permute-start.22 = (bf16[8,128,128]{2,1,0:T(8,128)(2,1)}, bf16[8,128,128]{2,1,0:T(8,128)(2,1)S(1)}, u32[]{:S(2)}, u32[]{:S(2)}) collective-permute-start(bf16[8,128,128]{2,1,0:T(8,128)(2,1)} %combine.2.refs_1_), channel_id=1, source_target_pairs={{0,16},{8,24},{16,0},{24,8},{1,17},{9,25},{17,1},{25,9},{2,18},{10... | collective-permute-start | bytes 786440 | tf_op jit(solution)/shard_map/ppermute | solution.py:1378
  517.8 21.7 %collective-permute-start.21 = (bf16[8,128,128]{2,1,0:T(8,128)(2,1)}, bf16[8,128,128]{2,1,0:T(8,128)(2,1)S(1)}, u32[]{:S(2)}, u32[]{:S(2)}) collective-permute-start(bf16[8,128,128]{2,1,0:T(8,128)(2,1)} %combine.2.refs_1_), channel_id=1, source_target_pairs={{0,8},{8,16},{16,24},{24,0},{1,9},{9,17},{17,25},{25,1},{2,10},{10... | collective-permute-start | bytes 786440 | tf_op jit(solution)/shard_map/ppermute | solution.py:1378
  539.5 23.5 %all-to-all-start.3 = ((bf16[32,48,128]{2,1,0:T(8,128)(2,1)}), bf16[32,48,128]{2,1,0:T(8,128)(2,1)S(1)}, u32[]{:S(2)}, u32[]{:S(2)}) async-start(bf16[32,48,128]{2,1,0:T(8,128)(2,1)} %get-tuple-element.216), calls=%async_computation.3 | async-start | bytes 786432 | tf_op jit(solution)/shard_map/all_to_all | solution.py:1363
  565.7 8.6 %collective-permute-start.26 = (bf16[8,48,128]{2,1,0:T(8,128)(2,1)}, bf16[8,48,128]{2,1,0:T(8,128)(2,1)S(1)}, u32[]{:S(2)}, u32[]{:S(2)}) collective-permute-start(bf16[8,48,128]{2,1,0:T(8,128)(2,1)} %combine.3.refs_5_), channel_id=1, source_target_pairs={{0,24},{8,0},{16,8},{24,16},{1,25},{9,1},{17,9},{25,17},{2,26},{10... | collective-permute-start | bytes 294920 | tf_op jit(solution)/shard_map/ppermute | solution.py:1378
  569.3 9.5 %collective-permute-start.25 = (bf16[8,48,128]{2,1,0:T(8,128)(2,1)}, bf16[8,48,128]{2,1,0:T(8,128)(2,1)S(1)}, u32[]{:S(2)}, u32[]{:S(2)}) collective-permute-start(bf16[8,48,128]{2,1,0:T(8,128)(2,1)} %combine.3.refs_5_), channel_id=1, source_target_pairs={{0,16},{8,24},{16,0},{24,8},{1,17},{9,25},{17,1},{25,9},{2,18},{10... | collective-permute-start | bytes 294920 | tf_op jit(solution)/shard_map/ppermute | solution.py:1378
  569.3 9.5 %collective-permute-start.24 = (bf16[8,48,128]{2,1,0:T(8,128)(2,1)}, bf16[8,48,128]{2,1,0:T(8,128)(2,1)S(1)}, u32[]{:S(2)}, u32[]{:S(2)}) collective-permute-start(bf16[8,48,128]{2,1,0:T(8,128)(2,1)} %combine.3.refs_5_), channel_id=1, source_target_pairs={{0,8},{8,16},{16,24},{24,0},{1,9},{9,17},{17,25},{25,1},{2,10},{10... | collective-permute-start | bytes 294920 | tf_op jit(solution)/shard_map/ppermute | solution.py:1378
  (39 other events, 584.8 us)
Sparse Core Ops, SparseCore 0:
  15.2 88.8 all-gather.3
  106.6 108.9 all-gather.5
  217.5 63.7 all-gather.7

commit v8 on v7

--- a/solution.py
+++ b/solution.py
@@ -758,7 +758,7 @@
         out_ref[0, pl.ds(place_of(seq_ref, k, len(pieces), places), places), :] = ref[0]
 
 
-def pack_early(clips, shares, *refs):
+def pack_early(clips, shares, counts, *refs):
     gw_refs, refs = refs[:shares], refs[shares:]
     dk_refs, refs = refs[:shares], refs[shares:]
     dv_refs, refs = refs[:shares], refs[shares:]
@@ -773,9 +773,11 @@
     at = gw_refs[0].shape[0]
     table_ref[:at, :] = added([ref[...] for ref in gw_refs])
     width = table_ref.shape[1]
-    for ref in others:
-        for k in range(ref.shape[1] // width):
-            table_ref[at : at + RANK, :] = ref[:, k * width : (k + 1) * width]
+    for count in counts:
+        each, others = others[:count], others[count:]
+        for k in range(each[0].shape[1] // width):
+            cols = slice(k * width, (k + 1) * width)
+            table_ref[at : at + RANK, :] = added([ref[:, cols] for ref in each])
             at += RANK
     table_ref[at:, :] = jnp.zeros((table_ref.shape[0] - at, width), F32)
     context = ctx_ref[...].astype(F32)
@@ -1281,12 +1283,12 @@
     return pl.BlockSpec(memory_space=pltpu.VMEM)
 
 
-def run_pack_early(gw, dk, dv, sources, clips, parts):
+def run_pack_early(gw, dk, dv, others, sources, clips, parts):
     d = gw[0].shape[1]
     packed = (clips * parts, *packed_rows(EARLY_BLOCKS // parts, d // clips))
 
     def body(*refs):
-        pack_early(clips, len(gw), *refs)
+        pack_early(clips, len(gw), [len(each) for each in others], *refs)
 
     return pl.pallas_call(
         body,
@@ -1295,7 +1297,7 @@
         compiler_params=PLAIN,
         cost_estimate=cost(50000000, 8000000, 64),
         name="pack_early",
-    )(*gw, *dk, *dv, *sources)
+    )(*gw, *dk, *dv, *[array for each in others for array in each], *sources)
 
 
 def run_assemble(seq, early, late, wide_shape, narrow_shape):
@@ -1504,12 +1506,24 @@
     g3 = g3.reshape(FRAMES, places, d)
     groups = FRAMES * places // ROWS
     saved = kept_t + kept_c
-    *x4, grad_b25, grad_down = run_feed_forward_out(
-        active, x3, cot, mods, maps_f, down, parts, 0, 1
-    )
-    x4[0], g3 = lax.optimization_barrier((x4[0], g3))
-    output = to_frames([piece.reshape(frames, places, d) for piece in x4])
-    shares = [groups - 1, 1] if groups > 1 else [1]
+    turns = 2 if groups % 2 == 0 and parts % 2 == 0 else 1
+    output, grad_b25, grad_down = [None] * parts, [], []
+
+    def finish_tokens(turn, active):
+        *x4, b25, rows = run_feed_forward_out(active, x3, cot, mods, maps_f, down, parts, turn, turns)
+        grad_b25.append(b25)
+        grad_down.append(rows)
+        for k, piece in enumerate(x4, turn * parts // turns):
+            output[k] = piece.reshape(frames, places, d)
+
+    def send_tokens(turn):
+        for k in range(turn * parts // turns, (turn + 1) * parts // turns):
+            output[k] = send(output[k], "seq", -k) if k else output[k]
+
+    finish_tokens(turns - 1, active)
+    output[-1], g3 = lax.optimization_barrier((output[-1], g3))
+    send_tokens(turns - 1)
+    shares = [groups - groups // 2, groups // 2] if groups > 1 else [1]
     g1, gw, dk, dv = [], [], [], []
     for share, size in enumerate(shares):
         *pieces, gw_part, dk_part, dv_part = run_cross_temporal_backward(
@@ -1518,30 +1532,29 @@
         gw.append(gw_part)
         dk.append(dk_part)
         dv.append(dv_part)
-        pieces[0], g3 = lax.optimization_barrier((pieces[0], g3))
-        if share == 0:
-            g3, *output = lax.optimization_barrier((g3, *output))
+        if share == 0 and turns > 1:
+            half = parts // turns
+            pieces[0], g3, *output[half:] = lax.optimization_barrier((pieces[0], g3, *output[half:]))
+        else:
+            pieces[0], g3 = lax.optimization_barrier((pieces[0], g3))
         g1.append(to_frames(pieces))
-    sources = [grad_a24, grad_b25, grad_b24, grad_down, kept_c[7], kept_c[8], ctx, masks, wide]
-    packed = run_pack_early(gw, dk, dv, sources, clips, parts)
+    if len(shares) > 1:
+        active, gw[-1], *g1[0] = lax.optimization_barrier((active, gw[-1], *g1[0]))
+    if turns > 1:
+        finish_tokens(0, active)
+        send_tokens(0)
+    others = [[grad_a24], grad_b25, [grad_b24], grad_down]
+    sources = [kept_c[7], kept_c[8], ctx, masks, wide]
+    packed = run_pack_early(gw, dk, dv, others, sources, clips, parts)
     g1 = [piece for done in g1 for piece in done]
     packed, *g1 = lax.optimization_barrier((packed, *g1))
     got = exchange(packed, ("fsdp", "seq"))
     halves = len(shares)
-    before = []
-    spatial = [frames - frames // 2, frames // 2] if frames > 1 else [1]
-    for turn, size in enumerate(spatial):
-        grads, sums = before = run_spatial_backward(
-            seq, g1, halves, frames_in, kept_s, mods, masks, wide, w_s, clips, sum(spatial[:turn]), size, before
-        )
-        if turn == 0:
-            got, sums = lax.optimization_barrier((got, sums))
-            table = run_combine(all_index, got, adapters)
-            if len(spatial) > 1:
-                table, sums = lax.optimization_barrier((table, sums))
-            early = to_all(table)
-        before = [grads, sums]
-    packed, *early = lax.optimization_barrier((sums, *early))
+    grads, packed = run_spatial_backward(
+        seq, g1, halves, frames_in, kept_s, mods, masks, wide, w_s, clips, 0, frames, []
+    )
+    packed, got, *output = lax.optimization_barrier((packed, got, *output))
+    early = to_all(run_combine(all_index, got, adapters))
     g0 = run_spatial_input_grad(seq, g1, halves, frames_in, grads, mods, wide, w_s)
     got, g0 = lax.optimization_barrier((exchange(packed, ("fsdp", "seq")), g0))
     late = run_combine(all_index, got, adapters)

time: 597 us -> 586 us (0.982)
  waiting for transfers between devices: 104 us -> 87.6 us
    ppermute x24, waiting for transfers between devices: 79.5 us -> 67.9 us  [send(): lax.ppermute(array, axis, [(i, (i + shift) % size) for i in range(size)])]
    pallas_call x1 -> x2, Pallas kernels: 26.3 us -> 33.1 us  [run_feed_forward_out(): pl.pallas_call(body, grid=(steps,), in_specs=[in_smem(), pl.BlockSpec((RO...]
    pallas_call x2 -> x1, Pallas kernels: 40.3 us -> 34.6 us  [run_spatial_backward(): pl.pallas_call(body, grid=(count,), in_specs=[in_smem()] + [pl.BlockSpec(...]
  transfers between devices with their start and end apart: 33 -> 33, of which waited for: 10 -> 7; matrix products, arithmetic and copies ran while one was open for 6% -> 6% of each run, Pallas kernels for 46% -> 50%
where the time goes in v8:
time: 586 us; the launch traced here: 580 us
  Pallas kernels  361 us (62%)
  waiting for transfers between devices  87.6 us (15%)
  starting transfers between devices  59.8 us (10%)
  local copies, waits for them, and re-layouts  35.1 us (6%)
  between operations  15.5 us (3%)
  other arithmetic  11.7 us (2%)
  blocking collectives  9.63 us (2%)
    pallas_call x2, Pallas kernels, run_cross_temporal_backward(): pl.pallas_call(body, grid=(groups,), in_specs=[pl.BlockSpec((own_frames,...  84.4 us
    ppermute x24, waiting for transfers between devices, send(): lax.ppermute(array, axis, [(i, (i + shift) % size) for i in range(size)])  67.9 us
    pallas_call x1, Pallas kernels, run_feed_forward(): pl.pallas_call(body, grid=(tokens // ROWS,), in_specs=[in_smem(), rows, r...  52.5 us
    ppermute x24, starting transfers between devices, send(): lax.ppermute(array, axis, [(i, (i + shift) % size) for i in range(size)])  46 us
    pallas_call x1, Pallas kernels, run_spatial_backward(): pl.pallas_call(body, grid=(count,), in_specs=[in_smem()] + [pl.BlockSpec(...  34.6 us
    pallas_call x2, Pallas kernels, run_feed_forward_out(): pl.pallas_call(body, grid=(steps,), in_specs=[in_smem(), pl.BlockSpec((RO...  33.1 us
    pallas_call x1, Pallas kernels, run_temporal_forward(): pl.pallas_call(body, grid=(groups,), in_specs=[pl.BlockSpec((own_frames,...  32.2 us
    pallas_call x1, Pallas kernels, run_spatial_forward(): pl.pallas_call(spatial_forward, grid=(frames,), in_specs=[in_smem(), row_...  31.6 us
  transfers between devices with their start and end apart: 33, of which 7 were waited for; matrix products, arithmetic and copies ran while one was open for 6% of the time, Pallas kernels for 50%

profile of v8, /device:TPU:0, one launch (start us, length us, event | category | flops | bytes accessed | tf_op | source)
XLA Modules:
  0.0 580.3 jit_solution(2791470284933582202)
XLA Ops:
  18.6 9.6 %all_to_all.23 = s32[8,1,1]{2,1,0:T(1,128)S(1)} all-to-all(s32[8,1,1]{2,1,0:T(1,128)S(1)} %broadcast_in_dim.23), channel_id=1, replica_groups=mesh['seq'=4,'fsdp'=8] {'fsdp'}, dimensions={0} | all-to-all | bytes 64 | tf_op jit(solution)/shard_map/all_to_all | solution.py:1365
  28.9 3.5 pick.1
  32.5 5.2 reshape_squeeze.7
  41.0 4.6 reshape.53
  45.7 3.6 all-to-all-start.1
  52.5 3.6 collective-permute-start.2
  58.9 19.5 %all-to-all-done.1.refs_0_ = bf16[8,624,128]{2,1,0:T(8,128)(2,1)S(1)} async-done(((bf16[8,624,128]{2,1,0:T(8,128)(2,1)}), bf16[8,624,128]{2,1,0:T(8,128)(2,1)S(1)}, u32[]{:S(2)}, u32[]{:S(2)}) %all-to-all-start.1) | async-done | bytes 1277984 | tf_op jit(solution)/shard_map/all_to_all | solution.py:1365
  79.5 4.7 unpick.1.ad_ref.refs_6_.refs_22_.refs_16_.refs_19_.refs_12_
  85.9 21.2 %collective-permute-done.1 = bf16[4,64,1152]{2,1,0:T(8,128)(2,1)S(1)} collective-permute-done((bf16[4,64,1152]{2,1,0:T(8,128)(2,1)}, bf16[4,64,1152]{2,1,0:T(8,128)(2,1)S(1)}, u32[]{:S(2)}, u32[]{:S(2)}) %collective-permute-start.1) | collective-permute-done | bytes 589856 | tf_op jit(solution)/shard_map/ppermute | solution.py:1380
  114.8 31.6 %spatial_forward.1 = (bf16[4,64,1152]{2,1,0:T(8,128)(2,1)}, bf16[4,64,1152]{2,1,0:T(8,128)(2,1)}, bf16[4,64,1152]{2,1,0:T(8,128)(2,1)}, bf16[4,64,1152]{2,1,0:T(...) custom-call(s32[1]{0:T(128)} %bitcast.seq_ref.refs_0_, ...), custom_call_target="tpu_custom_call" | custom-call | flops 3397386240 | bytes 7500000 | tf_op jit(solution)/shard_map/spatial_forward/pallas_call | solution.py:918
  149.8 22.3 %collective-permute-done.3.refs_5_.refs_7_ = bf16[576,1152]{1,0:T(8,128)(2,1)S(1)} collective-permute-done((bf16[576,1152]{1,0:T(8,128)(2,1)S(1)}, bf16[576,1152]{1,0:T(8,128)(2,1)S(1)}, u32[]{:S(2)}, u32[]{:S(2)}) %collective-permute-start.3) | collective-permute-done | bytes 1327136 | tf_op jit(solution)/shard_map/ppermute | solution.py:1380
  178.5 18.5 %feed_forward_grad.1.refs_3_ = bf16[3,1024,1152]{2,1,0:T(8,128)(2,1)} custom-call(s32[4]{0:T(128)} %pad_add_fusion.1.refs_0_, bf16[1024,1152]{1,0:T(8,128)(2,1)} %bitcast.48, f32[6,1152]{1,0:T(8,128)} %bitcast.62, bf16[10,16,1152]{2,1,0:T(8,128)(2,1)} %slice.44.refs_3_.refs_7_.refs_5_, bf16[576,1152]{1,0:T(8,128)(2,1)} %copy-done.2, ...), custom_call_target="tpu_custom_call" | custom-call | flops 2038431744 | bytes 5000000 | tf_op jit(solution)/shard_map/feed_forward_grad/pallas_call | solution.py:1033
  197.0 18.3 %collective-permute-done.8.refs_2_ = bf16[4,64,1152]{2,1,0:T(8,128)(2,1)} collective-permute-done((bf16[4,64,1152]{2,1,0:T(8,128)(2,1)}, bf16[4,64,1152]{2,1,0:T(8,128)(2,1)}, u32[]{:S(2)}, u32[]{:S(2)}) %collective-permute-start.8) | collective-permute-done | bytes 589856 | tf_op jit(solution)/shard_map/ppermute | solution.py:1380
  215.3 12.6 %collective-permute-start.10 = (bf16[576,1152]{1,0:T(8,128)(2,1)}, bf16[576,1152]{1,0:T(8,128)(2,1)S(1)}, u32[]{:S(2)}, u32[]{:S(2)}) collective-permute-start(bf16[576,1152]{1,0:T(8,128)(2,1)} %copy-done.6), channel_id=1, source_target_pairs={{0,8},{8,16},{16,24},{24,0},{1,9},{9,17},{17,25},{25,1},{2,10},{10... | collective-permute-start | bytes 3981320 | tf_op jit(solution)/shard_map/ppermute | solution.py:1380
  228.0 32.2 %temporal_forward.1 = (bf16[16,64,1152]{2,1,0:T(8,128)(2,1)}, bf16[16,64,1152]{2,1,0:T(8,128)(2,1)}, bf16[16,64,1152]{2,1,0:T(8,128)(2,1)}, bf16[16,64,1152]{2,1...) custom-call(bf16[4,64,1152]{2,1,0:T(8,128)(2,1)} %get-tuple-element., ...), custom_call_target="tpu_custom_call" | custom-call | flops 3397386240 | bytes 7500000 | tf_op jit(solution)/shard_map/temporal_forward/pallas_call | solution.py:964
  261.2 23.8 %cross_forward.1 = (bf16[16,64,1152]{2,1,0:T(8,128)(2,1)}, bf16[16,64,1152]{2,1,0:T(8,128)(2,1)}, f32[4,16,256]{2,1,0:T(8,128)}, bf16[4,256,16]{2,1,0:T(8,128)(2...) custom-call(f32[16,64,1152]{2,1,0:T(8,128)} %get-tuple-element.137.x, ...), custom_call_target="tpu_custom_call" | custom-call | flops 2717908992 | bytes 7500000 | tf_op jit(solution)/shard_map/cross_forward/pallas_call | solution.py:1004
  286.1 52.5 %feed_forward.1 = (bf16[1024,4608]{1,0:T(8,128)(2,1)}, f32[1024,1152]{1,0:T(8,128)}, f32[16,1152]{1,0:T(8,128)}, f32[16,4608]{1,0:T(8,128)}) custom-call(s32[5]{0:T(128)} %copy-done.35, f32[1024,1152]{1,0:T(8,128)} %bitcast.52, bf16[1024,1152]{1,0:T(8,128)(2,1)} %bitcast.49, bf16[3,1024,1152]{2,1,0:T(8,128)(2,1)} %feed_forward_grad.1.refs_3_, ...), custom_call_target="tpu_custom_call" | custom-call | flops 5435817984 | bytes 12500000 | tf_op jit(solution)/shard_map/feed_forward/pallas_call | solution.py:1062
  338.7 16.5 %feed_forward_out.2 = (bf16[256,1152]{1,0:T(8,128)(2,1)}, bf16[256,1152]{1,0:T(8,128)(2,1)}, f32[16,1152]{1,0:T(8,128)}, f32[16,4608]{1,0:T(8,128)}) custom-call(s32[5]{0:T(128)} %copy-done.35, bf16[1024,4608]{1,0:T(8,128)(2,1)} %get-tuple-element.178.refs_1_, f32[1024,1152]{1,0:T(8,128)} %bitcast.53, bf16[1024,1152]{1,0:T(8,128)(2,1)} %bitcast.50, ...), custom_call_target="tpu_custom_call" | custom-call | flops 84934656 | bytes 312500 | tf_op jit(solution)/shard_map/feed_forward_out/pallas_call | solution.py:1107
  355.6 42.1 %cross_temporal_backward.2 = (bf16[4,32,1152]{2,1,0:T(8,128)(2,1)}, bf16[4,32,1152]{2,1,0:T(8,128)(2,1)}, bf16[4,32,1152]{2,1,0:T(8,128)(2,1)}, bf16[4,32,1152]{...) custom-call(bf16[4,64,1152]{2,1,0:T(8,128)(2,1)} %get-tuple-element.131.refs_0_, ...), custom_call_target="tpu_custom_call" | custom-call | flops 148635648 | bytes 468750 | tf_op jit(solution)/shard_map/cross_temporal_backward/pallas_call | solution.py:1155
  403.2 42.3 %cross_temporal_backward.3 = (bf16[4,32,1152]{2,1,0:T(8,128)(2,1)}, bf16[4,32,1152]{2,1,0:T(8,128)(2,1)}, bf16[4,32,1152]{2,1,0:T(8,128)(2,1)}, bf16[4,32,1152]{...) custom-call(bf16[4,64,1152]{2,1,0:T(8,128)(2,1)} %get-tuple-element.131.refs_0_, ...), custom_call_target="tpu_custom_call" | custom-call | flops 148635648 | bytes 468750 | tf_op jit(solution)/shard_map/cross_temporal_backward/pallas_call | solution.py:1155
  445.5 3.9 collective-permute-start.17
  450.1 16.7 %feed_forward_out.3 = (bf16[256,1152]{1,0:T(8,128)(2,1)}, bf16[256,1152]{1,0:T(8,128)(2,1)}, f32[16,1152]{1,0:T(8,128)}, f32[16,4608]{1,0:T(8,128)}) custom-call(s32[5]{0:T(128)} %copy-done.35, bf16[1024,4608]{1,0:T(8,128)(2,1)} %get-tuple-element.178.refs_1_, f32[1024,1152]{1,0:T(8,128)} %bitcast.54, bf16[1024,1152]{1,0:T(8,128)(2,1)} %bitcast.51, ...), custom_call_target="tpu_custom_call" | custom-call | flops 84934656 | bytes 312500 | tf_op jit(solution)/shard_map/feed_forward_out/pallas_call | solution.py:1107
  466.8 9.7 %pack_early.1 = bf16[32,128,128]{2,1,0:T(8,128)(2,1)} custom-call(f32[256,1152]{1,0:T(8,128)} %get-tuple-element.161.refs_0_, f32[256,1152]{1,0:T(8,128)} %get-tuple-element.171.refs_1_, f32[8,256,256]{2,1,0:T(8,128)} %get-tuple-element.172.refs_2_, f32[8,256,256]{2,1,0:T(8,128)} %get-tuple-element.173.refs_3_, f32[8,256,256]{2,1,0:T(8,128)} %get-tuple-element.174.refs_4_, ...), custom_call_target="tpu_custom_call" | custom-call | flops 781250 | bytes 125000 | tf_op jit(solution)/shard_map/pack_early/pallas_call | solution.py:1293
  476.5 5.7 all-to-all-start.2
  482.3 3.7 collective-permute-start.20
  485.9 34.6 %spatial_backward.1 = (bf16[4,256,3584]{2,1,0:T(8,128)(2,1)}, bf16[32,48,128]{2,1,0:T(8,128)(2,1)}) custom-call(s32[1]{0:T(128)} %bitcast.seq_ref.refs_0_, bf16[4,32,1152]{2,1,0:T(8,128)(2,1)} %get-tuple-element.194.refs_1_, bf16[4,32,1152]{2,1,0:T(8,128)(2,1)} %copy-done.15, bf16[4,32,1152]{2,1,0:T(8,128)(2,1)} %copy-done.16, ...), custom_call_target="tpu_custom_call" | custom-call | flops 127401984 | bytes 312500 | tf_op jit(solution)/shard_map/spatial_backward/pallas_call | solution.py:1202
  520.6 3.8 all-to-all-start.3
  526.6 3.6 collective-permute-start.23
  531.3 19.6 %spatial_input_grad.1 = bf16[4,256,1152]{2,1,0:T(8,128)(2,1)} custom-call(s32[1]{0:T(128)} %bitcast.seq_ref.refs_0_, bf16[4,32,1152]{2,1,0:T(8,128)(2,1)} %get-tuple-element.194.refs_1_, bf16[4,32,1152]{2,1,0:T(8,128)(2,1)} %copy-done.15, bf16[4,32,1152]{2,1,0:T(8,128)(2,1)} %copy-done.16, bf16[4,32,1152]{2,1,0:T(8,128)(2,1)} %copy-done.17, ...), custom_call_target="tpu_custom_call" | custom-call | flops 127401984 | bytes 312500 | tf_op jit(solution)/shard_map/spatial_input_grad/pallas_call | solution.py:1239
  557.5 4.0 put_in_place.1
  562.8 4.8 collective-permute-done.25.refs_7_
  568.8 4.5 assemble.1
  (153 shorter events, 61.8 us)
Async XLA Ops:
  7.2 100.0 %all-gather.4.cloned.1.call-start = ((), (), s32[]{:S(2)}) async-start(), calls=%async_computation.4 | async-start | bytes 14929920 | tf_op jit(solution)/shard_map/all_gather | solution.py:1375
  15.1 212.9 %all-gather.6.cloned.1.call-start = ((), (), s32[]{:S(2)}) async-start(), calls=%async_computation.5 | async-start | bytes 23887872 | tf_op jit(solution)/shard_map/all_gather | solution.py:1375
  17.8 267.3 %all-gather.8.cloned.1.call-start = ((), (), s32[]{:S(2)}) async-start(), calls=%async_computation.6 | async-start | bytes 11943936 | tf_op jit(solution)/shard_map/all_gather | solution.py:1375
  45.7 32.7 %all-to-all-start.1 = ((bf16[8,624,128]{2,1,0:T(8,128)(2,1)}), bf16[8,624,128]{2,1,0:T(8,128)(2,1)S(1)}, u32[]{:S(2)}, u32[]{:S(2)}) async-start(bf16[8,624,128]{2,1,0:T(8,128)(2,1)} %pick.1), calls=%async_computation.1 | async-start | bytes 2555904 | tf_op jit(solution)/shard_map/all_to_all | solution.py:1365
  52.5 33.5 %collective-permute-start.2 = (bf16[4,64,1152]{2,1,0:T(8,128)(2,1)}, bf16[4,64,1152]{2,1,0:T(8,128)(2,1)S(1)}, u32[]{:S(2)}, u32[]{:S(2)}) collective-permute-start(bf16[4,64,1152]{2,1,0:T(8,128)(2,1)} %get-tuple-element.231), channel_id=1, source_target_pairs={{0,24},{8,0},{16,8},{24,16},{1,25},{9,1},{17,9},{25,17},{2,26},{10... | collective-permute-start | bytes 1769480 | tf_op jit(solution)/shard_map/ppermute | solution.py:1380
  56.1 51.1 %collective-permute-start.1 = (bf16[4,64,1152]{2,1,0:T(8,128)(2,1)}, bf16[4,64,1152]{2,1,0:T(8,128)(2,1)S(1)}, u32[]{:S(2)}, u32[]{:S(2)}) collective-permute-start(bf16[4,64,1152]{2,1,0:T(8,128)(2,1)} %get-tuple-element.232), channel_id=1, source_target_pairs={{0,16},{8,24},{16,0},{24,8},{1,17},{9,25},{17,1},{25,9},{2,18},{10... | collective-permute-start | bytes 1769480 | tf_op jit(solution)/shard_map/ppermute | solution.py:1380
  56.1 51.1 %collective-permute-start = (bf16[4,64,1152]{2,1,0:T(8,128)(2,1)}, bf16[4,64,1152]{2,1,0:T(8,128)(2,1)S(1)}, u32[]{:S(2)}, u32[]{:S(2)}) collective-permute-start(bf16[4,64,1152]{2,1,0:T(8,128)(2,1)} %get-tuple-element.233), channel_id=1, source_target_pairs={{0,8},{8,16},{16,24},{24,0},{1,9},{9,17},{17,25},{25,1},{2,10},{10... | collective-permute-start | bytes 1769480 | tf_op jit(solution)/shard_map/ppermute | solution.py:1380
  111.3 38.5 %collective-permute-start.4 = (bf16[576,1152]{1,0:T(8,128)(2,1)S(1)}, bf16[576,1152]{1,0:T(8,128)(2,1)S(1)}, u32[]{:S(2)}, u32[]{:S(2)}) collective-permute-start(bf16[576,1152]{1,0:T(8,128)(2,1)S(1)} %get-tuple-element.227.refs_4_.refs_6_), channel_id=1, source_target_pairs={{0,24},{8,0},{16,8},{24,16},{1,25},{9,1},{17,9},{25,17},{2,26},{10... | collective-permute-start | bytes 3981320 | tf_op jit(solution)/shard_map/ppermute | solution.py:1380
  111.3 60.8 %collective-permute-start.3 = (bf16[576,1152]{1,0:T(8,128)(2,1)S(1)}, bf16[576,1152]{1,0:T(8,128)(2,1)S(1)}, u32[]{:S(2)}, u32[]{:S(2)}) collective-permute-start(bf16[576,1152]{1,0:T(8,128)(2,1)S(1)} %get-tuple-element.227.refs_4_.refs_6_), channel_id=1, source_target_pairs={{0,8},{8,16},{16,24},{24,0},{1,9},{9,17},{17,25},{25,1},{2,10},{10... | collective-permute-start | bytes 3981320 | tf_op jit(solution)/shard_map/ppermute | solution.py:1380
  172.1 5.0 collective-permute-start.5
  172.6 24.4 %collective-permute-start.7 = (bf16[4,64,1152]{2,1,0:T(8,128)(2,1)}, bf16[4,64,1152]{2,1,0:T(8,128)(2,1)}, u32[]{:S(2)}, u32[]{:S(2)}) collective-permute-start(bf16[4,64,1152]{2,1,0:T(8,128)(2,1)} %get-tuple-element.128), channel_id=1, source_target_pairs={{0,8},{8,16},{16,24},{24,0},{1,9},{9,17},{17,25},{25,1},{2,10},{10... | collective-permute-start | bytes 1769480 | tf_op jit(solution)/shard_map/ppermute | solution.py:1380
  172.6 42.7 %collective-permute-start.8 = (bf16[4,64,1152]{2,1,0:T(8,128)(2,1)}, bf16[4,64,1152]{2,1,0:T(8,128)(2,1)}, u32[]{:S(2)}, u32[]{:S(2)}) collective-permute-start(bf16[4,64,1152]{2,1,0:T(8,128)(2,1)} %get-tuple-element.129), channel_id=1, source_target_pairs={{0,16},{8,24},{16,0},{24,8},{1,17},{9,25},{17,1},{25,9},{2,18},{10... | collective-permute-start | bytes 1769480 | tf_op jit(solution)/shard_map/ppermute | solution.py:1380
  173.5 41.9 %collective-permute-start.9 = (bf16[4,64,1152]{2,1,0:T(8,128)(2,1)}, bf16[4,64,1152]{2,1,0:T(8,128)(2,1)}, u32[]{:S(2)}, u32[]{:S(2)}) collective-permute-start(bf16[4,64,1152]{2,1,0:T(8,128)(2,1)} %get-tuple-element.130), channel_id=1, source_target_pairs={{0,24},{8,0},{16,8},{24,16},{1,25},{9,1},{17,9},{25,17},{2,26},{10... | collective-permute-start | bytes 1769480 | tf_op jit(solution)/shard_map/ppermute | solution.py:1380
  215.3 44.9 %collective-permute-start.10 = (bf16[576,1152]{1,0:T(8,128)(2,1)}, bf16[576,1152]{1,0:T(8,128)(2,1)S(1)}, u32[]{:S(2)}, u32[]{:S(2)}) collective-permute-start(bf16[576,1152]{1,0:T(8,128)(2,1)} %copy-done.6), channel_id=1, source_target_pairs={{0,8},{8,16},{16,24},{24,0},{1,9},{9,17},{17,25},{25,1},{2,10},{10... | collective-permute-start | bytes 3981320 | tf_op jit(solution)/shard_map/ppermute | solution.py:1380
  260.2 24.8 %collective-permute-start.11 = (bf16[576,1152]{1,0:T(8,128)(2,1)S(1)}, bf16[576,1152]{1,0:T(8,128)(2,1)S(1)}, u32[]{:S(2)}, u32[]{:S(2)}) collective-permute-start(bf16[576,1152]{1,0:T(8,128)(2,1)S(1)} %collective-permute-done.10.refs_4_.refs_9_), channel_id=1, source_target_pairs={{0,1},{1,0},{2,3},{3,2},{4,5},{5,4},{6,7},{7,6},{8,9},{9,8},{10,11... | collective-permute-start | bytes 3981320 | tf_op jit(solution)/shard_map/ppermute | solution.py:1409
  355.1 48.1 %collective-permute-start.13 = (bf16[4,64,1152]{2,1,0:T(8,128)(2,1)}, bf16[4,64,1152]{2,1,0:T(8,128)(2,1)S(1)}, u32[]{:S(2)}, u32[]{:S(2)}) collective-permute-start(bf16[4,64,1152]{2,1,0:T(8,128)(2,1)} %bitcast.84), channel_id=1, source_target_pairs={{0,8},{8,16},{16,24},{24,0},{1,9},{9,17},{17,25},{25,1},{2,10},{10... | collective-permute-start | bytes 1769480 | tf_op jit(solution)/shard_map/ppermute | solution.py:1380
  355.6 47.6 %collective-permute-start.12 = (bf16[4,64,1152]{2,1,0:T(8,128)(2,1)}, bf16[4,64,1152]{2,1,0:T(8,128)(2,1)S(1)}, u32[]{:S(2)}, u32[]{:S(2)}) collective-permute-start(bf16[4,64,1152]{2,1,0:T(8,128)(2,1)} %bitcast.83), channel_id=1, source_target_pairs={{0,16},{8,24},{16,0},{24,8},{1,17},{9,25},{17,1},{25,9},{2,18},{10... | collective-permute-start | bytes 1769480 | tf_op jit(solution)/shard_map/ppermute | solution.py:1380
  397.8 51.7 %collective-permute-start.14 = (bf16[4,32,1152]{2,1,0:T(8,128)(2,1)}, bf16[4,32,1152]{2,1,0:T(8,128)(2,1)S(1)}, u32[]{:S(2)}, u32[]{:S(2)}) collective-permute-start(bf16[4,32,1152]{2,1,0:T(8,128)(2,1)} %get-tuple-element.168), channel_id=1, source_target_pairs={{0,24},{8,0},{16,8},{24,16},{1,25},{9,1},{17,9},{25,17},{2,26},{10... | collective-permute-start | bytes 884744 | tf_op jit(solution)/shard_map/ppermute | solution.py:1380
  401.2 48.9 %collective-permute-start.15 = (bf16[4,32,1152]{2,1,0:T(8,128)(2,1)}, bf16[4,32,1152]{2,1,0:T(8,128)(2,1)S(1)}, u32[]{:S(2)}, u32[]{:S(2)}) collective-permute-start(bf16[4,32,1152]{2,1,0:T(8,128)(2,1)} %get-tuple-element.169), channel_id=1, source_target_pairs={{0,16},{8,24},{16,0},{24,8},{1,17},{9,25},{17,1},{25,9},{2,18},{10... | collective-permute-start | bytes 884744 | tf_op jit(solution)/shard_map/ppermute | solution.py:1380
  403.2 46.9 %collective-permute-start.16 = (bf16[4,32,1152]{2,1,0:T(8,128)(2,1)}, bf16[4,32,1152]{2,1,0:T(8,128)(2,1)S(1)}, u32[]{:S(2)}, u32[]{:S(2)}) collective-permute-start(bf16[4,32,1152]{2,1,0:T(8,128)(2,1)} %get-tuple-element.170), channel_id=1, source_target_pairs={{0,8},{8,16},{16,24},{24,0},{1,9},{9,17},{17,25},{25,1},{2,10},{10... | collective-permute-start | bytes 884744 | tf_op jit(solution)/shard_map/ppermute | solution.py:1380
  445.5 30.9 %collective-permute-start.17 = (bf16[4,32,1152]{2,1,0:T(8,128)(2,1)}, bf16[4,32,1152]{2,1,0:T(8,128)(2,1)S(1)}, u32[]{:S(2)}, u32[]{:S(2)}) collective-permute-start(bf16[4,32,1152]{2,1,0:T(8,128)(2,1)} %get-tuple-element.191), channel_id=1, source_target_pairs={{0,24},{8,0},{16,8},{24,16},{1,25},{9,1},{17,9},{25,17},{2,26},{10... | collective-permute-start | bytes 884744 | tf_op jit(solution)/shard_map/ppermute | solution.py:1380
  449.4 27.0 %collective-permute-start.18 = (bf16[4,32,1152]{2,1,0:T(8,128)(2,1)}, bf16[4,32,1152]{2,1,0:T(8,128)(2,1)S(1)}, u32[]{:S(2)}, u32[]{:S(2)}) collective-permute-start(bf16[4,32,1152]{2,1,0:T(8,128)(2,1)} %get-tuple-element.192), channel_id=1, source_target_pairs={{0,16},{8,24},{16,0},{24,8},{1,17},{9,25},{17,1},{25,9},{2,18},{10... | collective-permute-start | bytes 884744 | tf_op jit(solution)/shard_map/ppermute | solution.py:1380
  449.4 27.1 %collective-permute-start.19 = (bf16[4,32,1152]{2,1,0:T(8,128)(2,1)}, bf16[4,32,1152]{2,1,0:T(8,128)(2,1)S(1)}, u32[]{:S(2)}, u32[]{:S(2)}) collective-permute-start(bf16[4,32,1152]{2,1,0:T(8,128)(2,1)} %get-tuple-element.193), channel_id=1, source_target_pairs={{0,8},{8,16},{16,24},{24,0},{1,9},{9,17},{17,25},{25,1},{2,10},{10... | collective-permute-start | bytes 884744 | tf_op jit(solution)/shard_map/ppermute | solution.py:1380
  476.5 44.1 %all-to-all-start.2 = ((bf16[32,128,128]{2,1,0:T(8,128)(2,1)}), bf16[32,128,128]{2,1,0:T(8,128)(2,1)S(1)}, u32[]{:S(2)}, u32[]{:S(2)}) async-start(bf16[32,128,128]{2,1,0:T(8,128)(2,1)} %pack_early.1), calls=%async_computation.2 | async-start | bytes 2097152 | tf_op jit(solution)/shard_map/all_to_all | solution.py:1365
  482.3 38.3 %collective-permute-start.20 = (bf16[4,64,1152]{2,1,0:T(8,128)(2,1)}, bf16[4,64,1152]{2,1,0:T(8,128)(2,1)S(1)}, u32[]{:S(2)}, u32[]{:S(2)}) collective-permute-start(bf16[4,64,1152]{2,1,0:T(8,128)(2,1)} %bitcast.82), channel_id=1, source_target_pairs={{0,24},{8,0},{16,8},{24,16},{1,25},{9,1},{17,9},{25,17},{2,26},{10... | collective-permute-start | bytes 1769480 | tf_op jit(solution)/shard_map/ppermute | solution.py:1380
  520.6 30.4 %all-to-all-start.3 = ((bf16[32,48,128]{2,1,0:T(8,128)(2,1)}), bf16[32,48,128]{2,1,0:T(8,128)(2,1)S(1)}, u32[]{:S(2)}, u32[]{:S(2)}) async-start(bf16[32,48,128]{2,1,0:T(8,128)(2,1)} %get-tuple-element.219), calls=%async_computation.3 | async-start | bytes 786432 | tf_op jit(solution)/shard_map/all_to_all | solution.py:1365
  526.6 30.9 %collective-permute-start.23 = (bf16[8,128,128]{2,1,0:T(8,128)(2,1)}, bf16[8,128,128]{2,1,0:T(8,128)(2,1)S(1)}, u32[]{:S(2)}, u32[]{:S(2)}) collective-permute-start(bf16[8,128,128]{2,1,0:T(8,128)(2,1)} %combine.2.refs_1_), channel_id=1, source_target_pairs={{0,24},{8,0},{16,8},{24,16},{1,25},{9,1},{17,9},{25,17},{2,26},{10... | collective-permute-start | bytes 786440 | tf_op jit(solution)/shard_map/ppermute | solution.py:1380
  530.2 32.5 %collective-permute-start.22 = (bf16[8,128,128]{2,1,0:T(8,128)(2,1)}, bf16[8,128,128]{2,1,0:T(8,128)(2,1)S(1)}, u32[]{:S(2)}, u32[]{:S(2)}) collective-permute-start(bf16[8,128,128]{2,1,0:T(8,128)(2,1)} %combine.2.refs_1_), channel_id=1, source_target_pairs={{0,16},{8,24},{16,0},{24,8},{1,17},{9,25},{17,1},{25,9},{2,18},{10... | collective-permute-start | bytes 786440 | tf_op jit(solution)/shard_map/ppermute | solution.py:1380
  530.2 32.5 %collective-permute-start.21 = (bf16[8,128,128]{2,1,0:T(8,128)(2,1)}, bf16[8,128,128]{2,1,0:T(8,128)(2,1)S(1)}, u32[]{:S(2)}, u32[]{:S(2)}) collective-permute-start(bf16[8,128,128]{2,1,0:T(8,128)(2,1)} %combine.2.refs_1_), channel_id=1, source_target_pairs={{0,8},{8,16},{16,24},{24,0},{1,9},{9,17},{17,25},{25,1},{2,10},{10... | collective-permute-start | bytes 786440 | tf_op jit(solution)/shard_map/ppermute | solution.py:1380
  553.6 9.2 %collective-permute-start.26 = (bf16[8,48,128]{2,1,0:T(8,128)(2,1)}, bf16[8,48,128]{2,1,0:T(8,128)(2,1)S(1)}, u32[]{:S(2)}, u32[]{:S(2)}) collective-permute-start(bf16[8,48,128]{2,1,0:T(8,128)(2,1)} %combine.3.refs_5_), channel_id=1, source_target_pairs={{0,24},{8,0},{16,8},{24,16},{1,25},{9,1},{17,9},{25,17},{2,26},{10... | collective-permute-start | bytes 294920 | tf_op jit(solution)/shard_map/ppermute | solution.py:1380
  556.3 11.2 %collective-permute-start.25 = (bf16[8,48,128]{2,1,0:T(8,128)(2,1)}, bf16[8,48,128]{2,1,0:T(8,128)(2,1)S(1)}, u32[]{:S(2)}, u32[]{:S(2)}) collective-permute-start(bf16[8,48,128]{2,1,0:T(8,128)(2,1)} %combine.3.refs_5_), channel_id=1, source_target_pairs={{0,16},{8,24},{16,0},{24,8},{1,17},{9,25},{17,1},{25,9},{2,18},{10... | collective-permute-start | bytes 294920 | tf_op jit(solution)/shard_map/ppermute | solution.py:1380
  557.5 10.1 %collective-permute-start.24 = (bf16[8,48,128]{2,1,0:T(8,128)(2,1)}, bf16[8,48,128]{2,1,0:T(8,128)(2,1)S(1)}, u32[]{:S(2)}, u32[]{:S(2)}) collective-permute-start(bf16[8,48,128]{2,1,0:T(8,128)(2,1)} %combine.3.refs_5_), channel_id=1, source_target_pairs={{0,8},{8,16},{16,24},{24,0},{1,9},{9,17},{17,25},{25,1},{2,10},{10... | collective-permute-start | bytes 294920 | tf_op jit(solution)/shard_map/ppermute | solution.py:1380
  (39 other events, 594.4 us)
Sparse Core Ops, SparseCore 0:
  15.2 88.7 all-gather.3
  106.5 108.9 all-gather.5
  217.4 63.7 all-gather.7

commit v9 on v8

--- a/solution.py
+++ b/solution.py
@@ -987,7 +987,7 @@
         + [pltpu.VMEM((ROWS, d), BF16)] * 3
         + [pltpu.SemaphoreType.DMA((4,))],
         compiler_params=PARAMS,
-        cost_estimate=cost(10 * places * frames * d * d, 30_000_000),
+        cost_estimate=cost(10 * places * frames * d * d, 30_000_000, 64),
         name="temporal_forward",
     )(*x1, mods, masks, wide, w_t)
 
@@ -1014,7 +1014,7 @@
         + [pltpu.VMEM((ROWS, d), BF16), pltpu.VMEM((PAD, d), BF16)]
         + [pltpu.SemaphoreType.DMA((4,))],
         compiler_params=PARAMS,
-        cost_estimate=cost(8 * places * frames * d * d, 30_000_000),
+        cost_estimate=cost(8 * places * frames * d * d, 30_000_000, 64),
         name="cross_forward",
     )(x2, context, masks, wide, w_c)
 
@@ -1402,7 +1402,7 @@
     core = lax.axis_index("fsdp") % 2
     first = lax.dynamic_slice(got, (times, core * half, 0), (1, half, d))[0]
     other = lax.dynamic_slice(got, (times, (1 - core) * half, 0), (1, half, d))[0]
-    return first, other, send(first, "seq", 1), send(first, "seq", -1)
+    return first, other, send(first, "seq", 1)
 
 
 def swap_cores(piece, clips):
@@ -1483,20 +1483,26 @@
         late_pieces = []
         grad_active = [run_feed_forward_grad(cot, mods, maps_f, packed_order, sides[0] + sides[1])]
     else:
-        first, other, second, third = started
-        second, third, cot, x1_own = lax.optimization_barrier((second, third, cot, u1[0]))
-        mine = [first, second, third]
-        others = [other] + [swap_cores(piece, clips) for piece in mine[1:]]
-        early_order = jnp.concatenate([packed_order[:3], core])
-        grad_active = run_feed_forward_grad(cot, mods, maps_f, early_order, mine + others)
-        second, grad_active, *u1 = lax.optimization_barrier((second, grad_active, x1_own, *u1[1:]))
+        first, other, second = started
+        second, cot, x1_own = lax.optimization_barrier((second, cot, u1[0]))
+        mine = [first, second]
+        others = [other, swap_cores(second, clips)]
+        early_order = jnp.concatenate([packed_order[:2], core])
+        grad_early = run_feed_forward_grad(cot, mods, maps_f, early_order, mine + others)
+        first, second, grad_early, *u1 = lax.optimization_barrier(
+            (first, second, grad_early, x1_own, *u1[1:])
+        )
+        third = send(first, "seq", -1)
         rest = [send(second, "seq", 1)] + [send(first, "seq", k) for k in range(3, parts - 1)]
         *kept_t, x2 = run_temporal_forward(u1, mods, masks, wide, w_tc)
-        x2, *rest = lax.optimization_barrier((x2, *rest))
+        *kept_c, x3 = run_cross_forward(x2, ctx, masks, wide, w_tc)
+        x3, third, *rest = lax.optimization_barrier((x3, third, *rest))
+        rest = [third] + rest
         rest_others = [swap_cores(piece, clips) for piece in rest]
-        *kept_c, x3 = run_cross_forward(x2, ctx, masks, wide, w_tc)
-        grad_active = [grad_active]
-        late_pieces = rest + rest_others
+        late_order = jnp.concatenate([packed_order[2:parts], core])
+        grad_late = run_feed_forward_grad(cot, mods, maps_f, late_order, rest + rest_others)
+        grad_active = [grad_early, grad_late]
+        late_pieces = []
         sides = [mine + rest, others + rest_others]
     down = [packed_order, *sides[0], *sides[1]]
     x3 = x3.reshape(FRAMES * places, d)

time: 586 us -> 582 us (level)
    ppermute x24, waiting for transfers between devices: 67.9 us -> 47.6 us  [send(): lax.ppermute(array, axis, [(i, (i + shift) % size) for i in range(size)])]
    pallas_call x1 -> x2, Pallas kernels: 18.5 us -> 29.4 us  [run_feed_forward_grad(): pl.pallas_call(body, grid=(tokens // ROWS,), in_specs=[in_smem(), pl.Bloc...]
    all_gather x3, waiting for transfers between devices: 0.04 us -> 10.3 us  [gather(): return lax.all_gather(array, 'fsdp', axis=1, tiled=True)]
    pallas_call x1, Pallas kernels: 52.5 us -> 43.1 us  [run_feed_forward(): pl.pallas_call(body, grid=(tokens // ROWS,), in_specs=[in_smem(), rows, r...]
  transfers between devices with their start and end apart: 33 -> 33, of which waited for: 7 -> 8; matrix products, arithmetic and copies ran while one was open for 6% -> 6% of each run, Pallas kernels for 50% -> 52%
where the time goes in v9:
time: 582 us; the launch traced here: 576 us
  Pallas kernels  364 us (63%)
  waiting for transfers between devices  81.9 us (14%)
  starting transfers between devices  59.3 us (10%)
  local copies, waits for them, and re-layouts  34 us (6%)
  between operations  15.5 us (3%)
  other arithmetic  12.4 us (2%)
  blocking collectives  9.63 us (2%)
    pallas_call x2, Pallas kernels, run_cross_temporal_backward(): pl.pallas_call(body, grid=(groups,), in_specs=[pl.BlockSpec((own_frames,...  84.4 us
    ppermute x24, waiting for transfers between devices, send(): lax.ppermute(array, axis, [(i, (i + shift) % size) for i in range(size)])  47.6 us
    ppermute x24, starting transfers between devices, send(): lax.ppermute(array, axis, [(i, (i + shift) % size) for i in range(size)])  46.6 us
    pallas_call x1, Pallas kernels, run_feed_forward(): pl.pallas_call(body, grid=(tokens // ROWS,), in_specs=[in_smem(), rows, r...  43.1 us
    pallas_call x1, Pallas kernels, run_spatial_backward(): pl.pallas_call(body, grid=(count,), in_specs=[in_smem()] + [pl.BlockSpec(...  34.6 us
    pallas_call x2, Pallas kernels, run_feed_forward_out(): pl.pallas_call(body, grid=(steps,), in_specs=[in_smem(), pl.BlockSpec((RO...  33.2 us
    pallas_call x1, Pallas kernels, run_temporal_forward(): pl.pallas_call(body, grid=(groups,), in_specs=[pl.BlockSpec((own_frames,...  32.6 us
    pallas_call x1, Pallas kernels, run_spatial_forward(): pl.pallas_call(spatial_forward, grid=(frames,), in_specs=[in_smem(), row_...  31.6 us
  transfers between devices with their start and end apart: 33, of which 8 were waited for; matrix products, arithmetic and copies ran while one was open for 6% of the time, Pallas kernels for 52%

profile of v9, /device:TPU:0, one launch (start us, length us, event | category | flops | bytes accessed | tf_op | source)
XLA Modules:
  0.0 576.4 jit_solution(16220217827067365440)
XLA Ops:
  18.6 9.6 %all_to_all.23 = s32[8,1,1]{2,1,0:T(1,128)S(1)} all-to-all(s32[8,1,1]{2,1,0:T(1,128)S(1)} %broadcast_in_dim.23), channel_id=1, replica_groups=mesh['seq'=4,'fsdp'=8] {'fsdp'}, dimensions={0} | all-to-all | bytes 64 | tf_op jit(solution)/shard_map/all_to_all | solution.py:1365
  32.6 5.2 reshape_squeeze.7
  41.1 4.7 reshape.53
  52.3 3.6 collective-permute-start.2
  59.0 19.6 %all-to-all-done.1.refs_0_ = bf16[8,624,128]{2,1,0:T(8,128)(2,1)S(1)} async-done(((bf16[8,624,128]{2,1,0:T(8,128)(2,1)}), bf16[8,624,128]{2,1,0:T(8,128)(2,1)S(1)}, u32[]{:S(2)}, u32[]{:S(2)}) %all-to-all-start.1) | async-done | bytes 1277984 | tf_op jit(solution)/shard_map/all_to_all | solution.py:1365
  79.7 4.7 unpick.1.ad_ref.refs_6_.refs_22_.refs_16_.refs_19_.refs_12_
  86.2 20.9 %collective-permute-done.1 = bf16[4,64,1152]{2,1,0:T(8,128)(2,1)S(1)} collective-permute-done((bf16[4,64,1152]{2,1,0:T(8,128)(2,1)}, bf16[4,64,1152]{2,1,0:T(8,128)(2,1)S(1)}, u32[]{:S(2)}, u32[]{:S(2)}) %collective-permute-start.1) | collective-permute-done | bytes 589856 | tf_op jit(solution)/shard_map/ppermute | solution.py:1380
  112.7 31.6 %spatial_forward.1 = (bf16[4,64,1152]{2,1,0:T(8,128)(2,1)}, bf16[4,64,1152]{2,1,0:T(8,128)(2,1)}, bf16[4,64,1152]{2,1,0:T(8,128)(2,1)}, bf16[4,64,1152]{2,1,0:T(...) custom-call(s32[1]{0:T(128)} %bitcast.seq_ref.refs_0_, ...), custom_call_target="tpu_custom_call" | custom-call | flops 3397386240 | bytes 7500000 | tf_op jit(solution)/shard_map/spatial_forward/pallas_call | solution.py:918
  154.4 15.8 %feed_forward_grad.2.refs_3_ = bf16[2,1024,1152]{2,1,0:T(8,128)(2,1)} custom-call(s32[3]{0:T(128)} %pad_add_fusion.1.refs_0_, bf16[1024,1152]{1,0:T(8,128)(2,1)} %bitcast.47, f32[6,1152]{1,0:T(8,128)} %bitcast.62, bf16[10,16,1152]{2,1,0:T(8,128)(2,1)} %slice.48.refs_3_.refs_6_.refs_5_, bf16[576,1152]{1,0:T(8,128)(2,1)} %copy-done.2, ...), custom_call_target="tpu_custom_call" | custom-call | flops 1358954496 | bytes 5000000 | tf_op jit(solution)/shard_map/feed_forward_grad/pallas_call | solution.py:1033
  170.2 20.6 %collective-permute-done.6.refs_2_ = bf16[4,64,1152]{2,1,0:T(8,128)(2,1)} collective-permute-done((bf16[4,64,1152]{2,1,0:T(8,128)(2,1)}, bf16[4,64,1152]{2,1,0:T(8,128)(2,1)}, u32[]{:S(2)}, u32[]{:S(2)}) %collective-permute-start.6) | collective-permute-done | bytes 589856 | tf_op jit(solution)/shard_map/ppermute | solution.py:1380
  190.8 13.7 %collective-permute-start.8 = (bf16[576,1152]{1,0:T(8,128)(2,1)S(1)}, bf16[576,1152]{1,0:T(8,128)(2,1)S(1)}, u32[]{:S(2)}, u32[]{:S(2)}) collective-permute-start(bf16[576,1152]{1,0:T(8,128)(2,1)S(1)} %copy-done.3), channel_id=1, source_target_pairs={{0,24},{8,0},{16,8},{24,16},{1,25},{9,1},{17,9},{25,17},{2,26},{10... | collective-permute-start | bytes 3981320 | tf_op jit(solution)/shard_map/ppermute | solution.py:1380
  205.3 10.3 %all-gather.6.cloned.1.call-done.refs_7_.w_hbm.refs_23_ = bf16[8,1152,1152]{2,1,0:T(8,128)(2,1)} async-done(((bf16[8,144,1152]{2,1,0:T(8,128)(2,1)}), bf16[8,1152,1152]{2,1,0:T(8,128)(2,1)}) %all-gather.6.cloned.1.call-update) | async-done | bytes 21233680 | tf_op jit(solution)/shard_map/all_gather | solution.py:1375
  215.6 32.6 %temporal_forward.1 = (bf16[16,64,1152]{2,1,0:T(8,128)(2,1)}, bf16[16,64,1152]{2,1,0:T(8,128)(2,1)}, bf16[16,64,1152]{2,1,0:T(8,128)(2,1)}, bf16[16,64,1152]{2,1...) custom-call(bf16[4,64,1152]{2,1,0:T(8,128)(2,1)} %get-tuple-element., ...), custom_call_target="tpu_custom_call" | custom-call | flops 212336640 | bytes 468750 | tf_op jit(solution)/shard_map/temporal_forward/pallas_call | solution.py:964
  248.2 24.7 %cross_forward.1 = (bf16[16,64,1152]{2,1,0:T(8,128)(2,1)}, bf16[16,64,1152]{2,1,0:T(8,128)(2,1)}, f32[4,16,256]{2,1,0:T(8,128)}, bf16[4,256,16]{2,1,0:T(8,128)(2...) custom-call(f32[16,64,1152]{2,1,0:T(8,128)} %get-tuple-element.135.x, ...), custom_call_target="tpu_custom_call" | custom-call | flops 169869312 | bytes 468750 | tf_op jit(solution)/shard_map/cross_forward/pallas_call | solution.py:1004
  274.2 3.8 collective-permute-done.10.refs_6_.refs_12_
  279.1 13.6 %feed_forward_grad.3.refs_4_ = bf16[2,1024,1152]{2,1,0:T(8,128)(2,1)} custom-call(s32[3]{0:T(128)} %pad_add_fusion.2.refs_0_, bf16[1024,1152]{1,0:T(8,128)(2,1)} %bitcast.48, f32[6,1152]{1,0:T(8,128)} %bitcast.64, bf16[10,16,1152]{2,1,0:T(8,128)(2,1)} %slice.48.refs_3_.refs_6_.refs_5_, bf16[576,1152]{1,0:T(8,128)(2,1)} %copy-done.6, ...), custom_call_target="tpu_custom_call" | custom-call | flops 1358954496 | bytes 5000000 | tf_op jit(solution)/shard_map/feed_forward_grad/pallas_call | solution.py:1033
  292.7 43.1 %feed_forward.1 = (bf16[1024,4608]{1,0:T(8,128)(2,1)}, f32[1024,1152]{1,0:T(8,128)}, f32[16,1152]{1,0:T(8,128)}, f32[16,4608]{1,0:T(8,128)}) custom-call(s32[5]{0:T(128)} %copy-done.33, f32[1024,1152]{1,0:T(8,128)} %bitcast.52, bf16[1024,1152]{1,0:T(8,128)(2,1)} %bitcast.49, bf16[2,1024,1152]{2,1,0:T(8,128)(2,1)} %feed_forward_grad.2.refs_3_, ...), custom_call_target="tpu_custom_call" | custom-call | flops 5435817984 | bytes 12500000 | tf_op jit(solution)/shard_map/feed_forward/pallas_call | solution.py:1062
  335.9 16.5 %feed_forward_out.2 = (bf16[256,1152]{1,0:T(8,128)(2,1)}, bf16[256,1152]{1,0:T(8,128)(2,1)}, f32[16,1152]{1,0:T(8,128)}, f32[16,4608]{1,0:T(8,128)}) custom-call(s32[5]{0:T(128)} %copy-done.33, bf16[1024,4608]{1,0:T(8,128)(2,1)} %get-tuple-element.180.refs_1_, f32[1024,1152]{1,0:T(8,128)} %bitcast.53, bf16[1024,1152]{1,0:T(8,128)(2,1)} %bitcast.50, ...), custom_call_target="tpu_custom_call" | custom-call | flops 84934656 | bytes 312500 | tf_op jit(solution)/shard_map/feed_forward_out/pallas_call | solution.py:1107
  355.9 42.1 %cross_temporal_backward.2 = (bf16[4,32,1152]{2,1,0:T(8,128)(2,1)}, bf16[4,32,1152]{2,1,0:T(8,128)(2,1)}, bf16[4,32,1152]{2,1,0:T(8,128)(2,1)}, bf16[4,32,1152]{...) custom-call(bf16[4,64,1152]{2,1,0:T(8,128)(2,1)} %get-tuple-element.131.refs_0_, ...), custom_call_target="tpu_custom_call" | custom-call | flops 148635648 | bytes 468750 | tf_op jit(solution)/shard_map/cross_temporal_backward/pallas_call | solution.py:1155
  400.7 42.2 %cross_temporal_backward.3 = (bf16[4,32,1152]{2,1,0:T(8,128)(2,1)}, bf16[4,32,1152]{2,1,0:T(8,128)(2,1)}, bf16[4,32,1152]{2,1,0:T(8,128)(2,1)}, bf16[4,32,1152]{...) custom-call(bf16[4,64,1152]{2,1,0:T(8,128)(2,1)} %get-tuple-element.131.refs_0_, ...), custom_call_target="tpu_custom_call" | custom-call | flops 148635648 | bytes 468750 | tf_op jit(solution)/shard_map/cross_temporal_backward/pallas_call | solution.py:1155
  443.0 3.7 collective-permute-start.17
  447.5 16.7 %feed_forward_out.3 = (bf16[256,1152]{1,0:T(8,128)(2,1)}, bf16[256,1152]{1,0:T(8,128)(2,1)}, f32[16,1152]{1,0:T(8,128)}, f32[16,4608]{1,0:T(8,128)}) custom-call(s32[5]{0:T(128)} %copy-done.33, bf16[1024,4608]{1,0:T(8,128)(2,1)} %get-tuple-element.180.refs_1_, f32[1024,1152]{1,0:T(8,128)} %bitcast.54, bf16[1024,1152]{1,0:T(8,128)(2,1)} %bitcast.51, ...), custom_call_target="tpu_custom_call" | custom-call | flops 84934656 | bytes 312500 | tf_op jit(solution)/shard_map/feed_forward_out/pallas_call | solution.py:1107
  464.2 9.7 %pack_early.1 = bf16[32,128,128]{2,1,0:T(8,128)(2,1)} custom-call(f32[256,1152]{1,0:T(8,128)} %get-tuple-element.163.refs_0_, f32[256,1152]{1,0:T(8,128)} %get-tuple-element.173.refs_1_, f32[8,256,256]{2,1,0:T(8,128)} %get-tuple-element.174.refs_2_, f32[8,256,256]{2,1,0:T(8,128)} %get-tuple-element.175.refs_3_, f32[8,256,256]{2,1,0:T(8,128)} %get-tuple-element.176.refs_4_, ...), custom_call_target="tpu_custom_call" | custom-call | flops 781250 | bytes 125000 | tf_op jit(solution)/shard_map/pack_early/pallas_call | solution.py:1293
  473.9 4.5 all-to-all-start.2
  478.4 3.7 collective-permute-start.20
  482.1 34.6 %spatial_backward.1 = (bf16[4,256,3584]{2,1,0:T(8,128)(2,1)}, bf16[32,48,128]{2,1,0:T(8,128)(2,1)}) custom-call(s32[1]{0:T(128)} %bitcast.seq_ref.refs_0_, bf16[4,32,1152]{2,1,0:T(8,128)(2,1)} %get-tuple-element.196.refs_1_, bf16[4,32,1152]{2,1,0:T(8,128)(2,1)} %copy-done.15, bf16[4,32,1152]{2,1,0:T(8,128)(2,1)} %copy-done.16, ...), custom_call_target="tpu_custom_call" | custom-call | flops 127401984 | bytes 312500 | tf_op jit(solution)/shard_map/spatial_backward/pallas_call | solution.py:1202
  516.8 3.8 all-to-all-start.3
  522.8 3.6 collective-permute-start.23
  527.5 19.6 %spatial_input_grad.1 = bf16[4,256,1152]{2,1,0:T(8,128)(2,1)} custom-call(s32[1]{0:T(128)} %bitcast.seq_ref.refs_0_, bf16[4,32,1152]{2,1,0:T(8,128)(2,1)} %get-tuple-element.196.refs_1_, bf16[4,32,1152]{2,1,0:T(8,128)(2,1)} %copy-done.15, bf16[4,32,1152]{2,1,0:T(8,128)(2,1)} %copy-done.16, bf16[4,32,1152]{2,1,0:T(8,128)(2,1)} %copy-done.17, ...), custom_call_target="tpu_custom_call" | custom-call | flops 127401984 | bytes 312500 | tf_op jit(solution)/shard_map/spatial_input_grad/pallas_call | solution.py:1239
  553.6 4.0 put_in_place.1
  558.9 4.8 collective-permute-done.25.refs_7_
  565.0 4.5 assemble.1
  (152 shorter events, 68.7 us)
Async XLA Ops:
  7.2 99.9 %all-gather.4.cloned.1.call-start = ((), (), s32[]{:S(2)}) async-start(), calls=%async_computation.4 | async-start | bytes 14929920 | tf_op jit(solution)/shard_map/all_gather | solution.py:1375
  15.1 200.5 %all-gather.6.cloned.1.call-start = ((), (), s32[]{:S(2)}) async-start(), calls=%async_computation.5 | async-start | bytes 23887872 | tf_op jit(solution)/shard_map/all_gather | solution.py:1375
  17.8 274.9 %all-gather.8.cloned.1.call-start = ((), (), s32[]{:S(2)}) async-start(), calls=%async_computation.6 | async-start | bytes 11943936 | tf_op jit(solution)/shard_map/all_gather | solution.py:1375
  45.8 32.9 %all-to-all-start.1 = ((bf16[8,624,128]{2,1,0:T(8,128)(2,1)}), bf16[8,624,128]{2,1,0:T(8,128)(2,1)S(1)}, u32[]{:S(2)}, u32[]{:S(2)}) async-start(bf16[8,624,128]{2,1,0:T(8,128)(2,1)} %pick.1), calls=%async_computation.1 | async-start | bytes 2555904 | tf_op jit(solution)/shard_map/all_to_all | solution.py:1365
  52.3 33.8 %collective-permute-start.2 = (bf16[4,64,1152]{2,1,0:T(8,128)(2,1)}, bf16[4,64,1152]{2,1,0:T(8,128)(2,1)S(1)}, u32[]{:S(2)}, u32[]{:S(2)}) collective-permute-start(bf16[4,64,1152]{2,1,0:T(8,128)(2,1)} %get-tuple-element.233), channel_id=1, source_target_pairs={{0,24},{8,0},{16,8},{24,16},{1,25},{9,1},{17,9},{25,17},{2,26},{10... | collective-permute-start | bytes 1769480 | tf_op jit(solution)/shard_map/ppermute | solution.py:1380
  55.9 51.1 %collective-permute-start.1 = (bf16[4,64,1152]{2,1,0:T(8,128)(2,1)}, bf16[4,64,1152]{2,1,0:T(8,128)(2,1)S(1)}, u32[]{:S(2)}, u32[]{:S(2)}) collective-permute-start(bf16[4,64,1152]{2,1,0:T(8,128)(2,1)} %get-tuple-element.234), channel_id=1, source_target_pairs={{0,16},{8,24},{16,0},{24,8},{1,17},{9,25},{17,1},{25,9},{2,18},{10... | collective-permute-start | bytes 1769480 | tf_op jit(solution)/shard_map/ppermute | solution.py:1380
  55.9 51.1 %collective-permute-start = (bf16[4,64,1152]{2,1,0:T(8,128)(2,1)}, bf16[4,64,1152]{2,1,0:T(8,128)(2,1)}, u32[]{:S(2)}, u32[]{:S(2)}) collective-permute-start(bf16[4,64,1152]{2,1,0:T(8,128)(2,1)} %get-tuple-element.235), channel_id=1, source_target_pairs={{0,8},{8,16},{16,24},{24,0},{1,9},{9,17},{17,25},{25,1},{2,10},{10... | collective-permute-start | bytes 1769480 | tf_op jit(solution)/shard_map/ppermute | solution.py:1380
  111.0 36.4 %collective-permute-start.3 = (bf16[576,1152]{1,0:T(8,128)(2,1)S(1)}, bf16[576,1152]{1,0:T(8,128)(2,1)S(1)}, u32[]{:S(2)}, u32[]{:S(2)}) collective-permute-start(bf16[576,1152]{1,0:T(8,128)(2,1)S(1)} %get-tuple-element.137.refs_4_.refs_6_), channel_id=1, source_target_pairs={{0,8},{8,16},{16,24},{24,0},{1,9},{9,17},{17,25},{25,1},{2,10},{10... | collective-permute-start | bytes 3981320 | tf_op jit(solution)/shard_map/ppermute | solution.py:1380
  147.4 5.9 %collective-permute-start.4 = (bf16[576,1152]{1,0:T(8,128)(2,1)S(1)}, bf16[576,1152]{1,0:T(8,128)(2,1)S(1)}, u32[]{:S(2)}, u32[]{:S(2)}) collective-permute-start(bf16[576,1152]{1,0:T(8,128)(2,1)S(1)} %collective-permute-done.3.refs_5_.refs_7_), channel_id=1, source_target_pairs={{0,1},{1,0},{2,3},{3,2},{4,5},{5,4},{6,7},{7,6},{8,9},{9,8},{10,11... | collective-permute-start | bytes 3981320 | tf_op jit(solution)/shard_map/ppermute | solution.py:1409
  147.4 22.7 %collective-permute-start.5 = (bf16[4,64,1152]{2,1,0:T(8,128)(2,1)}, bf16[4,64,1152]{2,1,0:T(8,128)(2,1)S(1)}, u32[]{:S(2)}, u32[]{:S(2)}) collective-permute-start(bf16[4,64,1152]{2,1,0:T(8,128)(2,1)} %get-tuple-element.128), channel_id=1, source_target_pairs={{0,8},{8,16},{16,24},{24,0},{1,9},{9,17},{17,25},{25,1},{2,10},{10... | collective-permute-start | bytes 1769480 | tf_op jit(solution)/shard_map/ppermute | solution.py:1380
  150.0 40.8 %collective-permute-start.6 = (bf16[4,64,1152]{2,1,0:T(8,128)(2,1)}, bf16[4,64,1152]{2,1,0:T(8,128)(2,1)}, u32[]{:S(2)}, u32[]{:S(2)}) collective-permute-start(bf16[4,64,1152]{2,1,0:T(8,128)(2,1)} %get-tuple-element.129), channel_id=1, source_target_pairs={{0,16},{8,24},{16,0},{24,8},{1,17},{9,25},{17,1},{25,9},{2,18},{10... | collective-permute-start | bytes 1769480 | tf_op jit(solution)/shard_map/ppermute | solution.py:1380
  151.7 39.1 %collective-permute-start.7 = (bf16[4,64,1152]{2,1,0:T(8,128)(2,1)}, bf16[4,64,1152]{2,1,0:T(8,128)(2,1)}, u32[]{:S(2)}, u32[]{:S(2)}) collective-permute-start(bf16[4,64,1152]{2,1,0:T(8,128)(2,1)} %get-tuple-element.130), channel_id=1, source_target_pairs={{0,24},{8,0},{16,8},{24,16},{1,25},{9,1},{17,9},{25,17},{2,26},{10... | collective-permute-start | bytes 1769480 | tf_op jit(solution)/shard_map/ppermute | solution.py:1380
  190.8 82.1 %collective-permute-start.8 = (bf16[576,1152]{1,0:T(8,128)(2,1)S(1)}, bf16[576,1152]{1,0:T(8,128)(2,1)S(1)}, u32[]{:S(2)}, u32[]{:S(2)}) collective-permute-start(bf16[576,1152]{1,0:T(8,128)(2,1)S(1)} %copy-done.3), channel_id=1, source_target_pairs={{0,24},{8,0},{16,8},{24,16},{1,25},{9,1},{17,9},{25,17},{2,26},{10... | collective-permute-start | bytes 3981320 | tf_op jit(solution)/shard_map/ppermute | solution.py:1380
  204.5 68.4 %collective-permute-start.9 = (bf16[576,1152]{1,0:T(8,128)(2,1)}, bf16[576,1152]{1,0:T(8,128)(2,1)}, u32[]{:S(2)}, u32[]{:S(2)}) collective-permute-start(bf16[576,1152]{1,0:T(8,128)(2,1)} %copy-done.4), channel_id=1, source_target_pairs={{0,8},{8,16},{16,24},{24,0},{1,9},{9,17},{17,25},{25,1},{2,10},{10... | collective-permute-start | bytes 3981320 | tf_op jit(solution)/shard_map/ppermute | solution.py:1380
  273.3 5.2 collective-permute-start.11
  352.4 48.3 %collective-permute-start.13 = (bf16[4,64,1152]{2,1,0:T(8,128)(2,1)}, bf16[4,64,1152]{2,1,0:T(8,128)(2,1)S(1)}, u32[]{:S(2)}, u32[]{:S(2)}) collective-permute-start(bf16[4,64,1152]{2,1,0:T(8,128)(2,1)} %bitcast.84), channel_id=1, source_target_pairs={{0,8},{8,16},{16,24},{24,0},{1,9},{9,17},{17,25},{25,1},{2,10},{10... | collective-permute-start | bytes 1769480 | tf_op jit(solution)/shard_map/ppermute | solution.py:1380
  353.5 47.2 %collective-permute-start.12 = (bf16[4,64,1152]{2,1,0:T(8,128)(2,1)}, bf16[4,64,1152]{2,1,0:T(8,128)(2,1)S(1)}, u32[]{:S(2)}, u32[]{:S(2)}) collective-permute-start(bf16[4,64,1152]{2,1,0:T(8,128)(2,1)} %bitcast.83), channel_id=1, source_target_pairs={{0,16},{8,24},{16,0},{24,8},{1,17},{9,25},{17,1},{25,9},{2,18},{10... | collective-permute-start | bytes 1769480 | tf_op jit(solution)/shard_map/ppermute | solution.py:1380
  398.1 48.8 %collective-permute-start.14 = (bf16[4,32,1152]{2,1,0:T(8,128)(2,1)}, bf16[4,32,1152]{2,1,0:T(8,128)(2,1)S(1)}, u32[]{:S(2)}, u32[]{:S(2)}) collective-permute-start(bf16[4,32,1152]{2,1,0:T(8,128)(2,1)} %get-tuple-element.170), channel_id=1, source_target_pairs={{0,24},{8,0},{16,8},{24,16},{1,25},{9,1},{17,9},{25,17},{2,26},{10... | collective-permute-start | bytes 884744 | tf_op jit(solution)/shard_map/ppermute | solution.py:1380
  399.5 47.9 %collective-permute-start.15 = (bf16[4,32,1152]{2,1,0:T(8,128)(2,1)}, bf16[4,32,1152]{2,1,0:T(8,128)(2,1)S(1)}, u32[]{:S(2)}, u32[]{:S(2)}) collective-permute-start(bf16[4,32,1152]{2,1,0:T(8,128)(2,1)} %get-tuple-element.171), channel_id=1, source_target_pairs={{0,16},{8,24},{16,0},{24,8},{1,17},{9,25},{17,1},{25,9},{2,18},{10... | collective-permute-start | bytes 884744 | tf_op jit(solution)/shard_map/ppermute | solution.py:1380
  400.5 47.0 %collective-permute-start.16 = (bf16[4,32,1152]{2,1,0:T(8,128)(2,1)}, bf16[4,32,1152]{2,1,0:T(8,128)(2,1)S(1)}, u32[]{:S(2)}, u32[]{:S(2)}) collective-permute-start(bf16[4,32,1152]{2,1,0:T(8,128)(2,1)} %get-tuple-element.172), channel_id=1, source_target_pairs={{0,8},{8,16},{16,24},{24,0},{1,9},{9,17},{17,25},{25,1},{2,10},{10... | collective-permute-start | bytes 884744 | tf_op jit(solution)/shard_map/ppermute | solution.py:1380
  443.0 30.9 %collective-permute-start.17 = (bf16[4,32,1152]{2,1,0:T(8,128)(2,1)}, bf16[4,32,1152]{2,1,0:T(8,128)(2,1)S(1)}, u32[]{:S(2)}, u32[]{:S(2)}) collective-permute-start(bf16[4,32,1152]{2,1,0:T(8,128)(2,1)} %get-tuple-element.193), channel_id=1, source_target_pairs={{0,24},{8,0},{16,8},{24,16},{1,25},{9,1},{17,9},{25,17},{2,26},{10... | collective-permute-start | bytes 884744 | tf_op jit(solution)/shard_map/ppermute | solution.py:1380
  446.7 27.2 %collective-permute-start.18 = (bf16[4,32,1152]{2,1,0:T(8,128)(2,1)}, bf16[4,32,1152]{2,1,0:T(8,128)(2,1)S(1)}, u32[]{:S(2)}, u32[]{:S(2)}) collective-permute-start(bf16[4,32,1152]{2,1,0:T(8,128)(2,1)} %get-tuple-element.194), channel_id=1, source_target_pairs={{0,16},{8,24},{16,0},{24,8},{1,17},{9,25},{17,1},{25,9},{2,18},{10... | collective-permute-start | bytes 884744 | tf_op jit(solution)/shard_map/ppermute | solution.py:1380
  446.8 27.0 %collective-permute-start.19 = (bf16[4,32,1152]{2,1,0:T(8,128)(2,1)}, bf16[4,32,1152]{2,1,0:T(8,128)(2,1)S(1)}, u32[]{:S(2)}, u32[]{:S(2)}) collective-permute-start(bf16[4,32,1152]{2,1,0:T(8,128)(2,1)} %get-tuple-element.195), channel_id=1, source_target_pairs={{0,8},{8,16},{16,24},{24,0},{1,9},{9,17},{17,25},{25,1},{2,10},{10... | collective-permute-start | bytes 884744 | tf_op jit(solution)/shard_map/ppermute | solution.py:1380
  473.9 42.9 %all-to-all-start.2 = ((bf16[32,128,128]{2,1,0:T(8,128)(2,1)}), bf16[32,128,128]{2,1,0:T(8,128)(2,1)S(1)}, u32[]{:S(2)}, u32[]{:S(2)}) async-start(bf16[32,128,128]{2,1,0:T(8,128)(2,1)} %pack_early.1), calls=%async_computation.2 | async-start | bytes 2097152 | tf_op jit(solution)/shard_map/all_to_all | solution.py:1365
  478.4 38.3 %collective-permute-start.20 = (bf16[4,64,1152]{2,1,0:T(8,128)(2,1)}, bf16[4,64,1152]{2,1,0:T(8,128)(2,1)S(1)}, u32[]{:S(2)}, u32[]{:S(2)}) collective-permute-start(bf16[4,64,1152]{2,1,0:T(8,128)(2,1)} %bitcast.82), channel_id=1, source_target_pairs={{0,24},{8,0},{16,8},{24,16},{1,25},{9,1},{17,9},{25,17},{2,26},{10... | collective-permute-start | bytes 1769480 | tf_op jit(solution)/shard_map/ppermute | solution.py:1380
  516.8 30.3 %all-to-all-start.3 = ((bf16[32,48,128]{2,1,0:T(8,128)(2,1)}), bf16[32,48,128]{2,1,0:T(8,128)(2,1)S(1)}, u32[]{:S(2)}, u32[]{:S(2)}) async-start(bf16[32,48,128]{2,1,0:T(8,128)(2,1)} %get-tuple-element.221), calls=%async_computation.3 | async-start | bytes 786432 | tf_op jit(solution)/shard_map/all_to_all | solution.py:1365
  522.8 30.8 %collective-permute-start.23 = (bf16[8,128,128]{2,1,0:T(8,128)(2,1)}, bf16[8,128,128]{2,1,0:T(8,128)(2,1)S(1)}, u32[]{:S(2)}, u32[]{:S(2)}) collective-permute-start(bf16[8,128,128]{2,1,0:T(8,128)(2,1)} %combine.2.refs_1_), channel_id=1, source_target_pairs={{0,24},{8,0},{16,8},{24,16},{1,25},{9,1},{17,9},{25,17},{2,26},{10... | collective-permute-start | bytes 786440 | tf_op jit(solution)/shard_map/ppermute | solution.py:1380
  526.4 32.5 %collective-permute-start.22 = (bf16[8,128,128]{2,1,0:T(8,128)(2,1)}, bf16[8,128,128]{2,1,0:T(8,128)(2,1)S(1)}, u32[]{:S(2)}, u32[]{:S(2)}) collective-permute-start(bf16[8,128,128]{2,1,0:T(8,128)(2,1)} %combine.2.refs_1_), channel_id=1, source_target_pairs={{0,16},{8,24},{16,0},{24,8},{1,17},{9,25},{17,1},{25,9},{2,18},{10... | collective-permute-start | bytes 786440 | tf_op jit(solution)/shard_map/ppermute | solution.py:1380
  526.4 32.5 %collective-permute-start.21 = (bf16[8,128,128]{2,1,0:T(8,128)(2,1)}, bf16[8,128,128]{2,1,0:T(8,128)(2,1)S(1)}, u32[]{:S(2)}, u32[]{:S(2)}) collective-permute-start(bf16[8,128,128]{2,1,0:T(8,128)(2,1)} %combine.2.refs_1_), channel_id=1, source_target_pairs={{0,8},{8,16},{16,24},{24,0},{1,9},{9,17},{17,25},{25,1},{2,10},{10... | collective-permute-start | bytes 786440 | tf_op jit(solution)/shard_map/ppermute | solution.py:1380
  549.7 9.2 %collective-permute-start.26 = (bf16[8,48,128]{2,1,0:T(8,128)(2,1)}, bf16[8,48,128]{2,1,0:T(8,128)(2,1)S(1)}, u32[]{:S(2)}, u32[]{:S(2)}) collective-permute-start(bf16[8,48,128]{2,1,0:T(8,128)(2,1)} %combine.3.refs_5_), channel_id=1, source_target_pairs={{0,24},{8,0},{16,8},{24,16},{1,25},{9,1},{17,9},{25,17},{2,26},{10... | collective-permute-start | bytes 294920 | tf_op jit(solution)/shard_map/ppermute | solution.py:1380
  552.5 11.2 %collective-permute-start.25 = (bf16[8,48,128]{2,1,0:T(8,128)(2,1)}, bf16[8,48,128]{2,1,0:T(8,128)(2,1)S(1)}, u32[]{:S(2)}, u32[]{:S(2)}) collective-permute-start(bf16[8,48,128]{2,1,0:T(8,128)(2,1)} %combine.3.refs_5_), channel_id=1, source_target_pairs={{0,16},{8,24},{16,0},{24,8},{1,17},{9,25},{17,1},{25,9},{2,18},{10... | collective-permute-start | bytes 294920 | tf_op jit(solution)/shard_map/ppermute | solution.py:1380
  553.6 10.1 %collective-permute-start.24 = (bf16[8,48,128]{2,1,0:T(8,128)(2,1)}, bf16[8,48,128]{2,1,0:T(8,128)(2,1)S(1)}, u32[]{:S(2)}, u32[]{:S(2)}) collective-permute-start(bf16[8,48,128]{2,1,0:T(8,128)(2,1)} %combine.3.refs_5_), channel_id=1, source_target_pairs={{0,8},{8,16},{16,24},{24,0},{1,9},{9,17},{17,25},{25,1},{2,10},{10... | collective-permute-start | bytes 294920 | tf_op jit(solution)/shard_map/ppermute | solution.py:1380
  (37 other events, 554.1 us)
Sparse Core Ops, SparseCore 0:
  15.2 88.8 all-gather.3
  106.6 108.9 all-gather.5
  217.5 63.7 all-gather.7

commit v10 on v9

--- a/solution.py
+++ b/solution.py
@@ -18,7 +18,6 @@
 SCALE = HEAD_DIM ** (-0.5)
 EXP_SCALE = SCALE * math.log2(math.e)
 LN2 = math.log(2.0)
-HIGHEST = lax.Precision.HIGHEST
 F32 = jnp.float32
 BF16 = jnp.bfloat16
 VMEM_LIMIT = 60 * 1024 * 1024
@@ -780,7 +779,6 @@
             table_ref[at : at + RANK, :] = added([ref[:, cols] for ref in each])
             at += RANK
     table_ref[at:, :] = jnp.zeros((table_ref.shape[0] - at, width), F32)
-    context = ctx_ref[...].astype(F32)
     for accs, factor, rank_ref, number, at in (
         (dk_refs, LN2, rk_ref, 9, 10),
         (dv_refs, 1.0, rv_ref, 10, 12),
@@ -794,19 +792,10 @@
             ctx_s[:, tile(pair)] = low if held is None else low + held
             held = out[:, 128:]
         ctx_s[:, tile(PAIRS)] = held
-        grad_kv = ctx_s[...]
-        grad_rank = lax.dot_general(
-            grad_kv, ad_ref[2 * number + 1].astype(F32), (((1,), (1,)), ((), ())),
-            precision=HIGHEST, preferred_element_type=F32,
-        )
-        table_ref[block_rows(at), :] = lax.dot_general(
-            grad_rank, context, (((0,), (0,)), ((), ())),
-            precision=HIGHEST, preferred_element_type=F32,
-        )
-        table_ref[block_rows(at + 1), :] = lax.dot_general(
-            rank_ref[...].astype(F32), grad_kv, (((0,), (0,)), ((), ())),
-            precision=HIGHEST, preferred_element_type=F32,
-        )
+        grad_kv = ctx_s[...].astype(BF16)
+        grad_rank = nt(grad_kv, ad_ref[2 * number + 1]).astype(BF16)
+        table_ref[block_rows(at), :] = tn(grad_rank, ctx_ref[...])
+        table_ref[block_rows(at + 1), :] = tn(rank_ref[...], grad_kv)
     pack_columns(table_ref, packed_ref, clips)
 
 

time: 582 us -> 580 us (level)
  transfers between devices with their start and end apart: 33 -> 33, of which waited for: 8 -> 9; matrix products, arithmetic and copies ran while one was open for 6% -> 6% of each run, Pallas kernels for 52% -> 52%
where the time goes in v10:
time: 580 us; the launch traced here: 574 us
  Pallas kernels  361 us (62%)
  waiting for transfers between devices  82.3 us (14%)
  starting transfers between devices  59.2 us (10%)
  local copies, waits for them, and re-layouts  34 us (6%)
  between operations  15.4 us (3%)
  other arithmetic  12.4 us (2%)
  blocking collectives  9.63 us (2%)
    pallas_call x2, Pallas kernels, run_cross_temporal_backward(): pl.pallas_call(body, grid=(groups,), in_specs=[pl.BlockSpec((own_frames,...  84.4 us
    ppermute x24, waiting for transfers between devices, send(): lax.ppermute(array, axis, [(i, (i + shift) % size) for i in range(size)])  47.9 us
    ppermute x24, starting transfers between devices, send(): lax.ppermute(array, axis, [(i, (i + shift) % size) for i in range(size)])  46.7 us
    pallas_call x1, Pallas kernels, run_feed_forward(): pl.pallas_call(body, grid=(tokens // ROWS,), in_specs=[in_smem(), rows, r...  43.1 us
    pallas_call x1, Pallas kernels, run_spatial_backward(): pl.pallas_call(body, grid=(count,), in_specs=[in_smem()] + [pl.BlockSpec(...  34.4 us
    pallas_call x2, Pallas kernels, run_feed_forward_out(): pl.pallas_call(body, grid=(steps,), in_specs=[in_smem(), pl.BlockSpec((RO...  33.2 us
    pallas_call x1, Pallas kernels, run_temporal_forward(): pl.pallas_call(body, grid=(groups,), in_specs=[pl.BlockSpec((own_frames,...  32.6 us
    pallas_call x1, Pallas kernels, run_spatial_forward(): pl.pallas_call(spatial_forward, grid=(frames,), in_specs=[in_smem(), row_...  31.6 us
  transfers between devices with their start and end apart: 33, of which 9 were waited for; matrix products, arithmetic and copies ran while one was open for 6% of the time, Pallas kernels for 52%

profile of v10, /device:TPU:0, one launch (start us, length us, event | category | flops | bytes accessed | tf_op | source)
XLA Modules:
  0.0 573.8 jit_solution(11329415557510751250)
XLA Ops:
  18.6 9.6 %all_to_all.23 = s32[8,1,1]{2,1,0:T(1,128)S(1)} all-to-all(s32[8,1,1]{2,1,0:T(1,128)S(1)} %broadcast_in_dim.23), channel_id=1, replica_groups=mesh['seq'=4,'fsdp'=8] {'fsdp'}, dimensions={0} | all-to-all | bytes 64 | tf_op jit(solution)/shard_map/all_to_all | solution.py:1354
  32.6 5.2 reshape_squeeze.7
  41.1 4.7 reshape.53
  52.3 3.6 collective-permute-start.2
  59.0 19.6 %all-to-all-done.1.refs_0_ = bf16[8,624,128]{2,1,0:T(8,128)(2,1)S(1)} async-done(((bf16[8,624,128]{2,1,0:T(8,128)(2,1)}), bf16[8,624,128]{2,1,0:T(8,128)(2,1)S(1)}, u32[]{:S(2)}, u32[]{:S(2)}) %all-to-all-start.1) | async-done | bytes 1277984 | tf_op jit(solution)/shard_map/all_to_all | solution.py:1354
  79.7 4.7 unpick.1.ad_ref.refs_6_.refs_22_.refs_16_.refs_19_.refs_12_
  86.2 20.9 %collective-permute-done.1 = bf16[4,64,1152]{2,1,0:T(8,128)(2,1)S(1)} collective-permute-done((bf16[4,64,1152]{2,1,0:T(8,128)(2,1)}, bf16[4,64,1152]{2,1,0:T(8,128)(2,1)S(1)}, u32[]{:S(2)}, u32[]{:S(2)}) %collective-permute-start.1) | collective-permute-done | bytes 589856 | tf_op jit(solution)/shard_map/ppermute | solution.py:1369
  112.7 31.6 %spatial_forward.1 = (bf16[4,64,1152]{2,1,0:T(8,128)(2,1)}, bf16[4,64,1152]{2,1,0:T(8,128)(2,1)}, bf16[4,64,1152]{2,1,0:T(8,128)(2,1)}, bf16[4,64,1152]{2,1,0:T(...) custom-call(s32[1]{0:T(128)} %bitcast.seq_ref.refs_0_, ...), custom_call_target="tpu_custom_call" | custom-call | flops 3397386240 | bytes 7500000 | tf_op jit(solution)/shard_map/spatial_forward/pallas_call | solution.py:907
  154.4 15.8 %feed_forward_grad.2.refs_3_ = bf16[2,1024,1152]{2,1,0:T(8,128)(2,1)} custom-call(s32[3]{0:T(128)} %pad_add_fusion.1.refs_0_, bf16[1024,1152]{1,0:T(8,128)(2,1)} %bitcast.47, f32[6,1152]{1,0:T(8,128)} %bitcast.62, bf16[10,16,1152]{2,1,0:T(8,128)(2,1)} %slice.48.refs_3_.refs_6_.refs_5_, bf16[576,1152]{1,0:T(8,128)(2,1)} %copy-done.2, ...), custom_call_target="tpu_custom_call" | custom-call | flops 1358954496 | bytes 5000000 | tf_op jit(solution)/shard_map/feed_forward_grad/pallas_call | solution.py:1022
  170.2 20.6 %collective-permute-done.6.refs_2_ = bf16[4,64,1152]{2,1,0:T(8,128)(2,1)} collective-permute-done((bf16[4,64,1152]{2,1,0:T(8,128)(2,1)}, bf16[4,64,1152]{2,1,0:T(8,128)(2,1)}, u32[]{:S(2)}, u32[]{:S(2)}) %collective-permute-start.6) | collective-permute-done | bytes 589856 | tf_op jit(solution)/shard_map/ppermute | solution.py:1369
  190.8 13.7 %collective-permute-start.8 = (bf16[576,1152]{1,0:T(8,128)(2,1)S(1)}, bf16[576,1152]{1,0:T(8,128)(2,1)S(1)}, u32[]{:S(2)}, u32[]{:S(2)}) collective-permute-start(bf16[576,1152]{1,0:T(8,128)(2,1)S(1)} %copy-done.3), channel_id=1, source_target_pairs={{0,24},{8,0},{16,8},{24,16},{1,25},{9,1},{17,9},{25,17},{2,26},{10... | collective-permute-start | bytes 3981320 | tf_op jit(solution)/shard_map/ppermute | solution.py:1369
  205.3 10.3 %all-gather.6.cloned.1.call-done.refs_7_.w_hbm.refs_23_ = bf16[8,1152,1152]{2,1,0:T(8,128)(2,1)} async-done(((bf16[8,144,1152]{2,1,0:T(8,128)(2,1)}), bf16[8,1152,1152]{2,1,0:T(8,128)(2,1)}) %all-gather.6.cloned.1.call-update) | async-done | bytes 21233680 | tf_op jit(solution)/shard_map/all_gather | solution.py:1364
  215.6 32.6 %temporal_forward.1 = (bf16[16,64,1152]{2,1,0:T(8,128)(2,1)}, bf16[16,64,1152]{2,1,0:T(8,128)(2,1)}, bf16[16,64,1152]{2,1,0:T(8,128)(2,1)}, bf16[16,64,1152]{2,1...) custom-call(bf16[4,64,1152]{2,1,0:T(8,128)(2,1)} %get-tuple-element., ...), custom_call_target="tpu_custom_call" | custom-call | flops 212336640 | bytes 468750 | tf_op jit(solution)/shard_map/temporal_forward/pallas_call | solution.py:953
  248.2 24.7 %cross_forward.1 = (bf16[16,64,1152]{2,1,0:T(8,128)(2,1)}, bf16[16,64,1152]{2,1,0:T(8,128)(2,1)}, f32[4,16,256]{2,1,0:T(8,128)}, bf16[4,256,16]{2,1,0:T(8,128)(2...) custom-call(f32[16,64,1152]{2,1,0:T(8,128)} %get-tuple-element.135.x, ...), custom_call_target="tpu_custom_call" | custom-call | flops 169869312 | bytes 468750 | tf_op jit(solution)/shard_map/cross_forward/pallas_call | solution.py:993
  274.2 3.8 collective-permute-done.10.refs_6_.refs_12_
  279.1 13.6 %feed_forward_grad.3.refs_4_ = bf16[2,1024,1152]{2,1,0:T(8,128)(2,1)} custom-call(s32[3]{0:T(128)} %pad_add_fusion.2.refs_0_, bf16[1024,1152]{1,0:T(8,128)(2,1)} %bitcast.48, f32[6,1152]{1,0:T(8,128)} %bitcast.64, bf16[10,16,1152]{2,1,0:T(8,128)(2,1)} %slice.48.refs_3_.refs_6_.refs_5_, bf16[576,1152]{1,0:T(8,128)(2,1)} %copy-done.6, ...), custom_call_target="tpu_custom_call" | custom-call | flops 1358954496 | bytes 5000000 | tf_op jit(solution)/shard_map/feed_forward_grad/pallas_call | solution.py:1022
  292.7 43.1 %feed_forward.1 = (bf16[1024,4608]{1,0:T(8,128)(2,1)}, f32[1024,1152]{1,0:T(8,128)}, f32[16,1152]{1,0:T(8,128)}, f32[16,4608]{1,0:T(8,128)}) custom-call(s32[5]{0:T(128)} %copy-done.33, f32[1024,1152]{1,0:T(8,128)} %bitcast.52, bf16[1024,1152]{1,0:T(8,128)(2,1)} %bitcast.49, bf16[2,1024,1152]{2,1,0:T(8,128)(2,1)} %feed_forward_grad.2.refs_3_, ...), custom_call_target="tpu_custom_call" | custom-call | flops 5435817984 | bytes 12500000 | tf_op jit(solution)/shard_map/feed_forward/pallas_call | solution.py:1051
  335.9 16.5 %feed_forward_out.2 = (bf16[256,1152]{1,0:T(8,128)(2,1)}, bf16[256,1152]{1,0:T(8,128)(2,1)}, f32[16,1152]{1,0:T(8,128)}, f32[16,4608]{1,0:T(8,128)}) custom-call(s32[5]{0:T(128)} %copy-done.33, bf16[1024,4608]{1,0:T(8,128)(2,1)} %get-tuple-element.180.refs_1_, f32[1024,1152]{1,0:T(8,128)} %bitcast.53, bf16[1024,1152]{1,0:T(8,128)(2,1)} %bitcast.50, ...), custom_call_target="tpu_custom_call" | custom-call | flops 84934656 | bytes 312500 | tf_op jit(solution)/shard_map/feed_forward_out/pallas_call | solution.py:1096
  355.9 42.1 %cross_temporal_backward.2 = (bf16[4,32,1152]{2,1,0:T(8,128)(2,1)}, bf16[4,32,1152]{2,1,0:T(8,128)(2,1)}, bf16[4,32,1152]{2,1,0:T(8,128)(2,1)}, bf16[4,32,1152]{...) custom-call(bf16[4,64,1152]{2,1,0:T(8,128)(2,1)} %get-tuple-element.131.refs_0_, ...), custom_call_target="tpu_custom_call" | custom-call | flops 148635648 | bytes 468750 | tf_op jit(solution)/shard_map/cross_temporal_backward/pallas_call | solution.py:1144
  400.7 42.2 %cross_temporal_backward.3 = (bf16[4,32,1152]{2,1,0:T(8,128)(2,1)}, bf16[4,32,1152]{2,1,0:T(8,128)(2,1)}, bf16[4,32,1152]{2,1,0:T(8,128)(2,1)}, bf16[4,32,1152]{...) custom-call(bf16[4,64,1152]{2,1,0:T(8,128)(2,1)} %get-tuple-element.131.refs_0_, ...), custom_call_target="tpu_custom_call" | custom-call | flops 148635648 | bytes 468750 | tf_op jit(solution)/shard_map/cross_temporal_backward/pallas_call | solution.py:1144
  443.0 3.7 collective-permute-start.17
  447.5 16.7 %feed_forward_out.3 = (bf16[256,1152]{1,0:T(8,128)(2,1)}, bf16[256,1152]{1,0:T(8,128)(2,1)}, f32[16,1152]{1,0:T(8,128)}, f32[16,4608]{1,0:T(8,128)}) custom-call(s32[5]{0:T(128)} %copy-done.33, bf16[1024,4608]{1,0:T(8,128)(2,1)} %get-tuple-element.180.refs_1_, f32[1024,1152]{1,0:T(8,128)} %bitcast.54, bf16[1024,1152]{1,0:T(8,128)(2,1)} %bitcast.51, ...), custom_call_target="tpu_custom_call" | custom-call | flops 84934656 | bytes 312500 | tf_op jit(solution)/shard_map/feed_forward_out/pallas_call | solution.py:1096
  464.2 7.1 %pack_early.1 = bf16[32,128,128]{2,1,0:T(8,128)(2,1)} custom-call(f32[256,1152]{1,0:T(8,128)} %get-tuple-element.163.refs_0_, f32[256,1152]{1,0:T(8,128)} %get-tuple-element.173.refs_1_, f32[8,256,256]{2,1,0:T(8,128)} %get-tuple-element.174.refs_2_, f32[8,256,256]{2,1,0:T(8,128)} %get-tuple-element.175.refs_3_, f32[8,256,256]{2,1,0:T(8,128)} %get-tuple-element.176.refs_4_, ...), custom_call_target="tpu_custom_call" | custom-call | flops 781250 | bytes 125000 | tf_op jit(solution)/shard_map/pack_early/pallas_call | solution.py:1282
  471.7 4.2 all-to-all-start.2
  475.9 3.7 collective-permute-start.20
  479.6 34.4 %spatial_backward.1 = (bf16[4,256,3584]{2,1,0:T(8,128)(2,1)}, bf16[32,48,128]{2,1,0:T(8,128)(2,1)}) custom-call(s32[1]{0:T(128)} %bitcast.seq_ref.refs_0_, bf16[4,32,1152]{2,1,0:T(8,128)(2,1)} %get-tuple-element.196.refs_1_, bf16[4,32,1152]{2,1,0:T(8,128)(2,1)} %copy-done.15, bf16[4,32,1152]{2,1,0:T(8,128)(2,1)} %copy-done.16, ...), custom_call_target="tpu_custom_call" | custom-call | flops 127401984 | bytes 312500 | tf_op jit(solution)/shard_map/spatial_backward/pallas_call | solution.py:1191
  514.0 4.0 all-to-all-start.3
  520.2 3.6 collective-permute-start.23
  524.9 19.6 %spatial_input_grad.1 = bf16[4,256,1152]{2,1,0:T(8,128)(2,1)} custom-call(s32[1]{0:T(128)} %bitcast.seq_ref.refs_0_, bf16[4,32,1152]{2,1,0:T(8,128)(2,1)} %get-tuple-element.196.refs_1_, bf16[4,32,1152]{2,1,0:T(8,128)(2,1)} %copy-done.15, bf16[4,32,1152]{2,1,0:T(8,128)(2,1)} %copy-done.16, bf16[4,32,1152]{2,1,0:T(8,128)(2,1)} %copy-done.17, ...), custom_call_target="tpu_custom_call" | custom-call | flops 127401984 | bytes 312500 | tf_op jit(solution)/shard_map/spatial_input_grad/pallas_call | solution.py:1228
  551.1 4.0 put_in_place.1
  556.4 4.8 collective-permute-done.25.refs_7_
  562.5 4.5 assemble.1
  (152 shorter events, 69.1 us)
Async XLA Ops:
  7.2 99.9 %all-gather.4.cloned.1.call-start = ((), (), s32[]{:S(2)}) async-start(), calls=%async_computation.4 | async-start | bytes 14929920 | tf_op jit(solution)/shard_map/all_gather | solution.py:1364
  15.1 200.5 %all-gather.6.cloned.1.call-start = ((), (), s32[]{:S(2)}) async-start(), calls=%async_computation.5 | async-start | bytes 23887872 | tf_op jit(solution)/shard_map/all_gather | solution.py:1364
  17.8 274.9 %all-gather.8.cloned.1.call-start = ((), (), s32[]{:S(2)}) async-start(), calls=%async_computation.6 | async-start | bytes 11943936 | tf_op jit(solution)/shard_map/all_gather | solution.py:1364
  45.8 32.9 %all-to-all-start.1 = ((bf16[8,624,128]{2,1,0:T(8,128)(2,1)}), bf16[8,624,128]{2,1,0:T(8,128)(2,1)S(1)}, u32[]{:S(2)}, u32[]{:S(2)}) async-start(bf16[8,624,128]{2,1,0:T(8,128)(2,1)} %pick.1), calls=%async_computation.1 | async-start | bytes 2555904 | tf_op jit(solution)/shard_map/all_to_all | solution.py:1354
  52.3 33.8 %collective-permute-start.2 = (bf16[4,64,1152]{2,1,0:T(8,128)(2,1)}, bf16[4,64,1152]{2,1,0:T(8,128)(2,1)S(1)}, u32[]{:S(2)}, u32[]{:S(2)}) collective-permute-start(bf16[4,64,1152]{2,1,0:T(8,128)(2,1)} %get-tuple-element.233), channel_id=1, source_target_pairs={{0,24},{8,0},{16,8},{24,16},{1,25},{9,1},{17,9},{25,17},{2,26},{10... | collective-permute-start | bytes 1769480 | tf_op jit(solution)/shard_map/ppermute | solution.py:1369
  55.9 51.1 %collective-permute-start.1 = (bf16[4,64,1152]{2,1,0:T(8,128)(2,1)}, bf16[4,64,1152]{2,1,0:T(8,128)(2,1)S(1)}, u32[]{:S(2)}, u32[]{:S(2)}) collective-permute-start(bf16[4,64,1152]{2,1,0:T(8,128)(2,1)} %get-tuple-element.234), channel_id=1, source_target_pairs={{0,16},{8,24},{16,0},{24,8},{1,17},{9,25},{17,1},{25,9},{2,18},{10... | collective-permute-start | bytes 1769480 | tf_op jit(solution)/shard_map/ppermute | solution.py:1369
  55.9 51.1 %collective-permute-start = (bf16[4,64,1152]{2,1,0:T(8,128)(2,1)}, bf16[4,64,1152]{2,1,0:T(8,128)(2,1)}, u32[]{:S(2)}, u32[]{:S(2)}) collective-permute-start(bf16[4,64,1152]{2,1,0:T(8,128)(2,1)} %get-tuple-element.235), channel_id=1, source_target_pairs={{0,8},{8,16},{16,24},{24,0},{1,9},{9,17},{17,25},{25,1},{2,10},{10... | collective-permute-start | bytes 1769480 | tf_op jit(solution)/shard_map/ppermute | solution.py:1369
  111.0 36.4 %collective-permute-start.3 = (bf16[576,1152]{1,0:T(8,128)(2,1)S(1)}, bf16[576,1152]{1,0:T(8,128)(2,1)S(1)}, u32[]{:S(2)}, u32[]{:S(2)}) collective-permute-start(bf16[576,1152]{1,0:T(8,128)(2,1)S(1)} %get-tuple-element.137.refs_4_.refs_6_), channel_id=1, source_target_pairs={{0,8},{8,16},{16,24},{24,0},{1,9},{9,17},{17,25},{25,1},{2,10},{10... | collective-permute-start | bytes 3981320 | tf_op jit(solution)/shard_map/ppermute | solution.py:1369
  147.4 5.9 %collective-permute-start.4 = (bf16[576,1152]{1,0:T(8,128)(2,1)S(1)}, bf16[576,1152]{1,0:T(8,128)(2,1)S(1)}, u32[]{:S(2)}, u32[]{:S(2)}) collective-permute-start(bf16[576,1152]{1,0:T(8,128)(2,1)S(1)} %collective-permute-done.3.refs_5_.refs_7_), channel_id=1, source_target_pairs={{0,1},{1,0},{2,3},{3,2},{4,5},{5,4},{6,7},{7,6},{8,9},{9,8},{10,11... | collective-permute-start | bytes 3981320 | tf_op jit(solution)/shard_map/ppermute | solution.py:1398
  147.4 22.7 %collective-permute-start.5 = (bf16[4,64,1152]{2,1,0:T(8,128)(2,1)}, bf16[4,64,1152]{2,1,0:T(8,128)(2,1)S(1)}, u32[]{:S(2)}, u32[]{:S(2)}) collective-permute-start(bf16[4,64,1152]{2,1,0:T(8,128)(2,1)} %get-tuple-element.128), channel_id=1, source_target_pairs={{0,8},{8,16},{16,24},{24,0},{1,9},{9,17},{17,25},{25,1},{2,10},{10... | collective-permute-start | bytes 1769480 | tf_op jit(solution)/shard_map/ppermute | solution.py:1369
  150.0 40.8 %collective-permute-start.6 = (bf16[4,64,1152]{2,1,0:T(8,128)(2,1)}, bf16[4,64,1152]{2,1,0:T(8,128)(2,1)}, u32[]{:S(2)}, u32[]{:S(2)}) collective-permute-start(bf16[4,64,1152]{2,1,0:T(8,128)(2,1)} %get-tuple-element.129), channel_id=1, source_target_pairs={{0,16},{8,24},{16,0},{24,8},{1,17},{9,25},{17,1},{25,9},{2,18},{10... | collective-permute-start | bytes 1769480 | tf_op jit(solution)/shard_map/ppermute | solution.py:1369
  151.7 39.1 %collective-permute-start.7 = (bf16[4,64,1152]{2,1,0:T(8,128)(2,1)}, bf16[4,64,1152]{2,1,0:T(8,128)(2,1)}, u32[]{:S(2)}, u32[]{:S(2)}) collective-permute-start(bf16[4,64,1152]{2,1,0:T(8,128)(2,1)} %get-tuple-element.130), channel_id=1, source_target_pairs={{0,24},{8,0},{16,8},{24,16},{1,25},{9,1},{17,9},{25,17},{2,26},{10... | collective-permute-start | bytes 1769480 | tf_op jit(solution)/shard_map/ppermute | solution.py:1369
  190.8 82.1 %collective-permute-start.8 = (bf16[576,1152]{1,0:T(8,128)(2,1)S(1)}, bf16[576,1152]{1,0:T(8,128)(2,1)S(1)}, u32[]{:S(2)}, u32[]{:S(2)}) collective-permute-start(bf16[576,1152]{1,0:T(8,128)(2,1)S(1)} %copy-done.3), channel_id=1, source_target_pairs={{0,24},{8,0},{16,8},{24,16},{1,25},{9,1},{17,9},{25,17},{2,26},{10... | collective-permute-start | bytes 3981320 | tf_op jit(solution)/shard_map/ppermute | solution.py:1369
  204.5 68.4 %collective-permute-start.9 = (bf16[576,1152]{1,0:T(8,128)(2,1)}, bf16[576,1152]{1,0:T(8,128)(2,1)}, u32[]{:S(2)}, u32[]{:S(2)}) collective-permute-start(bf16[576,1152]{1,0:T(8,128)(2,1)} %copy-done.4), channel_id=1, source_target_pairs={{0,8},{8,16},{16,24},{24,0},{1,9},{9,17},{17,25},{25,1},{2,10},{10... | collective-permute-start | bytes 3981320 | tf_op jit(solution)/shard_map/ppermute | solution.py:1369
  273.3 5.2 collective-permute-start.11
  352.4 48.3 %collective-permute-start.13 = (bf16[4,64,1152]{2,1,0:T(8,128)(2,1)}, bf16[4,64,1152]{2,1,0:T(8,128)(2,1)S(1)}, u32[]{:S(2)}, u32[]{:S(2)}) collective-permute-start(bf16[4,64,1152]{2,1,0:T(8,128)(2,1)} %bitcast.84), channel_id=1, source_target_pairs={{0,8},{8,16},{16,24},{24,0},{1,9},{9,17},{17,25},{25,1},{2,10},{10... | collective-permute-start | bytes 1769480 | tf_op jit(solution)/shard_map/ppermute | solution.py:1369
  353.5 47.2 %collective-permute-start.12 = (bf16[4,64,1152]{2,1,0:T(8,128)(2,1)}, bf16[4,64,1152]{2,1,0:T(8,128)(2,1)S(1)}, u32[]{:S(2)}, u32[]{:S(2)}) collective-permute-start(bf16[4,64,1152]{2,1,0:T(8,128)(2,1)} %bitcast.83), channel_id=1, source_target_pairs={{0,16},{8,24},{16,0},{24,8},{1,17},{9,25},{17,1},{25,9},{2,18},{10... | collective-permute-start | bytes 1769480 | tf_op jit(solution)/shard_map/ppermute | solution.py:1369
  398.1 48.8 %collective-permute-start.14 = (bf16[4,32,1152]{2,1,0:T(8,128)(2,1)}, bf16[4,32,1152]{2,1,0:T(8,128)(2,1)S(1)}, u32[]{:S(2)}, u32[]{:S(2)}) collective-permute-start(bf16[4,32,1152]{2,1,0:T(8,128)(2,1)} %get-tuple-element.170), channel_id=1, source_target_pairs={{0,24},{8,0},{16,8},{24,16},{1,25},{9,1},{17,9},{25,17},{2,26},{10... | collective-permute-start | bytes 884744 | tf_op jit(solution)/shard_map/ppermute | solution.py:1369
  399.5 47.9 %collective-permute-start.15 = (bf16[4,32,1152]{2,1,0:T(8,128)(2,1)}, bf16[4,32,1152]{2,1,0:T(8,128)(2,1)S(1)}, u32[]{:S(2)}, u32[]{:S(2)}) collective-permute-start(bf16[4,32,1152]{2,1,0:T(8,128)(2,1)} %get-tuple-element.171), channel_id=1, source_target_pairs={{0,16},{8,24},{16,0},{24,8},{1,17},{9,25},{17,1},{25,9},{2,18},{10... | collective-permute-start | bytes 884744 | tf_op jit(solution)/shard_map/ppermute | solution.py:1369
  400.5 47.0 %collective-permute-start.16 = (bf16[4,32,1152]{2,1,0:T(8,128)(2,1)}, bf16[4,32,1152]{2,1,0:T(8,128)(2,1)S(1)}, u32[]{:S(2)}, u32[]{:S(2)}) collective-permute-start(bf16[4,32,1152]{2,1,0:T(8,128)(2,1)} %get-tuple-element.172), channel_id=1, source_target_pairs={{0,8},{8,16},{16,24},{24,0},{1,9},{9,17},{17,25},{25,1},{2,10},{10... | collective-permute-start | bytes 884744 | tf_op jit(solution)/shard_map/ppermute | solution.py:1369
  443.0 28.3 %collective-permute-start.17 = (bf16[4,32,1152]{2,1,0:T(8,128)(2,1)}, bf16[4,32,1152]{2,1,0:T(8,128)(2,1)S(1)}, u32[]{:S(2)}, u32[]{:S(2)}) collective-permute-start(bf16[4,32,1152]{2,1,0:T(8,128)(2,1)} %get-tuple-element.193), channel_id=1, source_target_pairs={{0,24},{8,0},{16,8},{24,16},{1,25},{9,1},{17,9},{25,17},{2,26},{10... | collective-permute-start | bytes 884744 | tf_op jit(solution)/shard_map/ppermute | solution.py:1369
  446.7 25.0 %collective-permute-start.18 = (bf16[4,32,1152]{2,1,0:T(8,128)(2,1)}, bf16[4,32,1152]{2,1,0:T(8,128)(2,1)S(1)}, u32[]{:S(2)}, u32[]{:S(2)}) collective-permute-start(bf16[4,32,1152]{2,1,0:T(8,128)(2,1)} %get-tuple-element.194), channel_id=1, source_target_pairs={{0,16},{8,24},{16,0},{24,8},{1,17},{9,25},{17,1},{25,9},{2,18},{10... | collective-permute-start | bytes 884744 | tf_op jit(solution)/shard_map/ppermute | solution.py:1369
  446.8 24.8 %collective-permute-start.19 = (bf16[4,32,1152]{2,1,0:T(8,128)(2,1)}, bf16[4,32,1152]{2,1,0:T(8,128)(2,1)S(1)}, u32[]{:S(2)}, u32[]{:S(2)}) collective-permute-start(bf16[4,32,1152]{2,1,0:T(8,128)(2,1)} %get-tuple-element.195), channel_id=1, source_target_pairs={{0,8},{8,16},{16,24},{24,0},{1,9},{9,17},{17,25},{25,1},{2,10},{10... | collective-permute-start | bytes 884744 | tf_op jit(solution)/shard_map/ppermute | solution.py:1369
  471.7 42.3 %all-to-all-start.2 = ((bf16[32,128,128]{2,1,0:T(8,128)(2,1)}), bf16[32,128,128]{2,1,0:T(8,128)(2,1)S(1)}, u32[]{:S(2)}, u32[]{:S(2)}) async-start(bf16[32,128,128]{2,1,0:T(8,128)(2,1)} %pack_early.1), calls=%async_computation.2 | async-start | bytes 2097152 | tf_op jit(solution)/shard_map/all_to_all | solution.py:1354
  475.9 38.1 %collective-permute-start.20 = (bf16[4,64,1152]{2,1,0:T(8,128)(2,1)}, bf16[4,64,1152]{2,1,0:T(8,128)(2,1)S(1)}, u32[]{:S(2)}, u32[]{:S(2)}) collective-permute-start(bf16[4,64,1152]{2,1,0:T(8,128)(2,1)} %bitcast.82), channel_id=1, source_target_pairs={{0,24},{8,0},{16,8},{24,16},{1,25},{9,1},{17,9},{25,17},{2,26},{10... | collective-permute-start | bytes 1769480 | tf_op jit(solution)/shard_map/ppermute | solution.py:1369
  514.0 30.6 %all-to-all-start.3 = ((bf16[32,48,128]{2,1,0:T(8,128)(2,1)}), bf16[32,48,128]{2,1,0:T(8,128)(2,1)S(1)}, u32[]{:S(2)}, u32[]{:S(2)}) async-start(bf16[32,48,128]{2,1,0:T(8,128)(2,1)} %get-tuple-element.221), calls=%async_computation.3 | async-start | bytes 786432 | tf_op jit(solution)/shard_map/all_to_all | solution.py:1354
  520.2 30.9 %collective-permute-start.23 = (bf16[8,128,128]{2,1,0:T(8,128)(2,1)}, bf16[8,128,128]{2,1,0:T(8,128)(2,1)S(1)}, u32[]{:S(2)}, u32[]{:S(2)}) collective-permute-start(bf16[8,128,128]{2,1,0:T(8,128)(2,1)} %combine.2.refs_1_), channel_id=1, source_target_pairs={{0,24},{8,0},{16,8},{24,16},{1,25},{9,1},{17,9},{25,17},{2,26},{10... | collective-permute-start | bytes 786440 | tf_op jit(solution)/shard_map/ppermute | solution.py:1369
  523.8 32.5 %collective-permute-start.22 = (bf16[8,128,128]{2,1,0:T(8,128)(2,1)}, bf16[8,128,128]{2,1,0:T(8,128)(2,1)S(1)}, u32[]{:S(2)}, u32[]{:S(2)}) collective-permute-start(bf16[8,128,128]{2,1,0:T(8,128)(2,1)} %combine.2.refs_1_), channel_id=1, source_target_pairs={{0,16},{8,24},{16,0},{24,8},{1,17},{9,25},{17,1},{25,9},{2,18},{10... | collective-permute-start | bytes 786440 | tf_op jit(solution)/shard_map/ppermute | solution.py:1369
  523.8 32.5 %collective-permute-start.21 = (bf16[8,128,128]{2,1,0:T(8,128)(2,1)}, bf16[8,128,128]{2,1,0:T(8,128)(2,1)S(1)}, u32[]{:S(2)}, u32[]{:S(2)}) collective-permute-start(bf16[8,128,128]{2,1,0:T(8,128)(2,1)} %combine.2.refs_1_), channel_id=1, source_target_pairs={{0,8},{8,16},{16,24},{24,0},{1,9},{9,17},{17,25},{25,1},{2,10},{10... | collective-permute-start | bytes 786440 | tf_op jit(solution)/shard_map/ppermute | solution.py:1369
  547.2 9.2 %collective-permute-start.26 = (bf16[8,48,128]{2,1,0:T(8,128)(2,1)}, bf16[8,48,128]{2,1,0:T(8,128)(2,1)S(1)}, u32[]{:S(2)}, u32[]{:S(2)}) collective-permute-start(bf16[8,48,128]{2,1,0:T(8,128)(2,1)} %combine.3.refs_5_), channel_id=1, source_target_pairs={{0,24},{8,0},{16,8},{24,16},{1,25},{9,1},{17,9},{25,17},{2,26},{10... | collective-permute-start | bytes 294920 | tf_op jit(solution)/shard_map/ppermute | solution.py:1369
  550.0 11.2 %collective-permute-start.25 = (bf16[8,48,128]{2,1,0:T(8,128)(2,1)}, bf16[8,48,128]{2,1,0:T(8,128)(2,1)S(1)}, u32[]{:S(2)}, u32[]{:S(2)}) collective-permute-start(bf16[8,48,128]{2,1,0:T(8,128)(2,1)} %combine.3.refs_5_), channel_id=1, source_target_pairs={{0,16},{8,24},{16,0},{24,8},{1,17},{9,25},{17,1},{25,9},{2,18},{10... | collective-permute-start | bytes 294920 | tf_op jit(solution)/shard_map/ppermute | solution.py:1369
  551.1 10.1 %collective-permute-start.24 = (bf16[8,48,128]{2,1,0:T(8,128)(2,1)}, bf16[8,48,128]{2,1,0:T(8,128)(2,1)S(1)}, u32[]{:S(2)}, u32[]{:S(2)}) collective-permute-start(bf16[8,48,128]{2,1,0:T(8,128)(2,1)} %combine.3.refs_5_), channel_id=1, source_target_pairs={{0,8},{8,16},{16,24},{24,0},{1,9},{9,17},{17,25},{25,1},{2,10},{10... | collective-permute-start | bytes 294920 | tf_op jit(solution)/shard_map/ppermute | solution.py:1369
  (37 other events, 553.8 us)
Sparse Core Ops, SparseCore 0:
  15.2 88.8 all-gather.3
  106.6 108.9 all-gather.5
  217.5 63.7 all-gather.7
